TPU v7x, 32 devices: a whole 2x2x4 slice. The times are simulated.
32 devices in a mesh: rep: 4 (over x, core), dp: 2 (over y), fsdp: 4 (over z).
Axes of the slice: x: 2, y: 2, z: 4, core: 2. Of those that a mesh axis runs over, the one named last changes fastest.
Arguments:
- images: bfloat16 [96, 256, 1152], P(('rep', 'dp', 'fsdp')), may hold values from -6 to 6
- cotangent: bfloat16 [96, 256, 1152], P(('rep', 'dp', 'fsdp')), may hold values from -6 to 6
- counts: int32 [32], P(('rep', 'dp', 'fsdp')), may hold values from 2 to 3, as said below
- timesteps: int32 [96], P(('rep', 'dp', 'fsdp')), may hold values from 0 to 999
- labels: int32 [96], P(('rep', 'dp', 'fsdp')), may hold values from 0 to 1000
- label_table: bfloat16 [1001, 1152], replicated, may hold values from -6 to 6
- step_count: int32 [1], replicated, may hold values from 2 to 20
- w_ada: float32 [1152, 6912], P('fsdp'), may hold values from -0.1875 to 0.1875
- w_qkv: float32 [1152, 3456], P('fsdp'), may hold values from -0.1875 to 0.1875
- w_proj: float32 [1152, 1152], P('fsdp'), may hold values from -1 to 1
- w_fc1: float32 [1152, 4608], P('fsdp'), may hold values from -0.1875 to 0.1875
- w_fc2: float32 [4608, 1152], P('fsdp'), may hold values from -0.09375 to 0.09375
- biases: float32 [16128], P('fsdp'), may hold values from -0.9 to 0.9
- first_ada: float32 [4, 1152, 6912], P('rep', 'fsdp'), may hold values from -40 to 40
- first_qkv: float32 [4, 1152, 3456], P('rep', 'fsdp'), may hold values from -28 to 28
- first_proj: float32 [4, 1152, 1152], P('rep', 'fsdp'), may hold values from -8 to 8
- first_fc1: float32 [4, 1152, 4608], P('rep', 'fsdp'), may hold values from -16 to 16
- first_fc2: float32 [4, 4608, 1152], P('rep', 'fsdp'), may hold values from -32 to 32
- first_bias: float32 [4, 16128], P('rep', 'fsdp'), may hold values from -32 to 32
- second_ada: float32 [4, 1152, 6912], P('rep', 'fsdp'), may hold values from 92.16 to 1505.28
- second_qkv: float32 [4, 1152, 3456], P('rep', 'fsdp'), may hold values from 49.152 to 774.144
- second_proj: float32 [4, 1152, 1152], P('rep', 'fsdp'), may hold values from 4.3008 to 67.584
- second_fc1: float32 [4, 1152, 4608], P('rep', 'fsdp'), may hold values from 13.5168 to 215.04
- second_fc2: float32 [4, 4608, 1152], P('rep', 'fsdp'), may hold values from 67.584 to 1075.2
- second_bias: float32 [4, 16128], P('rep', 'fsdp'), may hold values from 67.584 to 1075.2
- outer_ada: float32 [1152, 6912], P('fsdp'), may hold values from -0.09375 to 0.09375
- outer_qkv: float32 [1152, 3456], P('fsdp'), may hold values from -0.09375 to 0.09375
- outer_proj: float32 [1152, 1152], P('fsdp'), may hold values from -0.5 to 0.5
- outer_fc1: float32 [1152, 4608], P('fsdp'), may hold values from -0.09375 to 0.09375
- outer_fc2: float32 [4608, 1152], P('fsdp'), may hold values from -0.046875 to 0.046875
- outer_bias: float32 [16128], P('fsdp'), may hold values from -0.5 to 0.5
Outputs:
- output: bfloat16 [96, 256, 1152], P(('rep', 'dp', 'fsdp'))
- input_grad: bfloat16 [96, 256, 1152], P(('rep', 'dp', 'fsdp'))
- grad_ada: float32 [4, 1152, 6912], P('rep', 'fsdp')
- grad_qkv: float32 [4, 1152, 3456], P('rep', 'fsdp')
- grad_proj: float32 [4, 1152, 1152], P('rep', 'fsdp')
- grad_fc1: float32 [4, 1152, 4608], P('rep', 'fsdp')
- grad_fc2: float32 [4, 4608, 1152], P('rep', 'fsdp')
- grad_bias: float32 [4, 16128], P('rep', 'fsdp')
- first_next_ada: float32 [4, 1152, 6912], P('rep', 'fsdp')
- first_next_qkv: float32 [4, 1152, 3456], P('rep', 'fsdp')
- first_next_proj: float32 [4, 1152, 1152], P('rep', 'fsdp')
- first_next_fc1: float32 [4, 1152, 4608], P('rep', 'fsdp')
- first_next_fc2: float32 [4, 4608, 1152], P('rep', 'fsdp')
- first_next_bias: float32 [4, 16128], P('rep', 'fsdp')
- second_next_ada: float32 [4, 1152, 6912], P('rep', 'fsdp')
- second_next_qkv: float32 [4, 1152, 3456], P('rep', 'fsdp')
- second_next_proj: float32 [4, 1152, 1152], P('rep', 'fsdp')
- second_next_fc1: float32 [4, 1152, 4608], P('rep', 'fsdp')
- second_next_fc2: float32 [4, 4608, 1152], P('rep', 'fsdp')
- second_next_bias: float32 [4, 16128], P('rep', 'fsdp')
- delta_ada: float32 [1152, 6912], P('fsdp')
- delta_qkv: float32 [1152, 3456], P('fsdp')
- delta_proj: float32 [1152, 1152], P('fsdp')
- delta_fc1: float32 [1152, 4608], P('fsdp')
- delta_fc2: float32 [4608, 1152], P('fsdp')
- delta_bias: float32 [16128], P('fsdp')
- outer_next_ada: float32 [1152, 6912], P('fsdp')
- outer_next_qkv: float32 [1152, 3456], P('fsdp')
- outer_next_proj: float32 [1152, 1152], P('fsdp')
- outer_next_fc1: float32 [1152, 4608], P('fsdp')
- outer_next_fc2: float32 [4608, 1152], P('fsdp')
- outer_next_bias: float32 [16128], P('fsdp')
- weight_ada: float32 [1152, 6912], P('fsdp')
- weight_qkv: float32 [1152, 3456], P('fsdp')
- weight_proj: float32 [1152, 1152], P('fsdp')
- weight_fc1: float32 [1152, 4608], P('fsdp')
- weight_fc2: float32 [4608, 1152], P('fsdp')
- weight_bias: float32 [16128], P('fsdp')
Inputs may be any that keep to these rules, and one draw needn't show every extreme that they name: `counts`: A device's live images fill its first slots; in every draw some device has 3 live images and some has one fewer.
All inputs are finite; a program needn't handle non-finite values.
Results may differ from a plain program's by a relative error of at most 0.034.
The roundings to bfloat16 on the way count: a program that leaves them out, or rounds other values in their place, can miss the bound.
Values may be sent and summed in bfloat16 or wider, within the bound.
No kernel may reach another device: no remote copies, remote signals or barrier semaphores. Data moves between devices by JAX's collectives and lax.ppermute only.
A program may use at most 512 MiB of HBM per device.

v0:
```python
import functools
import math

import jax
import jax.numpy as jnp
from jax import lax
from jax.sharding import PartitionSpec as P

D = 1152
HEADS = 16
FF = 4608


NORM_EPS = 1e-06
BETA_ONE = 0.9
BETA_TWO = 0.95
ADAM_EPS = 1e-08
WEIGHT_DECAY = 0.1
OUTER_RATE = 0.7
OUTER_MOMENTUM = 0.9


def normalize(values):
    center = values - jnp.mean(values, axis=-1, keepdims=True)
    return center * lax.rsqrt(jnp.mean(center * center, axis=-1, keepdims=True) + NORM_EPS)


def modulate(values, shift, scale):
    return normalize(values) * (1.0 + scale) + shift


def time_embed(steps, width):
    half = width // 2
    frequency = jnp.exp(-math.log(10000.0) * jnp.arange(half).astype(jnp.float32) / half)
    angles = steps.astype(jnp.float32)[:, None] * frequency[None, :]
    return jnp.concatenate([jnp.cos(angles), jnp.sin(angles)], axis=1)


def learning_rates(width, hidden):
    return (
        2.0 / math.sqrt(width),
        2.0 / math.sqrt(width),
        2.0 / math.sqrt(width // 32),
        2.0 / math.sqrt(width),
        2.0 / math.sqrt(hidden),
        0.3,
    )


def image_pass(whole, image, cotangent_rows, style_row, live_one):
    w_ada, w_qkv, w_proj, w_fc1, w_fc2, bias_low = whole
    length, width = image.shape
    hidden = w_fc1.shape[1]
    head_dim = width // HEADS
    factor = 1.0 / math.sqrt(head_dim)
    bias_all = bias_low.astype(jnp.float32)
    b_ada = bias_all[: 6 * width]
    b_query = bias_all[6 * width : 7 * width]
    b_value = bias_all[7 * width : 8 * width]
    b_proj = bias_all[8 * width : 9 * width]
    b_fc1 = bias_all[9 * width : 9 * width + hidden]
    b_fc2 = bias_all[9 * width + hidden :]
    modulation = jnp.dot(style_row[None, :], w_ada, preferred_element_type=jnp.float32)[0] + b_ada
    shift_one = modulation[0:width]
    scale_one = modulation[width : 2 * width]
    gate_one = modulation[2 * width : 3 * width]
    shift_two = modulation[3 * width : 4 * width]
    scale_two = modulation[4 * width : 5 * width]
    gate_two = modulation[5 * width : 6 * width]
    residual = image.astype(jnp.float32)
    attn_float, attn_back = jax.vjp(modulate, residual, shift_one, scale_one)
    attn_in = attn_float.astype(jnp.bfloat16)
    bias_packed = jnp.concatenate([b_query, jnp.zeros_like(b_query), b_value])
    packed = (jnp.dot(attn_in, w_qkv, preferred_element_type=jnp.float32) + bias_packed).astype(
        jnp.bfloat16
    )
    query = packed[:, :width].reshape(length, HEADS, head_dim)
    keys = packed[:, width : 2 * width].reshape(length, HEADS, head_dim)
    values = packed[:, 2 * width :].reshape(length, HEADS, head_dim)
    scores = jnp.einsum("qhd,khd->hqk", query, keys, preferred_element_type=jnp.float32) * factor
    top = jnp.max(scores, axis=-1, keepdims=True)
    raised = jnp.exp(scores - top)
    summed = jnp.sum(raised, axis=-1, keepdims=True)
    attention = (raised / summed).astype(jnp.bfloat16)
    log_total = top + jnp.log(summed)
    attended = jnp.einsum("hqk,khd->qhd", attention, values, preferred_element_type=jnp.float32)
    attended = attended.reshape(length, width).astype(jnp.bfloat16)
    attn_out = jnp.dot(attended, w_proj, preferred_element_type=jnp.float32) + b_proj
    middle = residual + gate_one * attn_out
    mlp_float, mlp_back = jax.vjp(modulate, middle, shift_two, scale_two)
    mlp_in = mlp_float.astype(jnp.bfloat16)
    hidden_pre = jnp.dot(mlp_in, w_fc1, preferred_element_type=jnp.float32) + b_fc1
    activated_float, gelu_back = jax.vjp(
        functools.partial(jax.nn.gelu, approximate=True), hidden_pre
    )
    activated = activated_float.astype(jnp.bfloat16)
    mlp_out = jnp.dot(activated, w_fc2, preferred_element_type=jnp.float32) + b_fc2
    result = ((middle + gate_two * mlp_out) * live_one).astype(jnp.bfloat16)
    upstream = cotangent_rows.astype(jnp.float32) * live_one
    d_mlp = (gate_two * upstream).astype(jnp.bfloat16)
    d_gate_two = jnp.sum(upstream * mlp_out, axis=0)
    grad_fc2 = jnp.einsum("sf,sd->fd", activated, d_mlp, preferred_element_type=jnp.float32)
    d_activated = jnp.einsum("sd,fd->sf", d_mlp, w_fc2, preferred_element_type=jnp.float32)
    d_hidden = gelu_back(d_activated)[0].astype(jnp.bfloat16)
    grad_fc1 = jnp.einsum("sd,sf->df", mlp_in, d_hidden, preferred_element_type=jnp.float32)
    d_mlp_in = jnp.einsum("sf,df->sd", d_hidden, w_fc1, preferred_element_type=jnp.float32)
    d_middle_norm, d_shift_two, d_scale_two = mlp_back(d_mlp_in)
    d_middle = upstream + d_middle_norm
    d_attn = (gate_one * d_middle).astype(jnp.bfloat16)
    d_gate_one = jnp.sum(d_middle * attn_out, axis=0)
    grad_proj = jnp.einsum("sd,se->de", attended, d_attn, preferred_element_type=jnp.float32)
    d_attended = jnp.einsum("se,de->sd", d_attn, w_proj, preferred_element_type=jnp.float32)
    d_attended = d_attended.astype(jnp.bfloat16).reshape(length, HEADS, head_dim)
    scores_again = (
        jnp.einsum("qhd,khd->hqk", query, keys, preferred_element_type=jnp.float32) * factor
    )
    weights_again = jnp.exp(scores_again - log_total)
    d_weights = jnp.einsum("qhd,khd->hqk", d_attended, values, preferred_element_type=jnp.float32)
    d_scores = weights_again * (
        d_weights - jnp.sum(weights_again * d_weights, axis=-1, keepdims=True)
    )
    d_scores = d_scores.astype(jnp.bfloat16)
    d_query = (
        jnp.einsum("hqk,khd->qhd", d_scores, keys, preferred_element_type=jnp.float32) * factor
    )
    d_keys = (
        jnp.einsum("hqk,qhd->khd", d_scores, query, preferred_element_type=jnp.float32) * factor
    )
    d_values = jnp.einsum("hqk,qhd->khd", attention, d_attended, preferred_element_type=jnp.float32)
    d_packed = jnp.concatenate(
        [
            d_query.reshape(length, width),
            d_keys.reshape(length, width),
            d_values.reshape(length, width),
        ],
        axis=1,
    ).astype(jnp.bfloat16)
    grad_qkv = jnp.einsum("sd,se->de", attn_in, d_packed, preferred_element_type=jnp.float32)
    d_attn_in = jnp.einsum("se,de->sd", d_packed, w_qkv, preferred_element_type=jnp.float32)
    d_residual_norm, d_shift_one, d_scale_one = attn_back(d_attn_in)
    in_grad = (d_middle + d_residual_norm).astype(jnp.bfloat16)
    d_modulation = jnp.concatenate(
        [d_shift_one, d_scale_one, d_gate_one, d_shift_two, d_scale_two, d_gate_two]
    ).astype(jnp.bfloat16)
    packed_sums = jnp.sum(d_packed.astype(jnp.float32), axis=0)
    grad_bias = jnp.concatenate(
        [
            d_modulation.astype(jnp.float32),
            packed_sums[:width],
            packed_sums[2 * width :],
            jnp.sum(d_attn.astype(jnp.float32), axis=0),
            jnp.sum(d_hidden.astype(jnp.float32), axis=0),
            jnp.sum(d_mlp.astype(jnp.float32), axis=0),
        ]
    )
    return (result, in_grad, d_modulation, (grad_qkv, grad_proj, grad_fc1, grad_fc2, grad_bias))


def body(
    images,
    cotangent,
    counts,
    timesteps,
    labels,
    label_table,
    step_count,
    w_ada,
    w_qkv,
    w_proj,
    w_fc1,
    w_fc2,
    biases,
    first_ada,
    first_qkv,
    first_proj,
    first_fc1,
    first_fc2,
    first_bias,
    second_ada,
    second_qkv,
    second_proj,
    second_fc1,
    second_fc2,
    second_bias,
    outer_ada,
    outer_qkv,
    outer_proj,
    outer_fc1,
    outer_fc2,
    outer_bias,
):
    masters = (w_ada, w_qkv, w_proj, w_fc1, w_fc2, biases)
    firsts = (first_ada, first_qkv, first_proj, first_fc1, first_fc2, first_bias)
    seconds = (second_ada, second_qkv, second_proj, second_fc1, second_fc2, second_bias)
    outers = (outer_ada, outer_qkv, outer_proj, outer_fc1, outer_fc2, outer_bias)
    lowered = tuple((weight.astype(jnp.bfloat16) for weight in masters))
    slots = images.shape[0]
    live = (jnp.arange(slots) < counts[0]).astype(jnp.float32)
    condition = time_embed(timesteps, D) + jnp.take(label_table, labels, axis=0).astype(jnp.float32)
    style = jax.nn.silu(condition).astype(jnp.bfloat16)
    results = []
    in_grads = []
    mod_grads = []
    accumulated = None
    owned = None
    for slot_index in range(slots):
        whole = (
            lax.all_gather(lowered[0], "fsdp", axis=0, tiled=True),
            lax.all_gather(lowered[1], "fsdp", axis=0, tiled=True),
            lax.all_gather(lowered[2], "fsdp", axis=0, tiled=True),
            lax.all_gather(lowered[3], "fsdp", axis=0, tiled=True),
            lax.all_gather(lowered[4], "fsdp", axis=0, tiled=True),
            lax.all_gather(lowered[5], "fsdp", axis=0, tiled=True),
        )
        result, in_grad, d_modulation, grads = image_pass(
            whole, images[slot_index], cotangent[slot_index], style[slot_index], live[slot_index]
        )
        results.append(result)
        in_grads.append(in_grad)
        mod_grads.append(d_modulation)
        accumulated = (
            grads
            if accumulated is None
            else tuple((old + new for old, new in zip(accumulated, grads)))
        )
    owned = (
        lax.psum_scatter(
            accumulated[0].astype(jnp.bfloat16), "fsdp", scatter_dimension=0, tiled=True
        ).astype(jnp.float32),
        lax.psum_scatter(
            accumulated[1].astype(jnp.bfloat16), "fsdp", scatter_dimension=0, tiled=True
        ).astype(jnp.float32),
        lax.psum_scatter(
            accumulated[2].astype(jnp.bfloat16), "fsdp", scatter_dimension=0, tiled=True
        ).astype(jnp.float32),
        lax.psum_scatter(
            accumulated[3].astype(jnp.bfloat16), "fsdp", scatter_dimension=0, tiled=True
        ).astype(jnp.float32),
        lax.psum_scatter(
            accumulated[4].astype(jnp.bfloat16), "fsdp", scatter_dimension=0, tiled=True
        ).astype(jnp.float32),
    )
    mod_stack = jnp.stack(mod_grads)
    ada_local = jnp.einsum("id,ie->de", style, mod_stack, preferred_element_type=jnp.float32)
    ada_owned = lax.psum_scatter(
        ada_local.astype(jnp.bfloat16), "fsdp", scatter_dimension=0, tiled=True
    )
    reduced = (
        lax.psum(ada_owned, "dp").astype(jnp.float32),
        lax.psum(owned[0].astype(jnp.bfloat16), "dp").astype(jnp.float32),
        lax.psum(owned[1].astype(jnp.bfloat16), "dp").astype(jnp.float32),
        lax.psum(owned[2].astype(jnp.bfloat16), "dp").astype(jnp.float32),
        lax.psum(owned[3].astype(jnp.bfloat16), "dp").astype(jnp.float32),
        lax.psum(owned[4].astype(jnp.bfloat16), "dp").astype(jnp.float32),
    )
    power = step_count[0].astype(jnp.float32)
    fix_one = 1.0 - jnp.power(BETA_ONE, power)
    fix_two = 1.0 - jnp.power(BETA_TWO, power)
    rates = learning_rates(D, FF)
    firsts_out = []
    seconds_out = []
    local_deltas = []
    for index in range(6):
        gradient = reduced[index]
        first_next = BETA_ONE * firsts[index][0] + (1.0 - BETA_ONE) * gradient
        second_next = BETA_TWO * seconds[index][0] + (1.0 - BETA_TWO) * gradient * gradient
        master = masters[index]
        local = master - rates[index] * (
            first_next / fix_one / (jnp.sqrt(second_next / fix_two) + ADAM_EPS)
            + WEIGHT_DECAY * master
        )
        firsts_out.append(first_next[None])
        seconds_out.append(second_next[None])
        local_deltas.append(master - local)
    summed = (
        lax.psum(local_deltas[0].astype(jnp.bfloat16), "rep").astype(jnp.float32),
        lax.psum(local_deltas[1].astype(jnp.bfloat16), "rep").astype(jnp.float32),
        lax.psum(local_deltas[2].astype(jnp.bfloat16), "rep").astype(jnp.float32),
        lax.psum(local_deltas[3].astype(jnp.bfloat16), "rep").astype(jnp.float32),
        lax.psum(local_deltas[4].astype(jnp.bfloat16), "rep").astype(jnp.float32),
        lax.psum(local_deltas[5].astype(jnp.bfloat16), "rep").astype(jnp.float32),
    )
    groups = lax.axis_size("rep")
    deltas_out = []
    outers_out = []
    weights_out = []
    for index in range(6):
        delta = summed[index] / groups
        outer_next = OUTER_MOMENTUM * outers[index] + delta
        deltas_out.append(delta)
        outers_out.append(outer_next)
        weights_out.append(masters[index] - OUTER_RATE * (delta + OUTER_MOMENTUM * outer_next))
    grads_out = tuple((gradient[None] for gradient in reduced))
    return (
        (jnp.stack(results), jnp.stack(in_grads))
        + grads_out
        + tuple(firsts_out)
        + tuple(seconds_out)
        + tuple(deltas_out)
        + tuple(outers_out)
        + tuple(weights_out)
    )


def solution(mesh):
    in_specs = (
        P(("rep", "dp", "fsdp"), None, None),
        P(("rep", "dp", "fsdp"), None, None),
        P(("rep", "dp", "fsdp")),
        P(("rep", "dp", "fsdp")),
        P(("rep", "dp", "fsdp")),
        P(),
        P(),
        P("fsdp", None),
        P("fsdp", None),
        P("fsdp", None),
        P("fsdp", None),
        P("fsdp", None),
        P("fsdp"),
        P("rep", "fsdp", None),
        P("rep", "fsdp", None),
        P("rep", "fsdp", None),
        P("rep", "fsdp", None),
        P("rep", "fsdp", None),
        P("rep", "fsdp"),
        P("rep", "fsdp", None),
        P("rep", "fsdp", None),
        P("rep", "fsdp", None),
        P("rep", "fsdp", None),
        P("rep", "fsdp", None),
        P("rep", "fsdp"),
        P("fsdp", None),
        P("fsdp", None),
        P("fsdp", None),
        P("fsdp", None),
        P("fsdp", None),
        P("fsdp"),
    )
    out_specs = (
        P(("rep", "dp", "fsdp"), None, None),
        P(("rep", "dp", "fsdp"), None, None),
        P("rep", "fsdp", None),
        P("rep", "fsdp", None),
        P("rep", "fsdp", None),
        P("rep", "fsdp", None),
        P("rep", "fsdp", None),
        P("rep", "fsdp"),
        P("rep", "fsdp", None),
        P("rep", "fsdp", None),
        P("rep", "fsdp", None),
        P("rep", "fsdp", None),
        P("rep", "fsdp", None),
        P("rep", "fsdp"),
        P("rep", "fsdp", None),
        P("rep", "fsdp", None),
        P("rep", "fsdp", None),
        P("rep", "fsdp", None),
        P("rep", "fsdp", None),
        P("rep", "fsdp"),
        P("fsdp", None),
        P("fsdp", None),
        P("fsdp", None),
        P("fsdp", None),
        P("fsdp", None),
        P("fsdp"),
        P("fsdp", None),
        P("fsdp", None),
        P("fsdp", None),
        P("fsdp", None),
        P("fsdp", None),
        P("fsdp"),
        P("fsdp", None),
        P("fsdp", None),
        P("fsdp", None),
        P("fsdp", None),
        P("fsdp", None),
        P("fsdp"),
    )
    return jax.shard_map(body, mesh=mesh, in_specs=in_specs, out_specs=out_specs, check_vma=False)
```

profile of v0, /device:TPU:1, one launch (start us, length us, event | category | flops | bytes accessed | tf_op | source)
XLA Modules:
  0.0 2467.6 jit_solution(12279298164873872853)
XLA Ops:
  7.3 5.7 convert_element_type.371
  30.9 24.7 %all-reduce = bf16[16128]{0:T(1024)(128)(2,1)S(1)} all-reduce(bf16[16128]{0:T(1024)(128)(2,1)S(1)} %dynamic-update-slice), channel_id=1, replica_groups=mesh['rep'=4,'dp'=2,'fsdp'=4] {'fsdp'}, use_global_device_ids=true, to_apply=%add | all-reduce | flops 16128 | bytes 64512
  61.8 227.6 %all-gather.6.cloned.1.call-done = bf16[1152,6912]{1,0:T(8,128)(2,1)} async-done(((bf16[288,6912]{1,0:T(8,128)(2,1)}), bf16[1152,6912]{1,0:T(8,128)(2,1)}) %all-gather.6.cloned.1.call-update) | async-done | bytes 15925264 | tf_op jit(solution)/shard_map/all_gather | solution.py:208
  289.4 7.9 convolution_reduce_fusion.1
  305.2 127.3 %all-gather.8.cloned.1.call-done = bf16[1152,3456]{1,0:T(8,128)(2,1)} async-done(((bf16[288,3456]{1,0:T(8,128)(2,1)}), bf16[1152,3456]{1,0:T(8,128)(2,1)}) %all-gather.8.cloned.1.call-update) | async-done | bytes 7962640 | tf_op jit(solution)/shard_map/all_gather | solution.py:209
  432.5 6.0 fusion.13
  450.3 37.7 %all-gather.10.cloned.1.call-done = bf16[1152,1152]{1,0:T(8,128)(2,1)} async-done(((bf16[288,1152]{1,0:T(8,128)(2,1)}), bf16[1152,1152]{1,0:T(8,128)(2,1)}) %all-gather.10.cloned.1.call-update) | async-done | bytes 2654224 | tf_op jit(solution)/shard_map/all_gather | solution.py:210
  492.3 182.8 %all-gather.12.cloned.1.call-done = bf16[1152,4608]{1,0:T(8,128)(2,1)} async-done(((bf16[288,4608]{1,0:T(8,128)(2,1)}), bf16[1152,4608]{1,0:T(8,128)(2,1)}) %all-gather.12.cloned.1.call-update) | async-done | bytes 10616848 | tf_op jit(solution)/shard_map/all_gather | solution.py:211
  675.1 9.0 convolution_add_fusion.10
  684.1 177.3 %all-gather.14.cloned.1.call-done = bf16[4608,1152]{1,0:T(8,128)(2,1)} async-done(((bf16[1152,1152]{1,0:T(8,128)(2,1)}), bf16[4608,1152]{1,0:T(8,128)(2,1)}) %all-gather.14.cloned.1.call-update) | async-done | bytes 10616848 | tf_op jit(solution)/shard_map/all_gather | solution.py:212
  861.4 9.9 convert_reduce_fusion.2
  910.5 6.2 fusion.14
  939.6 10.0 convert_reduce_fusion.1
  949.6 9.8 multiply_reduce_fusion.8
  959.4 7.7 convolution_add_fusion.18
  969.8 6.2 convolution_add_fusion.8
  976.0 10.1 convert_reduce_fusion
  986.1 9.9 multiply_reduce_fusion.6
  998.3 11.8 convert_reduce_fusion.11
  1018.4 5.4 multiply_reduce_fusion
  1051.2 8.1 fusion.146
  1059.3 13.7 convolution_add_fusion.5
  1073.1 11.9 fusion.2
  1085.8 13.0 fusion.157
  1098.8 13.5 convolution_add_fusion.1
  1112.3 14.9 fusion.1
  1127.5 14.7 fusion.113
  1142.1 21.0 convolution_add_fusion.3
  1163.1 15.1 fusion
  1178.9 6.6 fusion.144
  1185.6 7.3 fusion.92
  1195.0 10.8 fusion.102
  1206.0 8.3 convolution_convert_fusion
  1214.4 14.8 reduce-scatter.8.cloned.1.call-done
  1229.2 183.4 %reduce-scatter.12.cloned.1.call-done = bf16[288,4608]{1,0:T(8,128)(2,1)} async-done(((bf16[1152,4608]{1,0:T(8,128)(2,1)}), bf16[288,4608]{1,0:T(8,128)(2,1)}) %reduce-scatter.12.cloned.1.call-update) | async-done | bytes 2654224 | tf_op jit(solution)/shard_map/reduce_scatter | solution.py:233
  1412.6 183.6 %reduce-scatter.14.cloned.1.call-done = bf16[1152,1152]{1,0:T(8,128)(2,1)} async-done(((bf16[4608,1152]{1,0:T(8,128)(2,1)}), bf16[1152,1152]{1,0:T(8,128)(2,1)}) %reduce-scatter.14.cloned.1.call-update) | async-done | bytes 2654224 | tf_op jit(solution)/shard_map/reduce_scatter | solution.py:236
  1596.2 270.6 %reduce-scatter.6.cloned.1.call-done = bf16[288,6912]{1,0:T(8,128)(2,1)} async-done(((bf16[1152,6912]{1,0:T(8,128)(2,1)}), bf16[288,6912]{1,0:T(8,128)(2,1)}) %reduce-scatter.6.cloned.1.call-update) | async-done | bytes 3981328 | tf_op jit(solution)/shard_map/reduce_scatter | solution.py:245
  1879.5 15.2 all-reduce.1
  1900.4 10.1 psum.95
  1920.6 227.2 %all-reduce.9.cloned.1.call-done = (bf16[288,6912]{1,0:T(8,128)(2,1)}, bf16[288,3456]{1,0:T(8,128)(2,1)}, bf16[288,1152]{1,0:T(8,128)(2,1)}, bf16[288,4608]{1,0:T(8,128)(2,1)}, bf16[1152,1152]{1,0:T(8,128)(2,1)}) async-done(((bf16[288,6912]{1,0:T(8,128)(2,1)}, bf16[288,3456]{1,0:T(8,128)(2,1)}, bf16[288,1152]{1,0:T(8,128)(2,1)}, bf16[288,4608]{1,0:T(8,128)(2,1)}, bf16[1152,1152]{1,0:T(8,128)(2,1)}), ...) | async-done | bytes 11943952 | tf_op jit(solution)/shard_map/psum | solution.py:249
  2147.8 19.2 fusion.3
  2175.9 10.9 fusion.7
  2187.6 8.7 fusion.8
  2212.8 197.0 %all-reduce.7.cloned.1.call-done = (bf16[288,6912]{1,0:T(8,128)(2,1)}, bf16[288,3456]{1,0:T(8,128)(2,1)}, bf16[288,1152]{1,0:T(8,128)(2,1)}, bf16[288,4608]{1,0:T(8,128)(2,1)}, bf16[1152,1152]{1,0:T(8,128)(2,1)}) async-done(((bf16[288,6912]{1,0:T(8,128)(2,1)}, bf16[288,3456]{1,0:T(8,128)(2,1)}, bf16[288,1152]{1,0:T(8,128)(2,1)}, bf16[288,4608]{1,0:T(8,128)(2,1)}, bf16[1152,1152]{1,0:T(8,128)(2,1)}), ...) | async-done | bytes 11943952 | tf_op jit(solution)/shard_map/psum | solution.py:276
  2409.8 16.6 multiply_subtract_fusion
  2427.6 5.3 multiply_subtract_fusion.3
  2436.5 12.3 multiply_subtract_fusion.2
  2448.8 11.7 multiply_subtract_fusion.1
  (602 shorter events, 209.4 us)
Async XLA Ops:
  7.2 49.2 %copy-start = (bf16[1001,1152]{1,0:T(8,128)(2,1)S(1)}, bf16[1001,1152]{1,0:T(8,128)(2,1)}, u32[]{:S(2)}) copy-start(bf16[1001,1152]{1,0:T(8,128)(2,1)} %param.36) | copy-start | bytes 6918916
  7.2 282.1 %all-gather.6.cloned.1.call-start = ((), (), s32[]{:S(2)}) async-start(), calls=%async_computation.5 | async-start | bytes 19906560 | tf_op jit(solution)/shard_map/all_gather | solution.py:208
  13.0 419.4 %all-gather.8.cloned.1.call-start = ((), (), s32[]{:S(2)}) async-start(), calls=%async_computation.6 | async-start | bytes 9953280 | tf_op jit(solution)/shard_map/all_gather | solution.py:209
  16.7 471.2 %all-gather.10.cloned.1.call-start = ((), (), s32[]{:S(2)}) async-start(), calls=%async_computation.7 | async-start | bytes 3317760 | tf_op jit(solution)/shard_map/all_gather | solution.py:210
  19.0 656.0 %all-gather.12.cloned.1.call-start = ((), (), s32[]{:S(2)}) async-start(), calls=%async_computation.8 | async-start | bytes 13271040 | tf_op jit(solution)/shard_map/all_gather | solution.py:211
  23.4 838.0 %all-gather.14.cloned.1.call-start = ((), (), s32[]{:S(2)}) async-start(), calls=%async_computation.9 | async-start | bytes 13271040 | tf_op jit(solution)/shard_map/all_gather | solution.py:212
  28.6 27.1 %copy-start.167 = (s32[3]{0:T(128)S(1)}, s32[3]{0:T(128)}, u32[]{:S(2)}) copy-start(s32[3]{0:T(128)} %param.34) | copy-start | bytes 40
  28.6 27.8 %copy-start.168 = (s32[3]{0:T(128)S(1)}, s32[3]{0:T(128)}, u32[]{:S(2)}) copy-start(s32[3]{0:T(128)} %param.35) | copy-start | bytes 40
  28.7 1185.7 %reduce-scatter.10.cloned.1.call-start = ((), (), s32[]{:S(2)}) async-start(), calls=%async_computation.12 | async-start | bytes 3317760 | tf_op jit(solution)/shard_map/reduce_scatter | solution.py:230
  60.1 837.1 %copy-start.131 = (f32[256]{0:T(256)}, f32[256]{0:T(256)S(1)}, u32[]{:S(2)}) copy-start(f32[256]{0:T(256)S(1)} %get-tuple-element.219) | copy-start | bytes 3076
  61.4 235.8 %copy-start.148 = (f32[256]{0:T(256)}, f32[256]{0:T(256)S(1)}, u32[]{:S(2)}) copy-start(f32[256]{0:T(256)S(1)} %fusion.93) | copy-start | bytes 3076
  61.5 371.0 %copy-start.125 = (f32[256]{0:T(256)}, f32[256]{0:T(256)S(1)}, u32[]{:S(2)}) copy-start(f32[256]{0:T(256)S(1)} %fusion.137) | copy-start | bytes 3076
  61.7 241.2 %copy-start.107 = (bf16[3,1152]{1,0:T(4,128)(2,1)}, bf16[3,1152]{1,0:T(4,128)(2,1)S(1)}, u32[]{:S(2)}) copy-start(bf16[3,1152]{1,0:T(4,128)(2,1)S(1)} %fusion.134) | copy-start | bytes 20740
  302.9 129.5 %copy-start.8 = (bf16[3,256,1152]{2,1,0:T(8,128)(2,1)S(1)}, bf16[3,256,1152]{2,1,0:T(8,128)(2,1)}, u32[]{:S(2)}) copy-start(bf16[3,256,1152]{2,1,0:T(8,128)(2,1)} %param.31) | copy-start | bytes 5308420
  305.2 133.3 %copy-start.115 = (f32[1152]{0:T(1024)}, f32[1152]{0:T(1024)S(1)}, u32[]{:S(2)}) copy-start(f32[1152]{0:T(1024)S(1)} %get-tuple-element.178) | copy-start | bytes 13828
  305.2 369.9 %copy-start.113 = (f32[1152]{0:T(1024)}, f32[1152]{0:T(1024)S(1)}, u32[]{:S(2)}) copy-start(f32[1152]{0:T(1024)S(1)} %get-tuple-element.176) | copy-start | bytes 13828
  305.2 570.1 %copy-start.109 = (f32[1152]{0:T(1024)}, f32[1152]{0:T(1024)S(1)}, u32[]{:S(2)}) copy-start(f32[1152]{0:T(1024)S(1)} %get-tuple-element.177) | copy-start | bytes 13828
  492.0 383.3 %copy-start.13 = (f32[256,1152]{1,0:T(8,128)}, f32[256,1152]{1,0:T(8,128)S(1)}, u32[]{:S(2)}) copy-start(f32[256,1152]{1,0:T(8,128)S(1)} %get-tuple-element.123) | copy-start | bytes 3538948
  492.0 383.3 %copy-start.119 = (f32[256]{0:T(256)}, f32[256]{0:T(256)S(1)}, u32[]{:S(2)}) copy-start(f32[256]{0:T(256)S(1)} %broadcast_multiply_fusion.6) | copy-start | bytes 3076
  492.3 383.0 %copy-start.127 = (f32[256]{0:T(256)}, f32[256]{0:T(256)S(1)}, u32[]{:S(2)}) copy-start(f32[256]{0:T(256)S(1)} %fusion.138) | copy-start | bytes 3076
  875.7 122.2 %copy-start.150 = (f32[256]{0:T(256)}, f32[256]{0:T(256)S(1)}, u32[]{:S(2)}) copy-start(f32[256]{0:T(256)S(1)} %negate_multiply_fusion.5) | copy-start | bytes 3076
  910.4 17.4 copy-start.49
  935.9 31.3 %copy-start.11 = (f32[256,1152]{1,0:T(8,128)}, f32[256,1152]{1,0:T(8,128)S(1)}, u32[]{:S(2)}) copy-start(f32[256,1152]{1,0:T(8,128)S(1)} %get-tuple-element.117) | copy-start | bytes 3538948
  939.6 19.9 copy-start.21
  969.5 54.3 %copy-start.156 = (f32[256]{0:T(256)}, f32[256]{0:T(256)S(1)}, u32[]{:S(2)}) copy-start(f32[256]{0:T(256)S(1)} %negate_multiply_fusion.3) | copy-start | bytes 3076
  1037.8 191.4 %reduce-scatter.8.cloned.1.call-start = ((), (), s32[]{:S(2)}) async-start(), calls=%async_computation.11 | async-start | bytes 9953280 | tf_op jit(solution)/shard_map/reduce_scatter | solution.py:227
  1043.5 29.6 %copy-start.71 = (bf16[16,72,256]{2,1,0:T(8,128)(2,1)}, bf16[16,72,256]{2,1,0:T(8,128)(2,1)S(1)}, u32[]{:S(2)}) copy-start(bf16[16,72,256]{2,1,0:T(8,128)(2,1)S(1)} %fusion.83) | copy-start | bytes 1769476
  1044.0 29.1 %copy-start.72 = (bf16[16,72,256]{2,1,0:T(8,128)(2,1)}, bf16[16,72,256]{2,1,0:T(8,128)(2,1)S(1)}, u32[]{:S(2)}) copy-start(bf16[16,72,256]{2,1,0:T(8,128)(2,1)S(1)} %fusion.82) | copy-start | bytes 1769476
  1059.3 13.8 copy-start.64
  1085.1 327.5 %reduce-scatter.12.cloned.1.call-start = ((), (), s32[]{:S(2)}) async-start(), calls=%async_computation.13 | async-start | bytes 13271040 | tf_op jit(solution)/shard_map/reduce_scatter | solution.py:233
  1127.2 468.9 %reduce-scatter.14.cloned.1.call-start = ((), (), s32[]{:S(2)}) async-start(), calls=%async_computation.14 | async-start | bytes 13271040 | tf_op jit(solution)/shard_map/reduce_scatter | solution.py:236
  1127.5 14.7 copy-start.34
  1178.2 688.6 %reduce-scatter.6.cloned.1.call-start = ((), (), s32[]{:S(2)}) async-start(), calls=%async_computation.10 | async-start | bytes 19906560 | tf_op jit(solution)/shard_map/reduce_scatter | solution.py:245
  1214.3 933.4 %all-reduce.9.cloned.1.call-start = ((), (), s32[]{:S(2)}) async-start(), calls=%async_computation.16 | async-start | bytes 23887872 | tf_op jit(solution)/shard_map/psum | solution.py:249
  1866.9 542.9 %all-reduce.7.cloned.1.call-start = ((), (), s32[]{:S(2)}) async-start(), calls=%async_computation.15 | async-start | bytes 23887872 | tf_op jit(solution)/shard_map/psum | solution.py:276
  1875.3 24.5 copy-start.112
  1875.3 35.3 %copy-start.147 = (f32[4032]{0:T(1024)S(1)}, f32[4032]{0:T(1024)}, u32[]{:S(2)}) copy-start(f32[4032]{0:T(1024)} %param.61) | copy-start | bytes 48388
  1879.3 34.9 %copy-start.76 = (f32[256,1152]{1,0:T(8,128)S(1)}, f32[256,1152]{1,0:T(8,128)}, u32[]{:S(2)}) copy-start(f32[256,1152]{1,0:T(8,128)} %copy-done.75) | copy-start | bytes 3538948
  1879.4 34.9 %copy-start.163 = (f32[256]{0:T(256)S(1)}, f32[256]{0:T(256)}, u32[]{:S(2)}) copy-start(f32[256]{0:T(256)} %copy-done.162) | copy-start | bytes 3076
  1916.7 259.2 %slice-start = ((s8[5308416]{0:T(1024)(128)(4,1)}), s8[1114112]{0:T(1024)(128)(4,1)S(1)}, s32[]{:S(2)}) async-start(s8[5308416]{0:T(1024)(128)(4,1)} %bitcast.435), calls=%async_computation.17 | async-start | bytes 2228224
  2147.7 19.2 copy-start.9
  2147.7 19.2 copy-start.35
  2147.7 19.2 copy-start.79
  2147.7 20.2 copy-start.80
  2147.7 28.1 %slice-start.1 = ((s8[5308416]{0:T(1024)(128)(4,1)}), s8[4194304]{0:T(1024)(128)(4,1)S(1)}, s32[]{:S(2)}) async-start(s8[5308416]{0:T(1024)(128)(4,1)} %bitcast.435), calls=%async_computation.18 | async-start | bytes 8388608
  2409.8 16.7 copy-start.10
  2409.8 16.7 copy-start.81
  2409.8 17.8 copy-start.93
  (148 other events, 817.0 us)
Sparse Core Ops, SparseCore 0:
  13.2 276.1 all-gather.5
  291.5 140.8 all-gather.7
  434.6 53.3 all-gather.9
  489.9 185.0 all-gather.11
  677.1 184.2 all-gather.13
  1037.9 50.4 reduce-scatter.9
  1091.4 137.7 reduce-scatter.7
  1231.6 180.9 reduce-scatter.11
  1415.0 181.1 reduce-scatter.13
  1598.5 268.2 reduce-scatter.5
  1869.7 278.0 all-reduce.8
  2196.4 213.3 all-reduce.6
where the time goes:
time: 2470 us
  waiting for transfers between devices  1830 us (74%)
  matrix products  333 us (13%)
  other arithmetic  176 us (7%)
  blocking collectives  54.4 us (2%)
  local copies, waits for them, and re-layouts  53.9 us (2%)
    reduce_scatter x1, waiting for transfers between devices, body(): lax.psum_scatter(ada_local.astype(jnp.bfloat16), 'fsdp', scatter_dimensio...  271 us
    all_gather x1, waiting for transfers between devices, body(): lax.all_gather(lowered[0], 'fsdp', axis=0, tiled=True)  228 us
    psum x1, waiting for transfers between devices, body(): lax.psum(ada_owned, 'dp').astype(jnp.float32)  227 us
    psum x1, waiting for transfers between devices, body(): lax.psum(local_deltas[0].astype(jnp.bfloat16), 'rep').astype(jnp.float32)  197 us
    reduce_scatter x1, waiting for transfers between devices, body(): lax.psum_scatter(accumulated[3].astype(jnp.bfloat16), 'fsdp', scatter_dim...  184 us
    reduce_scatter x1, waiting for transfers between devices, body(): lax.psum_scatter(accumulated[2].astype(jnp.bfloat16), 'fsdp', scatter_dim...  183 us
    all_gather x1, waiting for transfers between devices, body(): lax.all_gather(lowered[3], 'fsdp', axis=0, tiled=True)  183 us
    all_gather x1, waiting for transfers between devices, body(): lax.all_gather(lowered[4], 'fsdp', axis=0, tiled=True)  177 us
  transfers between devices with their start and end apart: 12, of which 11 were waited for; matrix products, arithmetic and copies ran while one was open for 11% of the time, Pallas kernels for 0%

commit v1 on v0

v1 whole, which is shorter than its diff:
```python
import math

import jax
import jax.numpy as jnp
from jax import lax
from jax.sharding import PartitionSpec as P

D = 1152
HEADS = 16
FF = 4608


NORM_EPS = 1e-06
BETA_ONE = 0.9
BETA_TWO = 0.95
ADAM_EPS = 1e-08
WEIGHT_DECAY = 0.1
OUTER_RATE = 0.7
OUTER_MOMENTUM = 0.9
FEW = 8

F32 = jnp.float32
BF16 = jnp.bfloat16


def dot(left, right):
    return jnp.dot(left, right, preferred_element_type=F32)


def dot_nt(left, right):
    return lax.dot_general(left, right, (((1,), (1,)), ((), ())), preferred_element_type=F32)


def dot_tn(left, right):
    return lax.dot_general(left, right, (((0,), (0,)), ((), ())), preferred_element_type=F32)


def time_embed(steps, width):
    half = width // 2
    frequency = jnp.exp(-math.log(10000.0) * jnp.arange(half).astype(F32) / half)
    angles = steps.astype(F32)[:, None] * frequency[None, :]
    return jnp.concatenate([jnp.cos(angles), jnp.sin(angles)], axis=1)


def learning_rates(width, hidden):
    return (
        2.0 / math.sqrt(width),
        2.0 / math.sqrt(width),
        2.0 / math.sqrt(width // 32),
        2.0 / math.sqrt(width),
        2.0 / math.sqrt(hidden),
        0.3,
    )


def shift_by(value, axis, step):
    size = lax.axis_size(axis)
    return lax.ppermute(value, axis, [(i, (i + step) % size) for i in range(size)])


def swap_with(value, axis, bit):
    size = lax.axis_size(axis)
    return lax.ppermute(value, axis, [(i, i ^ bit) for i in range(size)])


def gather_line(value, axis):
    size = lax.axis_size(axis)
    if size > FEW:
        return lax.all_gather(value, axis, axis=0)
    place = lax.axis_index(axis)
    result = jnp.zeros((size,) + value.shape, value.dtype)
    for step in range(size):
        piece = value if step == 0 else shift_by(value, axis, step)
        result = lax.dynamic_update_index_in_dim(result, piece, (place - step) % size, 0)
    return result


def scatter_line(value, axis):
    size = lax.axis_size(axis)
    if size > FEW:
        return lax.psum_scatter(value, axis, scatter_dimension=0, tiled=False)
    place = lax.axis_index(axis)
    total = lax.dynamic_index_in_dim(value, place, 0, keepdims=False)
    for step in range(1, size):
        piece = lax.dynamic_index_in_dim(value, (place + step) % size, 0, keepdims=False)
        total = total + shift_by(piece, axis, step)
    return total


def moments(values):
    center = values - jnp.mean(values, axis=-1, keepdims=True)
    inverse = lax.rsqrt(jnp.mean(center * center, axis=-1, keepdims=True) + NORM_EPS)
    return center * inverse, inverse


def norm_back(normed, inverse, upstream):
    first = jnp.mean(upstream, axis=-1, keepdims=True)
    second = jnp.mean(upstream * normed, axis=-1, keepdims=True)
    return (upstream - first - normed * second) * inverse


def gelu_pair(h):
    c = math.sqrt(2.0 / math.pi)
    inner = c * (h + 0.044715 * h * h * h)
    t = jnp.tanh(inner)
    value = 0.5 * h * (1.0 + t)
    slope = 0.5 * (1.0 + t) + 0.5 * h * (1.0 - t * t) * c * (1.0 + 3.0 * 0.044715 * h * h)
    return value, slope


def attention_forward(packed, slots, length):
    width = packed.shape[1] // 3
    head_dim = width // HEADS
    factor = 1.0 / math.sqrt(head_dim)
    split = packed.reshape(slots, length, 3, HEADS, head_dim)
    query, keys, values = split[:, :, 0], split[:, :, 1], split[:, :, 2]
    scores = jnp.einsum("iqhd,ikhd->ihqk", query, keys, preferred_element_type=F32) * factor
    top = jnp.max(scores, axis=-1, keepdims=True)
    raised = jnp.exp(scores - top)
    summed = jnp.sum(raised, axis=-1, keepdims=True)
    probs = (raised / summed).astype(BF16)
    log_total = top + jnp.log(summed)
    attended = jnp.einsum("ihqk,ikhd->iqhd", probs, values, preferred_element_type=F32)
    return attended.astype(BF16).reshape(slots * length, width), (query, keys, values, probs, log_total)


def attention_backward(saved, d_attended, slots, length):
    query, keys, values, probs, log_total = saved
    width = d_attended.shape[1]
    head_dim = width // HEADS
    factor = 1.0 / math.sqrt(head_dim)
    d_att = d_attended.reshape(slots, length, HEADS, head_dim)
    scores = jnp.einsum("iqhd,ikhd->ihqk", query, keys, preferred_element_type=F32) * factor
    weights = jnp.exp(scores - log_total)
    d_probs = jnp.einsum("iqhd,ikhd->ihqk", d_att, values, preferred_element_type=F32)
    d_scores = weights * (d_probs - jnp.sum(weights * d_probs, axis=-1, keepdims=True))
    d_scores = d_scores.astype(BF16)
    d_query = jnp.einsum("ihqk,ikhd->iqhd", d_scores, keys, preferred_element_type=F32) * factor
    d_keys = jnp.einsum("ihqk,iqhd->ikhd", d_scores, query, preferred_element_type=F32) * factor
    d_values = jnp.einsum("ihqk,iqhd->ikhd", probs, d_att, preferred_element_type=F32)
    pieces = [piece.astype(BF16).reshape(slots * length, width) for piece in (d_query, d_keys, d_values)]
    return jnp.concatenate(pieces, axis=1)


def own_half(value, index):
    return lax.dynamic_index_in_dim(value, index, 1, keepdims=False)


def body(
    images,
    cotangent,
    counts,
    timesteps,
    labels,
    label_table,
    step_count,
    w_ada,
    w_qkv,
    w_proj,
    w_fc1,
    w_fc2,
    biases,
    first_ada,
    first_qkv,
    first_proj,
    first_fc1,
    first_fc2,
    first_bias,
    second_ada,
    second_qkv,
    second_proj,
    second_fc1,
    second_fc2,
    second_bias,
    outer_ada,
    outer_qkv,
    outer_proj,
    outer_fc1,
    outer_fc2,
    outer_bias,
):
    masters = (w_ada, w_qkv, w_proj, w_fc1, w_fc2, biases)
    firsts = (first_ada, first_qkv, first_proj, first_fc1, first_fc2, first_bias)
    seconds = (second_ada, second_qkv, second_proj, second_fc1, second_fc2, second_bias)
    outers = (outer_ada, outer_qkv, outer_proj, outer_fc1, outer_fc2, outer_bias)
    slots, length, width = images.shape
    tokens = slots * length
    rows = w_qkv.shape[0]
    rows_two = w_fc2.shape[0]
    lines = lax.axis_size("fsdp")
    groups = lax.axis_size("rep")
    rep = lax.axis_index("rep")
    pair = lax.axis_index("dp")
    line = lax.axis_index("fsdp")
    half = rows // 2
    everyone = ("rep", "fsdp", "dp")

    def rows_of(weight):
        return lax.dynamic_slice_in_dim(weight, pair * half, half, axis=0).astype(BF16)

    attention_cut = jnp.concatenate([rows_of(w_qkv), rows_of(w_proj)], axis=1)
    attention_cut = lax.dynamic_slice_in_dim(attention_cut, rep * width, width, axis=1)
    gathered = lax.all_gather(attention_cut, everyone, axis=0, tiled=True).reshape(4, width, width)
    w_qkv_all = jnp.transpose(gathered[:3], (1, 0, 2)).reshape(width, 3 * width)
    w_proj_all = gathered[3]
    one_cut = lax.dynamic_slice(w_fc1, (pair * half, rep * width), (half, width)).astype(BF16)
    one_all = lax.all_gather(one_cut, everyone, axis=0, tiled=True).reshape(FF // width, width, width)
    w_fc1_all = jnp.transpose(one_all, (1, 0, 2)).reshape(width, FF)
    eighth = rows_two // (2 * groups)
    two_cut = lax.dynamic_slice_in_dim(w_fc2, (rep * 2 + pair) * eighth, eighth, axis=0).astype(BF16)
    w_fc2_all = lax.all_gather(two_cut, ("fsdp", "rep", "dp"), axis=0, tiled=True)

    live = (jnp.arange(slots) < counts[0]).astype(F32)
    condition = time_embed(timesteps, D) + jnp.take(label_table, labels, axis=0).astype(F32)
    style = jax.nn.silu(condition).astype(BF16)
    message = jnp.concatenate([style.reshape(-1), biases.astype(BF16)])
    heard = gather_line(message, "fsdp")
    bias_all = heard[:, slots * width :].reshape(-1).astype(F32)
    style_line = heard[:, : slots * width].reshape(lines * slots, width)
    style_cut = lax.dynamic_slice_in_dim(style_line, line * rows, rows, axis=1)
    mod_part = dot(style_cut, w_ada.astype(BF16))
    b_ada = bias_all[: 6 * width]
    b_query = bias_all[6 * width : 7 * width]
    b_value = bias_all[7 * width : 8 * width]
    b_proj = bias_all[8 * width : 9 * width]
    b_fc1 = bias_all[9 * width : 9 * width + FF]
    b_fc2 = bias_all[9 * width + FF :]
    modulation = scatter_line(mod_part.reshape(lines, slots, 6 * width), "fsdp") + b_ada

    def spread(index):
        return modulation[:, None, index * width : (index + 1) * width]

    shift_one, scale_one, gate_one, shift_two, scale_two, gate_two = (spread(i) for i in range(6))

    def flat(value):
        return value.reshape(tokens, value.shape[-1])

    def cube(value):
        return value.reshape(slots, length, value.shape[-1])

    residual = images.astype(F32)
    normed_one, inverse_one = moments(residual)
    attn_in = flat((normed_one * (1.0 + scale_one) + shift_one).astype(BF16))
    bias_packed = jnp.concatenate([b_query, jnp.zeros_like(b_query), b_value])
    packed = (dot(attn_in, w_qkv_all) + bias_packed).astype(BF16)
    attended, saved = attention_forward(packed, slots, length)
    attn_out = cube(dot(attended, w_proj_all) + b_proj)
    middle = residual + gate_one * attn_out
    normed_two, inverse_two = moments(middle)
    mlp_in = flat((normed_two * (1.0 + scale_two) + shift_two).astype(BF16))
    hidden = dot(mlp_in, w_fc1_all) + b_fc1
    activated_float, slope = gelu_pair(hidden)
    activated = activated_float.astype(BF16)

    upstream = cotangent.astype(F32) * live[:, None, None]
    d_mlp = flat((gate_two * upstream).astype(BF16))
    grad_two = dot_tn(activated, d_mlp).astype(BF16)
    d_hidden = (dot_nt(d_mlp, w_fc2_all) * slope).astype(BF16)
    grad_one = dot_tn(mlp_in, d_hidden).astype(BF16)

    def pair_first(gradient):
        parts = gradient.reshape(lines, 2, gradient.shape[0] // (2 * lines), gradient.shape[1])
        there = swap_with(own_half(parts, 1 - pair), "dp", 1)
        both = (own_half(parts, pair).astype(F32) + there.astype(F32)).astype(BF16)
        return lax.psum_scatter(
            both.reshape(-1, gradient.shape[1]), "fsdp", scatter_dimension=0, tiled=True
        )

    two_half = pair_first(grad_two)
    one_half = pair_first(grad_one)

    mlp_out = cube(dot(activated, w_fc2_all) + b_fc2)
    result = ((middle + gate_two * mlp_out) * live[:, None, None]).astype(BF16)
    d_gate_two = jnp.sum(upstream * mlp_out, axis=1)
    d_mlp_in = cube(dot_nt(d_hidden, w_fc1_all))
    d_shift_two = jnp.sum(d_mlp_in, axis=1)
    d_scale_two = jnp.sum(d_mlp_in * normed_two, axis=1)
    d_middle = upstream + norm_back(normed_two, inverse_two, d_mlp_in * (1.0 + scale_two))
    d_attn = flat((gate_one * d_middle).astype(BF16))
    d_gate_one = jnp.sum(d_middle * attn_out, axis=1)
    grad_proj = dot_tn(attended, d_attn).astype(BF16)
    proj_half = lax.psum_scatter(grad_proj, ("fsdp", "dp"), scatter_dimension=0, tiled=True)
    d_attended = dot_nt(d_attn, w_proj_all).astype(BF16)
    d_packed = attention_backward(saved, d_attended, slots, length)
    grad_qkv = dot_tn(attn_in, d_packed).astype(BF16)
    qkv_half = lax.psum_scatter(grad_qkv, ("fsdp", "dp"), scatter_dimension=0, tiled=True)
    d_attn_in = cube(dot_nt(d_packed, w_qkv_all))
    d_shift_one = jnp.sum(d_attn_in, axis=1)
    d_scale_one = jnp.sum(d_attn_in * normed_one, axis=1)
    d_residual = norm_back(normed_one, inverse_one, d_attn_in * (1.0 + scale_one))
    in_grad = (d_middle + d_residual).astype(BF16)
    d_modulation = jnp.concatenate(
        [d_shift_one, d_scale_one, d_gate_one, d_shift_two, d_scale_two, d_gate_two], axis=1
    ).astype(BF16)
    packed_sums = jnp.sum(d_packed.astype(F32), axis=0)
    bias_sums = jnp.concatenate(
        [
            packed_sums[:width],
            packed_sums[2 * width :],
            jnp.sum(d_attn.astype(F32), axis=0),
            jnp.sum(d_hidden.astype(F32), axis=0),
            jnp.sum(d_mlp.astype(F32), axis=0),
        ]
    ).astype(BF16)

    report = jnp.concatenate([style.reshape(-1), d_modulation.reshape(-1), bias_sums])
    report = jnp.stack([report, swap_with(report, "dp", 1)])
    reports = gather_line(report, "fsdp").reshape(2 * lines, -1)
    edge = slots * width
    style_group = reports[:, :edge].reshape(2 * lines * slots, width)
    mod_group = reports[:, edge : 7 * edge].reshape(2 * lines * slots, 6 * width)
    style_own = lax.dynamic_slice_in_dim(style_group, line * rows, rows, axis=1)
    grad_ada = dot_tn(style_own, mod_group)
    bias_group = jnp.concatenate(
        [
            jnp.sum(mod_group.astype(F32), axis=0),
            jnp.sum(reports[:, 7 * edge :].astype(F32), axis=0),
        ]
    )
    own_bias = biases.shape[0]
    grad_bias = lax.dynamic_slice_in_dim(bias_group, line * own_bias, own_bias, axis=0)

    def both_halves(piece):
        other = swap_with(piece, "dp", 1)
        first = jnp.where(pair == 0, piece, other)
        second = jnp.where(pair == 0, other, piece)
        return jnp.concatenate([first, second], axis=0).astype(F32)

    reduced = (
        grad_ada,
        both_halves(qkv_half),
        both_halves(proj_half),
        both_halves(one_half),
        both_halves(two_half),
        grad_bias,
    )

    power = step_count[0].astype(F32)
    fix_one = 1.0 - jnp.power(BETA_ONE, power)
    fix_two = 1.0 - jnp.power(BETA_TWO, power)
    rates = learning_rates(D, FF)
    firsts_out = []
    seconds_out = []
    local_deltas = []
    for index in range(6):
        gradient = reduced[index]
        first_next = BETA_ONE * firsts[index][0] + (1.0 - BETA_ONE) * gradient
        second_next = BETA_TWO * seconds[index][0] + (1.0 - BETA_TWO) * gradient * gradient
        master = masters[index]
        local = master - rates[index] * (
            first_next / fix_one / (jnp.sqrt(second_next / fix_two) + ADAM_EPS)
            + WEIGHT_DECAY * master
        )
        firsts_out.append(first_next[None])
        seconds_out.append(second_next[None])
        local_deltas.append((master - local).astype(BF16))

    def sum_groups(delta):
        if delta.ndim == 1:
            total = (delta.astype(F32) + swap_with(delta, "rep", 1).astype(F32)).astype(BF16)
            return total.astype(F32) + swap_with(total, "rep", 2).astype(F32)
        quarter = delta.shape[0] // 4
        columns = delta.shape[1]
        low = rep % 2
        mine = lax.dynamic_slice_in_dim(delta, pair * 2 * quarter, 2 * quarter, axis=0)
        mine = mine.reshape(2, quarter, columns)
        keep = lax.dynamic_index_in_dim(mine, low, 0, keepdims=False)
        give = lax.dynamic_index_in_dim(mine, 1 - low, 0, keepdims=False)
        total = (keep.astype(F32) + swap_with(give, "rep", 1).astype(F32)).astype(BF16)
        total = (total.astype(F32) + swap_with(total, "rep", 2).astype(F32)).astype(BF16)
        other = swap_with(total, "dp", 1)
        twin = jnp.stack([jnp.where(pair == 0, total, other), jnp.where(pair == 0, other, total)])
        twin_other = swap_with(twin, "rep", 1)
        first = jnp.where(low == 0, twin, twin_other)
        second = jnp.where(low == 0, twin_other, twin)
        return jnp.stack([first, second], axis=1).reshape(4 * quarter, columns).astype(F32)

    deltas_out = []
    outers_out = []
    weights_out = []
    for index in range(6):
        delta = sum_groups(local_deltas[index]) / groups
        outer_next = OUTER_MOMENTUM * outers[index] + delta
        deltas_out.append(delta)
        outers_out.append(outer_next)
        weights_out.append(masters[index] - OUTER_RATE * (delta + OUTER_MOMENTUM * outer_next))
    grads_out = tuple((gradient[None] for gradient in reduced))
    return (
        (cube(result) if result.ndim == 2 else result, in_grad)
        + grads_out
        + tuple(firsts_out)
        + tuple(seconds_out)
        + tuple(deltas_out)
        + tuple(outers_out)
        + tuple(weights_out)
    )


def solution(mesh):
    in_specs = (
        P(("rep", "dp", "fsdp"), None, None),
        P(("rep", "dp", "fsdp"), None, None),
        P(("rep", "dp", "fsdp")),
        P(("rep", "dp", "fsdp")),
        P(("rep", "dp", "fsdp")),
        P(),
        P(),
        P("fsdp", None),
        P("fsdp", None),
        P("fsdp", None),
        P("fsdp", None),
        P("fsdp", None),
        P("fsdp"),
        P("rep", "fsdp", None),
        P("rep", "fsdp", None),
        P("rep", "fsdp", None),
        P("rep", "fsdp", None),
        P("rep", "fsdp", None),
        P("rep", "fsdp"),
        P("rep", "fsdp", None),
        P("rep", "fsdp", None),
        P("rep", "fsdp", None),
        P("rep", "fsdp", None),
        P("rep", "fsdp", None),
        P("rep", "fsdp"),
        P("fsdp", None),
        P("fsdp", None),
        P("fsdp", None),
        P("fsdp", None),
        P("fsdp", None),
        P("fsdp"),
    )
    out_specs = (
        P(("rep", "dp", "fsdp"), None, None),
        P(("rep", "dp", "fsdp"), None, None),
        P("rep", "fsdp", None),
        P("rep", "fsdp", None),
        P("rep", "fsdp", None),
        P("rep", "fsdp", None),
        P("rep", "fsdp", None),
        P("rep", "fsdp"),
        P("rep", "fsdp", None),
        P("rep", "fsdp", None),
        P("rep", "fsdp", None),
        P("rep", "fsdp", None),
        P("rep", "fsdp", None),
        P("rep", "fsdp"),
        P("rep", "fsdp", None),
        P("rep", "fsdp", None),
        P("rep", "fsdp", None),
        P("rep", "fsdp", None),
        P("rep", "fsdp", None),
        P("rep", "fsdp"),
        P("fsdp", None),
        P("fsdp", None),
        P("fsdp", None),
        P("fsdp", None),
        P("fsdp", None),
        P("fsdp"),
        P("fsdp", None),
        P("fsdp", None),
        P("fsdp", None),
        P("fsdp", None),
        P("fsdp", None),
        P("fsdp"),
        P("fsdp", None),
        P("fsdp", None),
        P("fsdp", None),
        P("fsdp", None),
        P("fsdp", None),
        P("fsdp"),
    )
    return jax.shard_map(body, mesh=mesh, in_specs=in_specs, out_specs=out_specs, check_vma=False)
```

time: 2470 us -> 1180 us (0.48)
  waiting for transfers between devices: 1830 us -> 500 us
  local copies, waits for them, and re-layouts: 53.9 us -> 211 us
  matrix products: 333 us -> 182 us
  blocking collectives: 54.4 us -> 0 us
  starting transfers between devices: 0.88 us -> 48.2 us
  other arithmetic: 176 us -> 210 us
    all_gather x5 -> x3, waiting for transfers between devices: 753 us -> 100 us  [the longest x1 54.7 us: body(): lax.all_gather(attention_cut, everyone, axis=0, tiled=True)]
    reduce_scatter x5 -> x4, waiting for transfers between devices: 652 us -> 53.2 us  [the longest x2 53.2 us: pair_first(): lax.psum_scatter(both.reshape(-1, gradient.shape[1]), 'fsdp', scatter_dim...]
    psum x2 -> x0, waiting for transfers between devices: 424 us -> none  [the longest x1 227 us: body(): lax.psum(ada_owned, 'dp').astype(jnp.float32)]
    ppermute x0 -> x38, waiting for transfers between devices: none -> 347 us  [the longest x29 328 us: swap_with(): return lax.ppermute(value, axis, [(i, i ^ bit) for i in range(size)])]
    dot_general x58 -> x20, matrix products: 333 us -> 182 us  [the longest x4 55.7 us: dot_nt(): lax.dot_general(left, right, (((1,), (1,)), ((), ())), preferred_element_...]
    reshape x0 -> x10, local copies, waits for them, and re-layouts: none -> 80.5 us  [the longest x1 34.7 us: body(): lax.all_gather(one_cut, everyone, axis=0, tiled=True)]
    add x4 -> x15, other arithmetic: 0.04 us -> 52.7 us  [the longest x8 37.9 us: body(): first_next = BETA_ONE * firsts[index][0] + (1.0 - BETA_ONE) * gradient]
    ppermute x0 -> x38, starting transfers between devices: none -> 47.5 us  [the longest x29 34.6 us: swap_with(): return lax.ppermute(value, axis, [(i, i ^ bit) for i in range(size)])]
  transfers between devices with their start and end apart: 12 -> 45, of which waited for: 11 -> 20; matrix products, arithmetic and copies ran while one was open for 11% -> 39% of each run, Pallas kernels for 0% -> 0%
where the time goes in v1:
time: 1180 us; the launch traced here: 1170 us
  waiting for transfers between devices  500 us (42%)
  local copies, waits for them, and re-layouts  211 us (18%)
  other arithmetic  210 us (18%)
  matrix products  182 us (15%)
  starting transfers between devices  48.2 us (4%)
  between operations  17.5 us (1%)
    ppermute x29, waiting for transfers between devices, swap_with(): return lax.ppermute(value, axis, [(i, i ^ bit) for i in range(size)])  328 us
    unnamed x191, local copies, waits for them, and re-layouts  59.7 us
    dot_general x4, matrix products, dot_nt(): lax.dot_general(left, right, (((1,), (1,)), ((), ())), preferred_element_...  55.7 us
    all_gather x1, waiting for transfers between devices, body(): lax.all_gather(attention_cut, everyone, axis=0, tiled=True)  54.7 us
    reduce_scatter x2, waiting for transfers between devices, pair_first(): lax.psum_scatter(both.reshape(-1, gradient.shape[1]), 'fsdp', scatter_dim...  53.2 us
    dot_general x5, matrix products, dot(): return jnp.dot(left, right, preferred_element_type=F32)  51.8 us
    dot_general x5, matrix products, dot_tn(): lax.dot_general(left, right, (((0,), (0,)), ((), ())), preferred_element_...  49 us
    all_gather x1, waiting for transfers between devices, body(): lax.all_gather(one_cut, everyone, axis=0, tiled=True)  45.7 us
  transfers between devices with their start and end apart: 45, of which 20 were waited for; matrix products, arithmetic and copies ran while one was open for 39% of the time, Pallas kernels for 0%

profile of v1, /device:TPU:1, one launch (start us, length us, event | category | flops | bytes accessed | tf_op | source)
XLA Modules:
  0.0 1167.9 jit_solution(17446758146167249801)
XLA Ops:
  41.1 10.2 collective-permute-done.4
  57.8 45.7 %all-gather.6.cloned.1.call-done = bf16[4608,1152]{1,0:T(8,128)(2,1)} async-done(((bf16[144,1152]{1,0:T(8,128)(2,1)}), bf16[4608,1152]{1,0:T(8,128)(2,1)}) %all-gather.6.cloned.1.call-update) | async-done | bytes 10616848 | tf_op jit(solution)/shard_map/all_gather | solution.py:207
  103.5 34.7 %copy.185 = bf16[4,1152,1152]{2,0,1:T(4,128)(2,1)} copy(bf16[4,1152,1152]{2,1,0:T(8,128)(2,1)} %bitcast.311) | data formatting | bytes 21233664 | tf_op jit(solution)/shard_map/reshape | solution.py:207
  138.2 54.7 %all-gather.4.cloned.1.call-done = bf16[4608,1152]{1,0:T(8,128)(2,1)} async-done(((bf16[144,1152]{1,0:T(8,128)(2,1)}), bf16[4608,1152]{1,0:T(8,128)(2,1)}) %all-gather.4.cloned.1.call-update) | async-done | bytes 10616848 | tf_op jit(solution)/shard_map/all_gather | solution.py:203
  192.9 7.1 slice.111
  200.0 12.9 %copy.139 = bf16[1152,3,1152]{0,2,1:T(8,128)(2,1)} copy(bf16[1152,3,1152]{2,0,1:T(8,128)(2,1)} %bitcast.280) | data formatting | bytes 15925248 | tf_op jit(solution)/shard_map/transpose | solution.py:204
  212.9 12.5 %add_convert_fusion = bf16[768,3456]{1,0:T(8,128)(2,1)} fusion(bf16[768,1152]{1,0:T(8,128)(2,1)} %bitcast.343, bf16[1152,3456]{0,1:T(8,128)(2,1)} %bitcast.321, f32[3456]{0:T(1024)S(1)} %pad_maximum_fusion.11), kind=kOutput, calls=%fused_computation.25 | convolution fusion | flops 6120603648 | bytes 15054336 | tf_op jit(solution)/shard_map/dot_general | solution.py:27
  225.4 19.6 %reshape.605 = bf16[3,256,3,16,72]{4,3,2,1,0:T(8,128)(2,1)} reshape(bf16[768,3456]{1,0:T(8,128)(2,1)} %add_convert_fusion) | data formatting | bytes 10616832 | tf_op jit(solution)/shard_map/reshape | solution.py:115
  245.0 8.2 fusion.114
  267.2 15.4 %reshape.602 = bf16[1152,4608,1]{1,0,2:T(8,128)(2,1)} reshape(bf16[1152,4,1152]{2,1,0:T(4,128)(2,1)} %bitcast.272) | data formatting | bytes 21233664 | tf_op jit(solution)/shard_map/reshape | solution.py:208
  282.6 11.7 %copy.179 = bf16[144,8,4,1152]{3,1,2,0:T(8,128)(2,1)} copy(bf16[144,8,4,1152]{3,2,1,0:T(4,128)(2,1)} %bitcast.273) | data formatting | bytes 21233664
  309.1 5.2 convolution_add_fusion.1
  320.4 11.8 %fusion.119 = f32[768,4608]{1,0:T(8,128)} fusion(bf16[768,1152]{1,0:T(8,128)(2,1)S(1)} %bitcast.339, bf16[1152,4608]{1,0:T(8,128)(2,1)S(1)} %bitcast.314), kind=kOutput, calls=%fused_computation.319 | convolution fusion | flops 8153726976 | bytes 26542080 | tf_op jit(solution)/shard_map/dot_general | solution.py:27
  332.2 17.8 %convolution_convert_fusion = bf16[4608,1152]{1,0:T(8,128)(2,1)} fusion(bf16[768,1152]{1,0:T(8,128)(2,1)S(1)} %bitcast.345, f32[768,4608]{1,0:T(8,128)} %fusion.119, f32[4608]{0:T(1024)S(1)} %slice.122), kind=kOutput, calls=%fused_computation.3 | convolution fusion | flops 8194424832 | bytes 26560512 | tf_op jit(solution)/shard_map/dot_general | solution.py:35
  350.1 20.1 %fusion.118 = (bf16[4608]{0:T(1024)(128)(2,1)S(1)}, bf16[768,4608]{1,0:T(8,128)(2,1)}) fusion(f32[768,4608]{1,0:T(8,128)} %fusion.119, f32[4608]{0:T(1024)S(1)} %slice.122, bf16[768,1152]{1,0:T(8,128)(2,1)S(1)} %bitcast.346, bf16[4608,1152]{1,0:T(8,128)(2,1)} %all-gather.8.cloned.1.call-done), kind=kOutput, calls=%fused_computation.318 | convolution fusion | flops 8228040192 | bytes 33647616 | tf_op jit(solution)/shard_map/dot_general | solution.py:31
  370.3 18.3 %convolution_add_fusion = f32[768,1152]{1,0:T(8,128)} fusion(bf16[4608,1152]{1,0:T(8,128)(2,1)} %all-gather.8.cloned.1.call-done, f32[1152]{0:T(1024)S(1)} %copy-done.62, f32[768,4608]{1,0:T(8,128)} %fusion.119, f32[4608]{0:T(1024)S(1)} %slice.122), kind=kOutput, calls=%fused_computation.83 | convolution fusion | flops 8190001152 | bytes 28334592 | tf_op jit(solution)/shard_map/dot_general | solution.py:27
  388.6 18.4 %multiply_reduce_fusion.2 = (bf16[3,1152]{1,0:T(4,128)(2,1)S(1)}, bf16[3,256,1152]{2,1,0:T(8,128)(2,1)}, bf16[3,1152]{1,0:T(4,128)(2,1)S(1)}, f32[3,256]{1,0:T(4...) fusion(f32[3,256,1152]{2,1,0:T(8,128)} %bitcast.355, ...), kind=kOutput, calls=%fused_computation.113 | convolution fusion | flops 8168754688 | bytes 31911180 | tf_op jit(solution)/shard_map/dot_general | solution.py:31
  407.0 5.5 fusion.112
  422.7 6.4 reshape.606
  432.7 6.2 convolution_convert_fusion.5
  438.9 10.4 multiply_reduce_fusion
  449.6 6.4 multiply_convert_fusion.1
  475.6 12.2 %fusion.56 = (bf16[3,1152]{1,0:T(4,128)(2,1)S(1)}, f32[3,256]{1,0:T(4,128)S(1)}, f32[3,256]{1,0:T(4,128)S(1)}, bf16[3,1152]{1,0:T(4,128)(2,1)S(1)}, f32[3,256,1152]{2,1,0:T(8,128)S(1)}) fusion(bf16[3,256,1152]{2,1,0:T(8,128)(2,1)S(1)} %copy-done.6, f32[3,256]{1,0:T(4,128)S(1)} %copy-done.57, f32[3,256]{1,0:T(4,128)S(1)} %copy-done.55, ...), kind=kOutput, calls=%fused_computation.111 | convolution fusion | flops 6140059136 | bytes 18619392 | tf_op jit(solution)/shard_map/dot_general | solution.py:31
  514.7 11.4 convolution_convert_fusion.2
  529.2 5.3 dynamic-slice_bitcast_fusion
  538.0 5.1 collective-permute-done.8
  548.4 17.7 %add_multiply_fusion = (f32[288,6912]{1,0:T(8,128)}, f32[1,288,6912]{2,1,0:T(8,128)}, f32[288,6912]{1,0:T(8,128)}) fusion(f32[]{:T(128)} %bitcast.59, f32[]{:T(128)} %bitcast.58, f32[288,6912]{1,0:T(8,128)} %fusion.100, f32[1,288,6912]{2,1,0:T(8,128)} %param.50, f32[1,288,6912]{2,1,0:T(8,128)} %param.44), kind=kLoop, calls=%fused_computation.34 | loop fusion | flops 19906560 | bytes 47775752 | tf_op jit(solution)/shard_map/multiply.9
  566.2 5.7 fusion.39
  574.9 128.2 %collective-permute-done.14 = bf16[4,576,1152]{2,1,0:T(8,128)(2,1)} collective-permute-done((bf16[4,576,1152]{2,1,0:T(8,128)(2,1)}, bf16[4,576,1152]{2,1,0:T(8,128)(2,1)}, u32[]{:S(2)}, u32[]{:S(2)}) %collective-permute-start.14) | collective-permute-done | bytes 5308448 | tf_op jit(solution)/shard_map/ppermute | solution.py:63
  703.1 7.8 fusion.8
  713.3 11.3 convolution_convert_fusion.1
  735.3 130.3 %collective-permute-done.18 = bf16[72,6912]{1,0:T(8,128)(2,1)S(1)} collective-permute-done((bf16[72,6912]{1,0:T(8,128)(2,1)S(1)}, bf16[72,6912]{1,0:T(8,128)(2,1)S(1)}, u32[]{:S(2)}, u32[]{:S(2)}) %collective-permute-start.18) | collective-permute-done | bytes 995360 | tf_op jit(solution)/shard_map/ppermute | solution.py:63
  876.9 7.8 fusion.9
  901.6 10.5 multiply_subtract_fusion
  926.2 53.2 %reduce-scatter.9.cloned.1.call-done = bf16[144,4608]{1,0:T(8,128)(2,1)} async-done(((bf16[576,4608]{1,0:T(8,128)(2,1)}), bf16[144,4608]{1,0:T(8,128)(2,1)}) %reduce-scatter.9.cloned.1.call-update) | async-done | bytes 1327120 | tf_op jit(solution)/shard_map/reduce_scatter | solution.py:265
  982.0 6.2 fusion.37
  998.7 11.0 collective-permute-done.13
  1021.2 5.6 fusion.13
  1026.8 5.9 multiply_add_fusion.5
  1034.3 10.4 fusion.12
  1044.8 5.0 fusion.14
  1049.8 6.2 multiply_add_fusion.4
  1064.4 9.7 collective-permute-done.21
  1076.8 8.0 collective-permute-done.22
  1092.4 10.1 collective-permute-done.33
  1107.1 10.7 collective-permute-done.34
  1133.8 11.5 multiply_subtract_fusion.2
  1149.7 11.1 multiply_subtract_fusion.1
  (435 shorter events, 273.4 us)
Async XLA Ops:
  7.3 96.2 %all-gather.6.cloned.1.call-start = ((), (), s32[]{:S(2)}) async-start(), calls=%async_computation.5 | async-start | bytes 10948608 | tf_op jit(solution)/shard_map/all_gather | solution.py:207
  9.3 183.5 %all-gather.4.cloned.1.call-start = ((), (), s32[]{:S(2)}) async-start(), calls=%async_computation.4 | async-start | bytes 10948608 | tf_op jit(solution)/shard_map/all_gather | solution.py:203
  13.1 337.0 %all-gather.8.cloned.1.call-start = ((), (), s32[]{:S(2)}) async-start(), calls=%async_computation.6 | async-start | bytes 10948608 | tf_op jit(solution)/shard_map/all_gather | solution.py:211
  15.0 869.7 %reduce-scatter.7.cloned.1.call-start = ((), (), s32[]{:S(2)}) async-start(), calls=%async_computation.8 | async-start | bytes 2985984 | tf_op jit(solution)/shard_map/reduce_scatter | solution.py:282
  16.1 12.8 %collective-permute-start.2 = (bf16[7488]{0:T(1024)(128)(2,1)S(1)}, bf16[7488]{0:T(1024)(128)(2,1)S(1)}, u32[]{:S(2)}, u32[]{:S(2)}) collective-permute-start(bf16[7488]{0:T(1024)(128)(2,1)S(1)} %pad_maximum_fusion.10), channel_id=1, source_target_pairs={{0,3},{1,0},{2,1},{3,2},{4,7},{5,4},{6,5},{7,6},{8,11},{9,8},{10,9... | collective-permute-start | bytes 44936 | tf_op jit(solution)/shard_map/ppermute | solution.py:58
  20.3 8.3 collective-permute-start.1
  20.3 7.9 collective-permute-start
  33.7 5.6 collective-permute-start.3
  35.9 5.2 collective-permute-start.5
  37.0 14.3 %collective-permute-start.4 = (f32[3,6912]{1,0:T(4,128)S(1)}, f32[3,6912]{1,0:T(4,128)S(1)}, u32[]{:S(2)}, u32[]{:S(2)}) collective-permute-start(f32[3,6912]{1,0:T(4,128)S(1)} %get-tuple-element.132), channel_id=1, source_target_pairs={{0,2},{1,3},{2,0},{3,1},{4,6},{5,7},{6,4},{7,5},{8,10},{9,11},{10,... | collective-permute-start | bytes 248840 | tf_op jit(solution)/shard_map/ppermute | solution.py:58
  51.4 86.9 %copy-start.48 = (f32[3,1152]{1,0:T(4,128)}, f32[3,1152]{1,0:T(4,128)S(1)}, u32[]{:S(2)}) copy-start(f32[3,1152]{1,0:T(4,128)S(1)} %get-tuple-element.139) | copy-start | bytes 41476
  461.7 458.7 %reduce-scatter.5.cloned.1.call-start = ((), (), s32[]{:S(2)}) async-start(), calls=%async_computation.7 | async-start | bytes 8957952 | tf_op jit(solution)/shard_map/reduce_scatter | solution.py:286
  512.8 14.2 %collective-permute-start.6 = (bf16[33408]{0:T(1024)(128)(2,1)}, bf16[33408]{0:T(1024)(128)(2,1)S(1)}, u32[]{:S(2)}, u32[]{:S(2)}) collective-permute-start(bf16[33408]{0:T(1024)(128)(2,1)} %dynamic-update-slice.6), channel_id=1, source_target_pairs={{0,4},{4,0},{1,5},{5,1},{2,6},{6,2},{3,7},{7,3},{8,12},{12,8},{9,1... | collective-permute-start | bytes 200456 | tf_op jit(solution)/shard_map/ppermute | solution.py:63
  527.8 10.2 collective-permute-start.7
  534.5 168.5 %collective-permute-start.14 = (bf16[4,576,1152]{2,1,0:T(8,128)(2,1)}, bf16[4,576,1152]{2,1,0:T(8,128)(2,1)}, u32[]{:S(2)}, u32[]{:S(2)}) collective-permute-start(bf16[4,576,1152]{2,1,0:T(8,128)(2,1)} %dynamic-slice_bitcast_fusion), channel_id=1, source_target_pairs={{0,4},{4,0},{1,5},{5,1},{2,6},{6,2},{3,7},{7,3},{8,12},{12,8},{9,1... | collective-permute-start | bytes 15925256 | tf_op jit(solution)/shard_map/ppermute | solution.py:63
  534.6 390.3 %reduce-scatter.11.cloned.1.call-start = ((), (), s32[]{:S(2)}) async-start(), calls=%async_computation.10 | async-start | bytes 6635520 | tf_op jit(solution)/shard_map/reduce_scatter | solution.py:265
  534.7 8.5 collective-permute-start.8
  535.4 7.8 collective-permute-start.9
  572.9 138.5 %collective-permute-start.16 = (bf16[72,6912]{1,0:T(8,128)(2,1)}, bf16[72,6912]{1,0:T(8,128)(2,1)}, u32[]{:S(2)}, u32[]{:S(2)}) collective-permute-start(bf16[72,6912]{1,0:T(8,128)(2,1)} %dynamic-slice_bitcast_fusion.2), channel_id=1, source_target_pairs={{0,8},{8,0},{16,24},{24,16},{1,9},{9,1},{17,25},{25,17},{2,10},{10... | collective-permute-start | bytes 2985992 | tf_op jit(solution)/shard_map/ppermute | solution.py:63
  710.9 268.4 %reduce-scatter.9.cloned.1.call-start = ((), (), s32[]{:S(2)}) async-start(), calls=%async_computation.9 | async-start | bytes 6635520 | tf_op jit(solution)/shard_map/reduce_scatter | solution.py:265
  712.8 21.7 %collective-permute-start.17 = (bf16[72,6912]{1,0:T(8,128)(2,1)S(1)}, bf16[72,6912]{1,0:T(8,128)(2,1)S(1)}, u32[]{:S(2)}, u32[]{:S(2)}) collective-permute-start(bf16[72,6912]{1,0:T(8,128)(2,1)S(1)} %fusion.70), channel_id=1, source_target_pairs={{0,16},{8,24},{16,0},{24,8},{1,17},{9,25},{17,1},{25,9},{2,18},{10... | collective-permute-start | bytes 2985992 | tf_op jit(solution)/shard_map/ppermute | solution.py:63
  730.1 146.8 %collective-permute-start.12 = (bf16[4,144,4608]{2,1,0:T(8,128)(2,1)}, bf16[4,144,4608]{2,1,0:T(8,128)(2,1)}, u32[]{:S(2)}, u32[]{:S(2)}) collective-permute-start(bf16[4,144,4608]{2,1,0:T(8,128)(2,1)} %dynamic-slice_bitcast_fusion.1), channel_id=1, source_target_pairs={{0,4},{4,0},{1,5},{5,1},{2,6},{6,2},{3,7},{7,3},{8,12},{12,8},{9,1... | collective-permute-start | bytes 15925256 | tf_op jit(solution)/shard_map/ppermute | solution.py:63
  734.8 130.8 %collective-permute-start.18 = (bf16[72,6912]{1,0:T(8,128)(2,1)S(1)}, bf16[72,6912]{1,0:T(8,128)(2,1)S(1)}, u32[]{:S(2)}, u32[]{:S(2)}) collective-permute-start(bf16[72,6912]{1,0:T(8,128)(2,1)S(1)} %add_convert_fusion.2), channel_id=1, source_target_pairs={{0,4},{4,0},{1,5},{5,1},{2,6},{6,2},{3,7},{7,3},{8,12},{12,8},{9,1... | collective-permute-start | bytes 2985992 | tf_op jit(solution)/shard_map/ppermute | solution.py:63
  735.3 134.9 %copy-start.51 = (f32[4032]{0:T(1024)S(1)}, f32[4032]{0:T(1024)}, u32[]{:S(2)}) copy-start(f32[4032]{0:T(1024)} %param.43) | copy-start | bytes 48388
  735.3 141.0 %copy-start.60 = (f32[4032]{0:T(1024)S(1)}, f32[4032]{0:T(1024)}, u32[]{:S(2)}) copy-start(f32[4032]{0:T(1024)} %param.61) | copy-start | bytes 48388
  867.2 18.8 %collective-permute-start.19 = (bf16[2,72,6912]{2,1,0:T(8,128)(2,1)}, bf16[2,72,6912]{2,1,0:T(8,128)(2,1)}, u32[]{:S(2)}, u32[]{:S(2)}) collective-permute-start(bf16[2,72,6912]{2,1,0:T(8,128)(2,1)} %pad_maximum_fusion.2), channel_id=1, source_target_pairs={{0,8},{8,0},{16,24},{24,16},{1,9},{9,1},{17,25},{25,17},{2,10},{10... | collective-permute-start | bytes 5971976 | tf_op jit(solution)/shard_map/ppermute | solution.py:63
  870.8 2.9 collective-permute-start.36
  873.8 2.5 collective-permute-start.37
  884.8 8.0 collective-permute-start.11
  894.0 6.4 collective-permute-start.24
  900.4 11.7 %collective-permute-start.25 = (bf16[72,1152]{1,0:T(8,128)(2,1)S(1)}, bf16[72,1152]{1,0:T(8,128)(2,1)S(1)}, u32[]{:S(2)}, u32[]{:S(2)}) collective-permute-start(bf16[72,1152]{1,0:T(8,128)(2,1)S(1)} %fusion.96), channel_id=1, source_target_pairs={{0,16},{8,24},{16,0},{24,8},{1,17},{9,25},{17,1},{25,9},{2,18},{10... | collective-permute-start | bytes 497672 | tf_op jit(solution)/shard_map/ppermute | solution.py:63
  912.2 5.6 collective-permute-start.26
  917.9 2.4 collective-permute-start.27
  920.5 60.1 %collective-permute-start.10 = (bf16[144,3456]{1,0:T(8,128)(2,1)}, bf16[144,3456]{1,0:T(8,128)(2,1)}, u32[]{:S(2)}, u32[]{:S(2)}) collective-permute-start(bf16[144,3456]{1,0:T(8,128)(2,1)} %reduce-scatter.5.cloned.1.call-done), channel_id=1, source_target_pairs={{0,4},{4,0},{1,5},{5,1},{2,6},{6,2},{3,7},{7,3},{8,12},{12,8},{9,1... | collective-permute-start | bytes 2985992 | tf_op jit(solution)/shard_map/ppermute | solution.py:63
  924.9 107.8 %collective-permute-start.15 = (bf16[576,1152]{1,0:T(8,128)(2,1)}, bf16[576,1152]{1,0:T(8,128)(2,1)}, u32[]{:S(2)}, u32[]{:S(2)}) collective-permute-start(bf16[576,1152]{1,0:T(8,128)(2,1)} %reduce-scatter.11.cloned.1.call-done), channel_id=1, source_target_pairs={{0,4},{4,0},{1,5},{5,1},{2,6},{6,2},{3,7},{7,3},{8,12},{12,8},{9,1... | collective-permute-start | bytes 3981320 | tf_op jit(solution)/shard_map/ppermute | solution.py:63
  979.3 30.4 %collective-permute-start.13 = (bf16[144,4608]{1,0:T(8,128)(2,1)}, bf16[144,4608]{1,0:T(8,128)(2,1)}, u32[]{:S(2)}, u32[]{:S(2)}) collective-permute-start(bf16[144,4608]{1,0:T(8,128)(2,1)} %reduce-scatter.9.cloned.1.call-done), channel_id=1, source_target_pairs={{0,4},{4,0},{1,5},{5,1},{2,6},{6,2},{3,7},{7,3},{8,12},{12,8},{9,1... | collective-permute-start | bytes 3981320 | tf_op jit(solution)/shard_map/ppermute | solution.py:63
  991.1 69.2 %collective-permute-start.20 = (bf16[72,3456]{1,0:T(8,128)(2,1)}, bf16[72,3456]{1,0:T(8,128)(2,1)}, u32[]{:S(2)}, u32[]{:S(2)}) collective-permute-start(bf16[72,3456]{1,0:T(8,128)(2,1)} %dynamic-slice_bitcast_fusion.5), channel_id=1, source_target_pairs={{0,8},{8,0},{16,24},{24,16},{1,9},{9,1},{17,25},{25,17},{2,10},{10... | collective-permute-start | bytes 1493000 | tf_op jit(solution)/shard_map/ppermute | solution.py:63
  1019.7 43.1 %collective-permute-start.28 = (bf16[72,4608]{1,0:T(8,128)(2,1)S(1)}, bf16[72,4608]{1,0:T(8,128)(2,1)}, u32[]{:S(2)}, u32[]{:S(2)}) collective-permute-start(bf16[72,4608]{1,0:T(8,128)(2,1)S(1)} %dynamic-slice_bitcast_fusion.4), channel_id=1, source_target_pairs={{0,8},{8,0},{16,24},{24,16},{1,9},{9,1},{17,25},{25,17},{2,10},{10... | collective-permute-start | bytes 1990664 | tf_op jit(solution)/shard_map/ppermute | solution.py:63
  1060.2 15.2 %collective-permute-start.32 = (bf16[288,1152]{1,0:T(8,128)(2,1)S(1)}, bf16[288,1152]{1,0:T(8,128)(2,1)S(1)}, u32[]{:S(2)}, u32[]{:S(2)}) collective-permute-start(bf16[288,1152]{1,0:T(8,128)(2,1)S(1)} %dynamic-slice_bitcast_fusion.3), channel_id=1, source_target_pairs={{0,8},{8,0},{16,24},{24,16},{1,9},{9,1},{17,25},{25,17},{2,10},{10... | collective-permute-start | bytes 1990664 | tf_op jit(solution)/shard_map/ppermute | solution.py:63
  1061.5 12.5 %collective-permute-start.21 = (bf16[72,3456]{1,0:T(8,128)(2,1)S(1)}, bf16[72,3456]{1,0:T(8,128)(2,1)S(1)}, u32[]{:S(2)}, u32[]{:S(2)}) collective-permute-start(bf16[72,3456]{1,0:T(8,128)(2,1)S(1)} %fusion.91), channel_id=1, source_target_pairs={{0,16},{8,24},{16,0},{24,8},{1,17},{9,25},{17,1},{25,9},{2,18},{10... | collective-permute-start | bytes 1493000 | tf_op jit(solution)/shard_map/ppermute | solution.py:63
  1064.0 24.2 %collective-permute-start.29 = (bf16[72,4608]{1,0:T(8,128)(2,1)S(1)}, bf16[72,4608]{1,0:T(8,128)(2,1)S(1)}, u32[]{:S(2)}, u32[]{:S(2)}) collective-permute-start(bf16[72,4608]{1,0:T(8,128)(2,1)S(1)} %fusion.90), channel_id=1, source_target_pairs={{0,16},{8,24},{16,0},{24,8},{1,17},{9,25},{17,1},{25,9},{2,18},{10... | collective-permute-start | bytes 1990664 | tf_op jit(solution)/shard_map/ppermute | solution.py:63
  1074.1 10.7 collective-permute-start.22
  1075.6 26.9 %collective-permute-start.33 = (bf16[288,1152]{1,0:T(8,128)(2,1)S(1)}, bf16[288,1152]{1,0:T(8,128)(2,1)S(1)}, u32[]{:S(2)}, u32[]{:S(2)}) collective-permute-start(bf16[288,1152]{1,0:T(8,128)(2,1)S(1)} %fusion.89), channel_id=1, source_target_pairs={{0,16},{8,24},{16,0},{24,8},{1,17},{9,25},{17,1},{25,9},{2,18},{10... | collective-permute-start | bytes 1990664 | tf_op jit(solution)/shard_map/ppermute | solution.py:63
  1088.4 15.5 %collective-permute-start.30 = (bf16[72,4608]{1,0:T(8,128)(2,1)S(1)}, bf16[72,4608]{1,0:T(8,128)(2,1)S(1)}, u32[]{:S(2)}, u32[]{:S(2)}) collective-permute-start(bf16[72,4608]{1,0:T(8,128)(2,1)S(1)} %add_convert_fusion.4), channel_id=1, source_target_pairs={{0,4},{4,0},{1,5},{5,1},{2,6},{6,2},{3,7},{7,3},{8,12},{12,8},{9,1... | collective-permute-start | bytes 1990664 | tf_op jit(solution)/shard_map/ppermute | solution.py:63
  1089.8 31.6 %collective-permute-start.23 = (bf16[2,72,3456]{2,1,0:T(8,128)(2,1)S(1)}, bf16[2,72,3456]{2,1,0:T(8,128)(2,1)S(1)}, u32[]{:S(2)}, u32[]{:S(2)}) collective-permute-start(bf16[2,72,3456]{2,1,0:T(8,128)(2,1)S(1)} %pad_maximum_fusion.6), channel_id=1, source_target_pairs={{0,8},{8,0},{16,24},{24,16},{1,9},{9,1},{17,25},{25,17},{2,10},{10... | collective-permute-start | bytes 2985992 | tf_op jit(solution)/shard_map/ppermute | solution.py:63
  1102.6 15.1 %collective-permute-start.34 = (bf16[288,1152]{1,0:T(8,128)(2,1)S(1)}, bf16[288,1152]{1,0:T(8,128)(2,1)S(1)}, u32[]{:S(2)}, u32[]{:S(2)}) collective-permute-start(bf16[288,1152]{1,0:T(8,128)(2,1)S(1)} %add_convert_fusion.3), channel_id=1, source_target_pairs={{0,4},{4,0},{1,5},{5,1},{2,6},{6,2},{3,7},{7,3},{8,12},{12,8},{9,1... | collective-permute-start | bytes 1990664 | tf_op jit(solution)/shard_map/ppermute | solution.py:63
  1105.2 24.1 %collective-permute-start.31 = (bf16[2,72,4608]{2,1,0:T(8,128)(2,1)}, bf16[2,72,4608]{2,1,0:T(8,128)(2,1)}, u32[]{:S(2)}, u32[]{:S(2)}) collective-permute-start(bf16[2,72,4608]{2,1,0:T(8,128)(2,1)} %pad_maximum_fusion.4), channel_id=1, source_target_pairs={{0,8},{8,0},{16,24},{24,16},{1,9},{9,1},{17,25},{25,17},{2,10},{10... | collective-permute-start | bytes 3981320 | tf_op jit(solution)/shard_map/ppermute | solution.py:63
  1119.1 26.2 %collective-permute-start.35 = (bf16[2,288,1152]{2,1,0:T(8,128)(2,1)}, bf16[2,288,1152]{2,1,0:T(8,128)(2,1)}, u32[]{:S(2)}, u32[]{:S(2)}) collective-permute-start(bf16[2,288,1152]{2,1,0:T(8,128)(2,1)} %pad_maximum_fusion.5), channel_id=1, source_target_pairs={{0,8},{8,0},{16,24},{24,16},{1,9},{9,1},{17,25},{25,17},{2,10},{10... | collective-permute-start | bytes 3981320 | tf_op jit(solution)/shard_map/ppermute | solution.py:63
  (82 other events, 984.3 us)
Sparse Core Ops, SparseCore 0:
  11.6 91.8 all-gather.5
  107.0 85.8 all-gather.3
  196.4 85.8 all-gather.7
  461.9 68.2 reduce-scatter.6
  534.7 177.6 reduce-scatter.4
  715.3 93.7 reduce-scatter.10
  884.9 94.4 reduce-scatter.8

commit v2 on v1

v2 whole, which is shorter than its diff:
```python
import math

import jax
import jax.numpy as jnp
from jax import lax
from jax.experimental import pallas as pl
from jax.experimental.pallas import tpu as pltpu
from jax.sharding import PartitionSpec as P

D = 1152
HEADS = 16
FF = 4608


NORM_EPS = 1e-06
BETA_ONE = 0.9
BETA_TWO = 0.95
ADAM_EPS = 1e-08
WEIGHT_DECAY = 0.1
OUTER_RATE = 0.7
OUTER_MOMENTUM = 0.9
FEW = 8

F32 = jnp.float32
BF16 = jnp.bfloat16


def dot(left, right):
    return jnp.dot(left, right, preferred_element_type=F32)


def dot_nt(left, right):
    return lax.dot_general(left, right, (((1,), (1,)), ((), ())), preferred_element_type=F32)


def dot_tn(left, right):
    return lax.dot_general(left, right, (((0,), (0,)), ((), ())), preferred_element_type=F32)


def time_embed(steps, width):
    half = width // 2
    frequency = jnp.exp(-math.log(10000.0) * jnp.arange(half).astype(F32) / half)
    angles = steps.astype(F32)[:, None] * frequency[None, :]
    return jnp.concatenate([jnp.cos(angles), jnp.sin(angles)], axis=1)


def learning_rates(width, hidden):
    return (
        2.0 / math.sqrt(width),
        2.0 / math.sqrt(width),
        2.0 / math.sqrt(width // 32),
        2.0 / math.sqrt(width),
        2.0 / math.sqrt(hidden),
        0.3,
    )


def shift_by(value, axis, step):
    size = lax.axis_size(axis)
    return lax.ppermute(value, axis, [(i, (i + step) % size) for i in range(size)])


def swap_with(value, axis, bit):
    size = lax.axis_size(axis)
    return lax.ppermute(value, axis, [(i, i ^ bit) for i in range(size)])


def gather_line(value, axis):
    size = lax.axis_size(axis)
    if size > FEW:
        return lax.all_gather(value, axis, axis=0)
    place = lax.axis_index(axis)
    result = jnp.zeros((size,) + value.shape, value.dtype)
    for step in range(size):
        piece = value if step == 0 else shift_by(value, axis, step)
        result = lax.dynamic_update_index_in_dim(result, piece, (place - step) % size, 0)
    return result


def scatter_line(value, axis):
    size = lax.axis_size(axis)
    if size > FEW:
        return lax.psum_scatter(value, axis, scatter_dimension=0, tiled=False)
    place = lax.axis_index(axis)
    total = lax.dynamic_index_in_dim(value, place, 0, keepdims=False)
    for step in range(1, size):
        piece = lax.dynamic_index_in_dim(value, (place + step) % size, 0, keepdims=False)
        total = total + shift_by(piece, axis, step)
    return total


def moments(values):
    center = values - jnp.mean(values, axis=-1, keepdims=True)
    inverse = lax.rsqrt(jnp.mean(center * center, axis=-1, keepdims=True) + NORM_EPS)
    return center * inverse, inverse


def norm_back(normed, inverse, upstream):
    first = jnp.mean(upstream, axis=-1, keepdims=True)
    second = jnp.mean(upstream * normed, axis=-1, keepdims=True)
    return (upstream - first - normed * second) * inverse


def gelu_pair(h):
    c = math.sqrt(2.0 / math.pi)
    inner = c * (h + 0.044715 * h * h * h)
    t = jnp.tanh(inner)
    value = 0.5 * h * (1.0 + t)
    slope = 0.5 * (1.0 + t) + 0.5 * h * (1.0 - t * t) * c * (1.0 + 3.0 * 0.044715 * h * h)
    return value, slope


def head_window(head, head_dim):
    low = head * head_dim
    start = low // 128 * 128
    stop = -(-(low + head_dim) // 128) * 128
    return start, stop, low - start


def head_mask(shape, offset, head_dim):
    lane = lax.broadcasted_iota(jnp.int32, shape, 1)
    return (lane >= offset) & (lane < offset + head_dim)


def attention_forward_kernel(
    x_ref, cot_ref, mod_ref, bias_ref, weight_ref,
    attn_in_ref, packed_ref, attended_ref, log_ref, attn_ref, x1_ref, mlp_in_ref, d_mlp_ref, sums_ref,
    gather_ref,
):
    length, width = x_ref.shape
    head_dim = width // HEADS
    factor = 1.0 / math.sqrt(head_dim)
    residual = x_ref[...].astype(F32)
    normed, _ = moments(residual)
    attn_in_ref[...] = (normed * (1.0 + mod_ref[0, 1:2]) + mod_ref[0, 0:1]).astype(BF16)
    for unit in range(3):
        piece = dot(attn_in_ref[...], weight_ref[unit]) + bias_ref[unit : unit + 1]
        packed_ref[:, unit * width : (unit + 1) * width] = piece.astype(BF16)
    for head in range(HEADS):
        start, stop, offset = head_window(head, head_dim)
        mask = head_mask((length, stop - start), offset, head_dim)
        query = packed_ref[:, start:stop]
        query = jnp.where(mask, query, jnp.zeros_like(query))
        keys = packed_ref[:, width + start : width + stop]
        values = packed_ref[:, 2 * width + start : 2 * width + stop]
        scores = dot_nt(query, keys) * factor
        top = jnp.max(scores, axis=-1, keepdims=True)
        raised = jnp.exp(scores - top)
        summed = jnp.sum(raised, axis=-1, keepdims=True)
        probs = (raised * (1.0 / summed)).astype(BF16)
        log_ref[:, head : head + 1] = top + jnp.log(summed)
        out = dot(probs, values)
        if offset == 0:
            gather_ref[:, start:stop] = out
        else:
            gather_ref[:, start:stop] = jnp.where(mask, out, gather_ref[:, start:stop])
    attended_ref[...] = gather_ref[...].astype(BF16)
    attn = dot(attended_ref[...], weight_ref[3]) + bias_ref[3:4]
    attn_ref[...] = attn
    middle = residual + mod_ref[0, 2:3] * attn
    x1_ref[...] = middle
    normed_two, _ = moments(middle)
    mlp_in_ref[...] = (normed_two * (1.0 + mod_ref[0, 4:5]) + mod_ref[0, 3:4]).astype(BF16)
    d_mlp = (mod_ref[0, 5:6] * (cot_ref[...].astype(F32) * mod_ref[0, 6:7])).astype(BF16)
    d_mlp_ref[...] = d_mlp
    sums_ref[0, 0:1] = jnp.sum(d_mlp.astype(F32), axis=0, keepdims=True)


def rows_spec(length, width):
    return pl.BlockSpec((length, width), lambda i: (i, 0))


def whole_spec(shape):
    return pl.BlockSpec(shape, lambda i: (0,) * len(shape), pipeline_mode=pl.Buffered(1))


def lead_spec(rows, width):
    return pl.BlockSpec((1, rows, width), lambda i: (i, 0, 0))


def params(megabytes):
    return pltpu.CompilerParams(vmem_limit_bytes=megabytes << 20)


def attention_forward(x, cot, mod, bias, weights, slots, length, width):
    tokens = slots * length
    row = rows_spec(length, width)
    return pl.pallas_call(
        attention_forward_kernel,
        grid=(slots,),
        in_specs=[row, row, lead_spec(8, width), whole_spec((8, width)), whole_spec((4, width, width))],
        out_specs=[
            row, rows_spec(length, 3 * width), row, rows_spec(length, 128), row, row, row, row,
            lead_spec(8, width),
        ],
        out_shape=[
            jax.ShapeDtypeStruct((tokens, width), BF16),
            jax.ShapeDtypeStruct((tokens, 3 * width), BF16),
            jax.ShapeDtypeStruct((tokens, width), BF16),
            jax.ShapeDtypeStruct((tokens, 128), F32),
            jax.ShapeDtypeStruct((tokens, width), F32),
            jax.ShapeDtypeStruct((tokens, width), F32),
            jax.ShapeDtypeStruct((tokens, width), BF16),
            jax.ShapeDtypeStruct((tokens, width), BF16),
            jax.ShapeDtypeStruct((slots, 8, width), F32),
        ],
        scratch_shapes=[pltpu.VMEM((length, width), F32)],
        compiler_params=params(48),
        cost_estimate=pl.CostEstimate(
            flops=2 * tokens * width * width * 4, bytes_accessed=40 << 20, transcendentals=0
        ),
    )(x, cot, mod, bias, weights)


def hidden_kernel(mlp_in_ref, weight_ref, bias_ref, act_ref, slope_ref):
    step = 256

    def chunk(index, carry):
        here = pl.ds(pl.multiple_of(index * step, step), step)
        hidden = dot(mlp_in_ref[here, :], weight_ref[0]) + bias_ref[0:1]
        value, slope = gelu_pair(hidden)
        act_ref[here, :] = value.astype(BF16)
        slope_ref[here, :] = slope.astype(BF16)
        return carry

    lax.fori_loop(0, mlp_in_ref.shape[0] // step, chunk, 0)


def hidden_forward(mlp_in, weights, bias):
    tokens, width = mlp_in.shape
    units = weights.shape[0]
    column = pl.BlockSpec((tokens, width), lambda u: (0, u))
    return pl.pallas_call(
        hidden_kernel,
        grid=(units,),
        in_specs=[whole_spec((tokens, width)), lead_spec(width, width), pl.BlockSpec((1, width), lambda u: (0, u))],
        out_specs=[column, column],
        out_shape=[jax.ShapeDtypeStruct((tokens, units * width), BF16)] * 2,
        compiler_params=params(48),
        cost_estimate=pl.CostEstimate(
            flops=2 * tokens * width * width * units, bytes_accessed=26 << 20, transcendentals=0
        ),
    )(mlp_in, weights, bias)


def hidden_back_kernel(d_mlp_ref, weight_ref, slope_ref, d_hidden_ref, sums_ref):
    step = 256

    def chunk(index, carry):
        here = pl.ds(pl.multiple_of(index * step, step), step)
        d_hidden = dot_nt(d_mlp_ref[here, :], weight_ref[...]) * slope_ref[here, :].astype(F32)
        d_hidden = d_hidden.astype(BF16)
        d_hidden_ref[here, :] = d_hidden
        return carry + jnp.sum(d_hidden.astype(F32), axis=0, keepdims=True)

    zero = jnp.zeros((1, weight_ref.shape[0]), F32)
    sums_ref[0:1] = lax.fori_loop(0, d_mlp_ref.shape[0] // step, chunk, zero)


def hidden_back(d_mlp, weights, slope):
    tokens, width = d_mlp.shape
    units = weights.shape[0] // width
    column = pl.BlockSpec((tokens, width), lambda u: (0, u))
    return pl.pallas_call(
        hidden_back_kernel,
        grid=(units,),
        in_specs=[whole_spec((tokens, width)), rows_spec(width, width), column],
        out_specs=[column, pl.BlockSpec((8, width), lambda u: (0, u))],
        out_shape=[
            jax.ShapeDtypeStruct((tokens, units * width), BF16),
            jax.ShapeDtypeStruct((8, units * width), F32),
        ],
        compiler_params=params(48),
        cost_estimate=pl.CostEstimate(
            flops=2 * tokens * width * width * units, bytes_accessed=26 << 20, transcendentals=0
        ),
    )(d_mlp, weights, slope)


def mlp_rest_kernel(act_ref, two_ref, d_hidden_ref, one_ref, mlp_ref, d_in_ref):
    step = 256

    @pl.when(pl.program_id(0) == 0)
    def _():
        mlp_ref[...] = jnp.zeros_like(mlp_ref)
        d_in_ref[...] = jnp.zeros_like(d_in_ref)

    def chunk(index, carry):
        here = pl.ds(pl.multiple_of(index * step, step), step)
        mlp_ref[here, :] += dot(act_ref[here, :], two_ref[...])
        d_in_ref[here, :] += dot_nt(d_hidden_ref[here, :], one_ref[0])
        return carry

    lax.fori_loop(0, act_ref.shape[0] // step, chunk, 0)


def mlp_rest(act, two, d_hidden, one):
    tokens = act.shape[0]
    units, width = one.shape[:2]
    column = pl.BlockSpec((tokens, width), lambda u: (0, u))
    total = pl.BlockSpec((tokens, width), lambda u: (0, 0))
    return pl.pallas_call(
        mlp_rest_kernel,
        grid=(units,),
        in_specs=[column, rows_spec(width, width), column, lead_spec(width, width)],
        out_specs=[total, total],
        out_shape=[jax.ShapeDtypeStruct((tokens, width), F32)] * 2,
        compiler_params=params(48),
        cost_estimate=pl.CostEstimate(
            flops=4 * tokens * width * width * units, bytes_accessed=42 << 20, transcendentals=0
        ),
    )(act, two, d_hidden, one)


def middle_back_kernel(
    mlp_ref, bias_ref, d_in_ref, x1_ref, attn_ref, cot_ref, mod_ref, weight_ref,
    out_ref, d_mid_ref, d_attn_ref, d_att_ref, rows_ref,
):
    live = mod_ref[0, 6:7]
    gate_two = mod_ref[0, 5:6]
    upstream = cot_ref[...].astype(F32) * live
    middle = x1_ref[...]
    mlp = mlp_ref[...] + bias_ref[4:5]
    out_ref[...] = ((middle + gate_two * mlp) * live).astype(BF16)
    rows_ref[0, 5:6] = jnp.sum(upstream * mlp, axis=0, keepdims=True)
    normed, inverse = moments(middle)
    d_in = d_in_ref[...]
    rows_ref[0, 3:4] = jnp.sum(d_in, axis=0, keepdims=True)
    rows_ref[0, 4:5] = jnp.sum(d_in * normed, axis=0, keepdims=True)
    d_mid = upstream + norm_back(normed, inverse, d_in * (1.0 + mod_ref[0, 4:5]))
    d_mid_ref[...] = d_mid
    rows_ref[0, 2:3] = jnp.sum(d_mid * attn_ref[...], axis=0, keepdims=True)
    d_attn = (mod_ref[0, 2:3] * d_mid).astype(BF16)
    d_attn_ref[...] = d_attn
    rows_ref[0, 6:7] = jnp.sum(d_attn.astype(F32), axis=0, keepdims=True)
    d_att_ref[...] = dot_nt(d_attn_ref[...], weight_ref[0]).astype(BF16)


def middle_back(mlp, bias, d_in, x1, attn, cot, mod, weights, slots, length, width):
    tokens = slots * length
    row = rows_spec(length, width)
    proj = pl.BlockSpec((1, width, width), lambda i: (3, 0, 0), pipeline_mode=pl.Buffered(1))
    return pl.pallas_call(
        middle_back_kernel,
        grid=(slots,),
        in_specs=[row, whole_spec((8, width)), row, row, row, row, lead_spec(8, width), proj],
        out_specs=[row, row, row, row, lead_spec(8, width)],
        out_shape=[
            jax.ShapeDtypeStruct((tokens, width), BF16),
            jax.ShapeDtypeStruct((tokens, width), F32),
            jax.ShapeDtypeStruct((tokens, width), BF16),
            jax.ShapeDtypeStruct((tokens, width), BF16),
            jax.ShapeDtypeStruct((slots, 8, width), F32),
        ],
        compiler_params=params(48),
        cost_estimate=pl.CostEstimate(
            flops=2 * tokens * width * width, bytes_accessed=30 << 20, transcendentals=0
        ),
    )(mlp, bias, d_in, x1, attn, cot, mod, weights)


def attention_back_kernel(packed_ref, d_att_ref, log_ref, d_packed_ref, sums_ref, q_ref, k_ref, v_ref):
    length, width = d_att_ref.shape
    head_dim = width // HEADS
    factor = 1.0 / math.sqrt(head_dim)
    for head in range(HEADS):
        start, stop, offset = head_window(head, head_dim)
        mask = head_mask((length, stop - start), offset, head_dim)
        query = packed_ref[:, start:stop]
        query_one = jnp.where(mask, query, jnp.zeros_like(query))
        keys = packed_ref[:, width + start : width + stop]
        values = packed_ref[:, 2 * width + start : 2 * width + stop]
        d_att = d_att_ref[:, start:stop]
        d_att = jnp.where(mask, d_att, jnp.zeros_like(d_att))
        weights = jnp.exp(dot_nt(query_one, keys) * factor - log_ref[:, head : head + 1])
        d_probs = dot_nt(d_att, values)
        inner = jnp.sum(weights * d_probs, axis=-1, keepdims=True)
        d_scores = (weights * (d_probs - inner)).astype(BF16)
        probs = weights.astype(BF16)
        pieces = (
            (q_ref, dot(d_scores, keys) * factor),
            (k_ref, dot_tn(d_scores, query) * factor),
            (v_ref, dot_tn(probs, d_att)),
        )
        for ref, piece in pieces:
            if offset == 0:
                ref[:, start:stop] = piece
            else:
                ref[:, start:stop] = jnp.where(mask, piece, ref[:, start:stop])
    for unit, ref in enumerate((q_ref, k_ref, v_ref)):
        piece = ref[...].astype(BF16)
        d_packed_ref[:, unit * width : (unit + 1) * width] = piece
        sums_ref[0, unit : unit + 1] = jnp.sum(piece.astype(F32), axis=0, keepdims=True)


def attention_back(packed, d_att, log, slots, length, width):
    tokens = slots * length
    return pl.pallas_call(
        attention_back_kernel,
        grid=(slots,),
        in_specs=[rows_spec(length, 3 * width), rows_spec(length, width), rows_spec(length, 128)],
        out_specs=[rows_spec(length, 3 * width), lead_spec(8, width)],
        out_shape=[
            jax.ShapeDtypeStruct((tokens, 3 * width), BF16),
            jax.ShapeDtypeStruct((slots, 8, width), F32),
        ],
        scratch_shapes=[pltpu.VMEM((length, width), F32)] * 3,
        compiler_params=params(48),
        cost_estimate=pl.CostEstimate(
            flops=10 * tokens * length * 256 * HEADS, bytes_accessed=14 << 20, transcendentals=0
        ),
    )(packed, d_att, log)


def input_back_kernel(d_packed_ref, weight_ref, x_ref, d_mid_ref, mod_ref, grad_ref, rows_ref):
    width = x_ref.shape[1]
    d_in = dot_nt(d_packed_ref[:, :width], weight_ref[0])
    for unit in (1, 2):
        d_in = d_in + dot_nt(d_packed_ref[:, unit * width : (unit + 1) * width], weight_ref[unit])
    normed, inverse = moments(x_ref[...].astype(F32))
    rows_ref[0, 0:1] = jnp.sum(d_in, axis=0, keepdims=True)
    rows_ref[0, 1:2] = jnp.sum(d_in * normed, axis=0, keepdims=True)
    back = norm_back(normed, inverse, d_in * (1.0 + mod_ref[0, 1:2]))
    grad_ref[...] = (d_mid_ref[...] + back).astype(BF16)


def input_back(d_packed, weights, x, d_mid, mod, slots, length, width):
    tokens = slots * length
    row = rows_spec(length, width)
    return pl.pallas_call(
        input_back_kernel,
        grid=(slots,),
        in_specs=[
            rows_spec(length, 3 * width), whole_spec((3, width, width)), row, row, lead_spec(8, width),
        ],
        out_specs=[row, lead_spec(8, width)],
        out_shape=[
            jax.ShapeDtypeStruct((tokens, width), BF16),
            jax.ShapeDtypeStruct((slots, 8, width), F32),
        ],
        compiler_params=params(48),
        cost_estimate=pl.CostEstimate(
            flops=6 * tokens * width * width, bytes_accessed=20 << 20, transcendentals=0
        ),
    )(d_packed, weights, x, d_mid, mod)


def grad_kernel(left_ref, right_ref, grad_ref):
    step = grad_ref.shape[0] // 3

    def chunk(index, carry):
        here = pl.ds(pl.multiple_of(index * step, step), step)
        grad_ref[here, :] = dot_tn(left_ref[:, here], right_ref[...]).astype(BF16)
        return carry

    lax.fori_loop(0, 3, chunk, 0)


def grad_columns(left, right):
    tokens, rows = left.shape
    width = right.shape[1]
    return pl.pallas_call(
        grad_kernel,
        grid=(width // rows,),
        in_specs=[whole_spec((tokens, rows)), pl.BlockSpec((tokens, rows), lambda u: (0, u))],
        out_specs=pl.BlockSpec((rows, rows), lambda u: (0, u)),
        out_shape=jax.ShapeDtypeStruct((rows, width), BF16),
        compiler_params=params(48),
        cost_estimate=pl.CostEstimate(
            flops=2 * tokens * rows * width, bytes_accessed=2 * rows * width + 4 * tokens * width, transcendentals=0
        ),
    )(left, right)


def grad_rows(left, right):
    tokens, rows = left.shape
    width = right.shape[1]
    return pl.pallas_call(
        grad_kernel,
        grid=(rows // width,),
        in_specs=[pl.BlockSpec((tokens, width), lambda u: (0, u)), whole_spec((tokens, width))],
        out_specs=rows_spec(width, width),
        out_shape=jax.ShapeDtypeStruct((rows, width), BF16),
        compiler_params=params(48),
        cost_estimate=pl.CostEstimate(
            flops=2 * tokens * rows * width, bytes_accessed=2 * rows * width + 4 * tokens * rows, transcendentals=0
        ),
    )(left, right)


def after(*values):
    return lax.optimization_barrier(values)


def own_half(value, index):
    return lax.dynamic_index_in_dim(value, index, 1, keepdims=False)


def body(
    images,
    cotangent,
    counts,
    timesteps,
    labels,
    label_table,
    step_count,
    w_ada,
    w_qkv,
    w_proj,
    w_fc1,
    w_fc2,
    biases,
    first_ada,
    first_qkv,
    first_proj,
    first_fc1,
    first_fc2,
    first_bias,
    second_ada,
    second_qkv,
    second_proj,
    second_fc1,
    second_fc2,
    second_bias,
    outer_ada,
    outer_qkv,
    outer_proj,
    outer_fc1,
    outer_fc2,
    outer_bias,
):
    masters = (w_ada, w_qkv, w_proj, w_fc1, w_fc2, biases)
    firsts = (first_ada, first_qkv, first_proj, first_fc1, first_fc2, first_bias)
    seconds = (second_ada, second_qkv, second_proj, second_fc1, second_fc2, second_bias)
    outers = (outer_ada, outer_qkv, outer_proj, outer_fc1, outer_fc2, outer_bias)
    slots, length, width = images.shape
    tokens = slots * length
    rows = w_qkv.shape[0]
    rows_two = w_fc2.shape[0]
    lines = lax.axis_size("fsdp")
    groups = lax.axis_size("rep")
    rep = lax.axis_index("rep")
    pair = lax.axis_index("dp")
    line = lax.axis_index("fsdp")
    half = rows // 2
    everyone = ("rep", "fsdp", "dp")

    def rows_of(weight):
        return lax.dynamic_slice_in_dim(weight, pair * half, half, axis=0).astype(BF16)

    attention_cut = jnp.concatenate([rows_of(w_qkv), rows_of(w_proj)], axis=1)
    attention_cut = lax.dynamic_slice_in_dim(attention_cut, rep * width, width, axis=1)
    w_attn = lax.all_gather(attention_cut, everyone, axis=0, tiled=True).reshape(4, width, width)
    live = (jnp.arange(slots) < counts[0]).astype(F32)
    condition = time_embed(timesteps, D) + jnp.take(label_table, labels, axis=0).astype(F32)
    style = jax.nn.silu(condition).astype(BF16)
    one_cut = lax.dynamic_slice(w_fc1, (pair * half, rep * width), (half, width)).astype(BF16)
    one_cut, style = after(one_cut, style)
    w_one = lax.all_gather(one_cut, everyone, axis=0, tiled=True).reshape(FF // width, width, width)
    message = jnp.concatenate([style.reshape(-1), biases.astype(BF16)])
    heard = gather_line(message, "fsdp")
    bias_all = heard[:, slots * width :].reshape(-1).astype(F32)
    style_line = heard[:, : slots * width].reshape(lines * slots, width)
    style_cut = lax.dynamic_slice_in_dim(style_line, line * rows, rows, axis=1)
    mod_part = dot(style_cut, w_ada.astype(BF16))
    b_ada = bias_all[: 6 * width]
    modulation = scatter_line(mod_part.reshape(lines, slots, 6 * width), "fsdp") + b_ada
    eighth = rows_two // (2 * groups)
    two_cut = lax.dynamic_slice_in_dim(w_fc2, (rep * 2 + pair) * eighth, eighth, axis=0).astype(BF16)
    two_cut, modulation = after(two_cut, modulation)
    w_two = lax.all_gather(two_cut, ("fsdp", "rep", "dp"), axis=0, tiled=True)
    mod = jnp.concatenate(
        [
            modulation.reshape(slots, 6, width),
            jnp.broadcast_to(live[:, None, None], (slots, 2, width)),
        ],
        axis=1,
    )
    b_rest = bias_all[6 * width : 9 * width].reshape(3, width)
    bias = jnp.zeros((8, width), F32)
    bias = bias.at[0].set(b_rest[0]).at[2].set(b_rest[1]).at[3].set(b_rest[2])
    bias = bias.at[4].set(bias_all[9 * width + FF :])
    b_fc1 = bias_all[9 * width : 9 * width + FF].reshape(1, FF)
    x = images.reshape(tokens, width)
    cot = cotangent.reshape(tokens, width)

    attn_in, packed, attended, log_total, attn_out, middle, mlp_in, d_mlp, mlp_sums = attention_forward(
        x, cot, mod, bias, w_attn, slots, length, width
    )
    activated, slope = hidden_forward(mlp_in, w_one, b_fc1)
    grad_two = grad_rows(activated, d_mlp)

    def halves(gradient):
        return gradient.reshape(lines, 2, gradient.shape[0] // (2 * lines), gradient.shape[1])

    def line_sum(both):
        return lax.psum_scatter(
            both.reshape(-1, both.shape[-1]), "fsdp", scatter_dimension=0, tiled=True
        )

    def pair_sum(gradient, there):
        return (own_half(halves(gradient), pair).astype(F32) + there.astype(F32)).astype(BF16)

    grad_two, d_mlp = after(grad_two, d_mlp)
    two_line = line_sum(grad_two)
    d_hidden, hidden_sums = hidden_back(d_mlp, w_two, slope)
    grad_one = grad_columns(mlp_in, d_hidden)
    give_one = own_half(halves(grad_one), 1 - pair)
    give_one, d_hidden = after(give_one, d_hidden)
    there_one = swap_with(give_one, "dp", 1)
    mlp_out, d_mlp_in = mlp_rest(activated, w_two, d_hidden, w_one)
    result, d_middle, d_attn, d_attended, middle_rows = middle_back(
        mlp_out, bias, d_mlp_in, middle, attn_out, cot, mod, w_attn, slots, length, width
    )
    grad_proj = grad_columns(attended, d_attn)
    grad_proj, d_attended = after(grad_proj, d_attended)
    d_packed, packed_sums = attention_back(packed, d_attended, log_total, slots, length, width)
    grad_qkv = grad_columns(attn_in, d_packed)
    give_attn = jnp.concatenate(
        [own_half(halves(grad_qkv), 1 - pair), own_half(halves(grad_proj), 1 - pair)], axis=2
    )
    give_attn, d_packed = after(give_attn, d_packed)
    in_grad, input_rows = input_back(d_packed, w_attn, x, d_middle, mod, slots, length, width)

    two_line, there_one, give_attn, input_rows = after(two_line, there_one, give_attn, input_rows)
    there_attn = swap_with(give_attn, "dp", 1)
    one_both, input_rows = after(pair_sum(grad_one, there_one), input_rows)
    one_half = line_sum(one_both)
    d_modulation = jnp.concatenate([input_rows[:, :2], middle_rows[:, 2:6]], axis=1).astype(BF16)
    packed_total = jnp.sum(packed_sums, axis=0)
    bias_sums = jnp.concatenate(
        [
            packed_total[0],
            packed_total[2],
            jnp.sum(middle_rows[:, 6], axis=0),
            hidden_sums[0],
            jnp.sum(mlp_sums[:, 0], axis=0),
        ]
    ).astype(BF16)

    report = jnp.concatenate([style.reshape(-1), d_modulation.reshape(-1), bias_sums])
    report = jnp.stack([report, swap_with(report, "dp", 1)])
    reports = gather_line(report, "fsdp").reshape(2 * lines, -1)
    edge = slots * width
    style_group = reports[:, :edge].reshape(2 * lines * slots, width)
    mod_group = reports[:, edge : 7 * edge].reshape(2 * lines * slots, 6 * width)
    style_own = lax.dynamic_slice_in_dim(style_group, line * rows, rows, axis=1)
    grad_ada = dot_tn(style_own, mod_group)
    bias_group = jnp.concatenate(
        [
            jnp.sum(mod_group.astype(F32), axis=0),
            jnp.sum(reports[:, 7 * edge :].astype(F32), axis=0),
        ]
    )
    one_half, there_attn, grad_ada, bias_group = after(one_half, there_attn, grad_ada, bias_group)
    attn_both = jnp.concatenate(
        [own_half(halves(grad_qkv), pair), own_half(halves(grad_proj), pair)], axis=2
    )
    attn_both = (attn_both.astype(F32) + there_attn.astype(F32)).astype(BF16)
    attn_both, two_line, one_half, grad_ada = after(attn_both, two_line, one_half, grad_ada)
    attn_half = line_sum(attn_both)
    two_there = swap_with(two_line, "dp", 1)
    own_bias = biases.shape[0]
    grad_bias = lax.dynamic_slice_in_dim(bias_group, line * own_bias, own_bias, axis=0)

    def two_rows(own, other):
        first = jnp.where(pair == 0, own, other)
        second = jnp.where(pair == 0, other, own)
        return jnp.concatenate([first, second], axis=0)

    def both_halves(piece):
        return two_rows(piece, swap_with(piece, "dp", 1)).astype(F32)

    power = step_count[0].astype(F32)
    fix_one = 1.0 - jnp.power(BETA_ONE, power)
    fix_two = 1.0 - jnp.power(BETA_TWO, power)
    rates = learning_rates(D, FF)
    reduced = [None] * 6
    firsts_out = [None] * 6
    seconds_out = [None] * 6
    deltas_out = [None] * 6
    outers_out = [None] * 6
    weights_out = [None] * 6

    def moments_next(first, second, gradient):
        first_next = BETA_ONE * first + (1.0 - BETA_ONE) * gradient
        second_next = BETA_TWO * second + (1.0 - BETA_TWO) * gradient * gradient
        return first_next, second_next

    def local_delta(master, first, second, gradient, rate):
        first_next, second_next = moments_next(first, second, gradient)
        local = master - rate * (
            first_next / fix_one / (jnp.sqrt(second_next / fix_two) + ADAM_EPS)
            + WEIGHT_DECAY * master
        )
        return (master - local).astype(BF16)

    def sum_groups(mine):
        if mine.ndim == 1:
            total = (mine.astype(F32) + swap_with(mine, "rep", 1).astype(F32)).astype(BF16)
            return total.astype(F32) + swap_with(total, "rep", 2).astype(F32)
        quarter = mine.shape[0] // 2
        columns = mine.shape[1]
        low = rep % 2
        mine = mine.reshape(2, quarter, columns)
        keep = lax.dynamic_index_in_dim(mine, low, 0, keepdims=False)
        give = lax.dynamic_index_in_dim(mine, 1 - low, 0, keepdims=False)
        total = (keep.astype(F32) + swap_with(give, "rep", 1).astype(F32)).astype(BF16)
        total = (total.astype(F32) + swap_with(total, "rep", 2).astype(F32)).astype(BF16)
        twin = two_rows(total[None], swap_with(total, "dp", 1)[None])
        other = swap_with(twin, "rep", 1)
        first = jnp.where(low == 0, twin, other)
        second = jnp.where(low == 0, other, twin)
        return jnp.stack([first, second], axis=1).reshape(4 * quarter, columns).astype(F32)

    def own_rows(value):
        count = value.shape[0] // 2
        return lax.dynamic_slice_in_dim(value, pair * count, count, axis=0)

    def own_delta(index, own_gradient):
        master, first, second = masters[index], firsts[index][0], seconds[index][0]
        return local_delta(
            own_rows(master), own_rows(first), own_rows(second), own_gradient.astype(F32), rates[index]
        )

    def finish(index, gradient, summed):
        reduced[index] = gradient
        first_next, second_next = moments_next(firsts[index][0], seconds[index][0], gradient)
        firsts_out[index] = first_next[None]
        seconds_out[index] = second_next[None]
        delta = summed / groups
        outer_next = OUTER_MOMENTUM * outers[index] + delta
        deltas_out[index] = delta
        outers_out[index] = outer_next
        weights_out[index] = masters[index] - OUTER_RATE * (delta + OUTER_MOMENTUM * outer_next)

    finish(0, grad_ada, sum_groups(own_delta(0, own_rows(grad_ada))))
    bias_delta = local_delta(biases, first_bias[0], second_bias[0], grad_bias, rates[5])
    finish(5, grad_bias, sum_groups(bias_delta))
    finish(3, both_halves(one_half), sum_groups(own_delta(3, one_half)))
    grad_two_sum = two_line.astype(F32) + two_there.astype(F32)
    finish(4, grad_two_sum, sum_groups(own_delta(4, own_rows(grad_two_sum))))
    attn_half, weights_out[4], weights_out[3], weights_out[0] = after(
        attn_half, weights_out[4], weights_out[3], weights_out[0]
    )
    edge = 3 * width
    summed = sum_groups(
        jnp.concatenate([own_delta(1, attn_half[:, :edge]), own_delta(2, attn_half[:, edge:])], axis=1)
    )
    attn_full = both_halves(attn_half)
    finish(1, attn_full[:, :edge], summed[:, :edge])
    finish(2, attn_full[:, edge:], summed[:, edge:])
    grads_out = tuple((gradient[None] for gradient in reduced))
    return (
        (result.reshape(images.shape), in_grad.reshape(images.shape))
        + grads_out
        + tuple(firsts_out)
        + tuple(seconds_out)
        + tuple(deltas_out)
        + tuple(outers_out)
        + tuple(weights_out)
    )


def solution(mesh):
    in_specs = (
        P(("rep", "dp", "fsdp"), None, None),
        P(("rep", "dp", "fsdp"), None, None),
        P(("rep", "dp", "fsdp")),
        P(("rep", "dp", "fsdp")),
        P(("rep", "dp", "fsdp")),
        P(),
        P(),
        P("fsdp", None),
        P("fsdp", None),
        P("fsdp", None),
        P("fsdp", None),
        P("fsdp", None),
        P("fsdp"),
        P("rep", "fsdp", None),
        P("rep", "fsdp", None),
        P("rep", "fsdp", None),
        P("rep", "fsdp", None),
        P("rep", "fsdp", None),
        P("rep", "fsdp"),
        P("rep", "fsdp", None),
        P("rep", "fsdp", None),
        P("rep", "fsdp", None),
        P("rep", "fsdp", None),
        P("rep", "fsdp", None),
        P("rep", "fsdp"),
        P("fsdp", None),
        P("fsdp", None),
        P("fsdp", None),
        P("fsdp", None),
        P("fsdp", None),
        P("fsdp"),
    )
    out_specs = (
        P(("rep", "dp", "fsdp"), None, None),
        P(("rep", "dp", "fsdp"), None, None),
        P("rep", "fsdp", None),
        P("rep", "fsdp", None),
        P("rep", "fsdp", None),
        P("rep", "fsdp", None),
        P("rep", "fsdp", None),
        P("rep", "fsdp"),
        P("rep", "fsdp", None),
        P("rep", "fsdp", None),
        P("rep", "fsdp", None),
        P("rep", "fsdp", None),
        P("rep", "fsdp", None),
        P("rep", "fsdp"),
        P("rep", "fsdp", None),
        P("rep", "fsdp", None),
        P("rep", "fsdp", None),
        P("rep", "fsdp", None),
        P("rep", "fsdp", None),
        P("rep", "fsdp"),
        P("fsdp", None),
        P("fsdp", None),
        P("fsdp", None),
        P("fsdp", None),
        P("fsdp", None),
        P("fsdp"),
        P("fsdp", None),
        P("fsdp", None),
        P("fsdp", None),
        P("fsdp", None),
        P("fsdp", None),
        P("fsdp"),
        P("fsdp", None),
        P("fsdp", None),
        P("fsdp", None),
        P("fsdp", None),
        P("fsdp", None),
        P("fsdp"),
    )
    return jax.shard_map(body, mesh=mesh, in_specs=in_specs, out_specs=out_specs, check_vma=False)
```

time: 1180 us -> 939 us (0.80)
  Pallas kernels: 0 us -> 186 us
  matrix products: 182 us -> 8.57 us
  local copies, waits for them, and re-layouts: 211 us -> 50.1 us
  other arithmetic: 210 us -> 164 us
  waiting for transfers between devices: 500 us -> 472 us
    pallas_call x0 -> x11, Pallas kernels: none -> 186 us  [the longest x3 29.6 us: grad_columns(): pl.pallas_call(grad_kernel, grid=(width // rows,), in_specs=[whole_spec((...]
    dot_general x10 -> x0, matrix products: 80.9 us -> none  [the longest x4 55.7 us: dot_nt(): lax.dot_general(left, right, (((1,), (1,)), ((), ())), preferred_element_...]
    reshape x5 -> x3, local copies, waits for them, and re-layouts: 79.8 us -> 0.08 us  [the longest x1 0.05 us: body(): modulation.reshape(slots, 6, width)]
    ppermute x29 -> x24, waiting for transfers between devices: 328 us -> 255 us  [swap_with(): return lax.ppermute(value, axis, [(i, i ^ bit) for i in range(size)])]
    all_gather x1, waiting for transfers between devices: 0.01 us -> 51.1 us  [body(): w_two = lax.all_gather(two_cut, ('fsdp', 'rep', 'dp'), axis=0, tiled=True)]
    dot_general x5 -> x1, matrix products: 51.8 us -> 4.01 us  [dot(): return jnp.dot(left, right, preferred_element_type=F32)]
    dot_general x5 -> x1, matrix products: 49 us -> 4.56 us  [dot_tn(): lax.dot_general(left, right, (((0,), (0,)), ((), ())), preferred_element_...]
    add x14 -> x2, other arithmetic: 52.6 us -> 8.76 us  [the longest x1 5.32 us: moments_next(): second_next = BETA_TWO * second + (1.0 - BETA_TWO) * gradient * gradient]
  transfers between devices with their start and end apart: 45 -> 39, of which waited for: 20 -> 22; matrix products, arithmetic and copies ran while one was open for 39% -> 17% of each run, Pallas kernels for 0% -> 20%
where the time goes in v2:
time: 939 us; the launch traced here: 935 us
  waiting for transfers between devices  472 us (50%)
  Pallas kernels  186 us (20%)
  other arithmetic  164 us (17%)
  local copies, waits for them, and re-layouts  50.1 us (5%)
  starting transfers between devices  37.1 us (4%)
  between operations  16.8 us (2%)
    ppermute x24, waiting for transfers between devices, swap_with(): return lax.ppermute(value, axis, [(i, i ^ bit) for i in range(size)])  255 us
    all_gather x1, waiting for transfers between devices, body(): lax.all_gather(attention_cut, everyone, axis=0, tiled=True)  60.5 us
    all_gather x1, waiting for transfers between devices, body(): lax.all_gather(one_cut, everyone, axis=0, tiled=True)  60.4 us
    all_gather x1, waiting for transfers between devices, body(): w_two = lax.all_gather(two_cut, ('fsdp', 'rep', 'dp'), axis=0, tiled=True)  51.1 us
    sub x5, other arithmetic, finish(): masters[index] - OUTER_RATE * (delta + OUTER_MOMENTUM * outer_next)  44 us
    broadcast_in_dim x4, other arithmetic, finish(): seconds_out[index] = second_next[None]  37.7 us
    pallas_call x3, Pallas kernels, grad_columns(): pl.pallas_call(grad_kernel, grid=(width // rows,), in_specs=[whole_spec((...  29.6 us
    pallas_call x1, Pallas kernels, mlp_rest(): pl.pallas_call(mlp_rest_kernel, grid=(units,), in_specs=[column, rows_spe...  28.2 us
  transfers between devices with their start and end apart: 39, of which 22 were waited for; matrix products, arithmetic and copies ran while one was open for 17% of the time, Pallas kernels for 20%

profile of v2, /device:TPU:1, one launch (start us, length us, event | category | flops | bytes accessed | tf_op | source)
XLA Modules:
  0.0 934.7 jit_solution(2768696265149776188)
XLA Ops:
  14.8 4.2 collective-permute-start.2
  24.5 4.0 fusion.18
  32.2 4.6 collective-permute-done.3
  39.1 6.0 collective-permute-done.4
  46.8 60.5 %all-gather.4.cloned.1.call-done = bf16[4608,1152]{1,0:T(8,128)(2,1)} async-done(((bf16[144,1152]{1,0:T(8,128)(2,1)}), bf16[4608,1152]{1,0:T(8,128)(2,1)}) %all-gather.4.cloned.1.call-update) | async-done | bytes 10616848 | tf_op jit(solution)/shard_map/all_gather | solution.py:553
  107.3 26.6 %shard_map.590 = (bf16[768,1152]{1,0:T(8,128)(2,1)S(1)}, bf16[768,3456]{1,0:T(8,128)(2,1)}, bf16[768,1152]{1,0:T(8,128)(2,1)S(1)}, f32[768,128]{1,0:T(8,128)S(1)...) custom-call(bf16[768,1152]{1,0:T(8,128)(2,1)} %bitcast.217, ...), custom_call_target="tpu_custom_call" | custom-call | flops 8153726976 | bytes 41943040 | tf_op jit(solution)/shard_map/pallas_call | solution.py:188
  136.3 60.4 %all-gather.6.cloned.1.call-done = bf16[4608,1152]{1,0:T(8,128)(2,1)} async-done(((bf16[144,1152]{1,0:T(8,128)(2,1)}), bf16[4608,1152]{1,0:T(8,128)(2,1)}) %all-gather.6.cloned.1.call-update) | async-done | bytes 10616848 | tf_op jit(solution)/shard_map/all_gather | solution.py:559
  196.7 21.3 %shard_map.591 = (bf16[768,4608]{1,0:T(8,128)(2,1)}, bf16[768,4608]{1,0:T(8,128)(2,1)}) custom-call(bf16[768,1152]{1,0:T(8,128)(2,1)S(1)} %get-tuple-element.142.mlp_in_ref.left_ref, bf16[4,1152,1152]{2,1,0:T(8,128)(2,1)} %bitcast.260, f32[1,4608]{1,0:T(1,128)S(1)} %reshape.441.bias_ref), custom_call_target="tpu_custom_call" | custom-call | flops 8153726976 | bytes 27262976 | tf_op jit(solution)/shard_map/pallas_call | solution.py:233
  218.0 14.8 %shard_map.592 = bf16[4608,1152]{1,0:T(8,128)(2,1)} custom-call(bf16[768,4608]{1,0:T(8,128)(2,1)} %get-tuple-element.144.left_ref.act_ref, bf16[768,1152]{1,0:T(8,128)(2,1)S(1)} %copy-done.10), custom_call_target="tpu_custom_call" | custom-call | flops 8153726976 | bytes 24772608 | tf_op jit(solution)/shard_map/pallas_call | solution.py:478
  235.0 51.1 %all-gather.8.cloned.1.call-done.weight_ref.two_ref = bf16[4608,1152]{1,0:T(8,128)(2,1)} async-done(((bf16[144,1152]{1,0:T(8,128)(2,1)}), bf16[4608,1152]{1,0:T(8,128)(2,1)}) %all-gather.8.cloned.1.call-update) | async-done | bytes 10616848 | tf_op jit(solution)/shard_map/all_gather | solution.py:571
  287.6 16.4 %shard_map.593 = (bf16[768,4608]{1,0:T(8,128)(2,1)}, f32[8,4608]{1,0:T(8,128)S(1)}) custom-call(bf16[768,1152]{1,0:T(8,128)(2,1)S(1)} %copy-done.11, bf16[4608,1152]{1,0:T(8,128)(2,1)} %all-gather.8.cloned.1.call-done.weight_ref.two_ref, bf16[768,4608]{1,0:T(8,128)(2,1)} %get-tuple-element.148.slope_ref), custom_call_target="tpu_custom_call" | custom-call | flops 8153726976 | bytes 27262976 | tf_op jit(solution)/shard_map/pallas_call | solution.py:264
  304.0 14.8 %shard_map.594 = bf16[1152,4608]{1,0:T(8,128)(2,1)} custom-call(bf16[768,1152]{1,0:T(8,128)(2,1)S(1)} %get-tuple-element.142.mlp_in_ref.left_ref, bf16[768,4608]{1,0:T(8,128)(2,1)} %get-tuple-element.150.right_ref.d_hidden_ref), custom_call_target="tpu_custom_call" | custom-call | flops 8153726976 | bytes 24772608 | tf_op jit(solution)/shard_map/pallas_call | solution.py:462
  318.8 5.2 dynamic-slice_bitcast_fusion
  325.2 28.2 %shard_map.595 = (f32[768,1152]{1,0:T(8,128)S(1)}, f32[768,1152]{1,0:T(8,128)}) custom-call(bf16[768,4608]{1,0:T(8,128)(2,1)} %get-tuple-element.144.left_ref.act_ref, bf16[4608,1152]{1,0:T(8,128)(2,1)} %all-gather.8.cloned.1.call-done.weight_ref.two_ref, bf16[768,4608]{1,0:T(8,128)(2,1)} %get-tuple-element.150.right_ref.d_hidden_ref, ...), custom_call_target="tpu_custom_call" | custom-call | flops 16307453952 | bytes 44040192 | tf_op jit(solution)/shard_map/pallas_call | solution.py:302
  355.2 11.9 %shard_map.596 = (bf16[768,1152]{1,0:T(8,128)(2,1)}, f32[768,1152]{1,0:T(8,128)}, bf16[768,1152]{1,0:T(8,128)(2,1)S(1)}, bf16[768,1152]{1,0:T(8,128)(2,1)S(1)}, f32[3,8,1152]{2,1,0:T(8,128)S(1)}) custom-call(f32[768,1152]{1,0:T(8,128)} %copy-done.2, f32[8,1152]{1,0:T(8,128)S(1)} %scatter.19.bias_ref, f32[768,1152]{1,0:T(8,128)} %get-tuple-element.152.d_in_ref, ...), custom_call_target="tpu_custom_call" | custom-call | flops 2038431744 | bytes 31457280 | tf_op jit(solution)/shard_map/pallas_call | solution.py:343
  370.8 23.4 %shard_map.598 = (bf16[768,3456]{1,0:T(8,128)(2,1)}, f32[3,8,1152]{2,1,0:T(8,128)S(1)}) custom-call(bf16[768,3456]{1,0:T(8,128)(2,1)} %get-tuple-element.157.packed_ref, bf16[768,1152]{1,0:T(8,128)(2,1)S(1)} %get-tuple-element.161.d_att_ref, f32[768,128]{1,0:T(8,128)S(1)} %get-tuple-element.162.log_ref), custom_call_target="tpu_custom_call" | custom-call | flops 8053063680 | bytes 14680064 | tf_op jit(solution)/shard_map/pallas_call | solution.py:398
  396.1 11.8 %shard_map.599 = bf16[1152,3456]{1,0:T(8,128)(2,1)} custom-call(bf16[768,1152]{1,0:T(8,128)(2,1)S(1)} %copy-done.9, bf16[768,3456]{1,0:T(8,128)(2,1)} %get-tuple-element.165.right_ref.d_packed_ref), custom_call_target="tpu_custom_call" | custom-call | flops 6115295232 | bytes 18579456 | tf_op jit(solution)/shard_map/pallas_call | solution.py:462
  408.0 5.8 dynamic-slice_bitcast_fusion.1
  418.3 14.1 %shard_map.600 = (bf16[768,1152]{1,0:T(8,128)(2,1)}, f32[3,8,1152]{2,1,0:T(8,128)S(1)}) custom-call(bf16[768,3456]{1,0:T(8,128)(2,1)} %get-tuple-element.165.right_ref.d_packed_ref, bf16[4,1152,1152]{2,1,0:T(8,128)(2,1)} %bitcast.245, bf16[768,1152]{1,0:T(8,128)(2,1)S(1)} %bitcast.218, f32[768,1152]{1,0:T(8,128)S(1)} %copy-done.4, ...), custom_call_target="tpu_custom_call" | custom-call | flops 6115295232 | bytes 20971520 | tf_op jit(solution)/shard_map/pallas_call | solution.py:430
  432.4 7.8 collective-permute-done.6
  440.1 26.4 %reduce-scatter.4.cloned.1.call-done = bf16[1152,1152]{1,0:T(8,128)(2,1)} async-done(((bf16[4608,1152]{1,0:T(8,128)(2,1)}), bf16[1152,1152]{1,0:T(8,128)(2,1)}) %reduce-scatter.4.cloned.1.call-update) | async-done | bytes 2654224 | tf_op jit(solution)/shard_map/reduce_scatter | solution.py:597
  466.6 7.8 fusion
  488.5 3.8 collective-permute-done.10
  493.2 4.6 fusion.70
  497.8 99.2 %collective-permute-done.7 = bf16[4,144,4608]{2,1,0:T(8,128)(2,1)} collective-permute-done((bf16[4,144,4608]{2,1,0:T(8,128)(2,1)}, bf16[4,144,4608]{2,1,0:T(8,128)(2,1)}, u32[]{:S(2)}, u32[]{:S(2)}) %collective-permute-start.7) | collective-permute-done | bytes 5308448 | tf_op jit(solution)/shard_map/ppermute | solution.py:65
  597.0 7.1 add_convert_fusion
  604.2 15.4 %fusion.2 = (f32[1,288,6912]{2,1,0:T(8,128)}, f32[1,288,6912]{2,1,0:T(8,128)}) fusion(f32[288,6912]{1,0:T(8,128)} %fusion.70, f32[1,288,6912]{2,1,0:T(8,128)} %param.58, f32[1,288,6912]{2,1,0:T(8,128)} %param.52), kind=kLoop, calls=%fused_computation.6 | loop fusion | flops 13934592 | bytes 39813120 | tf_op jit(solution)/shard_map/broadcast_in_dim | solution.py:730
  619.6 7.4 fusion.14
  632.0 4.7 fusion.36
  642.7 13.7 %collective-permute-done.18 = bf16[72,4608]{1,0:T(8,128)(2,1)S(1)} collective-permute-done((bf16[72,4608]{1,0:T(8,128)(2,1)S(1)}, bf16[72,4608]{1,0:T(8,128)(2,1)S(1)}, u32[]{:S(2)}, u32[]{:S(2)}) %collective-permute-start.18) | collective-permute-done | bytes 663584 | tf_op jit(solution)/shard_map/ppermute | solution.py:65
  657.1 4.7 collective-permute-done.26
  663.5 69.3 %collective-permute-done.19 = bf16[72,4608]{1,0:T(8,128)(2,1)S(1)} collective-permute-done((bf16[72,4608]{1,0:T(8,128)(2,1)S(1)}, bf16[72,4608]{1,0:T(8,128)(2,1)S(1)}, u32[]{:S(2)}, u32[]{:S(2)}) %collective-permute-start.19) | collective-permute-done | bytes 663584 | tf_op jit(solution)/shard_map/ppermute | solution.py:65
  736.3 10.8 %fusion.6 = (f32[1,1152,1152]{2,1,0:T(8,128)}, f32[1,1152,1152]{2,1,0:T(8,128)}, f32[1,1152,1152]{2,1,0:T(8,128)}, f32[1152,1152]{1,0:T(8,128)}) fusion(f32[1,1152,1152]{2,1,0:T(8,128)S(1)} %bitcast.234, bf16[1152,1152]{1,0:T(8,128)(2,1)} %collective-permute-done.12, bf16[1152,1152]{1,0:T(8,128)(2,1)} %reduce-scatter.4.cloned.1.call-done, ...), kind=kLoop, calls=%fused_computation.19 | loop fusion | flops 13271040 | bytes 37158912 | tf_op jit(solution)/shard_map/broadcast_in_dim | solution.py:730
  747.2 4.0 fusion.30
  751.3 7.6 collective-permute-done.23
  768.3 11.0 %collective-permute-done.14 = bf16[288,1152]{1,0:T(8,128)(2,1)S(1)} collective-permute-done((bf16[288,1152]{1,0:T(8,128)(2,1)S(1)}, bf16[288,1152]{1,0:T(8,128)(2,1)S(1)}, u32[]{:S(2)}, u32[]{:S(2)}) %collective-permute-start.14) | collective-permute-done | bytes 663584 | tf_op jit(solution)/shard_map/ppermute | solution.py:65
  780.6 11.5 %multiply_subtract_fusion.1 = (f32[288,4608]{1,0:T(8,128)}, f32[288,4608]{1,0:T(8,128)}) fusion(f32[288,4608]{1,0:T(8,128)} %param.49, f32[288,4608]{1,0:T(8,128)} %param.67, f32[2,2,72,4608]{3,2,1,0:T(8,128)} %convert_multiply_fusion.1), kind=kLoop, calls=%fused_computation.24 | loop fusion | flops 7962624 | bytes 26542080 | tf_op jit(solution)/shard_map/sub | solution.py:735
  800.2 4.0 convert_multiply_fusion
  804.2 4.0 copy.79
  808.6 11.9 %multiply_subtract_fusion = (f32[288,6912]{1,0:T(8,128)}, f32[288,6912]{1,0:T(8,128)}) fusion(f32[288,6912]{1,0:T(8,128)S(1)} %bitcast.221, f32[288,6912]{1,0:T(8,128)} %param.64, f32[2,2,72,6912]{3,2,1,0:T(8,128)S(1)} %copy.79), kind=kLoop, calls=%fused_computation.11 | loop fusion | flops 11943936 | bytes 39813120 | tf_op jit(solution)/shard_map/sub | solution.py:735
  825.5 11.1 %multiply_subtract_fusion.2 = (f32[1152,1152]{1,0:T(8,128)}, f32[1152,1152]{1,0:T(8,128)}) fusion(f32[1152,1152]{1,0:T(8,128)} %param.50, f32[1152,1152]{1,0:T(8,128)} %param.68, f32[2,2,288,1152]{3,2,1,0:T(8,128)} %copy.77), kind=kLoop, calls=%fused_computation.27 | loop fusion | flops 7962624 | bytes 26542080 | tf_op jit(solution)/shard_map/sub | solution.py:735
  838.6 4.5 fusion.47
  844.5 5.3 fusion.4
  857.7 11.8 %collective-permute-done.28 = bf16[72,4608]{1,0:T(8,128)(2,1)S(1)} collective-permute-done((bf16[72,4608]{1,0:T(8,128)(2,1)S(1)}, bf16[72,4608]{1,0:T(8,128)(2,1)S(1)}, u32[]{:S(2)}, u32[]{:S(2)}) %collective-permute-start.28) | collective-permute-done | bytes 663584 | tf_op jit(solution)/shard_map/ppermute | solution.py:65
  870.0 10.5 %collective-permute-done.25 = bf16[144,4608]{1,0:T(8,128)(2,1)S(1)} collective-permute-done((bf16[144,4608]{1,0:T(8,128)(2,1)}, bf16[144,4608]{1,0:T(8,128)(2,1)S(1)}, u32[]{:S(2)}, u32[]{:S(2)}) %collective-permute-start.25) | collective-permute-done | bytes 1327136 | tf_op jit(solution)/shard_map/ppermute | solution.py:65
  881.4 13.4 %collective-permute-done.29 = bf16[72,4608]{1,0:T(8,128)(2,1)S(1)} collective-permute-done((bf16[72,4608]{1,0:T(8,128)(2,1)S(1)}, bf16[72,4608]{1,0:T(8,128)(2,1)S(1)}, u32[]{:S(2)}, u32[]{:S(2)}) %collective-permute-start.29) | collective-permute-done | bytes 663584 | tf_op jit(solution)/shard_map/ppermute | solution.py:65
  898.0 8.7 fusion.16
  918.8 8.9 multiply_subtract_fusion.3
  (311 shorter events, 121.5 us)
Async XLA Ops:
  7.2 100.1 %all-gather.4.cloned.1.call-start = ((), (), s32[]{:S(2)}) async-start(), calls=%async_computation.3 | async-start | bytes 10948608 | tf_op jit(solution)/shard_map/all_gather | solution.py:553
  11.9 184.8 %all-gather.6.cloned.1.call-start = ((), (), s32[]{:S(2)}) async-start(), calls=%async_computation.4 | async-start | bytes 10948608 | tf_op jit(solution)/shard_map/all_gather | solution.py:559
  14.7 271.4 %all-gather.8.cloned.1.call-start = ((), (), s32[]{:S(2)}) async-start(), calls=%async_computation.5 | async-start | bytes 10948608 | tf_op jit(solution)/shard_map/all_gather | solution.py:571
  14.8 9.2 collective-permute-start.2
  19.0 4.7 collective-permute-start.1
  19.0 4.4 collective-permute-start
  28.7 8.0 collective-permute-start.3
  29.4 9.7 %collective-permute-start.5 = (f32[3,6912]{1,0:T(4,128)S(1)}, f32[3,6912]{1,0:T(4,128)S(1)}, u32[]{:S(2)}, u32[]{:S(2)}) collective-permute-start(f32[3,6912]{1,0:T(4,128)S(1)} %get-tuple-element.255), channel_id=1, source_target_pairs={{0,3},{1,0},{2,1},{3,2},{4,7},{5,4},{6,5},{7,6},{8,11},{9,8},{10,9... | collective-permute-start | bytes 248840 | tf_op jit(solution)/shard_map/ppermute | solution.py:60
  32.0 13.0 %collective-permute-start.4 = (f32[3,6912]{1,0:T(4,128)S(1)}, f32[3,6912]{1,0:T(4,128)S(1)}, u32[]{:S(2)}, u32[]{:S(2)}) collective-permute-start(f32[3,6912]{1,0:T(4,128)S(1)} %get-tuple-element.256), channel_id=1, source_target_pairs={{0,2},{1,3},{2,0},{3,1},{4,6},{5,7},{6,4},{7,5},{8,10},{9,11},{10,... | collective-permute-start | bytes 248840 | tf_op jit(solution)/shard_map/ppermute | solution.py:60
  45.1 421.4 %reduce-scatter.4.cloned.1.call-start = ((), (), s32[]{:S(2)}) async-start(), calls=%async_computation.6 | async-start | bytes 13271040 | tf_op jit(solution)/shard_map/reduce_scatter | solution.py:597
  232.9 364.1 %reduce-scatter.6.cloned.1.call-start = ((), (), s32[]{:S(2)}) async-start(), calls=%async_computation.7 | async-start | bytes 6635520 | tf_op jit(solution)/shard_map/reduce_scatter | solution.py:597
  324.0 31.2 %copy-start.3 = (bf16[3,256,1152]{2,1,0:T(8,128)(2,1)S(1)}, bf16[3,256,1152]{2,1,0:T(8,128)(2,1)}, u32[]{:S(2)}) copy-start(bf16[3,256,1152]{2,1,0:T(8,128)(2,1)} %param.40) | copy-start | bytes 5308420
  324.0 116.1 %collective-permute-start.6 = (bf16[4,144,4608]{2,1,0:T(8,128)(2,1)}, bf16[4,144,4608]{2,1,0:T(8,128)(2,1)}, u32[]{:S(2)}, u32[]{:S(2)}) collective-permute-start(bf16[4,144,4608]{2,1,0:T(8,128)(2,1)} %dynamic-slice_bitcast_fusion), channel_id=1, source_target_pairs={{0,4},{4,0},{1,5},{5,1},{2,6},{6,2},{3,7},{7,3},{8,12},{12,8},{9,1... | collective-permute-start | bytes 15925256 | tf_op jit(solution)/shard_map/ppermute | solution.py:65
  476.8 3.2 collective-permute-start.8
  480.6 7.7 collective-permute-start.9
  482.7 354.0 %reduce-scatter.8.cloned.1.call-start = ((), (), s32[]{:S(2)}) async-start(), calls=%async_computation.8 | async-start | bytes 6635520 | tf_op jit(solution)/shard_map/reduce_scatter | solution.py:597
  482.7 114.2 %collective-permute-start.7 = (bf16[4,144,4608]{2,1,0:T(8,128)(2,1)}, bf16[4,144,4608]{2,1,0:T(8,128)(2,1)}, u32[]{:S(2)}, u32[]{:S(2)}) collective-permute-start(bf16[4,144,4608]{2,1,0:T(8,128)(2,1)} %pad_maximum_fusion), channel_id=1, source_target_pairs={{0,4},{4,0},{1,5},{5,1},{2,6},{6,2},{3,7},{7,3},{8,12},{12,8},{9,1... | collective-permute-start | bytes 15925256 | tf_op jit(solution)/shard_map/ppermute | solution.py:65
  484.0 8.2 collective-permute-start.10
  486.1 6.2 collective-permute-start.11
  493.2 103.8 %copy-start.23 = (bf16[4,144,1152]{2,1,0:T(8,128)(2,1)S(1)}, bf16[4,144,1152]{2,1,0:T(8,128)(2,1)}, u32[]{:S(2)}) copy-start(bf16[4,144,1152]{2,1,0:T(8,128)(2,1)} %get-tuple-element.244) | copy-start | bytes 3981316
  604.1 27.8 %slice-start.2 = ((s8[5308416]{0:T(1024)(128)(4,1)}), s8[1114112]{0:T(1024)(128)(4,1)S(1)}, s32[]{:S(2)}) async-start(s8[5308416]{0:T(1024)(128)(4,1)} %bitcast.229), calls=%async_computation.11 | async-start | bytes 2228224
  604.2 27.8 %slice-start.3 = ((s8[5308416]{0:T(1024)(128)(4,1)}), s8[4194304]{0:T(1024)(128)(4,1)S(1)}, s32[]{:S(2)}) async-start(s8[5308416]{0:T(1024)(128)(4,1)} %bitcast.229), calls=%async_computation.12 | async-start | bytes 8388608
  627.7 9.4 %collective-permute-start.31 = (bf16[4032]{0:T(1024)(128)(2,1)S(1)}, bf16[4032]{0:T(1024)(128)(2,1)S(1)}, u32[]{:S(2)}, u32[]{:S(2)}) collective-permute-start(bf16[4032]{0:T(1024)(128)(2,1)S(1)} %get-tuple-element.205), channel_id=1, source_target_pairs={{0,8},{8,0},{16,24},{24,16},{1,9},{9,1},{17,25},{25,17},{2,10},{10... | collective-permute-start | bytes 24200 | tf_op jit(solution)/shard_map/ppermute | solution.py:65
  630.9 30.9 %collective-permute-start.26 = (bf16[144,4608]{1,0:T(8,128)(2,1)S(1)}, bf16[144,4608]{1,0:T(8,128)(2,1)S(1)}, u32[]{:S(2)}, u32[]{:S(2)}) collective-permute-start(bf16[144,4608]{1,0:T(8,128)(2,1)S(1)} %copy-done.24), channel_id=1, source_target_pairs={{0,4},{4,0},{1,5},{5,1},{2,6},{6,2},{3,7},{7,3},{8,12},{12,8},{9,1... | collective-permute-start | bytes 3981320 | tf_op jit(solution)/shard_map/ppermute | solution.py:65
  636.8 3.9 collective-permute-start.17
  637.1 2.9 collective-permute-start.32
  638.4 3.7 collective-permute-start.21
  639.0 97.2 %collective-permute-start.12 = (bf16[1152,1152]{1,0:T(8,128)(2,1)S(1)}, bf16[1152,1152]{1,0:T(8,128)(2,1)}, u32[]{:S(2)}, u32[]{:S(2)}) collective-permute-start(bf16[1152,1152]{1,0:T(8,128)(2,1)S(1)} %copy-done.32), channel_id=1, source_target_pairs={{0,4},{4,0},{1,5},{5,1},{2,6},{6,2},{3,7},{7,3},{8,12},{12,8},{9,1... | collective-permute-start | bytes 7962632 | tf_op jit(solution)/shard_map/ppermute | solution.py:65
  640.7 95.6 %slice-start.8 = ((s8[5308416]{0:T(1024)(128)(4,1)}), s8[4194304]{0:T(1024)(128)(4,1)S(1)}, s32[]{:S(2)}) async-start(s8[5308416]{0:T(1024)(128)(4,1)} %bitcast.235), calls=%async_computation.17 | async-start | bytes 8388608
  640.8 15.6 %collective-permute-start.18 = (bf16[72,4608]{1,0:T(8,128)(2,1)S(1)}, bf16[72,4608]{1,0:T(8,128)(2,1)S(1)}, u32[]{:S(2)}, u32[]{:S(2)}) collective-permute-start(bf16[72,4608]{1,0:T(8,128)(2,1)S(1)} %fusion.53), channel_id=1, source_target_pairs={{0,16},{8,24},{16,0},{24,8},{1,17},{9,25},{17,1},{25,9},{2,18},{10... | collective-permute-start | bytes 1990664 | tf_op jit(solution)/shard_map/ppermute | solution.py:65
  642.4 92.5 %collective-permute-start.22 = (bf16[72,6912]{1,0:T(8,128)(2,1)S(1)}, bf16[72,6912]{1,0:T(8,128)(2,1)S(1)}, u32[]{:S(2)}, u32[]{:S(2)}) collective-permute-start(bf16[72,6912]{1,0:T(8,128)(2,1)S(1)} %fusion.46), channel_id=1, source_target_pairs={{0,16},{8,24},{16,0},{24,8},{1,17},{9,25},{17,1},{25,9},{2,18},{10... | collective-permute-start | bytes 2985992 | tf_op jit(solution)/shard_map/ppermute | solution.py:65
  656.6 79.6 %slice-start.9 = ((s8[5308416]{0:T(1024)(128)(4,1)}), s8[1114112]{0:T(1024)(128)(4,1)S(1)}, s32[]{:S(2)}) async-start(s8[5308416]{0:T(1024)(128)(4,1)} %bitcast.235), calls=%async_computation.18 | async-start | bytes 2228224
  656.6 76.2 %collective-permute-start.19 = (bf16[72,4608]{1,0:T(8,128)(2,1)S(1)}, bf16[72,4608]{1,0:T(8,128)(2,1)S(1)}, u32[]{:S(2)}, u32[]{:S(2)}) collective-permute-start(bf16[72,4608]{1,0:T(8,128)(2,1)S(1)} %add_convert_fusion.3), channel_id=1, source_target_pairs={{0,4},{4,0},{1,5},{5,1},{2,6},{6,2},{3,7},{7,3},{8,12},{12,8},{9,1... | collective-permute-start | bytes 1990664 | tf_op jit(solution)/shard_map/ppermute | solution.py:65
  661.8 74.4 %slice-start.6 = ((s8[5308416]{0:T(1024)(128)(4,1)}), s8[4194304]{0:T(1024)(128)(4,1)S(1)}, s32[]{:S(2)}) async-start(s8[5308416]{0:T(1024)(128)(4,1)} %bitcast.233), calls=%async_computation.15 | async-start | bytes 8388608
  663.5 72.8 %slice-start.7 = ((s8[5308416]{0:T(1024)(128)(4,1)}), s8[1114112]{0:T(1024)(128)(4,1)S(1)}, s32[]{:S(2)}) async-start(s8[5308416]{0:T(1024)(128)(4,1)} %bitcast.233), calls=%async_computation.16 | async-start | bytes 2228224
  734.1 29.8 %collective-permute-start.20 = (bf16[2,72,4608]{2,1,0:T(8,128)(2,1)}, bf16[2,72,4608]{2,1,0:T(8,128)(2,1)}, u32[]{:S(2)}, u32[]{:S(2)}) collective-permute-start(bf16[2,72,4608]{2,1,0:T(8,128)(2,1)} %pad_maximum_fusion.3), channel_id=1, source_target_pairs={{0,8},{8,0},{16,24},{24,16},{1,9},{9,1},{17,25},{25,17},{2,10},{10... | collective-permute-start | bytes 3981320 | tf_op jit(solution)/shard_map/ppermute | solution.py:65
  735.1 23.8 %collective-permute-start.23 = (bf16[72,6912]{1,0:T(8,128)(2,1)S(1)}, bf16[72,6912]{1,0:T(8,128)(2,1)}, u32[]{:S(2)}, u32[]{:S(2)}) collective-permute-start(bf16[72,6912]{1,0:T(8,128)(2,1)S(1)} %add_convert_fusion.1), channel_id=1, source_target_pairs={{0,4},{4,0},{1,5},{5,1},{2,6},{6,2},{3,7},{7,3},{8,12},{12,8},{9,1... | collective-permute-start | bytes 2985992 | tf_op jit(solution)/shard_map/ppermute | solution.py:65
  751.2 11.3 %collective-permute-start.13 = (bf16[288,1152]{1,0:T(8,128)(2,1)S(1)}, bf16[288,1152]{1,0:T(8,128)(2,1)S(1)}, u32[]{:S(2)}, u32[]{:S(2)}) collective-permute-start(bf16[288,1152]{1,0:T(8,128)(2,1)S(1)} %dynamic-slice_bitcast_fusion.8), channel_id=1, source_target_pairs={{0,8},{8,0},{16,24},{24,16},{1,9},{9,1},{17,25},{25,17},{2,10},{10... | collective-permute-start | bytes 1990664 | tf_op jit(solution)/shard_map/ppermute | solution.py:65
  761.7 36.6 %collective-permute-start.24 = (bf16[2,72,6912]{2,1,0:T(8,128)(2,1)}, bf16[2,72,6912]{2,1,0:T(8,128)(2,1)}, u32[]{:S(2)}, u32[]{:S(2)}) collective-permute-start(bf16[2,72,6912]{2,1,0:T(8,128)(2,1)} %pad_maximum_fusion.1), channel_id=1, source_target_pairs={{0,8},{8,0},{16,24},{24,16},{1,9},{9,1},{17,25},{25,17},{2,10},{10... | collective-permute-start | bytes 5971976 | tf_op jit(solution)/shard_map/ppermute | solution.py:65
  762.7 16.6 %collective-permute-start.14 = (bf16[288,1152]{1,0:T(8,128)(2,1)S(1)}, bf16[288,1152]{1,0:T(8,128)(2,1)S(1)}, u32[]{:S(2)}, u32[]{:S(2)}) collective-permute-start(bf16[288,1152]{1,0:T(8,128)(2,1)S(1)} %fusion.54), channel_id=1, source_target_pairs={{0,16},{8,24},{16,0},{24,8},{1,17},{9,25},{17,1},{25,9},{2,18},{10... | collective-permute-start | bytes 1990664 | tf_op jit(solution)/shard_map/ppermute | solution.py:65
  779.5 15.7 %collective-permute-start.15 = (bf16[288,1152]{1,0:T(8,128)(2,1)S(1)}, bf16[288,1152]{1,0:T(8,128)(2,1)S(1)}, u32[]{:S(2)}, u32[]{:S(2)}) collective-permute-start(bf16[288,1152]{1,0:T(8,128)(2,1)S(1)} %add_convert_fusion.4), channel_id=1, source_target_pairs={{0,4},{4,0},{1,5},{5,1},{2,6},{6,2},{3,7},{7,3},{8,12},{12,8},{9,1... | collective-permute-start | bytes 1990664 | tf_op jit(solution)/shard_map/ppermute | solution.py:65
  796.7 23.8 %collective-permute-start.16 = (bf16[2,288,1152]{2,1,0:T(8,128)(2,1)}, bf16[2,288,1152]{2,1,0:T(8,128)(2,1)}, u32[]{:S(2)}, u32[]{:S(2)}) collective-permute-start(bf16[2,288,1152]{2,1,0:T(8,128)(2,1)} %pad_maximum_fusion.2), channel_id=1, source_target_pairs={{0,8},{8,0},{16,24},{24,16},{1,9},{9,1},{17,25},{25,17},{2,10},{10... | collective-permute-start | bytes 3981320 | tf_op jit(solution)/shard_map/ppermute | solution.py:65
  844.3 6.7 collective-permute-start.27
  849.9 30.7 %collective-permute-start.25 = (bf16[144,4608]{1,0:T(8,128)(2,1)}, bf16[144,4608]{1,0:T(8,128)(2,1)S(1)}, u32[]{:S(2)}, u32[]{:S(2)}) collective-permute-start(bf16[144,4608]{1,0:T(8,128)(2,1)} %reduce-scatter.8.cloned.1.call-done), channel_id=1, source_target_pairs={{0,4},{4,0},{1,5},{5,1},{2,6},{6,2},{3,7},{7,3},{8,12},{12,8},{9,1... | collective-permute-start | bytes 3981320 | tf_op jit(solution)/shard_map/ppermute | solution.py:65
  853.1 16.4 %collective-permute-start.28 = (bf16[72,4608]{1,0:T(8,128)(2,1)S(1)}, bf16[72,4608]{1,0:T(8,128)(2,1)S(1)}, u32[]{:S(2)}, u32[]{:S(2)}) collective-permute-start(bf16[72,4608]{1,0:T(8,128)(2,1)S(1)} %fusion.52), channel_id=1, source_target_pairs={{0,16},{8,24},{16,0},{24,8},{1,17},{9,25},{17,1},{25,9},{2,18},{10... | collective-permute-start | bytes 1990664 | tf_op jit(solution)/shard_map/ppermute | solution.py:65
  857.7 22.9 %copy-start.22 = (bf16[144,4608]{1,0:T(8,128)(2,1)S(1)}, bf16[144,4608]{1,0:T(8,128)(2,1)}, u32[]{:S(2)}) copy-start(bf16[144,4608]{1,0:T(8,128)(2,1)} %reduce-scatter.8.cloned.1.call-done) | copy-start | bytes 3981316
  869.7 25.1 %collective-permute-start.29 = (bf16[72,4608]{1,0:T(8,128)(2,1)S(1)}, bf16[72,4608]{1,0:T(8,128)(2,1)S(1)}, u32[]{:S(2)}, u32[]{:S(2)}) collective-permute-start(bf16[72,4608]{1,0:T(8,128)(2,1)S(1)} %add_convert_fusion.2), channel_id=1, source_target_pairs={{0,4},{4,0},{1,5},{5,1},{2,6},{6,2},{3,7},{7,3},{8,12},{12,8},{9,1... | collective-permute-start | bytes 1990664 | tf_op jit(solution)/shard_map/ppermute | solution.py:65
  896.9 9.8 %collective-permute-start.30 = (bf16[2,72,4608]{2,1,0:T(8,128)(2,1)}, bf16[2,72,4608]{2,1,0:T(8,128)(2,1)}, u32[]{:S(2)}, u32[]{:S(2)}) collective-permute-start(bf16[2,72,4608]{2,1,0:T(8,128)(2,1)} %pad_maximum_fusion.5), channel_id=1, source_target_pairs={{0,8},{8,0},{16,24},{24,16},{1,9},{9,1},{17,25},{25,17},{2,10},{10... | collective-permute-start | bytes 3981320 | tf_op jit(solution)/shard_map/ppermute | solution.py:65
  (47 other events, 309.2 us)
Sparse Core Ops, SparseCore 0:
  12.0 95.2 all-gather.3
  110.8 85.8 all-gather.5
  200.2 85.8 all-gather.7
  288.3 178.2 reduce-scatter.3
  482.8 98.5 reduce-scatter.5
  604.3 97.3 reduce-scatter.7

commit v3 on v2

--- a/solution.py
+++ b/solution.py
@@ -490,6 +490,87 @@
 
 def after(*values):
     return lax.optimization_barrier(values)
+
+
+def place_kernel(order_ref, *refs):
+    sources, target, held, came, left = refs[:-4], refs[-4], refs[-3], refs[-2], refs[-1]
+    inward, outward = [], []
+    for which, source in enumerate(sources):
+        for block in range(source.shape[0]):
+            index = which * source.shape[0] + block
+            inward.append(pltpu.make_async_copy(source.at[block], held.at[index], came.at[index]))
+            outward.append(
+                pltpu.make_async_copy(held.at[index], target.at[order_ref[index]], left.at[index])
+            )
+    for copy in inward:
+        copy.start()
+    for first, second in zip(inward, outward):
+        first.wait()
+        second.start()
+    for copy in outward:
+        copy.wait()
+
+
+def place_blocks(order, sources):
+    blocks = sum(source.shape[0] for source in sources)
+    shape = (blocks,) + sources[0].shape[1:]
+    return pl.pallas_call(
+        place_kernel,
+        grid_spec=pltpu.PrefetchScalarGridSpec(
+            num_scalar_prefetch=1,
+            grid=(1,),
+            in_specs=[pl.BlockSpec(memory_space=pl.ANY)] * len(sources),
+            out_specs=pl.BlockSpec(memory_space=pl.ANY),
+            scratch_shapes=[
+                pltpu.VMEM(shape, sources[0].dtype),
+                pltpu.SemaphoreType.DMA((blocks,)),
+                pltpu.SemaphoreType.DMA((blocks,)),
+            ],
+        ),
+        out_shape=jax.ShapeDtypeStruct(shape, sources[0].dtype),
+        compiler_params=params(48),
+        cost_estimate=pl.CostEstimate(
+            flops=0, bytes_accessed=4 * blocks * shape[1] * shape[2], transcendentals=0
+        ),
+    )(order, *sources)
+
+
+def hops_line(piece):
+    near = jnp.stack([piece, shift_by(piece, "fsdp", 1)])
+    far = jnp.stack([shift_by(piece, "fsdp", 2), shift_by(piece, "fsdp", 3)])
+    return near, far
+
+
+def hops_side(near, far):
+    near = jnp.concatenate([near, swap_with(near, "rep", 2)])
+    far = jnp.concatenate([far, swap_with(far, "dp", 1)])
+    return near, far
+
+
+def hops_other(near, far):
+    return near, far, swap_with(near, "dp", 1), swap_with(far, "rep", 2)
+
+
+def hops_core(sources):
+    return tuple(sources) + tuple(swap_with(source, "rep", 1) for source in sources)
+
+
+def hops_place(sources, weigh):
+    size = lax.axis_size("fsdp")
+    rep, pair, line = lax.axis_index("rep"), lax.axis_index("dp"), lax.axis_index("fsdp")
+    order = []
+    for core in (0, 1):
+        for kind in range(4):
+            for block in range(4):
+                hop, step = block // 2, block % 2
+                if kind in (0, 2):
+                    flip_rep, flip_pair, back = hop, kind // 2, step
+                else:
+                    flip_rep, flip_pair, back = kind // 2, hop, 2 + step
+                place = lax.rem(line - back + size, size) * weigh[0]
+                place = place + (rep ^ (2 * flip_rep + core)) * weigh[1] + (pair ^ flip_pair) * weigh[2]
+                order.append(place)
+    return place_blocks(jnp.stack(order).astype(jnp.int32), sources)
 
 
 def own_half(value, index):
@@ -556,7 +637,12 @@
     style = jax.nn.silu(condition).astype(BF16)
     one_cut = lax.dynamic_slice(w_fc1, (pair * half, rep * width), (half, width)).astype(BF16)
     one_cut, style = after(one_cut, style)
-    w_one = lax.all_gather(one_cut, everyone, axis=0, tiled=True).reshape(FF // width, width, width)
+    hops = lines == 4 and groups == 4
+    if hops:
+        w_one = hops_place(hops_core(hops_other(*hops_side(*hops_line(one_cut)))), (2, 8, 1))
+    else:
+        w_one = lax.all_gather(one_cut, everyone, axis=0, tiled=True)
+    w_one = w_one.reshape(FF // width, width, width)
     message = jnp.concatenate([style.reshape(-1), biases.astype(BF16)])
     heard = gather_line(message, "fsdp")
     bias_all = heard[:, slots * width :].reshape(-1).astype(F32)
@@ -568,7 +654,10 @@
     eighth = rows_two // (2 * groups)
     two_cut = lax.dynamic_slice_in_dim(w_fc2, (rep * 2 + pair) * eighth, eighth, axis=0).astype(BF16)
     two_cut, modulation = after(two_cut, modulation)
-    w_two = lax.all_gather(two_cut, ("fsdp", "rep", "dp"), axis=0, tiled=True)
+    if hops:
+        parts = hops_line(two_cut)
+    else:
+        w_two = lax.all_gather(two_cut, ("fsdp", "rep", "dp"), axis=0, tiled=True)
     mod = jnp.concatenate(
         [
             modulation.reshape(slots, 6, width),
@@ -584,10 +673,19 @@
     x = images.reshape(tokens, width)
     cot = cotangent.reshape(tokens, width)
 
+    if hops:
+        *parts, mod = after(*parts, mod)
+        parts = hops_side(*parts)
     attn_in, packed, attended, log_total, attn_out, middle, mlp_in, d_mlp, mlp_sums = attention_forward(
         x, cot, mod, bias, w_attn, slots, length, width
     )
+    if hops:
+        *parts, mlp_in = after(*parts, mlp_in)
+        parts = hops_other(*parts)
     activated, slope = hidden_forward(mlp_in, w_one, b_fc1)
+    if hops:
+        *parts, activated = after(*parts, activated)
+        parts = hops_core(parts)
     grad_two = grad_rows(activated, d_mlp)
 
     def halves(gradient):
@@ -601,8 +699,10 @@
     def pair_sum(gradient, there):
         return (own_half(halves(gradient), pair).astype(F32) + there.astype(F32)).astype(BF16)
 
+    if hops:
+        w_two = hops_place(parts, (8, 2, 1)).reshape(FF, width)
     grad_two, d_mlp = after(grad_two, d_mlp)
-    two_line = line_sum(grad_two)
+    two_half = lax.psum_scatter(grad_two, ("fsdp", "dp"), scatter_dimension=0, tiled=True)
     d_hidden, hidden_sums = hidden_back(d_mlp, w_two, slope)
     grad_one = grad_columns(mlp_in, d_hidden)
     give_one = own_half(halves(grad_one), 1 - pair)
@@ -622,7 +722,7 @@
     give_attn, d_packed = after(give_attn, d_packed)
     in_grad, input_rows = input_back(d_packed, w_attn, x, d_middle, mod, slots, length, width)
 
-    two_line, there_one, give_attn, input_rows = after(two_line, there_one, give_attn, input_rows)
+    two_half, there_one, give_attn, input_rows = after(two_half, there_one, give_attn, input_rows)
     there_attn = swap_with(give_attn, "dp", 1)
     one_both, input_rows = after(pair_sum(grad_one, there_one), input_rows)
     one_half = line_sum(one_both)
@@ -652,14 +752,6 @@
             jnp.sum(reports[:, 7 * edge :].astype(F32), axis=0),
         ]
     )
-    one_half, there_attn, grad_ada, bias_group = after(one_half, there_attn, grad_ada, bias_group)
-    attn_both = jnp.concatenate(
-        [own_half(halves(grad_qkv), pair), own_half(halves(grad_proj), pair)], axis=2
-    )
-    attn_both = (attn_both.astype(F32) + there_attn.astype(F32)).astype(BF16)
-    attn_both, two_line, one_half, grad_ada = after(attn_both, two_line, one_half, grad_ada)
-    attn_half = line_sum(attn_both)
-    two_there = swap_with(two_line, "dp", 1)
     own_bias = biases.shape[0]
     grad_bias = lax.dynamic_slice_in_dim(bias_group, line * own_bias, own_bias, axis=0)
 
@@ -695,23 +787,26 @@
         )
         return (master - local).astype(BF16)
 
-    def sum_groups(mine):
+    low = rep % 2
+
+    def sum_rep(mine):
         if mine.ndim == 1:
             total = (mine.astype(F32) + swap_with(mine, "rep", 1).astype(F32)).astype(BF16)
             return total.astype(F32) + swap_with(total, "rep", 2).astype(F32)
-        quarter = mine.shape[0] // 2
-        columns = mine.shape[1]
-        low = rep % 2
-        mine = mine.reshape(2, quarter, columns)
+        mine = mine.reshape(2, mine.shape[0] // 2, mine.shape[1])
         keep = lax.dynamic_index_in_dim(mine, low, 0, keepdims=False)
         give = lax.dynamic_index_in_dim(mine, 1 - low, 0, keepdims=False)
         total = (keep.astype(F32) + swap_with(give, "rep", 1).astype(F32)).astype(BF16)
-        total = (total.astype(F32) + swap_with(total, "rep", 2).astype(F32)).astype(BF16)
-        twin = two_rows(total[None], swap_with(total, "dp", 1)[None])
-        other = swap_with(twin, "rep", 1)
-        first = jnp.where(low == 0, twin, other)
-        second = jnp.where(low == 0, other, twin)
-        return jnp.stack([first, second], axis=1).reshape(4 * quarter, columns).astype(F32)
+        return (total.astype(F32) + swap_with(total, "rep", 2).astype(F32)).astype(BF16)
+
+    def join_cores(total):
+        other = swap_with(total, "rep", 1)
+        first = jnp.where(low == 0, total, other)
+        second = jnp.where(low == 0, other, total)
+        return jnp.stack([first, second], axis=1).reshape(-1, total.shape[2]).astype(F32)
+
+    def join_pair(total):
+        return join_cores(two_rows(total[None], swap_with(total, "dp", 1)[None]))
 
     def own_rows(value):
         count = value.shape[0] // 2
@@ -734,18 +829,29 @@
         outers_out[index] = outer_next
         weights_out[index] = masters[index] - OUTER_RATE * (delta + OUTER_MOMENTUM * outer_next)
 
-    finish(0, grad_ada, sum_groups(own_delta(0, own_rows(grad_ada))))
+    ada_delta = local_delta(w_ada, first_ada[0], second_ada[0], grad_ada, rates[0])
+    one_half, there_attn, two_half, ada_delta = after(one_half, there_attn, two_half, ada_delta)
+    attn_both = jnp.concatenate(
+        [own_half(halves(grad_qkv), pair), own_half(halves(grad_proj), pair)], axis=2
+    )
+    attn_both = (attn_both.astype(F32) + there_attn.astype(F32)).astype(BF16)
+    attn_both, two_half, one_half, ada_delta = after(attn_both, two_half, one_half, ada_delta)
+    attn_half = line_sum(attn_both)
+    finish(0, grad_ada, join_cores(sum_rep(ada_delta)[None]))
     bias_delta = local_delta(biases, first_bias[0], second_bias[0], grad_bias, rates[5])
-    finish(5, grad_bias, sum_groups(bias_delta))
-    finish(3, both_halves(one_half), sum_groups(own_delta(3, one_half)))
-    grad_two_sum = two_line.astype(F32) + two_there.astype(F32)
-    finish(4, grad_two_sum, sum_groups(own_delta(4, own_rows(grad_two_sum))))
-    attn_half, weights_out[4], weights_out[3], weights_out[0] = after(
-        attn_half, weights_out[4], weights_out[3], weights_out[0]
-    )
+    finish(5, grad_bias, sum_rep(bias_delta))
+    two_total = sum_rep(own_delta(4, two_half))
+    finish(4, both_halves(two_half), join_pair(two_total))
+    one_total = sum_rep(own_delta(3, one_half))
+    finish(3, both_halves(one_half), join_pair(one_total))
+    attn_half, one_total = after(attn_half, one_total)
     edge = 3 * width
-    summed = sum_groups(
-        jnp.concatenate([own_delta(1, attn_half[:, :edge]), own_delta(2, attn_half[:, edge:])], axis=1)
+    summed = join_pair(
+        sum_rep(
+            jnp.concatenate(
+                [own_delta(1, attn_half[:, :edge]), own_delta(2, attn_half[:, edge:])], axis=1
+            )
+        )
     )
     attn_full = both_halves(attn_half)
     finish(1, attn_full[:, :edge], summed[:, :edge])

time: 939 us -> 892 us (0.950)
  waiting for transfers between devices: 472 us -> 330 us
  starting transfers between devices: 37.1 us -> 92.5 us
  other arithmetic: 164 us -> 186 us
  Pallas kernels: 186 us -> 205 us
    all_gather x2 -> x0, waiting for transfers between devices: 112 us -> none  [the longest x1 60.4 us: body(): lax.all_gather(one_cut, everyone, axis=0, tiled=True)]
    all_gather x1, waiting for transfers between devices: 60.5 us -> 0.01 us  [body(): lax.all_gather(attention_cut, everyone, axis=0, tiled=True)]
    ppermute x9 -> x15, waiting for transfers between devices: 18.3 us -> 74.2 us  [shift_by(): lax.ppermute(value, axis, [(i, (i + step) % size) for i in range(size)])]
    ppermute x24 -> x39, starting transfers between devices: 22.8 us -> 62.3 us  [swap_with(): return lax.ppermute(value, axis, [(i, i ^ bit) for i in range(size)])]
    reduce_scatter x3 -> x2, waiting for transfers between devices: 26.4 us -> 0.01 us  [line_sum(): lax.psum_scatter(both.reshape(-1, both.shape[-1]), 'fsdp', scatter_dimens...]
    pallas_call x0 -> x2, Pallas kernels: none -> 17.9 us  [place_blocks(): pl.pallas_call(place_kernel, grid_spec=pltpu.PrefetchScalarGridSpec(num_s...]
    ppermute x9 -> x15, starting transfers between devices: 13.6 us -> 29.9 us  [shift_by(): lax.ppermute(value, axis, [(i, (i + step) % size) for i in range(size)])]
    add x1 -> x2, other arithmetic: 3.43 us -> 15.9 us  [moments_next(): first_next = BETA_ONE * first + (1.0 - BETA_ONE) * gradient]
  transfers between devices with their start and end apart: 39 -> 58, of which waited for: 22 -> 22; matrix products, arithmetic and copies ran while one was open for 17% -> 21% of each run, Pallas kernels for 20% -> 21%
where the time goes in v3:
time: 892 us; the launch traced here: 887 us
  waiting for transfers between devices  330 us (37%)
  Pallas kernels  205 us (23%)
  other arithmetic  186 us (21%)
  starting transfers between devices  92.5 us (10%)
  local copies, waits for them, and re-layouts  50.4 us (6%)
  between operations  16.8 us (2%)
    ppermute x39, waiting for transfers between devices, swap_with(): return lax.ppermute(value, axis, [(i, i ^ bit) for i in range(size)])  256 us
    ppermute x15, waiting for transfers between devices, shift_by(): lax.ppermute(value, axis, [(i, (i + step) % size) for i in range(size)])  74.2 us
    ppermute x39, starting transfers between devices, swap_with(): return lax.ppermute(value, axis, [(i, i ^ bit) for i in range(size)])  62.3 us
    sub x5, other arithmetic, finish(): masters[index] - OUTER_RATE * (delta + OUTER_MOMENTUM * outer_next)  41.7 us
    broadcast_in_dim x3, other arithmetic, finish(): seconds_out[index] = second_next[None]  34 us
    ppermute x15, starting transfers between devices, shift_by(): lax.ppermute(value, axis, [(i, (i + step) % size) for i in range(size)])  29.9 us
    pallas_call x3, Pallas kernels, grad_columns(): pl.pallas_call(grad_kernel, grid=(width // rows,), in_specs=[whole_spec((...  29.6 us
    pallas_call x1, Pallas kernels, mlp_rest(): pl.pallas_call(mlp_rest_kernel, grid=(units,), in_specs=[column, rows_spe...  28.3 us
  transfers between devices with their start and end apart: 58, of which 22 were waited for; matrix products, arithmetic and copies ran while one was open for 21% of the time, Pallas kernels for 21%

profile of v3, /device:TPU:1, one launch (start us, length us, event | category | flops | bytes accessed | tf_op | source)
XLA Modules:
  0.0 886.6 jit_solution(4536017727446456745)
XLA Ops:
  33.2 10.9 %collective-permute-done.3 = f32[3,6912]{1,0:T(4,128)S(1)} collective-permute-done((f32[3,6912]{1,0:T(4,128)S(1)}, f32[3,6912]{1,0:T(4,128)S(1)}, u32[]{:S(2)}, u32[]{:S(2)}) %collective-permute-start.3) | collective-permute-done | bytes 82976 | tf_op jit(solution)/shard_map/ppermute | solution.py:60
  44.1 13.6 %collective-permute-start.13 = (bf16[144,1152]{1,0:T(8,128)(2,1)S(1)}, bf16[144,1152]{1,0:T(8,128)(2,1)S(1)}, u32[]{:S(2)}, u32[]{:S(2)}) collective-permute-start(bf16[144,1152]{1,0:T(8,128)(2,1)S(1)} %dynamic_slice.227), channel_id=1, source_target_pairs={{0,1},{1,2},{2,3},{3,0},{4,5},{5,6},{6,7},{7,4},{8,9},{9,10},{10,1... | collective-permute-start | bytes 995336 | tf_op jit(solution)/shard_map/ppermute | solution.py:60
  57.7 16.7 %collective-permute-done.4 = f32[3,6912]{1,0:T(4,128)S(1)} collective-permute-done((f32[3,6912]{1,0:T(4,128)S(1)}, f32[3,6912]{1,0:T(4,128)S(1)}, u32[]{:S(2)}, u32[]{:S(2)}) %collective-permute-start.4) | collective-permute-done | bytes 82976 | tf_op jit(solution)/shard_map/ppermute | solution.py:60
  76.2 6.6 collective-permute-start.14
  85.4 39.1 %collective-permute-done.7 = bf16[144,1152]{1,0:T(8,128)(2,1)S(1)} collective-permute-done((bf16[144,1152]{1,0:T(8,128)(2,1)S(1)}, bf16[144,1152]{1,0:T(8,128)(2,1)S(1)}, u32[]{:S(2)}, u32[]{:S(2)}) %collective-permute-start.7) | collective-permute-done | bytes 331808 | tf_op jit(solution)/shard_map/ppermute | solution.py:60
  133.3 8.9 %collective-permute-start.20 = (bf16[4,144,1152]{2,1,0:T(8,128)(2,1)}, bf16[4,144,1152]{2,1,0:T(8,128)(2,1)}, u32[]{:S(2)}, u32[]{:S(2)}) collective-permute-start(bf16[4,144,1152]{2,1,0:T(8,128)(2,1)} %pad_maximum_fusion.3.refs_0_), channel_id=1, source_target_pairs={{0,8},{8,0},{16,24},{24,16},{1,9},{9,1},{17,25},{25,17},{2,10},{10... | collective-permute-start | bytes 3981320 | tf_op jit(solution)/shard_map/ppermute | solution.py:65
  142.2 24.7 %collective-permute-done.9 = bf16[2,144,1152]{2,1,0:T(8,128)(2,1)S(1)} collective-permute-done((bf16[2,144,1152]{2,1,0:T(8,128)(2,1)S(1)}, bf16[2,144,1152]{2,1,0:T(8,128)(2,1)S(1)}, u32[]{:S(2)}, u32[]{:S(2)}) %collective-permute-start.9) | collective-permute-done | bytes 663584 | tf_op jit(solution)/shard_map/ppermute | solution.py:65
  166.9 9.4 %collective-permute-start.21 = (bf16[4,144,1152]{2,1,0:T(8,128)(2,1)}, bf16[4,144,1152]{2,1,0:T(8,128)(2,1)}, u32[]{:S(2)}, u32[]{:S(2)}) collective-permute-start(bf16[4,144,1152]{2,1,0:T(8,128)(2,1)} %pad_maximum_fusion.4.refs_1_), channel_id=1, source_target_pairs={{0,8},{8,0},{16,24},{24,16},{1,9},{9,1},{17,25},{25,17},{2,10},{10... | collective-permute-start | bytes 3981320 | tf_op jit(solution)/shard_map/ppermute | solution.py:65
  178.3 26.6 %shard_map.590 = (bf16[768,1152]{1,0:T(8,128)(2,1)S(1)}, bf16[768,3456]{1,0:T(8,128)(2,1)}, bf16[768,1152]{1,0:T(8,128)(2,1)S(1)}, f32[768,128]{1,0:T(8,128)S(1)...) custom-call(bf16[768,1152]{1,0:T(8,128)(2,1)} %bitcast.274, ...), custom_call_target="tpu_custom_call" | custom-call | flops 8153726976 | bytes 41943040 | tf_op jit(solution)/shard_map/pallas_call | solution.py:188
  211.2 8.8 shard_map.591
  220.1 21.4 %shard_map.592 = (bf16[768,4608]{1,0:T(8,128)(2,1)}, bf16[768,4608]{1,0:T(8,128)(2,1)}) custom-call(bf16[768,1152]{1,0:T(8,128)(2,1)S(1)} %copy-done.11, bf16[4,1152,1152]{2,1,0:T(8,128)(2,1)} %bitcast.292, f32[1,4608]{1,0:T(1,128)S(1)} %reshape.486.bias_ref), custom_call_target="tpu_custom_call" | custom-call | flops 8153726976 | bytes 27262976 | tf_op jit(solution)/shard_map/pallas_call | solution.py:233
  241.5 14.8 %shard_map.594 = bf16[4608,1152]{1,0:T(8,128)(2,1)} custom-call(bf16[768,4608]{1,0:T(8,128)(2,1)} %get-tuple-element.160.left_ref.act_ref, bf16[768,1152]{1,0:T(8,128)(2,1)S(1)} %copy-done.13), custom_call_target="tpu_custom_call" | custom-call | flops 8153726976 | bytes 24772608 | tf_op jit(solution)/shard_map/pallas_call | solution.py:478
  266.0 9.1 %shard_map.593 = bf16[32,144,1152]{2,1,0:T(8,128)(2,1)} custom-call(s32[32]{0:T(128)S(1)} %stack.356.order_ref, bf16[4,144,1152]{2,1,0:T(8,128)(2,1)S(1)} %pad_maximum_fusion.1.refs_0_, bf16[4,144,1152]{2,1,0:T(8,128)(2,1)S(1)} %pad_maximum_fusion.2.refs_1_, bf16[4,144,1152]{2,1,0:T(8,128)(2,1)} %collective-permute-done.11.refs_2_, ...), custom_call_target="tpu_custom_call" | custom-call | bytes 21233664 | tf_op jit(solution)/shard_map/pallas_call | solution.py:517
  275.2 16.6 %shard_map.595 = (bf16[768,4608]{1,0:T(8,128)(2,1)}, f32[8,4608]{1,0:T(8,128)S(1)}) custom-call(bf16[768,1152]{1,0:T(8,128)(2,1)S(1)} %copy-done.14, bf16[4608,1152]{1,0:T(8,128)(2,1)} %bitcast.296, bf16[768,4608]{1,0:T(8,128)(2,1)} %get-tuple-element.167.slope_ref), custom_call_target="tpu_custom_call" | custom-call | flops 8153726976 | bytes 27262976 | tf_op jit(solution)/shard_map/pallas_call | solution.py:264
  291.7 14.9 %shard_map.596 = bf16[1152,4608]{1,0:T(8,128)(2,1)} custom-call(bf16[768,1152]{1,0:T(8,128)(2,1)S(1)} %copy-done.12, bf16[768,4608]{1,0:T(8,128)(2,1)} %get-tuple-element.169.right_ref.d_hidden_ref), custom_call_target="tpu_custom_call" | custom-call | flops 8153726976 | bytes 24772608 | tf_op jit(solution)/shard_map/pallas_call | solution.py:462
  306.6 5.5 dynamic-slice_bitcast_fusion
  313.3 28.3 %shard_map.597 = (f32[768,1152]{1,0:T(8,128)S(1)}, f32[768,1152]{1,0:T(8,128)}) custom-call(bf16[768,4608]{1,0:T(8,128)(2,1)} %get-tuple-element.160.left_ref.act_ref, bf16[4608,1152]{1,0:T(8,128)(2,1)} %bitcast.297, bf16[768,4608]{1,0:T(8,128)(2,1)} %get-tuple-element.169.right_ref.d_hidden_ref, bf16[4,1152,1152]{2,1,0:T(8,128)(2,1)} %bitcast.293), custom_call_target="tpu_custom_call" | custom-call | flops 16307453952 | bytes 44040192 | tf_op jit(solution)/shard_map/pallas_call | solution.py:302
  343.4 12.3 %shard_map.598 = (bf16[768,1152]{1,0:T(8,128)(2,1)}, f32[768,1152]{1,0:T(8,128)}, bf16[768,1152]{1,0:T(8,128)(2,1)S(1)}, bf16[768,1152]{1,0:T(8,128)(2,1)S(1)}, f32[3,8,1152]{2,1,0:T(8,128)S(1)}) custom-call(f32[768,1152]{1,0:T(8,128)} %copy-done.2, f32[8,1152]{1,0:T(8,128)S(1)} %scatter.19.bias_ref, f32[768,1152]{1,0:T(8,128)} %get-tuple-element.171.d_in_ref, ...), custom_call_target="tpu_custom_call" | custom-call | flops 2038431744 | bytes 31457280 | tf_op jit(solution)/shard_map/pallas_call | solution.py:343
  359.2 23.4 %shard_map.600 = (bf16[768,3456]{1,0:T(8,128)(2,1)}, f32[3,8,1152]{2,1,0:T(8,128)S(1)}) custom-call(bf16[768,3456]{1,0:T(8,128)(2,1)} %get-tuple-element.176.packed_ref, bf16[768,1152]{1,0:T(8,128)(2,1)S(1)} %get-tuple-element.180.d_att_ref, f32[768,128]{1,0:T(8,128)S(1)} %get-tuple-element.181.log_ref), custom_call_target="tpu_custom_call" | custom-call | flops 8053063680 | bytes 14680064 | tf_op jit(solution)/shard_map/pallas_call | solution.py:398
  384.6 11.8 %shard_map.601 = bf16[1152,3456]{1,0:T(8,128)(2,1)} custom-call(bf16[768,1152]{1,0:T(8,128)(2,1)S(1)} %copy-done.9, bf16[768,3456]{1,0:T(8,128)(2,1)} %get-tuple-element.184.right_ref.d_packed_ref), custom_call_target="tpu_custom_call" | custom-call | flops 6115295232 | bytes 18579456 | tf_op jit(solution)/shard_map/pallas_call | solution.py:462
  396.4 5.8 dynamic-slice_bitcast_fusion.1
  406.7 14.1 %shard_map.602 = (bf16[768,1152]{1,0:T(8,128)(2,1)}, f32[3,8,1152]{2,1,0:T(8,128)S(1)}) custom-call(bf16[768,3456]{1,0:T(8,128)(2,1)} %get-tuple-element.184.right_ref.d_packed_ref, bf16[4,1152,1152]{2,1,0:T(8,128)(2,1)} %bitcast.300, bf16[768,1152]{1,0:T(8,128)(2,1)S(1)} %bitcast.275, f32[768,1152]{1,0:T(8,128)S(1)} %copy-done.4, ...), custom_call_target="tpu_custom_call" | custom-call | flops 6115295232 | bytes 20971520 | tf_op jit(solution)/shard_map/pallas_call | solution.py:430
  420.8 50.3 %collective-permute-done.28 = bf16[4,144,4608]{2,1,0:T(8,128)(2,1)} collective-permute-done((bf16[4,144,4608]{2,1,0:T(8,128)(2,1)}, bf16[4,144,4608]{2,1,0:T(8,128)(2,1)}, u32[]{:S(2)}, u32[]{:S(2)}) %collective-permute-start.28) | collective-permute-done | bytes 5308448 | tf_op jit(solution)/shard_map/ppermute | solution.py:65
  471.1 7.8 fusion
  491.2 6.2 collective-permute-done.31
  499.0 7.4 collective-permute-start.52
  507.7 22.5 %fusion.32 = (f32[1,288,6912]{2,1,0:T(8,128)}, bf16[288,6912]{1,0:T(8,128)(2,1)}, f32[1,288,6912]{2,1,0:T(8,128)}) fusion(f32[288,6912]{1,0:T(8,128)S(1)} %fusion.66, f32[1,288,6912]{2,1,0:T(8,128)} %param.58, f32[288,6912]{1,0:T(8,128)} %param.46, f32[]{:T(128)} %bitcast.102, f32[]{:T(128)} %bitcast.100, f32[1,288,6912]{2,1,0:T(8,128)} %param.52), kind=kLoop, calls=%fused_computation.80 | loop fusion | flops 33841152 | bytes 51757064 | tf_op jit(solution)/shard_map/broadcast_in_dim | solution.py:825
  530.4 70.3 %collective-permute-done.33 = bf16[4,144,4608]{2,1,0:T(8,128)(2,1)} collective-permute-done((bf16[4,144,4608]{2,1,0:T(8,128)(2,1)}, bf16[4,144,4608]{2,1,0:T(8,128)(2,1)}, u32[]{:S(2)}, u32[]{:S(2)}) %collective-permute-start.33) | collective-permute-done | bytes 5308448 | tf_op jit(solution)/shard_map/ppermute | solution.py:65
  600.6 7.4 add_convert_fusion
  608.1 5.6 fusion.30
  617.5 5.9 fusion.29
  634.2 9.3 %collective-permute-done.49 = bf16[288,1152]{1,0:T(8,128)(2,1)S(1)} collective-permute-done((bf16[288,1152]{1,0:T(8,128)(2,1)S(1)}, bf16[288,1152]{1,0:T(8,128)(2,1)S(1)}, u32[]{:S(2)}, u32[]{:S(2)}) %collective-permute-start.49) | collective-permute-done | bytes 663584 | tf_op jit(solution)/shard_map/ppermute | solution.py:65
  645.6 12.1 %collective-permute-done.35 = bf16[72,4608]{1,0:T(8,128)(2,1)S(1)} collective-permute-done((bf16[72,4608]{1,0:T(8,128)(2,1)S(1)}, bf16[72,4608]{1,0:T(8,128)(2,1)S(1)}, u32[]{:S(2)}, u32[]{:S(2)}) %collective-permute-start.35) | collective-permute-done | bytes 663584 | tf_op jit(solution)/shard_map/ppermute | solution.py:65
  659.8 24.1 %collective-permute-done.38 = bf16[576,1152]{1,0:T(8,128)(2,1)} collective-permute-done((bf16[576,1152]{1,0:T(8,128)(2,1)S(1)}, bf16[576,1152]{1,0:T(8,128)(2,1)}, u32[]{:S(2)}, u32[]{:S(2)}) %collective-permute-start.38) | collective-permute-done | bytes 1327136 | tf_op jit(solution)/shard_map/ppermute | solution.py:65
  687.1 5.1 fusion.4
  692.1 8.0 multiply_add_fusion.3
  703.1 4.7 fusion.3
  707.9 7.9 multiply_add_fusion.4
  728.6 11.0 %multiply_subtract_fusion.1 = (f32[1152,1152]{1,0:T(8,128)}, f32[1152,1152]{1,0:T(8,128)}) fusion(f32[1152,1152]{1,0:T(8,128)} %param.50, f32[1152,1152]{1,0:T(8,128)} %param.68, f32[2,2,288,1152]{3,2,1,0:T(8,128)} %copy.77), kind=kLoop, calls=%fused_computation.18 | loop fusion | flops 7962624 | bytes 26542080 | tf_op jit(solution)/shard_map/sub | solution.py:830
  741.1 27.7 %collective-permute-done.40 = bf16[144,6912]{1,0:T(8,128)(2,1)} collective-permute-done((bf16[144,6912]{1,0:T(8,128)(2,1)S(1)}, bf16[144,6912]{1,0:T(8,128)(2,1)}, u32[]{:S(2)}, u32[]{:S(2)}) %collective-permute-start.40) | collective-permute-done | bytes 1990688 | tf_op jit(solution)/shard_map/ppermute | solution.py:65
  776.6 11.5 %multiply_subtract_fusion.2 = (f32[288,4608]{1,0:T(8,128)}, f32[288,4608]{1,0:T(8,128)}) fusion(f32[288,4608]{1,0:T(8,128)} %param.49, f32[288,4608]{1,0:T(8,128)} %param.67, f32[2,2,72,4608]{3,2,1,0:T(8,128)} %convert_multiply_fusion.2), kind=kLoop, calls=%fused_computation.19 | loop fusion | flops 7962624 | bytes 26542080 | tf_op jit(solution)/shard_map/sub | solution.py:830
  794.5 4.8 fusion.43
  804.9 9.7 %multiply_subtract_fusion = (f32[288,6912]{1,0:T(8,128)}, f32[288,6912]{1,0:T(8,128)}) fusion(f32[288,6912]{1,0:T(8,128)S(1)} %bitcast.277, f32[288,6912]{1,0:T(8,128)} %param.64, f32[1,2,144,6912]{3,2,1,0:T(8,128)S(1)} %convert_multiply_fusion), kind=kLoop, calls=%fused_computation.9 | loop fusion | flops 11943936 | bytes 39813120 | tf_op jit(solution)/shard_map/sub | solution.py:830
  814.7 6.0 collective-permute-done.43
  822.5 10.6 %collective-permute-done.36 = bf16[144,4608]{1,0:T(8,128)(2,1)} collective-permute-done((bf16[144,4608]{1,0:T(8,128)(2,1)}, bf16[144,4608]{1,0:T(8,128)(2,1)}, u32[]{:S(2)}, u32[]{:S(2)}) %collective-permute-start.36) | collective-permute-done | bytes 1327136 | tf_op jit(solution)/shard_map/ppermute | solution.py:65
  835.6 11.6 %collective-permute-done.44 = bf16[72,4608]{1,0:T(8,128)(2,1)S(1)} collective-permute-done((bf16[72,4608]{1,0:T(8,128)(2,1)S(1)}, bf16[72,4608]{1,0:T(8,128)(2,1)S(1)}, u32[]{:S(2)}, u32[]{:S(2)}) %collective-permute-start.44) | collective-permute-done | bytes 663584 | tf_op jit(solution)/shard_map/ppermute | solution.py:65
  850.1 8.7 fusion.6
  870.9 8.9 multiply_subtract_fusion.3
  (340 shorter events, 161.5 us)
Async XLA Ops:
  7.3 171.0 %all-gather.2.cloned.1.call-start = ((), (), s32[]{:S(2)}) async-start(), calls=%async_computation.3 | async-start | bytes 10948608 | tf_op jit(solution)/shard_map/all_gather | solution.py:634
  11.9 459.2 %reduce-scatter.4.cloned.1.call-start = ((), (), s32[]{:S(2)}) async-start(), calls=%async_computation.4 | async-start | bytes 11943936 | tf_op jit(solution)/shard_map/reduce_scatter | solution.py:705
  14.1 11.1 %collective-permute-start.2 = (bf16[7488]{0:T(1024)(128)(2,1)S(1)}, bf16[7488]{0:T(1024)(128)(2,1)S(1)}, u32[]{:S(2)}, u32[]{:S(2)}) collective-permute-start(bf16[7488]{0:T(1024)(128)(2,1)S(1)} %pad_maximum_fusion.17), channel_id=1, source_target_pairs={{0,3},{1,0},{2,1},{3,2},{4,7},{5,4},{6,5},{7,6},{8,11},{9,8},{10,9... | collective-permute-start | bytes 44936 | tf_op jit(solution)/shard_map/ppermute | solution.py:60
  18.7 57.5 %collective-permute-start.16 = (bf16[144,1152]{1,0:T(8,128)(2,1)S(1)}, bf16[144,1152]{1,0:T(8,128)(2,1)S(1)}, u32[]{:S(2)}, u32[]{:S(2)}) collective-permute-start(bf16[144,1152]{1,0:T(8,128)(2,1)S(1)} %dynamic_slice.227), channel_id=1, source_target_pairs={{0,3},{1,0},{2,1},{3,2},{4,7},{5,4},{6,5},{7,6},{8,11},{9,8},{10,9... | collective-permute-start | bytes 995336 | tf_op jit(solution)/shard_map/ppermute | solution.py:60
  21.5 61.3 %collective-permute-start.15 = (bf16[144,1152]{1,0:T(8,128)(2,1)S(1)}, bf16[144,1152]{1,0:T(8,128)(2,1)S(1)}, u32[]{:S(2)}, u32[]{:S(2)}) collective-permute-start(bf16[144,1152]{1,0:T(8,128)(2,1)S(1)} %dynamic_slice.227), channel_id=1, source_target_pairs={{0,2},{1,3},{2,0},{3,1},{4,6},{5,7},{6,4},{7,5},{8,10},{9,11},{10,... | collective-permute-start | bytes 995336 | tf_op jit(solution)/shard_map/ppermute | solution.py:60
  29.7 14.3 %collective-permute-start.3 = (f32[3,6912]{1,0:T(4,128)S(1)}, f32[3,6912]{1,0:T(4,128)S(1)}, u32[]{:S(2)}, u32[]{:S(2)}) collective-permute-start(f32[3,6912]{1,0:T(4,128)S(1)} %get-tuple-element.269), channel_id=1, source_target_pairs={{0,1},{1,2},{2,3},{3,0},{4,5},{5,6},{6,7},{7,4},{8,9},{9,10},{10,1... | collective-permute-start | bytes 248840 | tf_op jit(solution)/shard_map/ppermute | solution.py:60
  29.8 27.9 %collective-permute-start.5 = (f32[3,6912]{1,0:T(4,128)S(1)}, f32[3,6912]{1,0:T(4,128)S(1)}, u32[]{:S(2)}, u32[]{:S(2)}) collective-permute-start(f32[3,6912]{1,0:T(4,128)S(1)} %get-tuple-element.270), channel_id=1, source_target_pairs={{0,3},{1,0},{2,1},{3,2},{4,7},{5,4},{6,5},{7,6},{8,11},{9,8},{10,9... | collective-permute-start | bytes 248840 | tf_op jit(solution)/shard_map/ppermute | solution.py:60
  33.1 41.4 %collective-permute-start.4 = (f32[3,6912]{1,0:T(4,128)S(1)}, f32[3,6912]{1,0:T(4,128)S(1)}, u32[]{:S(2)}, u32[]{:S(2)}) collective-permute-start(f32[3,6912]{1,0:T(4,128)S(1)} %get-tuple-element.271), channel_id=1, source_target_pairs={{0,2},{1,3},{2,0},{3,1},{4,6},{5,7},{6,4},{7,5},{8,10},{9,11},{10,... | collective-permute-start | bytes 248840 | tf_op jit(solution)/shard_map/ppermute | solution.py:60
  44.1 30.6 %collective-permute-start.13 = (bf16[144,1152]{1,0:T(8,128)(2,1)S(1)}, bf16[144,1152]{1,0:T(8,128)(2,1)S(1)}, u32[]{:S(2)}, u32[]{:S(2)}) collective-permute-start(bf16[144,1152]{1,0:T(8,128)(2,1)S(1)} %dynamic_slice.227), channel_id=1, source_target_pairs={{0,1},{1,2},{2,3},{3,0},{4,5},{5,6},{6,7},{7,4},{8,9},{9,10},{10,1... | collective-permute-start | bytes 995336 | tf_op jit(solution)/shard_map/ppermute | solution.py:60
  74.5 10.9 %collective-permute-start.8 = (bf16[144,1152]{1,0:T(8,128)(2,1)S(1)}, bf16[144,1152]{1,0:T(8,128)(2,1)S(1)}, u32[]{:S(2)}, u32[]{:S(2)}) collective-permute-start(bf16[144,1152]{1,0:T(8,128)(2,1)S(1)} %dynamic-slice_convert_fusion.2), channel_id=1, source_target_pairs={{0,3},{1,0},{2,1},{3,2},{4,7},{5,4},{6,5},{7,6},{8,11},{9,8},{10,9... | collective-permute-start | bytes 995336 | tf_op jit(solution)/shard_map/ppermute | solution.py:60
  74.6 49.9 %collective-permute-start.7 = (bf16[144,1152]{1,0:T(8,128)(2,1)S(1)}, bf16[144,1152]{1,0:T(8,128)(2,1)S(1)}, u32[]{:S(2)}, u32[]{:S(2)}) collective-permute-start(bf16[144,1152]{1,0:T(8,128)(2,1)S(1)} %dynamic-slice_convert_fusion.2), channel_id=1, source_target_pairs={{0,2},{1,3},{2,0},{3,1},{4,6},{5,7},{6,4},{7,5},{8,10},{9,11},{10,... | collective-permute-start | bytes 995336 | tf_op jit(solution)/shard_map/ppermute | solution.py:60
  74.7 57.1 %collective-permute-start.6 = (bf16[144,1152]{1,0:T(8,128)(2,1)S(1)}, bf16[144,1152]{1,0:T(8,128)(2,1)S(1)}, u32[]{:S(2)}, u32[]{:S(2)}) collective-permute-start(bf16[144,1152]{1,0:T(8,128)(2,1)S(1)} %dynamic-slice_convert_fusion.2), channel_id=1, source_target_pairs={{0,1},{1,2},{2,3},{3,0},{4,5},{5,6},{6,7},{7,4},{8,9},{9,10},{10,1... | collective-permute-start | bytes 995336 | tf_op jit(solution)/shard_map/ppermute | solution.py:60
  76.2 48.4 %collective-permute-start.14 = (bf16[2,144,1152]{2,1,0:T(8,128)(2,1)S(1)}, bf16[2,144,1152]{2,1,0:T(8,128)(2,1)S(1)}, u32[]{:S(2)}, u32[]{:S(2)}) collective-permute-start(bf16[2,144,1152]{2,1,0:T(8,128)(2,1)S(1)} %pad_maximum_fusion.12), channel_id=1, source_target_pairs={{0,16},{8,24},{16,0},{24,8},{1,17},{9,25},{17,1},{25,9},{2,18},{10... | collective-permute-start | bytes 1990664 | tf_op jit(solution)/shard_map/ppermute | solution.py:65
  82.9 45.4 %collective-permute-start.17 = (bf16[2,144,1152]{2,1,0:T(8,128)(2,1)S(1)}, bf16[2,144,1152]{2,1,0:T(8,128)(2,1)S(1)}, u32[]{:S(2)}, u32[]{:S(2)}) collective-permute-start(bf16[2,144,1152]{2,1,0:T(8,128)(2,1)S(1)} %pad_maximum_fusion.13), channel_id=1, source_target_pairs={{0,4},{4,0},{1,5},{5,1},{2,6},{6,2},{3,7},{7,3},{8,12},{12,8},{9,1... | collective-permute-start | bytes 1990664 | tf_op jit(solution)/shard_map/ppermute | solution.py:65
  125.8 51.9 %collective-permute-start.18 = (bf16[4,144,1152]{2,1,0:T(8,128)(2,1)}, bf16[4,144,1152]{2,1,0:T(8,128)(2,1)}, u32[]{:S(2)}, u32[]{:S(2)}) collective-permute-start(bf16[4,144,1152]{2,1,0:T(8,128)(2,1)} %pad_maximum_fusion.3.refs_0_), channel_id=1, source_target_pairs={{0,4},{4,0},{1,5},{5,1},{2,6},{6,2},{3,7},{7,3},{8,12},{12,8},{9,1... | collective-permute-start | bytes 3981320 | tf_op jit(solution)/shard_map/ppermute | solution.py:65
  129.5 48.3 %collective-permute-start.19 = (bf16[4,144,1152]{2,1,0:T(8,128)(2,1)}, bf16[4,144,1152]{2,1,0:T(8,128)(2,1)}, u32[]{:S(2)}, u32[]{:S(2)}) collective-permute-start(bf16[4,144,1152]{2,1,0:T(8,128)(2,1)} %pad_maximum_fusion.4.refs_1_), channel_id=1, source_target_pairs={{0,16},{8,24},{16,0},{24,8},{1,17},{9,25},{17,1},{25,9},{2,18},{10... | collective-permute-start | bytes 3981320 | tf_op jit(solution)/shard_map/ppermute | solution.py:65
  131.9 35.0 %collective-permute-start.9 = (bf16[2,144,1152]{2,1,0:T(8,128)(2,1)S(1)}, bf16[2,144,1152]{2,1,0:T(8,128)(2,1)S(1)}, u32[]{:S(2)}, u32[]{:S(2)}) collective-permute-start(bf16[2,144,1152]{2,1,0:T(8,128)(2,1)S(1)} %pad_maximum_fusion.10), channel_id=1, source_target_pairs={{0,16},{8,24},{16,0},{24,8},{1,17},{9,25},{17,1},{25,9},{2,18},{10... | collective-permute-start | bytes 1990664 | tf_op jit(solution)/shard_map/ppermute | solution.py:65
  132.0 44.5 %collective-permute-start.10 = (bf16[2,144,1152]{2,1,0:T(8,128)(2,1)S(1)}, bf16[2,144,1152]{2,1,0:T(8,128)(2,1)}, u32[]{:S(2)}, u32[]{:S(2)}) collective-permute-start(bf16[2,144,1152]{2,1,0:T(8,128)(2,1)S(1)} %pad_maximum_fusion.11), channel_id=1, source_target_pairs={{0,4},{4,0},{1,5},{5,1},{2,6},{6,2},{3,7},{7,3},{8,12},{12,8},{9,1... | collective-permute-start | bytes 1990664 | tf_op jit(solution)/shard_map/ppermute | solution.py:65
  133.3 75.5 %collective-permute-start.20 = (bf16[4,144,1152]{2,1,0:T(8,128)(2,1)}, bf16[4,144,1152]{2,1,0:T(8,128)(2,1)}, u32[]{:S(2)}, u32[]{:S(2)}) collective-permute-start(bf16[4,144,1152]{2,1,0:T(8,128)(2,1)} %pad_maximum_fusion.3.refs_0_), channel_id=1, source_target_pairs={{0,8},{8,0},{16,24},{24,16},{1,9},{9,1},{17,25},{25,17},{2,10},{10... | collective-permute-start | bytes 3981320 | tf_op jit(solution)/shard_map/ppermute | solution.py:65
  166.9 44.3 %collective-permute-start.21 = (bf16[4,144,1152]{2,1,0:T(8,128)(2,1)}, bf16[4,144,1152]{2,1,0:T(8,128)(2,1)}, u32[]{:S(2)}, u32[]{:S(2)}) collective-permute-start(bf16[4,144,1152]{2,1,0:T(8,128)(2,1)} %pad_maximum_fusion.4.refs_1_), channel_id=1, source_target_pairs={{0,8},{8,0},{16,24},{24,16},{1,9},{9,1},{17,25},{25,17},{2,10},{10... | collective-permute-start | bytes 3981320 | tf_op jit(solution)/shard_map/ppermute | solution.py:65
  177.7 33.5 %collective-permute-start.22 = (bf16[4,144,1152]{2,1,0:T(8,128)(2,1)}, bf16[4,144,1152]{2,1,0:T(8,128)(2,1)}, u32[]{:S(2)}, u32[]{:S(2)}) collective-permute-start(bf16[4,144,1152]{2,1,0:T(8,128)(2,1)} %collective-permute-done.18.refs_2_), channel_id=1, source_target_pairs={{0,8},{8,0},{16,24},{24,16},{1,9},{9,1},{17,25},{25,17},{2,10},{10... | collective-permute-start | bytes 3981320 | tf_op jit(solution)/shard_map/ppermute | solution.py:65
  177.8 33.4 %collective-permute-start.23 = (bf16[4,144,1152]{2,1,0:T(8,128)(2,1)}, bf16[4,144,1152]{2,1,0:T(8,128)(2,1)}, u32[]{:S(2)}, u32[]{:S(2)}) collective-permute-start(bf16[4,144,1152]{2,1,0:T(8,128)(2,1)} %collective-permute-done.19.refs_3_), channel_id=1, source_target_pairs={{0,8},{8,0},{16,24},{24,16},{1,9},{9,1},{17,25},{25,17},{2,10},{10... | collective-permute-start | bytes 3981320 | tf_op jit(solution)/shard_map/ppermute | solution.py:65
  208.5 33.0 %collective-permute-start.11 = (bf16[4,144,1152]{2,1,0:T(8,128)(2,1)S(1)}, bf16[4,144,1152]{2,1,0:T(8,128)(2,1)}, u32[]{:S(2)}, u32[]{:S(2)}) collective-permute-start(bf16[4,144,1152]{2,1,0:T(8,128)(2,1)S(1)} %pad_maximum_fusion.1.refs_0_), channel_id=1, source_target_pairs={{0,4},{4,0},{1,5},{5,1},{2,6},{6,2},{3,7},{7,3},{8,12},{12,8},{9,1... | collective-permute-start | bytes 3981320 | tf_op jit(solution)/shard_map/ppermute | solution.py:65
  208.8 32.7 %collective-permute-start.12 = (bf16[4,144,1152]{2,1,0:T(8,128)(2,1)S(1)}, bf16[4,144,1152]{2,1,0:T(8,128)(2,1)}, u32[]{:S(2)}, u32[]{:S(2)}) collective-permute-start(bf16[4,144,1152]{2,1,0:T(8,128)(2,1)S(1)} %pad_maximum_fusion.2.refs_1_), channel_id=1, source_target_pairs={{0,16},{8,24},{16,0},{24,8},{1,17},{9,25},{17,1},{25,9},{2,18},{10... | collective-permute-start | bytes 3981320 | tf_op jit(solution)/shard_map/ppermute | solution.py:65
  256.4 344.3 %reduce-scatter.6.cloned.1.call-start = ((), (), s32[]{:S(2)}) async-start(), calls=%async_computation.5 | async-start | bytes 6635520 | tf_op jit(solution)/shard_map/reduce_scatter | solution.py:695
  257.8 8.2 collective-permute-start.27
  312.1 159.0 %collective-permute-start.28 = (bf16[4,144,4608]{2,1,0:T(8,128)(2,1)}, bf16[4,144,4608]{2,1,0:T(8,128)(2,1)}, u32[]{:S(2)}, u32[]{:S(2)}) collective-permute-start(bf16[4,144,4608]{2,1,0:T(8,128)(2,1)} %dynamic-slice_bitcast_fusion), channel_id=1, source_target_pairs={{0,4},{4,0},{1,5},{5,1},{2,6},{6,2},{3,7},{7,3},{8,12},{12,8},{9,1... | collective-permute-start | bytes 15925256 | tf_op jit(solution)/shard_map/ppermute | solution.py:65
  486.3 306.4 %reduce-scatter.8.cloned.1.call-start = ((), (), s32[]{:S(2)}) async-start(), calls=%async_computation.6 | async-start | bytes 6635520 | tf_op jit(solution)/shard_map/reduce_scatter | solution.py:695
  486.3 114.3 %collective-permute-start.33 = (bf16[4,144,4608]{2,1,0:T(8,128)(2,1)}, bf16[4,144,4608]{2,1,0:T(8,128)(2,1)}, u32[]{:S(2)}, u32[]{:S(2)}) collective-permute-start(bf16[4,144,4608]{2,1,0:T(8,128)(2,1)} %pad_maximum_fusion), channel_id=1, source_target_pairs={{0,4},{4,0},{1,5},{5,1},{2,6},{6,2},{3,7},{7,3},{8,12},{12,8},{9,1... | collective-permute-start | bytes 15925256 | tf_op jit(solution)/shard_map/ppermute | solution.py:65
  487.5 9.9 %collective-permute-start.31 = (bf16[2,33408]{1,0:T(2,128)(2,1)S(1)}, bf16[2,33408]{1,0:T(2,128)(2,1)S(1)}, u32[]{:S(2)}, u32[]{:S(2)}) collective-permute-start(bf16[2,33408]{1,0:T(2,128)(2,1)S(1)} %get-tuple-element.238), channel_id=1, source_target_pairs={{0,2},{1,3},{2,0},{3,1},{4,6},{5,7},{6,4},{7,5},{8,10},{9,11},{10,... | collective-permute-start | bytes 400904 | tf_op jit(solution)/shard_map/ppermute | solution.py:60
  487.5 10.0 %collective-permute-start.32 = (bf16[2,33408]{1,0:T(2,128)(2,1)S(1)}, bf16[2,33408]{1,0:T(2,128)(2,1)S(1)}, u32[]{:S(2)}, u32[]{:S(2)}) collective-permute-start(bf16[2,33408]{1,0:T(2,128)(2,1)S(1)} %get-tuple-element.238), channel_id=1, source_target_pairs={{0,3},{1,0},{2,1},{3,2},{4,7},{5,4},{6,5},{7,6},{8,11},{9,8},{10,9... | collective-permute-start | bytes 400904 | tf_op jit(solution)/shard_map/ppermute | solution.py:60
  499.0 31.2 %collective-permute-start.52 = (bf16[4032]{0:T(1024)(128)(2,1)S(1)}, bf16[4032]{0:T(1024)(128)(2,1)S(1)}, u32[]{:S(2)}, u32[]{:S(2)}) collective-permute-start(bf16[4032]{0:T(1024)(128)(2,1)S(1)} %get-tuple-element.227), channel_id=1, source_target_pairs={{0,8},{8,0},{16,24},{24,16},{1,9},{9,1},{17,25},{25,17},{2,10},{10... | collective-permute-start | bytes 24200 | tf_op jit(solution)/shard_map/ppermute | solution.py:65
  530.3 94.1 %collective-permute-start.53 = (bf16[4032]{0:T(1024)(128)(2,1)S(1)}, bf16[4032]{0:T(1024)(128)(2,1)S(1)}, u32[]{:S(2)}, u32[]{:S(2)}) collective-permute-start(bf16[4032]{0:T(1024)(128)(2,1)S(1)} %add_convert_fusion.5), channel_id=1, source_target_pairs={{0,16},{8,24},{16,0},{24,8},{1,17},{9,25},{17,1},{25,9},{2,18},{10... | collective-permute-start | bytes 24200 | tf_op jit(solution)/shard_map/ppermute | solution.py:65
  614.5 12.0 %collective-permute-start.48 = (bf16[288,1152]{1,0:T(8,128)(2,1)}, bf16[288,1152]{1,0:T(8,128)(2,1)}, u32[]{:S(2)}, u32[]{:S(2)}) collective-permute-start(bf16[288,1152]{1,0:T(8,128)(2,1)} %dynamic-slice_bitcast_fusion.6), channel_id=1, source_target_pairs={{0,8},{8,0},{16,24},{24,16},{1,9},{9,1},{17,25},{25,17},{2,10},{10... | collective-permute-start | bytes 1990664 | tf_op jit(solution)/shard_map/ppermute | solution.py:65
  625.0 75.1 %collective-permute-start.37 = (bf16[144,4608]{1,0:T(8,128)(2,1)}, bf16[144,4608]{1,0:T(8,128)(2,1)}, u32[]{:S(2)}, u32[]{:S(2)}) collective-permute-start(bf16[144,4608]{1,0:T(8,128)(2,1)} %reduce-scatter.6.cloned.1.call-done), channel_id=1, source_target_pairs={{0,4},{4,0},{1,5},{5,1},{2,6},{6,2},{3,7},{7,3},{8,12},{12,8},{9,1... | collective-permute-start | bytes 3981320 | tf_op jit(solution)/shard_map/ppermute | solution.py:65
  626.1 57.8 %collective-permute-start.38 = (bf16[576,1152]{1,0:T(8,128)(2,1)S(1)}, bf16[576,1152]{1,0:T(8,128)(2,1)}, u32[]{:S(2)}, u32[]{:S(2)}) collective-permute-start(bf16[576,1152]{1,0:T(8,128)(2,1)S(1)} %copy-done.26), channel_id=1, source_target_pairs={{0,4},{4,0},{1,5},{5,1},{2,6},{6,2},{3,7},{7,3},{8,12},{12,8},{9,1... | collective-permute-start | bytes 3981320 | tf_op jit(solution)/shard_map/ppermute | solution.py:65
  627.9 15.5 %collective-permute-start.49 = (bf16[288,1152]{1,0:T(8,128)(2,1)S(1)}, bf16[288,1152]{1,0:T(8,128)(2,1)S(1)}, u32[]{:S(2)}, u32[]{:S(2)}) collective-permute-start(bf16[288,1152]{1,0:T(8,128)(2,1)S(1)} %fusion.48), channel_id=1, source_target_pairs={{0,16},{8,24},{16,0},{24,8},{1,17},{9,25},{17,1},{25,9},{2,18},{10... | collective-permute-start | bytes 1990664 | tf_op jit(solution)/shard_map/ppermute | solution.py:65
  629.6 28.1 %collective-permute-start.35 = (bf16[72,4608]{1,0:T(8,128)(2,1)S(1)}, bf16[72,4608]{1,0:T(8,128)(2,1)S(1)}, u32[]{:S(2)}, u32[]{:S(2)}) collective-permute-start(bf16[72,4608]{1,0:T(8,128)(2,1)S(1)} %fusion.50), channel_id=1, source_target_pairs={{0,16},{8,24},{16,0},{24,8},{1,17},{9,25},{17,1},{25,9},{2,18},{10... | collective-permute-start | bytes 1990664 | tf_op jit(solution)/shard_map/ppermute | solution.py:65
  632.5 89.6 %collective-permute-start.39 = (bf16[144,6912]{1,0:T(8,128)(2,1)}, bf16[144,6912]{1,0:T(8,128)(2,1)}, u32[]{:S(2)}, u32[]{:S(2)}) collective-permute-start(bf16[144,6912]{1,0:T(8,128)(2,1)} %dynamic-slice_bitcast_fusion.3), channel_id=1, source_target_pairs={{0,8},{8,0},{16,24},{24,16},{1,9},{9,1},{17,25},{25,17},{2,10},{10... | collective-permute-start | bytes 5971976 | tf_op jit(solution)/shard_map/ppermute | solution.py:65
  644.5 76.0 %collective-permute-start.50 = (bf16[288,1152]{1,0:T(8,128)(2,1)}, bf16[288,1152]{1,0:T(8,128)(2,1)}, u32[]{:S(2)}, u32[]{:S(2)}) collective-permute-start(bf16[288,1152]{1,0:T(8,128)(2,1)} %add_convert_fusion.2), channel_id=1, source_target_pairs={{0,4},{4,0},{1,5},{5,1},{2,6},{6,2},{3,7},{7,3},{8,12},{12,8},{9,1... | collective-permute-start | bytes 1990664 | tf_op jit(solution)/shard_map/ppermute | solution.py:65
  658.7 57.1 %collective-permute-start.46 = (bf16[72,4608]{1,0:T(8,128)(2,1)}, bf16[72,4608]{1,0:T(8,128)(2,1)}, u32[]{:S(2)}, u32[]{:S(2)}) collective-permute-start(bf16[72,4608]{1,0:T(8,128)(2,1)} %add_convert_fusion.4), channel_id=1, source_target_pairs={{0,4},{4,0},{1,5},{5,1},{2,6},{6,2},{3,7},{7,3},{8,12},{12,8},{9,1... | collective-permute-start | bytes 1990664 | tf_op jit(solution)/shard_map/ppermute | solution.py:65
  718.3 21.3 %collective-permute-start.47 = (bf16[2,72,4608]{2,1,0:T(8,128)(2,1)}, bf16[2,72,4608]{2,1,0:T(8,128)(2,1)}, u32[]{:S(2)}, u32[]{:S(2)}) collective-permute-start(bf16[2,72,4608]{2,1,0:T(8,128)(2,1)} %pad_maximum_fusion.7), channel_id=1, source_target_pairs={{0,8},{8,0},{16,24},{24,16},{1,9},{9,1},{17,25},{25,17},{2,10},{10... | collective-permute-start | bytes 3981320 | tf_op jit(solution)/shard_map/ppermute | solution.py:65
  724.4 44.4 %collective-permute-start.40 = (bf16[144,6912]{1,0:T(8,128)(2,1)S(1)}, bf16[144,6912]{1,0:T(8,128)(2,1)}, u32[]{:S(2)}, u32[]{:S(2)}) collective-permute-start(bf16[144,6912]{1,0:T(8,128)(2,1)S(1)} %fusion.7), channel_id=1, source_target_pairs={{0,16},{8,24},{16,0},{24,8},{1,17},{9,25},{17,1},{25,9},{2,18},{10... | collective-permute-start | bytes 5971976 | tf_op jit(solution)/shard_map/ppermute | solution.py:65
  772.1 16.1 %collective-permute-start.41 = (bf16[1,144,6912]{2,1,0:T(8,128)(2,1)}, bf16[1,144,6912]{2,1,0:T(8,128)(2,1)}, u32[]{:S(2)}, u32[]{:S(2)}) collective-permute-start(bf16[1,144,6912]{2,1,0:T(8,128)(2,1)} %fusion.42), channel_id=1, source_target_pairs={{0,8},{8,0},{16,24},{24,16},{1,9},{9,1},{17,25},{25,17},{2,10},{10... | collective-permute-start | bytes 5971976 | tf_op jit(solution)/shard_map/ppermute | solution.py:65
  801.9 31.1 %collective-permute-start.36 = (bf16[144,4608]{1,0:T(8,128)(2,1)}, bf16[144,4608]{1,0:T(8,128)(2,1)}, u32[]{:S(2)}, u32[]{:S(2)}) collective-permute-start(bf16[144,4608]{1,0:T(8,128)(2,1)} %reduce-scatter.8.cloned.1.call-done), channel_id=1, source_target_pairs={{0,4},{4,0},{1,5},{5,1},{2,6},{6,2},{3,7},{7,3},{8,12},{12,8},{9,1... | collective-permute-start | bytes 3981320 | tf_op jit(solution)/shard_map/ppermute | solution.py:65
  804.1 16.5 %collective-permute-start.43 = (bf16[72,4608]{1,0:T(8,128)(2,1)}, bf16[72,4608]{1,0:T(8,128)(2,1)}, u32[]{:S(2)}, u32[]{:S(2)}) collective-permute-start(bf16[72,4608]{1,0:T(8,128)(2,1)} %fusion.49), channel_id=1, source_target_pairs={{0,16},{8,24},{16,0},{24,8},{1,17},{9,25},{17,1},{25,9},{2,18},{10... | collective-permute-start | bytes 1990664 | tf_op jit(solution)/shard_map/ppermute | solution.py:65
  822.1 25.1 %collective-permute-start.44 = (bf16[72,4608]{1,0:T(8,128)(2,1)S(1)}, bf16[72,4608]{1,0:T(8,128)(2,1)S(1)}, u32[]{:S(2)}, u32[]{:S(2)}) collective-permute-start(bf16[72,4608]{1,0:T(8,128)(2,1)S(1)} %add_convert_fusion.3), channel_id=1, source_target_pairs={{0,4},{4,0},{1,5},{5,1},{2,6},{6,2},{3,7},{7,3},{8,12},{12,8},{9,1... | collective-permute-start | bytes 1990664 | tf_op jit(solution)/shard_map/ppermute | solution.py:65
  849.3 9.5 %collective-permute-start.45 = (bf16[2,72,4608]{2,1,0:T(8,128)(2,1)}, bf16[2,72,4608]{2,1,0:T(8,128)(2,1)}, u32[]{:S(2)}, u32[]{:S(2)}) collective-permute-start(bf16[2,72,4608]{2,1,0:T(8,128)(2,1)} %pad_maximum_fusion.6), channel_id=1, source_target_pairs={{0,8},{8,0},{16,24},{24,16},{1,9},{9,1},{17,25},{25,17},{2,10},{10... | collective-permute-start | bytes 3981320 | tf_op jit(solution)/shard_map/ppermute | solution.py:65
  (60 other events, 695.4 us)
Sparse Core Ops, SparseCore 0:
  12.0 136.3 all-gather.1
  256.5 211.3 reduce-scatter.3
  486.4 99.1 reduce-scatter.5
  626.6 95.3 reduce-scatter.7

commit v4 on v3

--- a/solution.py
+++ b/solution.py
@@ -212,12 +212,33 @@
     )(x, cot, mod, bias, weights)
 
 
+def one_spec(joint):
+    lines, rows, width = joint.shape[1], joint.shape[4], joint.shape[5]
+    return pl.BlockSpec((1, lines, 2, 1, rows, width), lambda u: (u, 0, 0, 0, 0, 0))
+
+
+def two_spec(joint):
+    groups, lines, _, _, rows, width = joint.shape
+    return pl.BlockSpec((groups, lines // groups, 2, 1, rows, width), lambda u: (0, u, 0, 1, 0, 0))
+
+
+def one_of(ref):
+    return ref[...].reshape(ref.shape[-1], ref.shape[-1])
+
+
+def two_of(ref):
+    value = ref[...]
+    if value.shape[1] > 1:
+        value = jnp.swapaxes(value, 0, 1)
+    return value.reshape(ref.shape[-1], ref.shape[-1])
+
+
 def hidden_kernel(mlp_in_ref, weight_ref, bias_ref, act_ref, slope_ref):
     step = 256
 
     def chunk(index, carry):
         here = pl.ds(pl.multiple_of(index * step, step), step)
-        hidden = dot(mlp_in_ref[here, :], weight_ref[0]) + bias_ref[0:1]
+        hidden = dot(mlp_in_ref[here, :], one_of(weight_ref)) + bias_ref[0:1]
         value, slope = gelu_pair(hidden)
         act_ref[here, :] = value.astype(BF16)
         slope_ref[here, :] = slope.astype(BF16)
@@ -233,7 +254,7 @@
     return pl.pallas_call(
         hidden_kernel,
         grid=(units,),
-        in_specs=[whole_spec((tokens, width)), lead_spec(width, width), pl.BlockSpec((1, width), lambda u: (0, u))],
+        in_specs=[whole_spec((tokens, width)), one_spec(weights), pl.BlockSpec((1, width), lambda u: (0, u))],
         out_specs=[column, column],
         out_shape=[jax.ShapeDtypeStruct((tokens, units * width), BF16)] * 2,
         compiler_params=params(48),
@@ -248,23 +269,23 @@
 
     def chunk(index, carry):
         here = pl.ds(pl.multiple_of(index * step, step), step)
-        d_hidden = dot_nt(d_mlp_ref[here, :], weight_ref[...]) * slope_ref[here, :].astype(F32)
+        d_hidden = dot_nt(d_mlp_ref[here, :], two_of(weight_ref)) * slope_ref[here, :].astype(F32)
         d_hidden = d_hidden.astype(BF16)
         d_hidden_ref[here, :] = d_hidden
         return carry + jnp.sum(d_hidden.astype(F32), axis=0, keepdims=True)
 
-    zero = jnp.zeros((1, weight_ref.shape[0]), F32)
+    zero = jnp.zeros((1, slope_ref.shape[1]), F32)
     sums_ref[0:1] = lax.fori_loop(0, d_mlp_ref.shape[0] // step, chunk, zero)
 
 
 def hidden_back(d_mlp, weights, slope):
     tokens, width = d_mlp.shape
-    units = weights.shape[0] // width
+    units = weights.shape[0]
     column = pl.BlockSpec((tokens, width), lambda u: (0, u))
     return pl.pallas_call(
         hidden_back_kernel,
         grid=(units,),
-        in_specs=[whole_spec((tokens, width)), rows_spec(width, width), column],
+        in_specs=[whole_spec((tokens, width)), two_spec(weights), column],
         out_specs=[column, pl.BlockSpec((8, width), lambda u: (0, u))],
         out_shape=[
             jax.ShapeDtypeStruct((tokens, units * width), BF16),
@@ -277,7 +298,7 @@
     )(d_mlp, weights, slope)
 
 
-def mlp_rest_kernel(act_ref, two_ref, d_hidden_ref, one_ref, mlp_ref, d_in_ref):
+def mlp_rest_kernel(act_ref, d_hidden_ref, two_ref, one_ref, mlp_ref, d_in_ref):
     step = 256
 
     @pl.when(pl.program_id(0) == 0)
@@ -287,29 +308,29 @@
 
     def chunk(index, carry):
         here = pl.ds(pl.multiple_of(index * step, step), step)
-        mlp_ref[here, :] += dot(act_ref[here, :], two_ref[...])
-        d_in_ref[here, :] += dot_nt(d_hidden_ref[here, :], one_ref[0])
+        mlp_ref[here, :] += dot(act_ref[here, :], two_of(two_ref))
+        d_in_ref[here, :] += dot_nt(d_hidden_ref[here, :], one_of(one_ref))
         return carry
 
     lax.fori_loop(0, act_ref.shape[0] // step, chunk, 0)
 
 
-def mlp_rest(act, two, d_hidden, one):
+def mlp_rest(act, d_hidden, weights):
     tokens = act.shape[0]
-    units, width = one.shape[:2]
+    units, width = weights.shape[0], weights.shape[-1]
     column = pl.BlockSpec((tokens, width), lambda u: (0, u))
     total = pl.BlockSpec((tokens, width), lambda u: (0, 0))
     return pl.pallas_call(
         mlp_rest_kernel,
         grid=(units,),
-        in_specs=[column, rows_spec(width, width), column, lead_spec(width, width)],
+        in_specs=[column, column, two_spec(weights), one_spec(weights)],
         out_specs=[total, total],
         out_shape=[jax.ShapeDtypeStruct((tokens, width), F32)] * 2,
         compiler_params=params(48),
         cost_estimate=pl.CostEstimate(
             flops=4 * tokens * width * width * units, bytes_accessed=42 << 20, transcendentals=0
         ),
-    )(act, two, d_hidden, one)
+    )(act, d_hidden, weights, weights)
 
 
 def middle_back_kernel(
@@ -631,33 +652,36 @@
 
     attention_cut = jnp.concatenate([rows_of(w_qkv), rows_of(w_proj)], axis=1)
     attention_cut = lax.dynamic_slice_in_dim(attention_cut, rep * width, width, axis=1)
-    w_attn = lax.all_gather(attention_cut, everyone, axis=0, tiled=True).reshape(4, width, width)
+    hops = lines == 4 and groups == 4
+    one_cut = lax.dynamic_slice(w_fc1, (pair * half, rep * width), (half, width))
+    eighth = rows_two // (2 * groups)
+    two_cut = lax.dynamic_slice_in_dim(w_fc2, (rep * 2 + pair) * eighth, eighth, axis=0)
+    mlp_cut = jnp.concatenate([one_cut, two_cut]).astype(BF16)
+    w_mlp = lax.all_gather(mlp_cut, everyone, axis=0, tiled=True)
+    w_mlp = w_mlp.reshape(groups, lines, 2, 2, half, width)
     live = (jnp.arange(slots) < counts[0]).astype(F32)
     condition = time_embed(timesteps, D) + jnp.take(label_table, labels, axis=0).astype(F32)
     style = jax.nn.silu(condition).astype(BF16)
-    one_cut = lax.dynamic_slice(w_fc1, (pair * half, rep * width), (half, width)).astype(BF16)
-    one_cut, style = after(one_cut, style)
-    hops = lines == 4 and groups == 4
-    if hops:
-        w_one = hops_place(hops_core(hops_other(*hops_side(*hops_line(one_cut)))), (2, 8, 1))
-    else:
-        w_one = lax.all_gather(one_cut, everyone, axis=0, tiled=True)
-    w_one = w_one.reshape(FF // width, width, width)
     message = jnp.concatenate([style.reshape(-1), biases.astype(BF16)])
     heard = gather_line(message, "fsdp")
+    if hops:
+        attention_cut, message = after(attention_cut, message)
+        attention_parts = hops_line(attention_cut)
+        heard = after(heard, *attention_parts)[0]
+        attention_parts = hops_side(*attention_parts)
+    else:
+        w_attn = lax.all_gather(attention_cut, everyone, axis=0, tiled=True)
     bias_all = heard[:, slots * width :].reshape(-1).astype(F32)
     style_line = heard[:, : slots * width].reshape(lines * slots, width)
     style_cut = lax.dynamic_slice_in_dim(style_line, line * rows, rows, axis=1)
     mod_part = dot(style_cut, w_ada.astype(BF16))
+    if hops:
+        attention_parts = hops_other(*attention_parts)
+        attention_parts = after(*attention_parts, mod_part)[:-1]
+        w_attn = hops_place(hops_core(attention_parts), (2, 8, 1))
+    w_attn = w_attn.reshape(4, width, width)
     b_ada = bias_all[: 6 * width]
     modulation = scatter_line(mod_part.reshape(lines, slots, 6 * width), "fsdp") + b_ada
-    eighth = rows_two // (2 * groups)
-    two_cut = lax.dynamic_slice_in_dim(w_fc2, (rep * 2 + pair) * eighth, eighth, axis=0).astype(BF16)
-    two_cut, modulation = after(two_cut, modulation)
-    if hops:
-        parts = hops_line(two_cut)
-    else:
-        w_two = lax.all_gather(two_cut, ("fsdp", "rep", "dp"), axis=0, tiled=True)
     mod = jnp.concatenate(
         [
             modulation.reshape(slots, 6, width),
@@ -673,19 +697,10 @@
     x = images.reshape(tokens, width)
     cot = cotangent.reshape(tokens, width)
 
-    if hops:
-        *parts, mod = after(*parts, mod)
-        parts = hops_side(*parts)
     attn_in, packed, attended, log_total, attn_out, middle, mlp_in, d_mlp, mlp_sums = attention_forward(
         x, cot, mod, bias, w_attn, slots, length, width
     )
-    if hops:
-        *parts, mlp_in = after(*parts, mlp_in)
-        parts = hops_other(*parts)
-    activated, slope = hidden_forward(mlp_in, w_one, b_fc1)
-    if hops:
-        *parts, activated = after(*parts, activated)
-        parts = hops_core(parts)
+    activated, slope = hidden_forward(mlp_in, w_mlp, b_fc1)
     grad_two = grad_rows(activated, d_mlp)
 
     def halves(gradient):
@@ -699,16 +714,14 @@
     def pair_sum(gradient, there):
         return (own_half(halves(gradient), pair).astype(F32) + there.astype(F32)).astype(BF16)
 
-    if hops:
-        w_two = hops_place(parts, (8, 2, 1)).reshape(FF, width)
     grad_two, d_mlp = after(grad_two, d_mlp)
-    two_half = lax.psum_scatter(grad_two, ("fsdp", "dp"), scatter_dimension=0, tiled=True)
-    d_hidden, hidden_sums = hidden_back(d_mlp, w_two, slope)
+    two_line = line_sum(grad_two)
+    d_hidden, hidden_sums = hidden_back(d_mlp, w_mlp, slope)
     grad_one = grad_columns(mlp_in, d_hidden)
     give_one = own_half(halves(grad_one), 1 - pair)
     give_one, d_hidden = after(give_one, d_hidden)
     there_one = swap_with(give_one, "dp", 1)
-    mlp_out, d_mlp_in = mlp_rest(activated, w_two, d_hidden, w_one)
+    mlp_out, d_mlp_in = mlp_rest(activated, d_hidden, w_mlp)
     result, d_middle, d_attn, d_attended, middle_rows = middle_back(
         mlp_out, bias, d_mlp_in, middle, attn_out, cot, mod, w_attn, slots, length, width
     )
@@ -716,16 +729,18 @@
     grad_proj, d_attended = after(grad_proj, d_attended)
     d_packed, packed_sums = attention_back(packed, d_attended, log_total, slots, length, width)
     grad_qkv = grad_columns(attn_in, d_packed)
-    give_attn = jnp.concatenate(
-        [own_half(halves(grad_qkv), 1 - pair), own_half(halves(grad_proj), 1 - pair)], axis=2
-    )
-    give_attn, d_packed = after(give_attn, d_packed)
+    give_attn = own_half(halves(grad_qkv), 1 - pair)
+    give_proj = own_half(halves(grad_proj), 1 - pair)
+    give_attn, give_proj, d_packed = after(give_attn, give_proj, d_packed)
+    there_proj = swap_with(give_proj, "dp", 1)
     in_grad, input_rows = input_back(d_packed, w_attn, x, d_middle, mod, slots, length, width)
 
-    two_half, there_one, give_attn, input_rows = after(two_half, there_one, give_attn, input_rows)
+    there_one, give_attn, in_grad, input_rows = after(there_one, give_attn, in_grad, input_rows)
     there_attn = swap_with(give_attn, "dp", 1)
-    one_both, input_rows = after(pair_sum(grad_one, there_one), input_rows)
+    one_both = pair_sum(grad_one, there_one)
     one_half = line_sum(one_both)
+    two_line, one_both, there_proj, input_rows = after(two_line, one_both, there_proj, input_rows)
+
     d_modulation = jnp.concatenate([input_rows[:, :2], middle_rows[:, 2:6]], axis=1).astype(BF16)
     packed_total = jnp.sum(packed_sums, axis=0)
     bias_sums = jnp.concatenate(
@@ -760,9 +775,6 @@
         second = jnp.where(pair == 0, other, own)
         return jnp.concatenate([first, second], axis=0)
 
-    def both_halves(piece):
-        return two_rows(piece, swap_with(piece, "dp", 1)).astype(F32)
-
     power = step_count[0].astype(F32)
     fix_one = 1.0 - jnp.power(BETA_ONE, power)
     fix_two = 1.0 - jnp.power(BETA_TWO, power)
@@ -789,15 +801,20 @@
 
     low = rep % 2
 
+    def sum_near(mine):
+        mine = mine.reshape(2, mine.shape[0] // 2, mine.shape[1])
+        keep = lax.dynamic_index_in_dim(mine, low, 0, keepdims=False)
+        give = lax.dynamic_index_in_dim(mine, 1 - low, 0, keepdims=False)
+        return (keep.astype(F32) + swap_with(give, "rep", 1).astype(F32)).astype(BF16)
+
+    def sum_far(total):
+        return (total.astype(F32) + swap_with(total, "rep", 2).astype(F32)).astype(BF16)
+
     def sum_rep(mine):
         if mine.ndim == 1:
             total = (mine.astype(F32) + swap_with(mine, "rep", 1).astype(F32)).astype(BF16)
             return total.astype(F32) + swap_with(total, "rep", 2).astype(F32)
-        mine = mine.reshape(2, mine.shape[0] // 2, mine.shape[1])
-        keep = lax.dynamic_index_in_dim(mine, low, 0, keepdims=False)
-        give = lax.dynamic_index_in_dim(mine, 1 - low, 0, keepdims=False)
-        total = (keep.astype(F32) + swap_with(give, "rep", 1).astype(F32)).astype(BF16)
-        return (total.astype(F32) + swap_with(total, "rep", 2).astype(F32)).astype(BF16)
+        return sum_far(sum_near(mine))
 
     def join_cores(total):
         other = swap_with(total, "rep", 1)
@@ -818,11 +835,13 @@
             own_rows(master), own_rows(first), own_rows(second), own_gradient.astype(F32), rates[index]
         )
 
-    def finish(index, gradient, summed):
+    def keep_moments(index, gradient):
         reduced[index] = gradient
         first_next, second_next = moments_next(firsts[index][0], seconds[index][0], gradient)
         firsts_out[index] = first_next[None]
         seconds_out[index] = second_next[None]
+
+    def outer_step(index, summed):
         delta = summed / groups
         outer_next = OUTER_MOMENTUM * outers[index] + delta
         deltas_out[index] = delta
@@ -830,32 +849,45 @@
         weights_out[index] = masters[index] - OUTER_RATE * (delta + OUTER_MOMENTUM * outer_next)
 
     ada_delta = local_delta(w_ada, first_ada[0], second_ada[0], grad_ada, rates[0])
-    one_half, there_attn, two_half, ada_delta = after(one_half, there_attn, two_half, ada_delta)
+    one_half, there_attn, two_line, ada_delta, grad_bias = after(
+        one_half, there_attn, two_line, ada_delta, grad_bias
+    )
     attn_both = jnp.concatenate(
-        [own_half(halves(grad_qkv), pair), own_half(halves(grad_proj), pair)], axis=2
-    )
-    attn_both = (attn_both.astype(F32) + there_attn.astype(F32)).astype(BF16)
-    attn_both, two_half, one_half, ada_delta = after(attn_both, two_half, one_half, ada_delta)
+        [pair_sum(grad_qkv, there_attn), pair_sum(grad_proj, there_proj)], axis=2
+    )
+    attn_both, two_line, one_half, ada_delta = after(attn_both, two_line, one_half, ada_delta)
     attn_half = line_sum(attn_both)
-    finish(0, grad_ada, join_cores(sum_rep(ada_delta)[None]))
+    two_there = swap_with(two_line, "dp", 1)
+    ada_total = sum_rep(ada_delta)
+    one_total = sum_rep(own_delta(3, one_half))
+    one_other = swap_with(one_total, "dp", 1)
+    two_there, one_other, one_half = after(two_there, one_other, one_half)
+    one_there = swap_with(one_half, "dp", 1)
+    grad_two = two_line.astype(F32) + two_there.astype(F32)
+    two_delta = local_delta(w_fc2, first_fc2[0], second_fc2[0], grad_two, rates[4])
     bias_delta = local_delta(biases, first_bias[0], second_bias[0], grad_bias, rates[5])
-    finish(5, grad_bias, sum_rep(bias_delta))
-    two_total = sum_rep(own_delta(4, two_half))
-    finish(4, both_halves(two_half), join_pair(two_total))
-    one_total = sum_rep(own_delta(3, one_half))
-    finish(3, both_halves(one_half), join_pair(one_total))
-    attn_half, one_total = after(attn_half, one_total)
+    bias_total = sum_rep(bias_delta)
+    keep_moments(0, grad_ada)
+    keep_moments(5, grad_bias)
+    keep_moments(4, grad_two)
+    outer_step(5, bias_total)
+    attn_half, one_other, ada_total, two_delta = after(attn_half, one_other, ada_total, two_delta)
+    two_total = sum_rep(two_delta)
+    outer_step(0, join_cores(ada_total[None]))
+    keep_moments(3, two_rows(one_half, one_there).astype(F32))
     edge = 3 * width
-    summed = join_pair(
-        sum_rep(
-            jnp.concatenate(
-                [own_delta(1, attn_half[:, :edge]), own_delta(2, attn_half[:, edge:])], axis=1
-            )
-        )
-    )
-    attn_full = both_halves(attn_half)
-    finish(1, attn_full[:, :edge], summed[:, :edge])
-    finish(2, attn_full[:, edge:], summed[:, edge:])
+    attn_total = sum_rep(
+        jnp.concatenate([own_delta(1, attn_half[:, :edge]), own_delta(2, attn_half[:, edge:])], axis=1)
+    )
+    attn_there = swap_with(attn_half, "dp", 1)
+    outer_step(4, join_cores(two_total[None]))
+    outer_step(3, join_cores(two_rows(one_total[None], one_other[None])))
+    attn_full = two_rows(attn_half, attn_there).astype(F32)
+    keep_moments(1, attn_full[:, :edge])
+    keep_moments(2, attn_full[:, edge:])
+    summed = join_pair(attn_total)
+    outer_step(1, summed[:, :edge])
+    outer_step(2, summed[:, edge:])
     grads_out = tuple((gradient[None] for gradient in reduced))
     return (
         (result.reshape(images.shape), in_grad.reshape(images.shape))

time: 892 us -> 787 us (0.88)
  waiting for transfers between devices: 330 us -> 291 us
  starting transfers between devices: 92.5 us -> 55.1 us
  other arithmetic: 186 us -> 169 us
    ppermute x15 -> x12, waiting for transfers between devices: 74.2 us -> 38 us  [shift_by(): lax.ppermute(value, axis, [(i, (i + step) % size) for i in range(size)])]
    ppermute x39 -> x31, starting transfers between devices: 62.3 us -> 26.9 us  [swap_with(): return lax.ppermute(value, axis, [(i, i ^ bit) for i in range(size)])]
    ppermute x39 -> x31, waiting for transfers between devices: 256 us -> 227 us  [swap_with(): return lax.ppermute(value, axis, [(i, i ^ bit) for i in range(size)])]
    reduce_scatter x2 -> x3, waiting for transfers between devices: 0.01 us -> 15.1 us  [line_sum(): lax.psum_scatter(both.reshape(-1, both.shape[-1]), 'fsdp', scatter_dimens...]
    broadcast_in_dim x5 -> x6, other arithmetic: 38.5 us -> 50.8 us  [the longest x4 47.4 us: keep_moments(): seconds_out[index] = second_next[None]]
    all_gather x1, waiting for transfers between devices: 0.01 us -> 11.6 us  [body(): w_mlp = lax.all_gather(mlp_cut, everyone, axis=0, tiled=True)]
    pallas_call x2 -> x1, Pallas kernels: 17.9 us -> 9.11 us  [place_blocks(): pl.pallas_call(place_kernel, grid_spec=pltpu.PrefetchScalarGridSpec(num_s...]
    convert_element_type x5 -> x4, other arithmetic: 18.7 us -> 12.7 us  [local_delta(): return (master - local).astype(BF16)]
  transfers between devices with their start and end apart: 58 -> 47, of which waited for: 22 -> 23; matrix products, arithmetic and copies ran while one was open for 21% -> 22% of each run, Pallas kernels for 21% -> 21%
where the time goes in v4:
time: 787 us; the launch traced here: 781 us
  waiting for transfers between devices  291 us (37%)
  Pallas kernels  197 us (25%)
  other arithmetic  169 us (21%)
  starting transfers between devices  55.1 us (7%)
  local copies, waits for them, and re-layouts  45.8 us (6%)
  between operations  16.6 us (2%)
    ppermute x31, waiting for transfers between devices, swap_with(): return lax.ppermute(value, axis, [(i, i ^ bit) for i in range(size)])  227 us
    broadcast_in_dim x4, other arithmetic, keep_moments(): seconds_out[index] = second_next[None]  47.4 us
    sub x5, other arithmetic, outer_step(): masters[index] - OUTER_RATE * (delta + OUTER_MOMENTUM * outer_next)  43.8 us
    ppermute x12, waiting for transfers between devices, shift_by(): lax.ppermute(value, axis, [(i, (i + step) % size) for i in range(size)])  38 us
    pallas_call x3, Pallas kernels, grad_columns(): pl.pallas_call(grad_kernel, grid=(width // rows,), in_specs=[whole_spec((...  29.6 us
    pallas_call x1, Pallas kernels, mlp_rest(): pl.pallas_call(mlp_rest_kernel, grid=(units,), in_specs=[column, column,...  28.4 us
    ppermute x12, starting transfers between devices, shift_by(): lax.ppermute(value, axis, [(i, (i + step) % size) for i in range(size)])  27.8 us
    ppermute x31, starting transfers between devices, swap_with(): return lax.ppermute(value, axis, [(i, i ^ bit) for i in range(size)])  26.9 us
  transfers between devices with their start and end apart: 47, of which 23 were waited for; matrix products, arithmetic and copies ran while one was open for 22% of the time, Pallas kernels for 21%

profile of v4, /device:TPU:1, one launch (start us, length us, event | category | flops | bytes accessed | tf_op | source)
XLA Modules:
  0.0 780.8 jit_solution(3858838920810658487)
XLA Ops:
  14.6 4.2 collective-permute-start.5
  23.3 17.4 %collective-permute-done = bf16[7488]{0:T(1024)(128)(2,1)S(1)} collective-permute-done((bf16[7488]{0:T(1024)(128)(2,1)S(1)}, bf16[7488]{0:T(1024)(128)(2,1)S(1)}, u32[]{:S(2)}, u32[]{:S(2)}) %collective-permute-start) | collective-permute-done | bytes 15008 | tf_op jit(solution)/shard_map/ppermute | solution.py:60
  40.7 12.8 %collective-permute-start.3 = (bf16[144,1152]{1,0:T(8,128)(2,1)S(1)}, bf16[144,1152]{1,0:T(8,128)(2,1)S(1)}, u32[]{:S(2)}, u32[]{:S(2)}) collective-permute-start(bf16[144,1152]{1,0:T(8,128)(2,1)S(1)} %fusion.57), channel_id=1, source_target_pairs={{0,1},{1,2},{2,3},{3,0},{4,5},{5,6},{6,7},{7,4},{8,9},{9,10},{10,1... | collective-permute-start | bytes 995336 | tf_op jit(solution)/shard_map/ppermute | solution.py:60
  54.4 7.1 collective-permute-done.1
  65.1 25.0 %collective-permute-done.9 = bf16[2,144,1152]{2,1,0:T(8,128)(2,1)} collective-permute-done((bf16[2,144,1152]{2,1,0:T(8,128)(2,1)S(1)}, bf16[2,144,1152]{2,1,0:T(8,128)(2,1)}, u32[]{:S(2)}, u32[]{:S(2)}) %collective-permute-start.9) | collective-permute-done | bytes 663584 | tf_op jit(solution)/shard_map/ppermute | solution.py:65
  95.1 4.8 fusion.12
  101.8 3.3 collective-permute-start.8
  106.1 10.7 %collective-permute-done.11.refs_2_ = bf16[4,144,1152]{2,1,0:T(8,128)(2,1)} collective-permute-done((bf16[4,144,1152]{2,1,0:T(8,128)(2,1)S(1)}, bf16[4,144,1152]{2,1,0:T(8,128)(2,1)}, u32[]{:S(2)}, u32[]{:S(2)}) %collective-permute-start.11) | collective-permute-done | bytes 1327136 | tf_op jit(solution)/shard_map/ppermute | solution.py:65
  116.8 9.0 %collective-permute-done.12.refs_3_ = bf16[4,144,1152]{2,1,0:T(8,128)(2,1)} collective-permute-done((bf16[4,144,1152]{2,1,0:T(8,128)(2,1)S(1)}, bf16[4,144,1152]{2,1,0:T(8,128)(2,1)}, u32[]{:S(2)}, u32[]{:S(2)}) %collective-permute-start.12) | collective-permute-done | bytes 1327136 | tf_op jit(solution)/shard_map/ppermute | solution.py:65
  130.4 4.6 collective-permute-done.13.refs_4_
  135.0 5.7 collective-permute-done.14.refs_5_
  141.4 9.1 %shard_map.590 = bf16[32,144,1152]{2,1,0:T(8,128)(2,1)} custom-call(s32[32]{0:T(128)S(1)} %stack.200.order_ref, bf16[4,144,1152]{2,1,0:T(8,128)(2,1)S(1)} %pad_maximum_fusion.1.refs_0_, bf16[4,144,1152]{2,1,0:T(8,128)(2,1)S(1)} %pad_maximum_fusion.2.refs_1_, bf16[4,144,1152]{2,1,0:T(8,128)(2,1)} %collective-permute-done.11.refs_2_, ...), custom_call_target="tpu_custom_call" | custom-call | bytes 21233664 | tf_op jit(solution)/shard_map/pallas_call | solution.py:538
  150.5 26.6 %shard_map.591 = (bf16[768,1152]{1,0:T(8,128)(2,1)S(1)}, bf16[768,3456]{1,0:T(8,128)(2,1)}, bf16[768,1152]{1,0:T(8,128)(2,1)S(1)}, f32[768,128]{1,0:T(8,128)S(1)...) custom-call(bf16[768,1152]{1,0:T(8,128)(2,1)} %bitcast.245, ...), custom_call_target="tpu_custom_call" | custom-call | flops 8153726976 | bytes 41943040 | tf_op jit(solution)/shard_map/pallas_call | solution.py:188
  180.7 11.6 %all-gather.2.cloned.1.call-done = bf16[9216,1152]{1,0:T(8,128)(2,1)} async-done(((bf16[288,1152]{1,0:T(8,128)(2,1)}), bf16[9216,1152]{1,0:T(8,128)(2,1)}) %all-gather.2.cloned.1.call-update) | async-done | bytes 21233680 | tf_op jit(solution)/shard_map/all_gather | solution.py:660
  193.8 21.3 %shard_map.592 = (bf16[768,4608]{1,0:T(8,128)(2,1)}, bf16[768,4608]{1,0:T(8,128)(2,1)}) custom-call(bf16[768,1152]{1,0:T(8,128)(2,1)S(1)} %copy-done.10, bf16[4,4,2,2,144,1152]{5,4,3,2,1,0:T(8,128)(2,1)} %bitcast.288, f32[1,4608]{1,0:T(1,128)S(1)} %reshape.433.bias_ref), custom_call_target="tpu_custom_call" | custom-call | flops 8153726976 | bytes 27262976 | tf_op jit(solution)/shard_map/pallas_call | solution.py:254
  215.1 14.9 %shard_map.593 = bf16[4608,1152]{1,0:T(8,128)(2,1)} custom-call(bf16[768,4608]{1,0:T(8,128)(2,1)} %get-tuple-element.155.left_ref.act_ref, bf16[768,1152]{1,0:T(8,128)(2,1)S(1)} %copy-done.6), custom_call_target="tpu_custom_call" | custom-call | flops 8153726976 | bytes 24772608 | tf_op jit(solution)/shard_map/pallas_call | solution.py:499
  230.2 16.7 %shard_map.594 = (bf16[768,4608]{1,0:T(8,128)(2,1)}, f32[8,4608]{1,0:T(8,128)S(1)}) custom-call(bf16[768,1152]{1,0:T(8,128)(2,1)S(1)} %copy-done.6, bf16[4,4,2,2,144,1152]{5,4,3,2,1,0:T(8,128)(2,1)} %bitcast.289, bf16[768,4608]{1,0:T(8,128)(2,1)} %get-tuple-element.158.slope_ref), custom_call_target="tpu_custom_call" | custom-call | flops 8153726976 | bytes 27262976 | tf_op jit(solution)/shard_map/pallas_call | solution.py:285
  246.9 14.9 %shard_map.595 = bf16[1152,4608]{1,0:T(8,128)(2,1)} custom-call(bf16[768,1152]{1,0:T(8,128)(2,1)S(1)} %copy-done.11, bf16[768,4608]{1,0:T(8,128)(2,1)} %get-tuple-element.160.right_ref.d_hidden_ref), custom_call_target="tpu_custom_call" | custom-call | flops 8153726976 | bytes 24772608 | tf_op jit(solution)/shard_map/pallas_call | solution.py:483
  261.7 5.2 dynamic-slice_bitcast_fusion
  270.3 28.4 %shard_map.596 = (f32[768,1152]{1,0:T(8,128)S(1)}, f32[768,1152]{1,0:T(8,128)}) custom-call(bf16[768,4608]{1,0:T(8,128)(2,1)} %get-tuple-element.155.left_ref.act_ref, bf16[768,4608]{1,0:T(8,128)(2,1)} %get-tuple-element.160.right_ref.d_hidden_ref, bf16[4,4,2,2,144,1152]{5,4,3,2,1,0:T(8,128)(2,1)} %bitcast.290, bf16[4,4,2,2,144,1152]{5,4,3,2,1,0:T(8,128)(2,1)} %bitcast.291), custom_call_target="tpu_custom_call" | custom-call | flops 16307453952 | bytes 44040192 | tf_op jit(solution)/shard_map/pallas_call | solution.py:323
  300.5 12.6 %shard_map.597 = (bf16[768,1152]{1,0:T(8,128)(2,1)}, f32[768,1152]{1,0:T(8,128)}, bf16[768,1152]{1,0:T(8,128)(2,1)S(1)}, bf16[768,1152]{1,0:T(8,128)(2,1)S(1)}, f32[3,8,1152]{2,1,0:T(8,128)S(1)}) custom-call(f32[768,1152]{1,0:T(8,128)} %copy-done.2, f32[8,1152]{1,0:T(8,128)S(1)} %scatter.19.bias_ref, f32[768,1152]{1,0:T(8,128)} %get-tuple-element.162.d_in_ref, ...), custom_call_target="tpu_custom_call" | custom-call | flops 2038431744 | bytes 31457280 | tf_op jit(solution)/shard_map/pallas_call | solution.py:364
  316.7 23.4 %shard_map.599 = (bf16[768,3456]{1,0:T(8,128)(2,1)}, f32[3,8,1152]{2,1,0:T(8,128)S(1)}) custom-call(bf16[768,3456]{1,0:T(8,128)(2,1)} %get-tuple-element.168.packed_ref, bf16[768,1152]{1,0:T(8,128)(2,1)S(1)} %get-tuple-element.172.d_att_ref, f32[768,128]{1,0:T(8,128)S(1)} %get-tuple-element.173.log_ref), custom_call_target="tpu_custom_call" | custom-call | flops 8053063680 | bytes 14680064 | tf_op jit(solution)/shard_map/pallas_call | solution.py:419
  341.6 11.8 %shard_map.600 = bf16[1152,3456]{1,0:T(8,128)(2,1)} custom-call(bf16[768,1152]{1,0:T(8,128)(2,1)S(1)} %copy-done.13, bf16[768,3456]{1,0:T(8,128)(2,1)} %get-tuple-element.177.right_ref.d_packed_ref), custom_call_target="tpu_custom_call" | custom-call | flops 6115295232 | bytes 18579456 | tf_op jit(solution)/shard_map/pallas_call | solution.py:483
  353.4 4.5 dynamic-slice_bitcast_fusion.1
  358.3 14.0 %shard_map.601 = (bf16[768,1152]{1,0:T(8,128)(2,1)}, f32[3,8,1152]{2,1,0:T(8,128)S(1)}) custom-call(bf16[768,3456]{1,0:T(8,128)(2,1)} %get-tuple-element.177.right_ref.d_packed_ref, bf16[4,1152,1152]{2,1,0:T(8,128)(2,1)} %bitcast.252, bf16[768,1152]{1,0:T(8,128)(2,1)S(1)} %bitcast.246, f32[768,1152]{1,0:T(8,128)S(1)} %copy-done.4, ...), custom_call_target="tpu_custom_call" | custom-call | flops 6115295232 | bytes 20971520 | tf_op jit(solution)/shard_map/pallas_call | solution.py:451
  372.3 10.8 %collective-permute-done.17 = bf16[4,144,4608]{2,1,0:T(8,128)(2,1)} collective-permute-done((bf16[4,144,4608]{2,1,0:T(8,128)(2,1)}, bf16[4,144,4608]{2,1,0:T(8,128)(2,1)}, u32[]{:S(2)}, u32[]{:S(2)}) %collective-permute-start.17) | collective-permute-done | bytes 5308448 | tf_op jit(solution)/shard_map/ppermute | solution.py:65
  383.1 7.9 %fusion = bf16[4,144,4608]{2,1,0:T(8,128)(2,1)} fusion(bf16[4,144,4608]{2,1,0:T(8,128)(2,1)} %collective-permute-done.17, bf16[4,2,144,4608]{3,2,1,0:T(8,128)(2,1)} %bitcast.267, s32[]{:T(128)S(6)} %select_n.259), kind=kLoop, calls=%fused_computation.4 | loop fusion | flops 10616832 | bytes 15925252 | tf_op jit(solution)/shard_map/convert_element_type | solution.py:715
  391.0 20.5 %collective-permute-done.18 = bf16[4,144,1152]{2,1,0:T(8,128)(2,1)} collective-permute-done((bf16[4,144,1152]{2,1,0:T(8,128)(2,1)S(1)}, bf16[4,144,1152]{2,1,0:T(8,128)(2,1)}, u32[]{:S(2)}, u32[]{:S(2)}) %collective-permute-start.18) | collective-permute-done | bytes 1327136 | tf_op jit(solution)/shard_map/ppermute | solution.py:65
  424.5 12.9 %collective-permute-done.21 = bf16[2,33408]{1,0:T(2,128)(2,1)S(1)} collective-permute-done((bf16[2,33408]{1,0:T(2,128)(2,1)S(1)}, bf16[2,33408]{1,0:T(2,128)(2,1)S(1)}, u32[]{:S(2)}, u32[]{:S(2)}) %collective-permute-start.21) | collective-permute-done | bytes 133664 | tf_op jit(solution)/shard_map/ppermute | solution.py:60
  440.4 22.5 %fusion.27 = (f32[1,288,6912]{2,1,0:T(8,128)}, bf16[288,6912]{1,0:T(8,128)(2,1)}, f32[1,288,6912]{2,1,0:T(8,128)}) fusion(f32[288,6912]{1,0:T(8,128)S(1)} %fusion.62, f32[1,288,6912]{2,1,0:T(8,128)} %param.58, f32[288,6912]{1,0:T(8,128)} %param.46, f32[]{:T(128)} %bitcast.64, f32[]{:T(128)} %bitcast.62, f32[1,288,6912]{2,1,0:T(8,128)} %param.52), kind=kLoop, calls=%fused_computation.75 | loop fusion | flops 33841152 | bytes 51757064 | tf_op jit(solution)/shard_map/broadcast_in_dim | solution.py:842
  462.9 40.1 %collective-permute-done.23 = bf16[4,144,3456]{2,1,0:T(8,128)(2,1)} collective-permute-done((bf16[4,144,3456]{2,1,0:T(8,128)(2,1)}, bf16[4,144,3456]{2,1,0:T(8,128)(2,1)}, u32[]{:S(2)}, u32[]{:S(2)}) %collective-permute-start.23) | collective-permute-done | bytes 3981344 | tf_op jit(solution)/shard_map/ppermute | solution.py:65
  503.0 15.0 %reduce-scatter.6.cloned.1.call-done = bf16[144,4608]{1,0:T(8,128)(2,1)} async-done(((bf16[576,4608]{1,0:T(8,128)(2,1)}), bf16[144,4608]{1,0:T(8,128)(2,1)}) %reduce-scatter.6.cloned.1.call-update) | async-done | bytes 1327120 | tf_op jit(solution)/shard_map/reduce_scatter | solution.py:710
  518.0 4.4 fusion.3
  525.2 5.7 fusion.25
  538.6 11.1 %collective-permute-done.42 = bf16[4032]{0:T(1024)(128)(2,1)S(1)} collective-permute-done((bf16[4032]{0:T(1024)(128)(2,1)S(1)}, bf16[4032]{0:T(1024)(128)(2,1)S(1)}, u32[]{:S(2)}, u32[]{:S(2)}) %collective-permute-start.42) | collective-permute-done | bytes 8096 | tf_op jit(solution)/shard_map/ppermute | solution.py:65
  556.7 54.7 %collective-permute-done.27 = bf16[72,4608]{1,0:T(8,128)(2,1)S(1)} collective-permute-done((bf16[72,4608]{1,0:T(8,128)(2,1)S(1)}, bf16[72,4608]{1,0:T(8,128)(2,1)S(1)}, u32[]{:S(2)}, u32[]{:S(2)}) %collective-permute-start.27) | collective-permute-done | bytes 663584 | tf_op jit(solution)/shard_map/ppermute | solution.py:65
  612.7 12.4 %fusion.46 = (f32[1,1152,1152]{2,1,0:T(8,128)}, bf16[1152,1152]{1,0:T(8,128)(2,1)}, f32[1,1152,1152]{2,1,0:T(8,128)}, f32[1,1152,1152]{2,1,0:T(8,128)}) fusion(bf16[1152,1152]{1,0:T(8,128)(2,1)S(1)} %collective-permute-done.24, bf16[1152,1152]{1,0:T(8,128)(2,1)S(1)} %copy-done.34, f32[1,1152,1152]{2,1,0:T(8,128)} %param.62, f32[1152,1152]{1,0:T(8,128)S(1)} %bitcast.255, ...), kind=kLoop, calls=%fused_computation.124 | loop fusion | flops 26542080 | bytes 39813128 | tf_op jit(solution)/shard_map/broadcast_in_dim | solution.py:842
  625.2 16.6 %collective-permute-done.31 = bf16[144,4608]{1,0:T(8,128)(2,1)} collective-permute-done((bf16[144,4608]{1,0:T(8,128)(2,1)S(1)}, bf16[144,4608]{1,0:T(8,128)(2,1)}, u32[]{:S(2)}, u32[]{:S(2)}) %collective-permute-start.31) | collective-permute-done | bytes 1327136 | tf_op jit(solution)/shard_map/ppermute | solution.py:65
  643.3 5.9 fusion.6
  649.2 7.9 %multiply_add_fusion.3 = f32[1,288,4608]{2,1,0:T(8,128)} fusion(f32[1,288,4608]{2,1,0:T(8,128)S(1)} %get-tuple-element.231, f32[1,288,4608]{2,1,0:T(8,128)} %param.55), kind=kLoop, calls=%fused_computation.28 | loop fusion | flops 3981312 | bytes 15925248 | tf_op jit(solution)/shard_map/add | solution.py:790
  661.9 4.4 fusion.37
  673.6 13.5 %collective-permute-done.34 = bf16[72,4608]{1,0:T(8,128)(2,1)S(1)} collective-permute-done((bf16[72,4608]{1,0:T(8,128)(2,1)S(1)}, bf16[72,4608]{1,0:T(8,128)(2,1)S(1)}, u32[]{:S(2)}, u32[]{:S(2)}) %collective-permute-start.34) | collective-permute-done | bytes 663584 | tf_op jit(solution)/shard_map/ppermute | solution.py:65
  695.2 3.0 maximum_convert_fusion
  698.3 11.5 %multiply_subtract_fusion.2 = (f32[288,4608]{1,0:T(8,128)}, f32[288,4608]{1,0:T(8,128)}) fusion(f32[288,4608]{1,0:T(8,128)} %param.49, f32[288,4608]{1,0:T(8,128)} %param.67, f32[2,2,72,4608]{3,2,1,0:T(8,128)} %copy.77), kind=kLoop, calls=%fused_computation.23 | loop fusion | flops 7962624 | bytes 26542080 | tf_op jit(solution)/shard_map/sub | solution.py:849
  709.8 9.7 %fusion.9 = (f32[1,288,3456]{2,1,0:T(8,128)}, f32[1,288,3456]{2,1,0:T(8,128)}, f32[1,288,3456]{2,1,0:T(8,128)}) fusion(f32[1,288,3456]{2,1,0:T(8,128)} %param.59, f32[288,4608]{1,0:T(8,128)} %maximum_convert_fusion, f32[1,288,3456]{2,1,0:T(8,128)} %param.53), kind=kLoop, calls=%fused_computation.33 | loop fusion | flops 6967296 | bytes 23887872 | tf_op jit(solution)/shard_map/broadcast_in_dim | solution.py:842
  727.1 11.8 %multiply_subtract_fusion = (f32[288,6912]{1,0:T(8,128)}, f32[288,6912]{1,0:T(8,128)}) fusion(f32[288,6912]{1,0:T(8,128)S(1)} %bitcast.248, f32[288,6912]{1,0:T(8,128)} %param.64, f32[1,2,144,6912]{3,2,1,0:T(8,128)S(1)} %convert_multiply_fusion), kind=kLoop, calls=%fused_computation.10 | loop fusion | flops 11943936 | bytes 39813120 | tf_op jit(solution)/shard_map/sub | solution.py:849
  751.1 8.8 %multiply_subtract_fusion.3 = (f32[288,3456]{1,0:T(8,128)}, f32[288,3456]{1,0:T(8,128)}, f32[288,3456]{1,0:T(8,128)}) fusion(f32[288,3456]{1,0:T(8,128)} %param.47, f32[288,3456]{1,0:T(8,128)} %param.65, f32[288,4608]{1,0:T(8,128)S(1)} %bitcast.260), kind=kLoop, calls=%fused_computation.39 | loop fusion | flops 6967296 | bytes 23887872 | tf_op jit(solution)/shard_map/sub | solution.py:849
  762.9 11.1 %multiply_subtract_fusion.1 = (f32[1152,1152]{1,0:T(8,128)}, f32[1152,1152]{1,0:T(8,128)}) fusion(f32[1152,1152]{1,0:T(8,128)} %param.50, f32[1152,1152]{1,0:T(8,128)} %param.68, f32[1,2,576,1152]{3,2,1,0:T(8,128)} %convert_multiply_fusion.1), kind=kLoop, calls=%fused_computation.22 | loop fusion | flops 7962624 | bytes 26542080 | tf_op jit(solution)/shard_map/sub | solution.py:849
  (318 shorter events, 122.3 us)
Async XLA Ops:
  7.3 185.1 %all-gather.2.cloned.1.call-start = ((), (), s32[]{:S(2)}) async-start(), calls=%async_computation.3 | async-start | bytes 21897216 | tf_op jit(solution)/shard_map/all_gather | solution.py:660
  10.7 400.9 %reduce-scatter.4.cloned.1.call-start = ((), (), s32[]{:S(2)}) async-start(), calls=%async_computation.4 | async-start | bytes 13271040 | tf_op jit(solution)/shard_map/reduce_scatter | solution.py:710
  14.6 47.5 %collective-permute-start.5 = (bf16[144,1152]{1,0:T(8,128)(2,1)S(1)}, bf16[144,1152]{1,0:T(8,128)(2,1)S(1)}, u32[]{:S(2)}, u32[]{:S(2)}) collective-permute-start(bf16[144,1152]{1,0:T(8,128)(2,1)S(1)} %fusion.57), channel_id=1, source_target_pairs={{0,3},{1,0},{2,1},{3,2},{4,7},{5,4},{6,5},{7,6},{8,11},{9,8},{10,9... | collective-permute-start | bytes 995336 | tf_op jit(solution)/shard_map/ppermute | solution.py:60
  18.8 43.3 %collective-permute-start.4 = (bf16[144,1152]{1,0:T(8,128)(2,1)S(1)}, bf16[144,1152]{1,0:T(8,128)(2,1)S(1)}, u32[]{:S(2)}, u32[]{:S(2)}) collective-permute-start(bf16[144,1152]{1,0:T(8,128)(2,1)S(1)} %fusion.57), channel_id=1, source_target_pairs={{0,2},{1,3},{2,0},{3,1},{4,6},{5,7},{6,4},{7,5},{8,10},{9,11},{10,... | collective-permute-start | bytes 995336 | tf_op jit(solution)/shard_map/ppermute | solution.py:60
  18.9 21.9 %collective-permute-start = (bf16[7488]{0:T(1024)(128)(2,1)S(1)}, bf16[7488]{0:T(1024)(128)(2,1)S(1)}, u32[]{:S(2)}, u32[]{:S(2)}) collective-permute-start(bf16[7488]{0:T(1024)(128)(2,1)S(1)} %pad_maximum_fusion.13), channel_id=1, source_target_pairs={{0,1},{1,2},{2,3},{3,0},{4,5},{5,6},{6,7},{7,4},{8,9},{9,10},{10,1... | collective-permute-start | bytes 44936 | tf_op jit(solution)/shard_map/ppermute | solution.py:60
  19.3 42.5 %collective-permute-start.2 = (bf16[7488]{0:T(1024)(128)(2,1)S(1)}, bf16[7488]{0:T(1024)(128)(2,1)S(1)}, u32[]{:S(2)}, u32[]{:S(2)}) collective-permute-start(bf16[7488]{0:T(1024)(128)(2,1)S(1)} %pad_maximum_fusion.13), channel_id=1, source_target_pairs={{0,3},{1,0},{2,1},{3,2},{4,7},{5,4},{6,5},{7,6},{8,11},{9,8},{10,9... | collective-permute-start | bytes 44936 | tf_op jit(solution)/shard_map/ppermute | solution.py:60
  22.1 39.4 %collective-permute-start.1 = (bf16[7488]{0:T(1024)(128)(2,1)S(1)}, bf16[7488]{0:T(1024)(128)(2,1)S(1)}, u32[]{:S(2)}, u32[]{:S(2)}) collective-permute-start(bf16[7488]{0:T(1024)(128)(2,1)S(1)} %pad_maximum_fusion.13), channel_id=1, source_target_pairs={{0,2},{1,3},{2,0},{3,1},{4,6},{5,7},{6,4},{7,5},{8,10},{9,11},{10,... | collective-permute-start | bytes 44936 | tf_op jit(solution)/shard_map/ppermute | solution.py:60
  40.7 22.9 %collective-permute-start.3 = (bf16[144,1152]{1,0:T(8,128)(2,1)S(1)}, bf16[144,1152]{1,0:T(8,128)(2,1)S(1)}, u32[]{:S(2)}, u32[]{:S(2)}) collective-permute-start(bf16[144,1152]{1,0:T(8,128)(2,1)S(1)} %fusion.57), channel_id=1, source_target_pairs={{0,1},{1,2},{2,3},{3,0},{4,5},{5,6},{6,7},{7,4},{8,9},{9,10},{10,1... | collective-permute-start | bytes 995336 | tf_op jit(solution)/shard_map/ppermute | solution.py:60
  62.3 29.2 %collective-permute-start.10 = (bf16[2,144,1152]{2,1,0:T(8,128)(2,1)S(1)}, bf16[2,144,1152]{2,1,0:T(8,128)(2,1)}, u32[]{:S(2)}, u32[]{:S(2)}) collective-permute-start(bf16[2,144,1152]{2,1,0:T(8,128)(2,1)S(1)} %pad_maximum_fusion.8), channel_id=1, source_target_pairs={{0,4},{4,0},{1,5},{5,1},{2,6},{6,2},{3,7},{7,3},{8,12},{12,8},{9,1... | collective-permute-start | bytes 1990664 | tf_op jit(solution)/shard_map/ppermute | solution.py:65
  63.7 26.4 %collective-permute-start.9 = (bf16[2,144,1152]{2,1,0:T(8,128)(2,1)S(1)}, bf16[2,144,1152]{2,1,0:T(8,128)(2,1)}, u32[]{:S(2)}, u32[]{:S(2)}) collective-permute-start(bf16[2,144,1152]{2,1,0:T(8,128)(2,1)S(1)} %pad_maximum_fusion.7), channel_id=1, source_target_pairs={{0,16},{8,24},{16,0},{24,8},{1,17},{9,25},{17,1},{25,9},{2,18},{10... | collective-permute-start | bytes 1990664 | tf_op jit(solution)/shard_map/ppermute | solution.py:65
  91.4 25.4 %collective-permute-start.11 = (bf16[4,144,1152]{2,1,0:T(8,128)(2,1)S(1)}, bf16[4,144,1152]{2,1,0:T(8,128)(2,1)}, u32[]{:S(2)}, u32[]{:S(2)}) collective-permute-start(bf16[4,144,1152]{2,1,0:T(8,128)(2,1)S(1)} %pad_maximum_fusion.1.refs_0_), channel_id=1, source_target_pairs={{0,4},{4,0},{1,5},{5,1},{2,6},{6,2},{3,7},{7,3},{8,12},{12,8},{9,1... | collective-permute-start | bytes 3981320 | tf_op jit(solution)/shard_map/ppermute | solution.py:65
  92.7 33.1 %collective-permute-start.12 = (bf16[4,144,1152]{2,1,0:T(8,128)(2,1)S(1)}, bf16[4,144,1152]{2,1,0:T(8,128)(2,1)}, u32[]{:S(2)}, u32[]{:S(2)}) collective-permute-start(bf16[4,144,1152]{2,1,0:T(8,128)(2,1)S(1)} %pad_maximum_fusion.2.refs_1_), channel_id=1, source_target_pairs={{0,16},{8,24},{16,0},{24,8},{1,17},{9,25},{17,1},{25,9},{2,18},{10... | collective-permute-start | bytes 3981320 | tf_op jit(solution)/shard_map/ppermute | solution.py:65
  101.8 26.8 %collective-permute-start.6 = (f32[3,6912]{1,0:T(4,128)}, f32[3,6912]{1,0:T(4,128)S(1)}, u32[]{:S(2)}, u32[]{:S(2)}) collective-permute-start(f32[3,6912]{1,0:T(4,128)} %get-tuple-element.262), channel_id=1, source_target_pairs={{0,1},{1,2},{2,3},{3,0},{4,5},{5,6},{6,7},{7,4},{8,9},{9,10},{10,1... | collective-permute-start | bytes 248840 | tf_op jit(solution)/shard_map/ppermute | solution.py:60
  101.8 27.3 %collective-permute-start.8 = (f32[3,6912]{1,0:T(4,128)}, f32[3,6912]{1,0:T(4,128)}, u32[]{:S(2)}, u32[]{:S(2)}) collective-permute-start(f32[3,6912]{1,0:T(4,128)} %get-tuple-element.263), channel_id=1, source_target_pairs={{0,3},{1,0},{2,1},{3,2},{4,7},{5,4},{6,5},{7,6},{8,11},{9,8},{10,9... | collective-permute-start | bytes 248840 | tf_op jit(solution)/shard_map/ppermute | solution.py:60
  105.1 24.1 %collective-permute-start.7 = (f32[3,6912]{1,0:T(4,128)S(1)}, f32[3,6912]{1,0:T(4,128)}, u32[]{:S(2)}, u32[]{:S(2)}) collective-permute-start(f32[3,6912]{1,0:T(4,128)S(1)} %get-tuple-element.264), channel_id=1, source_target_pairs={{0,2},{1,3},{2,0},{3,1},{4,6},{5,7},{6,4},{7,5},{8,10},{9,11},{10,... | collective-permute-start | bytes 248840 | tf_op jit(solution)/shard_map/ppermute | solution.py:60
  125.8 9.1 %collective-permute-start.13 = (bf16[4,144,1152]{2,1,0:T(8,128)(2,1)S(1)}, bf16[4,144,1152]{2,1,0:T(8,128)(2,1)}, u32[]{:S(2)}, u32[]{:S(2)}) collective-permute-start(bf16[4,144,1152]{2,1,0:T(8,128)(2,1)S(1)} %pad_maximum_fusion.1.refs_0_), channel_id=1, source_target_pairs={{0,8},{8,0},{16,24},{24,16},{1,9},{9,1},{17,25},{25,17},{2,10},{10... | collective-permute-start | bytes 3981320 | tf_op jit(solution)/shard_map/ppermute | solution.py:65
  128.6 12.0 %collective-permute-start.14 = (bf16[4,144,1152]{2,1,0:T(8,128)(2,1)S(1)}, bf16[4,144,1152]{2,1,0:T(8,128)(2,1)}, u32[]{:S(2)}, u32[]{:S(2)}) collective-permute-start(bf16[4,144,1152]{2,1,0:T(8,128)(2,1)S(1)} %pad_maximum_fusion.2.refs_1_), channel_id=1, source_target_pairs={{0,8},{8,0},{16,24},{24,16},{1,9},{9,1},{17,25},{25,17},{2,10},{10... | collective-permute-start | bytes 3981320 | tf_op jit(solution)/shard_map/ppermute | solution.py:65
  128.6 12.0 %collective-permute-start.15 = (bf16[4,144,1152]{2,1,0:T(8,128)(2,1)}, bf16[4,144,1152]{2,1,0:T(8,128)(2,1)}, u32[]{:S(2)}, u32[]{:S(2)}) collective-permute-start(bf16[4,144,1152]{2,1,0:T(8,128)(2,1)} %collective-permute-done.11.refs_2_), channel_id=1, source_target_pairs={{0,8},{8,0},{16,24},{24,16},{1,9},{9,1},{17,25},{25,17},{2,10},{10... | collective-permute-start | bytes 3981320 | tf_op jit(solution)/shard_map/ppermute | solution.py:65
  129.1 12.3 %collective-permute-start.16 = (bf16[4,144,1152]{2,1,0:T(8,128)(2,1)}, bf16[4,144,1152]{2,1,0:T(8,128)(2,1)}, u32[]{:S(2)}, u32[]{:S(2)}) collective-permute-start(bf16[4,144,1152]{2,1,0:T(8,128)(2,1)} %collective-permute-done.12.refs_3_), channel_id=1, source_target_pairs={{0,8},{8,0},{16,24},{24,16},{1,9},{9,1},{17,25},{25,17},{2,10},{10... | collective-permute-start | bytes 3981320 | tf_op jit(solution)/shard_map/ppermute | solution.py:65
  230.0 288.0 %reduce-scatter.6.cloned.1.call-start = ((), (), s32[]{:S(2)}) async-start(), calls=%async_computation.5 | async-start | bytes 6635520 | tf_op jit(solution)/shard_map/reduce_scatter | solution.py:710
  267.0 116.1 %collective-permute-start.17 = (bf16[4,144,4608]{2,1,0:T(8,128)(2,1)}, bf16[4,144,4608]{2,1,0:T(8,128)(2,1)}, u32[]{:S(2)}, u32[]{:S(2)}) collective-permute-start(bf16[4,144,4608]{2,1,0:T(8,128)(2,1)} %dynamic-slice_bitcast_fusion), channel_id=1, source_target_pairs={{0,4},{4,0},{1,5},{5,1},{2,6},{6,2},{3,7},{7,3},{8,12},{12,8},{9,1... | collective-permute-start | bytes 15925256 | tf_op jit(solution)/shard_map/ppermute | solution.py:65
  357.9 53.7 %collective-permute-start.18 = (bf16[4,144,1152]{2,1,0:T(8,128)(2,1)S(1)}, bf16[4,144,1152]{2,1,0:T(8,128)(2,1)}, u32[]{:S(2)}, u32[]{:S(2)}) collective-permute-start(bf16[4,144,1152]{2,1,0:T(8,128)(2,1)S(1)} %dynamic-slice_bitcast_fusion.4), channel_id=1, source_target_pairs={{0,4},{4,0},{1,5},{5,1},{2,6},{6,2},{3,7},{7,3},{8,12},{12,8},{9,1... | collective-permute-start | bytes 3981320 | tf_op jit(solution)/shard_map/ppermute | solution.py:65
  414.1 3.2 collective-permute-start.19
  416.3 243.1 %reduce-scatter.8.cloned.1.call-start = ((), (), s32[]{:S(2)}) async-start(), calls=%async_computation.6 | async-start | bytes 6635520 | tf_op jit(solution)/shard_map/reduce_scatter | solution.py:710
  416.3 86.6 %collective-permute-start.23 = (bf16[4,144,3456]{2,1,0:T(8,128)(2,1)}, bf16[4,144,3456]{2,1,0:T(8,128)(2,1)}, u32[]{:S(2)}, u32[]{:S(2)}) collective-permute-start(bf16[4,144,3456]{2,1,0:T(8,128)(2,1)} %dynamic-slice_bitcast_fusion.1), channel_id=1, source_target_pairs={{0,4},{4,0},{1,5},{5,1},{2,6},{6,2},{3,7},{7,3},{8,12},{12,8},{9,1... | collective-permute-start | bytes 11943944 | tf_op jit(solution)/shard_map/ppermute | solution.py:65
  418.0 6.4 collective-permute-start.20
  420.8 16.7 %collective-permute-start.21 = (bf16[2,33408]{1,0:T(2,128)(2,1)S(1)}, bf16[2,33408]{1,0:T(2,128)(2,1)S(1)}, u32[]{:S(2)}, u32[]{:S(2)}) collective-permute-start(bf16[2,33408]{1,0:T(2,128)(2,1)S(1)} %get-tuple-element.235), channel_id=1, source_target_pairs={{0,2},{1,3},{2,0},{3,1},{4,6},{5,7},{6,4},{7,5},{8,10},{9,11},{10,... | collective-permute-start | bytes 400904 | tf_op jit(solution)/shard_map/ppermute | solution.py:60
  422.1 16.1 %collective-permute-start.22 = (bf16[2,33408]{1,0:T(2,128)(2,1)S(1)}, bf16[2,33408]{1,0:T(2,128)(2,1)S(1)}, u32[]{:S(2)}, u32[]{:S(2)}) collective-permute-start(bf16[2,33408]{1,0:T(2,128)(2,1)S(1)} %get-tuple-element.235), channel_id=1, source_target_pairs={{0,3},{1,0},{2,1},{3,2},{4,7},{5,4},{6,5},{7,6},{8,11},{9,8},{10,9... | collective-permute-start | bytes 400904 | tf_op jit(solution)/shard_map/ppermute | solution.py:60
  439.1 95.5 %copy-start.43 = (f32[4032]{0:T(1024)}, f32[4032]{0:T(1024)S(1)}, u32[]{:S(2)}) copy-start(f32[4032]{0:T(1024)S(1)} %fusion.66) | copy-start | bytes 48388
  531.0 2.2 collective-permute-start.25
  532.8 20.4 %collective-permute-start.28 = (bf16[144,6912]{1,0:T(8,128)(2,1)}, bf16[144,6912]{1,0:T(8,128)(2,1)}, u32[]{:S(2)}, u32[]{:S(2)}) collective-permute-start(bf16[144,6912]{1,0:T(8,128)(2,1)} %dynamic-slice_bitcast_fusion.2), channel_id=1, source_target_pairs={{0,8},{8,0},{16,24},{24,16},{1,9},{9,1},{17,25},{25,17},{2,10},{10... | collective-permute-start | bytes 5971976 | tf_op jit(solution)/shard_map/ppermute | solution.py:65
  533.3 17.1 %collective-permute-start.26 = (bf16[72,4608]{1,0:T(8,128)(2,1)S(1)}, bf16[72,4608]{1,0:T(8,128)(2,1)}, u32[]{:S(2)}, u32[]{:S(2)}) collective-permute-start(bf16[72,4608]{1,0:T(8,128)(2,1)S(1)} %fusion.45), channel_id=1, source_target_pairs={{0,16},{8,24},{16,0},{24,8},{1,17},{9,25},{17,1},{25,9},{2,18},{10... | collective-permute-start | bytes 1990664 | tf_op jit(solution)/shard_map/ppermute | solution.py:65
  535.2 1.7 collective-permute-start.41
  536.8 12.9 %collective-permute-start.42 = (bf16[4032]{0:T(1024)(128)(2,1)S(1)}, bf16[4032]{0:T(1024)(128)(2,1)S(1)}, u32[]{:S(2)}, u32[]{:S(2)}) collective-permute-start(bf16[4032]{0:T(1024)(128)(2,1)S(1)} %add_convert_fusion.4), channel_id=1, source_target_pairs={{0,16},{8,24},{16,0},{24,8},{1,17},{9,25},{17,1},{25,9},{2,18},{10... | collective-permute-start | bytes 24200 | tf_op jit(solution)/shard_map/ppermute | solution.py:65
  538.1 73.3 %collective-permute-start.24 = (bf16[1152,1152]{1,0:T(8,128)(2,1)}, bf16[1152,1152]{1,0:T(8,128)(2,1)S(1)}, u32[]{:S(2)}, u32[]{:S(2)}) collective-permute-start(bf16[1152,1152]{1,0:T(8,128)(2,1)} %reduce-scatter.4.cloned.1.call-done), channel_id=1, source_target_pairs={{0,4},{4,0},{1,5},{5,1},{2,6},{6,2},{3,7},{7,3},{8,12},{12,8},{9,1... | collective-permute-start | bytes 7962632 | tf_op jit(solution)/shard_map/ppermute | solution.py:65
  551.8 59.6 %collective-permute-start.27 = (bf16[72,4608]{1,0:T(8,128)(2,1)S(1)}, bf16[72,4608]{1,0:T(8,128)(2,1)S(1)}, u32[]{:S(2)}, u32[]{:S(2)}) collective-permute-start(bf16[72,4608]{1,0:T(8,128)(2,1)S(1)} %add_convert_fusion.3), channel_id=1, source_target_pairs={{0,4},{4,0},{1,5},{5,1},{2,6},{6,2},{3,7},{7,3},{8,12},{12,8},{9,1... | collective-permute-start | bytes 1990664 | tf_op jit(solution)/shard_map/ppermute | solution.py:65
  555.8 101.3 %collective-permute-start.29 = (bf16[144,6912]{1,0:T(8,128)(2,1)S(1)}, bf16[144,6912]{1,0:T(8,128)(2,1)}, u32[]{:S(2)}, u32[]{:S(2)}) collective-permute-start(bf16[144,6912]{1,0:T(8,128)(2,1)S(1)} %fusion.10), channel_id=1, source_target_pairs={{0,16},{8,24},{16,0},{24,8},{1,17},{9,25},{17,1},{25,9},{2,18},{10... | collective-permute-start | bytes 5971976 | tf_op jit(solution)/shard_map/ppermute | solution.py:65
  612.2 29.6 %collective-permute-start.31 = (bf16[144,4608]{1,0:T(8,128)(2,1)S(1)}, bf16[144,4608]{1,0:T(8,128)(2,1)}, u32[]{:S(2)}, u32[]{:S(2)}) collective-permute-start(bf16[144,4608]{1,0:T(8,128)(2,1)S(1)} %copy-done.28), channel_id=1, source_target_pairs={{0,4},{4,0},{1,5},{5,1},{2,6},{6,2},{3,7},{7,3},{8,12},{12,8},{9,1... | collective-permute-start | bytes 3981320 | tf_op jit(solution)/shard_map/ppermute | solution.py:65
  659.4 34.2 %collective-permute-start.30 = (bf16[144,4608]{1,0:T(8,128)(2,1)}, bf16[144,4608]{1,0:T(8,128)(2,1)S(1)}, u32[]{:S(2)}, u32[]{:S(2)}) collective-permute-start(bf16[144,4608]{1,0:T(8,128)(2,1)} %reduce-scatter.8.cloned.1.call-done), channel_id=1, source_target_pairs={{0,4},{4,0},{1,5},{5,1},{2,6},{6,2},{3,7},{7,3},{8,12},{12,8},{9,1... | collective-permute-start | bytes 3981320 | tf_op jit(solution)/shard_map/ppermute | solution.py:65
  666.6 4.2 collective-permute-start.33
  670.9 16.2 %collective-permute-start.34 = (bf16[72,4608]{1,0:T(8,128)(2,1)S(1)}, bf16[72,4608]{1,0:T(8,128)(2,1)S(1)}, u32[]{:S(2)}, u32[]{:S(2)}) collective-permute-start(bf16[72,4608]{1,0:T(8,128)(2,1)S(1)} %fusion.44), channel_id=1, source_target_pairs={{0,16},{8,24},{16,0},{24,8},{1,17},{9,25},{17,1},{25,9},{2,18},{10... | collective-permute-start | bytes 1990664 | tf_op jit(solution)/shard_map/ppermute | solution.py:65
  672.2 16.1 %collective-permute-start.38 = (bf16[576,1152]{1,0:T(8,128)(2,1)S(1)}, bf16[576,1152]{1,0:T(8,128)(2,1)S(1)}, u32[]{:S(2)}, u32[]{:S(2)}) collective-permute-start(bf16[576,1152]{1,0:T(8,128)(2,1)S(1)} %dynamic-slice_bitcast_fusion.3), channel_id=1, source_target_pairs={{0,8},{8,0},{16,24},{24,16},{1,9},{9,1},{17,25},{25,17},{2,10},{10... | collective-permute-start | bytes 3981320 | tf_op jit(solution)/shard_map/ppermute | solution.py:65
  673.0 17.0 %collective-permute-start.37 = (bf16[2,72,4608]{2,1,0:T(8,128)(2,1)S(1)}, bf16[2,72,4608]{2,1,0:T(8,128)(2,1)S(1)}, u32[]{:S(2)}, u32[]{:S(2)}) collective-permute-start(bf16[2,72,4608]{2,1,0:T(8,128)(2,1)S(1)} %pad_maximum_fusion.5), channel_id=1, source_target_pairs={{0,8},{8,0},{16,24},{24,16},{1,9},{9,1},{17,25},{25,17},{2,10},{10... | collective-permute-start | bytes 3981320 | tf_op jit(solution)/shard_map/ppermute | solution.py:65
  673.1 49.8 %collective-permute-start.32 = (bf16[1,144,6912]{2,1,0:T(8,128)(2,1)S(1)}, bf16[1,144,6912]{2,1,0:T(8,128)(2,1)}, u32[]{:S(2)}, u32[]{:S(2)}) collective-permute-start(bf16[1,144,6912]{2,1,0:T(8,128)(2,1)S(1)} %bitcast.270), channel_id=1, source_target_pairs={{0,8},{8,0},{16,24},{24,16},{1,9},{9,1},{17,25},{25,17},{2,10},{10... | collective-permute-start | bytes 5971976 | tf_op jit(solution)/shard_map/ppermute | solution.py:65
  687.3 32.2 %collective-permute-start.35 = (bf16[72,4608]{1,0:T(8,128)(2,1)S(1)}, bf16[72,4608]{1,0:T(8,128)(2,1)S(1)}, u32[]{:S(2)}, u32[]{:S(2)}) collective-permute-start(bf16[72,4608]{1,0:T(8,128)(2,1)S(1)} %add_convert_fusion.2), channel_id=1, source_target_pairs={{0,4},{4,0},{1,5},{5,1},{2,6},{6,2},{3,7},{7,3},{8,12},{12,8},{9,1... | collective-permute-start | bytes 1990664 | tf_op jit(solution)/shard_map/ppermute | solution.py:65
  689.7 49.2 %collective-permute-start.39 = (bf16[576,1152]{1,0:T(8,128)(2,1)}, bf16[576,1152]{1,0:T(8,128)(2,1)}, u32[]{:S(2)}, u32[]{:S(2)}) collective-permute-start(bf16[576,1152]{1,0:T(8,128)(2,1)} %fusion.23), channel_id=1, source_target_pairs={{0,16},{8,24},{16,0},{24,8},{1,17},{9,25},{17,1},{25,9},{2,18},{10... | collective-permute-start | bytes 3981320 | tf_op jit(solution)/shard_map/ppermute | solution.py:65
  721.1 20.0 %collective-permute-start.36 = (bf16[2,72,4608]{2,1,0:T(8,128)(2,1)}, bf16[2,72,4608]{2,1,0:T(8,128)(2,1)}, u32[]{:S(2)}, u32[]{:S(2)}) collective-permute-start(bf16[2,72,4608]{2,1,0:T(8,128)(2,1)} %pad_maximum_fusion.4), channel_id=1, source_target_pairs={{0,8},{8,0},{16,24},{24,16},{1,9},{9,1},{17,25},{25,17},{2,10},{10... | collective-permute-start | bytes 3981320 | tf_op jit(solution)/shard_map/ppermute | solution.py:65
  741.0 18.9 %collective-permute-start.40 = (bf16[1,576,1152]{2,1,0:T(8,128)(2,1)S(1)}, bf16[1,576,1152]{2,1,0:T(8,128)(2,1)S(1)}, u32[]{:S(2)}, u32[]{:S(2)}) collective-permute-start(bf16[1,576,1152]{2,1,0:T(8,128)(2,1)S(1)} %fusion.43), channel_id=1, source_target_pairs={{0,8},{8,0},{16,24},{24,16},{1,9},{9,1},{17,25},{25,17},{2,10},{10... | collective-permute-start | bytes 3981320 | tf_op jit(solution)/shard_map/ppermute | solution.py:65
  (53 other events, 541.9 us)
Sparse Core Ops, SparseCore 0:
  11.6 180.7 all-gather.1
  230.1 177.9 reduce-scatter.3
  416.4 101.5 reduce-scatter.5
  538.2 94.9 reduce-scatter.7

commit v5 on v4

--- a/solution.py
+++ b/solution.py
@@ -1,3 +1,4 @@
+import functools
 import math
 
 import jax
@@ -23,6 +24,7 @@
 
 F32 = jnp.float32
 BF16 = jnp.bfloat16
+SMALL = pl.CostEstimate(flops=1024, bytes_accessed=1024, transcendentals=0)
 
 
 def dot(left, right):
@@ -511,6 +513,195 @@
 
 def after(*values):
     return lax.optimization_barrier(values)
+
+
+def adam_moments(first, second, gradient):
+    first_next = BETA_ONE * first + (1.0 - BETA_ONE) * gradient
+    second_next = BETA_TWO * second + (1.0 - BETA_TWO) * gradient * gradient
+    return first_next, second_next
+
+
+def adam_delta(master, first_next, second_next, rate, fix_one, fix_two):
+    step = first_next / fix_one / (jnp.sqrt(second_next / fix_two) + ADAM_EPS)
+    return (rate * (step + WEIGHT_DECAY * master)).astype(BF16)
+
+
+def whole_kernel(mode, rate, where_ref, fix_ref, *refs):
+    half = pl.program_id(2)
+    if mode == "sum":
+        a_ref, b_ref, master_ref, first_ref, second_ref, grad_ref, m_ref, v_ref, keep_ref, give_ref = refs
+        gradient = a_ref[0].astype(F32) + b_ref[0].astype(F32)
+        grad_ref[0] = gradient
+    elif mode == "given":
+        g_ref, master_ref, first_ref, second_ref, m_ref, v_ref, keep_ref, give_ref = refs
+        gradient = g_ref[0]
+    else:
+        own_ref, other_ref, first_ref, second_ref, grad_ref, m_ref, v_ref = refs
+        gradient = jnp.where(half == where_ref[0], own_ref[...].astype(F32), other_ref[...].astype(F32))
+        grad_ref[0] = gradient
+    first_next, second_next = adam_moments(first_ref[0], second_ref[0], gradient)
+    m_ref[0] = first_next
+    v_ref[0] = second_next
+    if mode != "halves":
+        delta = adam_delta(master_ref[0], first_next, second_next, rate, fix_ref[0], fix_ref[1])
+
+        @pl.when(half == where_ref[1])
+        def _():
+            keep_ref[...] = delta
+
+        @pl.when(half != where_ref[1])
+        def _():
+            give_ref[...] = delta
+
+
+def row_block(rows):
+    return 144 if rows % 144 == 0 else rows
+
+
+def adam_whole(mode, where, fixes, gradients, master, first, second, rate, shift=0):
+    rows, columns = master.shape
+    half, width = rows // 2, D
+    block = row_block(half)
+    three = pl.BlockSpec((1, block, width), lambda c, r, h, w: (h, r, c))
+    flat = pl.BlockSpec((block, width), lambda c, r, h, w: (r, c))
+    moved = pl.BlockSpec((block, width), lambda c, r, h, w: (r, c + shift))
+    view = (2, half, columns)
+    state = [first.reshape(view), second.reshape(view)]
+    if mode == "halves":
+        operands = list(gradients) + state
+        in_specs = [moved, moved, three, three]
+    else:
+        operands = [g.reshape(view) for g in gradients] + [master.reshape(view)] + state
+        in_specs = [three] * len(operands)
+    wide = jax.ShapeDtypeStruct(view, F32)
+    thin = jax.ShapeDtypeStruct((half, columns), BF16)
+    count = 2 if mode == "given" else 3
+    extra = 0 if mode == "halves" else 2
+    outs = pl.pallas_call(
+        functools.partial(whole_kernel, mode, rate),
+        grid_spec=pltpu.PrefetchScalarGridSpec(
+            num_scalar_prefetch=1,
+            grid=(columns // width, half // block, 2),
+            in_specs=[pl.BlockSpec(memory_space=pltpu.SMEM)] + in_specs,
+            out_specs=[three] * count + [flat] * extra,
+        ),
+        out_shape=[wide] * count + [thin] * extra,
+        compiler_params=params(48),
+        cost_estimate=SMALL,
+    )(where, fixes, *operands)
+    return [out.reshape(1, rows, columns) for out in outs[:count]] + list(outs[count:])
+
+
+def own_kernel(rates, where_ref, fix_ref, g_ref, *refs):
+    states, keep_ref, give_ref = refs[:-2], refs[-2], refs[-1]
+    unit, core = pl.program_id(0), pl.program_id(1)
+
+    def run(kind):
+        master_ref, first_ref, second_ref = states[3 * kind : 3 * kind + 3]
+        first_next, second_next = adam_moments(first_ref[0, 0], second_ref[0, 0], g_ref[0].astype(F32))
+        delta = adam_delta(
+            master_ref[0, 0], first_next, second_next, rates[kind][1], fix_ref[0], fix_ref[1]
+        )
+
+        @pl.when(core == where_ref[1])
+        def _():
+            keep_ref[...] = delta
+
+        @pl.when(core != where_ref[1])
+        def _():
+            give_ref[...] = delta
+
+    start = 0
+    for kind, (units, _) in enumerate(rates):
+        stop = start + units
+
+        @pl.when((unit >= start) & (unit < stop))
+        def _():
+            run(kind)
+
+        start = stop
+
+
+def adam_own(where, fixes, gradient, weights):
+    half, columns = gradient.shape
+    quarter, width = half // 2, D
+    operands, in_specs, rates = [gradient.reshape(2, quarter, columns)], [], []
+    in_specs.append(pl.BlockSpec((1, quarter, width), lambda c, h, w: (h, 0, c)))
+    start = 0
+    for master, first, second, rate in weights:
+        units = master.shape[1] // width
+        low = start
+
+        def place(c, h, w, low=low, units=units):
+            return (w[0], h, 0, jnp.clip(c - low, 0, units - 1))
+
+        for value in (master, first, second):
+            operands.append(value.reshape(2, 2, quarter, value.shape[-1]))
+            in_specs.append(pl.BlockSpec((1, 1, quarter, width), place))
+        rates.append((units, rate))
+        start += units
+    flat = pl.BlockSpec((quarter, width), lambda c, h, w: (0, c))
+    return pl.pallas_call(
+        functools.partial(own_kernel, tuple(rates)),
+        grid_spec=pltpu.PrefetchScalarGridSpec(
+            num_scalar_prefetch=1,
+            grid=(columns // width, 2),
+            in_specs=[pl.BlockSpec(memory_space=pltpu.SMEM)] + in_specs,
+            out_specs=[flat, flat],
+        ),
+        out_shape=[jax.ShapeDtypeStruct((quarter, columns), BF16)] * 2,
+        compiler_params=params(48),
+        cost_estimate=SMALL,
+    )(where, fixes, *operands)
+
+
+def outer_kernel(scale, where_ref, *refs):
+    totals, master_ref, outer_ref, delta_ref, next_ref, weight_ref = refs[:-5], *refs[-5:]
+    core = pl.program_id(2)
+    if len(totals) == 2:
+        own, other = totals[0][...], totals[1][...]
+    else:
+        mine = pl.program_id(1) == where_ref[0]
+        own = jnp.where(mine, totals[0][...], totals[1][...])
+        other = jnp.where(mine, totals[2][...], totals[3][...])
+    delta = jnp.where(core == where_ref[1], own.astype(F32), other.astype(F32)) * scale
+    outer_next = OUTER_MOMENTUM * outer_ref[...].reshape(delta.shape) + delta
+    master = master_ref[...].reshape(delta.shape)
+    delta_ref[...] = delta.reshape(delta_ref.shape)
+    next_ref[...] = outer_next.reshape(next_ref.shape)
+    weight = master - OUTER_RATE * (delta + OUTER_MOMENTUM * outer_next)
+    weight_ref[...] = weight.reshape(weight_ref.shape)
+
+
+def outer_whole(where, totals, master, outer, groups, shift=0):
+    rows, columns = master.shape
+    width = D
+    if len(totals) == 2:
+        part = rows // 2
+        block = row_block(part)
+        view = (2, part, columns)
+        grid = (columns // width, part // block, 2)
+        state = pl.BlockSpec((1, block, width), lambda c, r, h, w: (h, r, c))
+        total = pl.BlockSpec((block, width), lambda c, r, h, w: (r, c + shift))
+    else:
+        part = rows // 4
+        view = (2, 2, part, columns)
+        grid = (columns // width, 2, 2)
+        state = pl.BlockSpec((1, 1, part, width), lambda c, p, h, w: (p, h, 0, c))
+        total = pl.BlockSpec((part, width), lambda c, p, h, w: (0, c + shift))
+    outs = pl.pallas_call(
+        functools.partial(outer_kernel, 1.0 / groups),
+        grid_spec=pltpu.PrefetchScalarGridSpec(
+            num_scalar_prefetch=1,
+            grid=grid,
+            in_specs=[total] * len(totals) + [state, state],
+            out_specs=[state] * 3,
+        ),
+        out_shape=[jax.ShapeDtypeStruct(view, F32)] * 3,
+        compiler_params=params(48),
+        cost_estimate=SMALL,
+    )(where, *totals, master.reshape(view), outer.reshape(view))
+    return [out.reshape(rows, columns) for out in outs]
 
 
 def place_kernel(order_ref, *refs):
@@ -770,11 +961,6 @@
     own_bias = biases.shape[0]
     grad_bias = lax.dynamic_slice_in_dim(bias_group, line * own_bias, own_bias, axis=0)
 
-    def two_rows(own, other):
-        first = jnp.where(pair == 0, own, other)
-        second = jnp.where(pair == 0, other, own)
-        return jnp.concatenate([first, second], axis=0)
-
     power = step_count[0].astype(F32)
     fix_one = 1.0 - jnp.power(BETA_ONE, power)
     fix_two = 1.0 - jnp.power(BETA_TWO, power)
@@ -786,109 +972,94 @@
     outers_out = [None] * 6
     weights_out = [None] * 6
 
-    def moments_next(first, second, gradient):
-        first_next = BETA_ONE * first + (1.0 - BETA_ONE) * gradient
-        second_next = BETA_TWO * second + (1.0 - BETA_TWO) * gradient * gradient
-        return first_next, second_next
+    low = rep % 2
+    where = jnp.stack([pair, low]).astype(jnp.int32)
+    fixes = jnp.stack([fix_one, fix_two])
 
     def local_delta(master, first, second, gradient, rate):
-        first_next, second_next = moments_next(first, second, gradient)
-        local = master - rate * (
-            first_next / fix_one / (jnp.sqrt(second_next / fix_two) + ADAM_EPS)
-            + WEIGHT_DECAY * master
-        )
-        return (master - local).astype(BF16)
-
-    low = rep % 2
-
-    def sum_near(mine):
-        mine = mine.reshape(2, mine.shape[0] // 2, mine.shape[1])
-        keep = lax.dynamic_index_in_dim(mine, low, 0, keepdims=False)
-        give = lax.dynamic_index_in_dim(mine, 1 - low, 0, keepdims=False)
+        first_next, second_next = adam_moments(first, second, gradient)
+        delta = adam_delta(master, first_next, second_next, rate, fix_one, fix_two)
+        return delta, first_next, second_next
+
+    def state(index):
+        return masters[index], firsts[index][0], seconds[index][0], rates[index]
+
+    def sum_near(keep, give):
         return (keep.astype(F32) + swap_with(give, "rep", 1).astype(F32)).astype(BF16)
 
     def sum_far(total):
         return (total.astype(F32) + swap_with(total, "rep", 2).astype(F32)).astype(BF16)
 
-    def sum_rep(mine):
-        if mine.ndim == 1:
-            total = (mine.astype(F32) + swap_with(mine, "rep", 1).astype(F32)).astype(BF16)
-            return total.astype(F32) + swap_with(total, "rep", 2).astype(F32)
-        return sum_far(sum_near(mine))
-
-    def join_cores(total):
-        other = swap_with(total, "rep", 1)
-        first = jnp.where(low == 0, total, other)
-        second = jnp.where(low == 0, other, total)
-        return jnp.stack([first, second], axis=1).reshape(-1, total.shape[2]).astype(F32)
-
-    def join_pair(total):
-        return join_cores(two_rows(total[None], swap_with(total, "dp", 1)[None]))
-
-    def own_rows(value):
-        count = value.shape[0] // 2
-        return lax.dynamic_slice_in_dim(value, pair * count, count, axis=0)
-
-    def own_delta(index, own_gradient):
-        master, first, second = masters[index], firsts[index][0], seconds[index][0]
-        return local_delta(
-            own_rows(master), own_rows(first), own_rows(second), own_gradient.astype(F32), rates[index]
+    def outer_step(index, totals, shift=0):
+        deltas_out[index], outers_out[index], weights_out[index] = outer_whole(
+            where, totals, masters[index], outers[index], groups, shift
         )
 
-    def keep_moments(index, gradient):
-        reduced[index] = gradient
-        first_next, second_next = moments_next(firsts[index][0], seconds[index][0], gradient)
-        firsts_out[index] = first_next[None]
-        seconds_out[index] = second_next[None]
-
-    def outer_step(index, summed):
-        delta = summed / groups
-        outer_next = OUTER_MOMENTUM * outers[index] + delta
-        deltas_out[index] = delta
-        outers_out[index] = outer_next
-        weights_out[index] = masters[index] - OUTER_RATE * (delta + OUTER_MOMENTUM * outer_next)
-
-    ada_delta = local_delta(w_ada, first_ada[0], second_ada[0], grad_ada, rates[0])
-    one_half, there_attn, two_line, ada_delta, grad_bias = after(
-        one_half, there_attn, two_line, ada_delta, grad_bias
+    reduced[0] = grad_ada
+    firsts_out[0], seconds_out[0], ada_keep, ada_give = adam_whole(
+        "given", where, fixes, [grad_ada], *state(0)
+    )
+    one_half, there_attn, two_line, ada_keep, ada_give, grad_bias = after(
+        one_half, there_attn, two_line, ada_keep, ada_give, grad_bias
     )
     attn_both = jnp.concatenate(
         [pair_sum(grad_qkv, there_attn), pair_sum(grad_proj, there_proj)], axis=2
     )
-    attn_both, two_line, one_half, ada_delta = after(attn_both, two_line, one_half, ada_delta)
+    attn_both, two_line, one_half, ada_give, grad_bias = after(
+        attn_both, two_line, one_half, ada_give, grad_bias
+    )
     attn_half = line_sum(attn_both)
+    ada_total = sum_far(sum_near(ada_keep, ada_give))
+    one_total = sum_far(sum_near(*adam_own(where, fixes, one_half, [state(3)])))
     two_there = swap_with(two_line, "dp", 1)
-    ada_total = sum_rep(ada_delta)
-    one_total = sum_rep(own_delta(3, one_half))
-    one_other = swap_with(one_total, "dp", 1)
-    two_there, one_other, one_half = after(two_there, one_other, one_half)
+    two_there, one_half = after(two_there, one_half)
     one_there = swap_with(one_half, "dp", 1)
-    grad_two = two_line.astype(F32) + two_there.astype(F32)
-    two_delta = local_delta(w_fc2, first_fc2[0], second_fc2[0], grad_two, rates[4])
-    bias_delta = local_delta(biases, first_bias[0], second_bias[0], grad_bias, rates[5])
-    bias_total = sum_rep(bias_delta)
-    keep_moments(0, grad_ada)
-    keep_moments(5, grad_bias)
-    keep_moments(4, grad_two)
-    outer_step(5, bias_total)
-    attn_half, one_other, ada_total, two_delta = after(attn_half, one_other, ada_total, two_delta)
-    two_total = sum_rep(two_delta)
-    outer_step(0, join_cores(ada_total[None]))
-    keep_moments(3, two_rows(one_half, one_there).astype(F32))
-    edge = 3 * width
-    attn_total = sum_rep(
-        jnp.concatenate([own_delta(1, attn_half[:, :edge]), own_delta(2, attn_half[:, edge:])], axis=1)
-    )
+    outer_step(0, [ada_total, swap_with(ada_total, "rep", 1)])
+    two_there, weights_out[0], one_total = after(two_there, weights_out[0], one_total)
+    one_pair = swap_with(one_total, "dp", 1)
+    reduced[4], firsts_out[4], seconds_out[4], two_keep, two_give = adam_whole(
+        "sum", where, fixes, [two_line, two_there], *state(4)
+    )
+    bias_delta, bias_first, bias_second = local_delta(
+        biases, first_bias[0], second_bias[0], grad_bias, rates[5]
+    )
+    reduced[5] = grad_bias
+    firsts_out[5], seconds_out[5] = bias_first[None], bias_second[None]
+    bias_total = (bias_delta.astype(F32) + swap_with(bias_delta, "rep", 1).astype(F32)).astype(BF16)
+    bias_total = bias_total.astype(F32) + swap_with(bias_total, "rep", 2).astype(F32)
+    deltas_out[5] = bias_total / groups
+    outers_out[5] = OUTER_MOMENTUM * outer_bias + deltas_out[5]
+    weights_out[5] = biases - OUTER_RATE * (deltas_out[5] + OUTER_MOMENTUM * outers_out[5])
+    attn_half, two_keep, two_give = after(attn_half, two_keep, two_give, one_pair, one_there)[:3]
+    attn_near = sum_near(*adam_own(where, fixes, attn_half, [state(1), state(2)]))
     attn_there = swap_with(attn_half, "dp", 1)
-    outer_step(4, join_cores(two_total[None]))
-    outer_step(3, join_cores(two_rows(one_total[None], one_other[None])))
-    attn_full = two_rows(attn_half, attn_there).astype(F32)
-    keep_moments(1, attn_full[:, :edge])
-    keep_moments(2, attn_full[:, edge:])
-    summed = join_pair(attn_total)
-    outer_step(1, summed[:, :edge])
-    outer_step(2, summed[:, edge:])
-    grads_out = tuple((gradient[None] for gradient in reduced))
+    attn_far = swap_with(attn_near, "rep", 2)
+    reduced[3], firsts_out[3], seconds_out[3] = adam_whole(
+        "halves", where, fixes, [one_half, one_there], *state(3)
+    )
+    attn_far, attn_there, firsts_out[3] = after(attn_far, attn_there, firsts_out[3])
+    attn_total = (attn_near.astype(F32) + attn_far.astype(F32)).astype(BF16)
+    attn_pair = swap_with(attn_total, "dp", 1)
+    two_near, attn_total = after(sum_near(two_keep, two_give), attn_total)
+    two_far = swap_with(two_near, "rep", 2)
+    outer_step(
+        3, [one_total, one_pair, swap_with(one_total, "rep", 1), swap_with(one_pair, "rep", 1)]
+    )
+    attn_pair, weights_out[3] = after(attn_pair, weights_out[3])
+    attn_units = 3
+    for index, shift in ((1, 0), (2, attn_units)):
+        reduced[index], firsts_out[index], seconds_out[index] = adam_whole(
+            "halves", where, fixes, [attn_half, attn_there], *state(index), shift=shift
+        )
+    two_far, firsts_out[1], firsts_out[2], weights_out[3] = after(
+        two_far, firsts_out[1], firsts_out[2], weights_out[3]
+    )
+    two_total = (two_near.astype(F32) + two_far.astype(F32)).astype(BF16)
+    outer_step(4, [two_total, swap_with(two_total, "rep", 1)])
+    totals = [attn_total, attn_pair, swap_with(attn_total, "rep", 1), swap_with(attn_pair, "rep", 1)]
+    outer_step(1, totals)
+    outer_step(2, totals, attn_units)
+    grads_out = tuple((g if g.ndim == f.ndim else g[None] for g, f in zip(reduced, firsts)))
     return (
         (result.reshape(images.shape), in_grad.reshape(images.shape))
         + grads_out

time: 787 us -> 762 us (0.968)
  Pallas kernels: 197 us -> 340 us
  other arithmetic: 169 us -> 31 us
  waiting for transfers between devices: 291 us -> 267 us
    pallas_call x0 -> x12, Pallas kernels: none -> 142 us  [the longest x5 63.8 us: adam_whole(): pl.pallas_call(functools.partial(whole_kernel, mode, rate), grid_spec=plt...]
    broadcast_in_dim x7 -> x0, other arithmetic: 52 us -> none  [the longest x4 47.4 us: keep_moments(): seconds_out[index] = second_next[None]]
    sub x5 -> x1, other arithmetic: 43.8 us -> 0.62 us  [body(): biases - OUTER_RATE * (deltas_out[5] + OUTER_MOMENTUM * outers_out[5])]
    ppermute x31 -> x33, waiting for transfers between devices: 227 us -> 197 us  [swap_with(): return lax.ppermute(value, axis, [(i, i ^ bit) for i in range(size)])]
    convert_element_type x7 -> x4, other arithmetic: 16 us -> 1.12 us  [the longest x1 0.62 us: adam_delta(): return (rate * (step + WEIGHT_DECAY * master)).astype(BF16)]
    ppermute x12, starting transfers between devices: 27.8 us -> 12.9 us  [shift_by(): lax.ppermute(value, axis, [(i, (i + step) % size) for i in range(size)])]
    ppermute x12, waiting for transfers between devices: 38 us -> 52 us  [shift_by(): lax.ppermute(value, axis, [(i, (i + step) % size) for i in range(size)])]
    add x2 -> x0, other arithmetic: 13.8 us -> none  [the longest x1 7.89 us: moments_next(): first_next = BETA_ONE * first + (1.0 - BETA_ONE) * gradient]
  transfers between devices with their start and end apart: 47 -> 49, of which waited for: 23 -> 30; matrix products, arithmetic and copies ran while one was open for 22% -> 7% of each run, Pallas kernels for 21% -> 38%
where the time goes in v5:
time: 762 us; the launch traced here: 752 us
  Pallas kernels  340 us (45%)
  waiting for transfers between devices  267 us (35%)
  starting transfers between devices  48.5 us (6%)
  local copies, waits for them, and re-layouts  40.5 us (5%)
  other arithmetic  31 us (4%)
  between operations  16.4 us (2%)
  matrix products  9.15 us (1%)
    ppermute x33, waiting for transfers between devices, swap_with(): return lax.ppermute(value, axis, [(i, i ^ bit) for i in range(size)])  197 us
    pallas_call x5, Pallas kernels, adam_whole(): pl.pallas_call(functools.partial(whole_kernel, mode, rate), grid_spec=plt...  63.8 us
    pallas_call x5, Pallas kernels, outer_whole(): pl.pallas_call(functools.partial(outer_kernel, 1.0 / groups), grid_spec=p...  61 us
    ppermute x12, waiting for transfers between devices, shift_by(): lax.ppermute(value, axis, [(i, (i + step) % size) for i in range(size)])  52 us
    ppermute x33, starting transfers between devices, swap_with(): return lax.ppermute(value, axis, [(i, i ^ bit) for i in range(size)])  35.2 us
    pallas_call x3, Pallas kernels, grad_columns(): pl.pallas_call(grad_kernel, grid=(width // rows,), in_specs=[whole_spec((...  29.8 us
    pallas_call x1, Pallas kernels, mlp_rest(): pl.pallas_call(mlp_rest_kernel, grid=(units,), in_specs=[column, column,...  29.2 us
    pallas_call x1, Pallas kernels, attention_forward(): pl.pallas_call(attention_forward_kernel, grid=(slots,), in_specs=[row, ro...  26.7 us
  transfers between devices with their start and end apart: 49, of which 30 were waited for; matrix products, arithmetic and copies ran while one was open for 7% of the time, Pallas kernels for 38%

profile of v5, /device:TPU:1, one launch (start us, length us, event | category | flops | bytes accessed | tf_op | source)
XLA Modules:
  0.0 751.8 jit_solution(6348464974137284566)
XLA Ops:
  22.3 4.5 collective-permute-done
  29.9 17.7 %collective-permute-done.5 = bf16[144,1152]{1,0:T(8,128)(2,1)S(1)} collective-permute-done((bf16[144,1152]{1,0:T(8,128)(2,1)S(1)}, bf16[144,1152]{1,0:T(8,128)(2,1)S(1)}, u32[]{:S(2)}, u32[]{:S(2)}) %collective-permute-start.5) | collective-permute-done | bytes 331808 | tf_op jit(solution)/shard_map/ppermute | solution.py:62
  47.7 16.4 %collective-permute-done.4 = bf16[144,1152]{1,0:T(8,128)(2,1)S(1)} collective-permute-done((bf16[144,1152]{1,0:T(8,128)(2,1)S(1)}, bf16[144,1152]{1,0:T(8,128)(2,1)S(1)}, u32[]{:S(2)}, u32[]{:S(2)}) %collective-permute-start.4) | collective-permute-done | bytes 331808 | tf_op jit(solution)/shard_map/ppermute | solution.py:62
  66.3 4.6 fusion.2
  72.4 18.4 %collective-permute-done.10 = bf16[2,144,1152]{2,1,0:T(8,128)(2,1)} collective-permute-done((bf16[2,144,1152]{2,1,0:T(8,128)(2,1)}, bf16[2,144,1152]{2,1,0:T(8,128)(2,1)}, u32[]{:S(2)}, u32[]{:S(2)}) %collective-permute-start.10) | collective-permute-done | bytes 663584 | tf_op jit(solution)/shard_map/ppermute | solution.py:67
  96.7 23.8 %collective-permute-done.11.refs_2_ = bf16[4,144,1152]{2,1,0:T(8,128)(2,1)} collective-permute-done((bf16[4,144,1152]{2,1,0:T(8,128)(2,1)S(1)}, bf16[4,144,1152]{2,1,0:T(8,128)(2,1)}, u32[]{:S(2)}, u32[]{:S(2)}) %collective-permute-start.11) | collective-permute-done | bytes 1327136 | tf_op jit(solution)/shard_map/ppermute | solution.py:67
  120.5 4.3 collective-permute-done.12.refs_3_
  124.8 8.8 %collective-permute-start.13 = (bf16[4,144,1152]{2,1,0:T(8,128)(2,1)S(1)}, bf16[4,144,1152]{2,1,0:T(8,128)(2,1)}, u32[]{:S(2)}, u32[]{:S(2)}) collective-permute-start(bf16[4,144,1152]{2,1,0:T(8,128)(2,1)S(1)} %pad_maximum_fusion.1.refs_0_), channel_id=1, source_target_pairs={{0,8},{8,0},{16,24},{24,16},{1,9},{9,1},{17,25},{25,17},{2,10},{10... | collective-permute-start | bytes 3981320 | tf_op jit(solution)/shard_map/ppermute | solution.py:67
  134.4 3.9 collective-permute-done.13.refs_4_
  142.6 9.0 %shard_map.590 = bf16[32,144,1152]{2,1,0:T(8,128)(2,1)} custom-call(s32[32]{0:T(128)S(1)} %stack.178.order_ref, bf16[4,144,1152]{2,1,0:T(8,128)(2,1)S(1)} %pad_maximum_fusion.1.refs_0_, bf16[4,144,1152]{2,1,0:T(8,128)(2,1)} %pad_maximum_fusion.2.refs_1_, bf16[4,144,1152]{2,1,0:T(8,128)(2,1)} %collective-permute-done.11.refs_2_, ...), custom_call_target="tpu_custom_call" | custom-call | bytes 21233664 | tf_op jit(solution)/shard_map/pallas_call | solution.py:729
  151.6 26.7 %shard_map.591 = (bf16[768,1152]{1,0:T(8,128)(2,1)S(1)}, bf16[768,3456]{1,0:T(8,128)(2,1)}, bf16[768,1152]{1,0:T(8,128)(2,1)S(1)}, f32[768,128]{1,0:T(8,128)S(1)...) custom-call(bf16[768,1152]{1,0:T(8,128)(2,1)} %bitcast.176, ...), custom_call_target="tpu_custom_call" | custom-call | flops 8153726976 | bytes 41943040 | tf_op jit(solution)/shard_map/pallas_call | solution.py:190
  186.1 21.3 %shard_map.592 = (bf16[768,4608]{1,0:T(8,128)(2,1)}, bf16[768,4608]{1,0:T(8,128)(2,1)}) custom-call(bf16[768,1152]{1,0:T(8,128)(2,1)S(1)} %copy-done.28, bf16[4,4,2,2,144,1152]{5,4,3,2,1,0:T(8,128)(2,1)} %bitcast.227, f32[1,4608]{1,0:T(1,128)S(1)} %reshape.445.bias_ref), custom_call_target="tpu_custom_call" | custom-call | flops 8153726976 | bytes 27262976 | tf_op jit(solution)/shard_map/pallas_call | solution.py:256
  207.3 14.9 %shard_map.593 = bf16[4608,1152]{1,0:T(8,128)(2,1)} custom-call(bf16[768,4608]{1,0:T(8,128)(2,1)} %get-tuple-element.206.left_ref.act_ref, bf16[768,1152]{1,0:T(8,128)(2,1)S(1)} %copy-done.23), custom_call_target="tpu_custom_call" | custom-call | flops 8153726976 | bytes 24772608 | tf_op jit(solution)/shard_map/pallas_call | solution.py:501
  223.7 16.7 %shard_map.594 = (bf16[768,4608]{1,0:T(8,128)(2,1)}, f32[8,4608]{1,0:T(8,128)S(1)}) custom-call(bf16[768,1152]{1,0:T(8,128)(2,1)S(1)} %copy-done.24, bf16[4,4,2,2,144,1152]{5,4,3,2,1,0:T(8,128)(2,1)} %bitcast.228, bf16[768,4608]{1,0:T(8,128)(2,1)} %get-tuple-element.209.slope_ref), custom_call_target="tpu_custom_call" | custom-call | flops 8153726976 | bytes 27262976 | tf_op jit(solution)/shard_map/pallas_call | solution.py:287
  240.4 14.9 %shard_map.595 = bf16[1152,4608]{1,0:T(8,128)(2,1)} custom-call(bf16[768,1152]{1,0:T(8,128)(2,1)S(1)} %copy-done.29, bf16[768,4608]{1,0:T(8,128)(2,1)} %get-tuple-element.211.right_ref.d_hidden_ref), custom_call_target="tpu_custom_call" | custom-call | flops 8153726976 | bytes 24772608 | tf_op jit(solution)/shard_map/pallas_call | solution.py:485
  255.4 5.2 dynamic-slice_bitcast_fusion
  264.0 29.2 %shard_map.596 = (f32[768,1152]{1,0:T(8,128)S(1)}, f32[768,1152]{1,0:T(8,128)}) custom-call(bf16[768,4608]{1,0:T(8,128)(2,1)} %get-tuple-element.206.left_ref.act_ref, bf16[768,4608]{1,0:T(8,128)(2,1)} %get-tuple-element.211.right_ref.d_hidden_ref, bf16[4,4,2,2,144,1152]{5,4,3,2,1,0:T(8,128)(2,1)} %bitcast.229, bf16[4,4,2,2,144,1152]{5,4,3,2,1,0:T(8,128)(2,1)} %bitcast.230), custom_call_target="tpu_custom_call" | custom-call | flops 16307453952 | bytes 44040192 | tf_op jit(solution)/shard_map/pallas_call | solution.py:325
  295.0 12.4 %shard_map.597 = (bf16[768,1152]{1,0:T(8,128)(2,1)}, f32[768,1152]{1,0:T(8,128)}, bf16[768,1152]{1,0:T(8,128)(2,1)S(1)}, bf16[768,1152]{1,0:T(8,128)(2,1)S(1)}, f32[3,8,1152]{2,1,0:T(8,128)S(1)}) custom-call(f32[768,1152]{1,0:T(8,128)} %copy-done.9, f32[8,1152]{1,0:T(8,128)S(1)} %scatter.19.bias_ref, f32[768,1152]{1,0:T(8,128)} %get-tuple-element.213.d_in_ref, ...), custom_call_target="tpu_custom_call" | custom-call | flops 2038431744 | bytes 31457280 | tf_op jit(solution)/shard_map/pallas_call | solution.py:366
  311.7 24.0 %shard_map.599 = (bf16[768,3456]{1,0:T(8,128)(2,1)}, f32[3,8,1152]{2,1,0:T(8,128)S(1)}) custom-call(bf16[768,3456]{1,0:T(8,128)(2,1)} %get-tuple-element.219.packed_ref, bf16[768,1152]{1,0:T(8,128)(2,1)S(1)} %get-tuple-element.223.d_att_ref, f32[768,128]{1,0:T(8,128)S(1)} %get-tuple-element.224.log_ref), custom_call_target="tpu_custom_call" | custom-call | flops 8053063680 | bytes 14680064 | tf_op jit(solution)/shard_map/pallas_call | solution.py:421
  335.7 11.9 %shard_map.600 = bf16[1152,3456]{1,0:T(8,128)(2,1)} custom-call(bf16[768,1152]{1,0:T(8,128)(2,1)S(1)} %copy-done.31, bf16[768,3456]{1,0:T(8,128)(2,1)} %get-tuple-element.228.right_ref.d_packed_ref), custom_call_target="tpu_custom_call" | custom-call | flops 6115295232 | bytes 18579456 | tf_op jit(solution)/shard_map/pallas_call | solution.py:485
  347.6 4.5 dynamic-slice_bitcast_fusion.1
  354.3 14.1 %shard_map.601 = (bf16[768,1152]{1,0:T(8,128)(2,1)}, f32[3,8,1152]{2,1,0:T(8,128)S(1)}) custom-call(bf16[768,3456]{1,0:T(8,128)(2,1)} %get-tuple-element.228.right_ref.d_packed_ref, bf16[4,1152,1152]{2,1,0:T(8,128)(2,1)} %bitcast.184, bf16[768,1152]{1,0:T(8,128)(2,1)S(1)} %bitcast.177, f32[768,1152]{1,0:T(8,128)S(1)} %copy-done.19, ...), custom_call_target="tpu_custom_call" | custom-call | flops 6115295232 | bytes 20971520 | tf_op jit(solution)/shard_map/pallas_call | solution.py:453
  368.4 9.4 %collective-permute-done.17 = bf16[4,144,4608]{2,1,0:T(8,128)(2,1)} collective-permute-done((bf16[4,144,4608]{2,1,0:T(8,128)(2,1)}, bf16[4,144,4608]{2,1,0:T(8,128)(2,1)}, u32[]{:S(2)}, u32[]{:S(2)}) %collective-permute-start.17) | collective-permute-done | bytes 5308448 | tf_op jit(solution)/shard_map/ppermute | solution.py:67
  377.8 7.8 %fusion = bf16[4,144,4608]{2,1,0:T(8,128)(2,1)} fusion(bf16[4,144,4608]{2,1,0:T(8,128)(2,1)} %collective-permute-done.17, bf16[4,2,144,4608]{3,2,1,0:T(8,128)(2,1)} %bitcast.202, s32[]{:T(128)S(6)} %select_n.139), kind=kLoop, calls=%fused_computation.2 | loop fusion | flops 10616832 | bytes 15925252 | tf_op jit(solution)/shard_map/convert_element_type | solution.py:906
  385.6 20.6 %collective-permute-done.18 = bf16[4,144,1152]{2,1,0:T(8,128)(2,1)} collective-permute-done((bf16[4,144,1152]{2,1,0:T(8,128)(2,1)}, bf16[4,144,1152]{2,1,0:T(8,128)(2,1)}, u32[]{:S(2)}, u32[]{:S(2)}) %collective-permute-start.18) | collective-permute-done | bytes 1327136 | tf_op jit(solution)/shard_map/ppermute | solution.py:67
  414.9 3.5 fusion.4
  420.3 13.1 %collective-permute-done.21 = bf16[2,33408]{1,0:T(2,128)(2,1)S(1)} collective-permute-done((bf16[2,33408]{1,0:T(2,128)(2,1)S(1)}, bf16[2,33408]{1,0:T(2,128)(2,1)S(1)}, u32[]{:S(2)}, u32[]{:S(2)}) %collective-permute-start.21) | collective-permute-done | bytes 133664 | tf_op jit(solution)/shard_map/ppermute | solution.py:62
  434.1 4.6 fusion.10
  438.7 21.9 %shard_map.602 = (f32[2,144,6912]{2,1,0:T(8,128)}, f32[2,144,6912]{2,1,0:T(8,128)}, bf16[144,6912]{1,0:T(8,128)(2,1)S(1)}, bf16[144,6912]{1,0:T(8,128)(2,1)}) custom-call(s32[2]{0:T(128)S(1)} %pad_add_fusion.where_ref, f32[2]{0:T(128)S(1)} %pad_maximum_fusion.10.fix_ref, f32[2,144,6912]{2,1,0:T(8,128)} %bitcast.180, f32[2,144,6912]{2,1,0:T(8,128)} %bitcast.178, ...), custom_call_target="tpu_custom_call" | custom-call | flops 1024 | bytes 1024 | tf_op jit(solution)/shard_map/pallas_call | solution.py:580
  462.2 34.9 %collective-permute-done.23 = bf16[4,144,3456]{2,1,0:T(8,128)(2,1)} collective-permute-done((bf16[4,144,3456]{2,1,0:T(8,128)(2,1)}, bf16[4,144,3456]{2,1,0:T(8,128)(2,1)}, u32[]{:S(2)}, u32[]{:S(2)}) %collective-permute-start.23) | collective-permute-done | bytes 3981344 | tf_op jit(solution)/shard_map/ppermute | solution.py:67
  497.1 15.2 %reduce-scatter.6.cloned.1.call-done.refs_0_ = bf16[144,4608]{1,0:T(8,128)(2,1)} async-done(((bf16[576,4608]{1,0:T(8,128)(2,1)}), bf16[144,4608]{1,0:T(8,128)(2,1)}) %reduce-scatter.6.cloned.1.call-update) | async-done | bytes 1327120 | tf_op jit(solution)/shard_map/reduce_scatter | solution.py:901
  512.3 4.4 fusion.1
  520.0 3.9 collective-permute-done.25
  529.0 8.0 %shard_map.604 = (bf16[72,4608]{1,0:T(8,128)(2,1)S(1)}, bf16[72,4608]{1,0:T(8,128)(2,1)S(1)}) custom-call(s32[2]{0:T(128)S(1)} %pad_add_fusion.where_ref, f32[2]{0:T(128)S(1)} %pad_maximum_fusion.10.fix_ref, bf16[2,72,4608]{2,1,0:T(8,128)(2,1)S(1)} %bitcast.169, f32[2,2,72,4608]{3,2,1,0:T(8,128)} %bitcast.185, f32[2,2,72,4608]{3,2,1,0:T(8,128)} %bitcast.190, ...), custom_call_target="tpu_custom_call" | custom-call | flops 1024 | bytes 1024 | tf_op jit(solution)/shard_map/pallas_call | solution.py:644
  537.9 33.3 %collective-permute-done.26 = bf16[144,6912]{1,0:T(8,128)(2,1)S(1)} collective-permute-done((bf16[144,6912]{1,0:T(8,128)(2,1)S(1)}, bf16[144,6912]{1,0:T(8,128)(2,1)S(1)}, u32[]{:S(2)}, u32[]{:S(2)}) %collective-permute-start.26) | collective-permute-done | bytes 1990688 | tf_op jit(solution)/shard_map/ppermute | solution.py:67
  574.3 12.1 %collective-permute-done.24 = bf16[1152,1152]{1,0:T(8,128)(2,1)S(1)} collective-permute-done((bf16[1152,1152]{1,0:T(8,128)(2,1)S(1)}, bf16[1152,1152]{1,0:T(8,128)(2,1)S(1)}, u32[]{:S(2)}, u32[]{:S(2)}) %collective-permute-start.24) | collective-permute-done | bytes 2654240 | tf_op jit(solution)/shard_map/ppermute | solution.py:67
  589.9 17.7 %shard_map.603 = (f32[2,144,6912]{2,1,0:T(8,128)}, f32[2,144,6912]{2,1,0:T(8,128)}, f32[2,144,6912]{2,1,0:T(8,128)}) custom-call(s32[2]{0:T(128)S(1)} %pad_add_fusion.where_ref, bf16[144,6912]{1,0:T(8,128)(2,1)S(1)} %add_convert_fusion.refs_0_, bf16[144,6912]{1,0:T(8,128)(2,1)S(1)} %collective-permute-done.27.refs_1_, f32[2,144,6912]{2,1,0:T(8,128)} %bitcast.179, ...), custom_call_target="tpu_custom_call" | custom-call | flops 1024 | bytes 1024 | tf_op jit(solution)/shard_map/pallas_call | solution.py:692
  608.8 15.9 %shard_map.605 = (f32[2,576,1152]{2,1,0:T(8,128)}, f32[2,576,1152]{2,1,0:T(8,128)}, f32[2,576,1152]{2,1,0:T(8,128)}, bf16[576,1152]{1,0:T(8,128)(2,1)S(1)}, bf16[576,1152]{1,0:T(8,128)(2,1)S(1)}) custom-call(s32[2]{0:T(128)S(1)} %pad_add_fusion.where_ref, f32[2]{0:T(128)S(1)} %pad_maximum_fusion.10.fix_ref, bf16[2,576,1152]{2,1,0:T(8,128)(2,1)S(1)} %bitcast.172, ...), custom_call_target="tpu_custom_call" | custom-call | flops 1024 | bytes 1024 | tf_op jit(solution)/shard_map/pallas_call | solution.py:580
  632.5 8.9 %shard_map.606 = (bf16[72,4608]{1,0:T(8,128)(2,1)S(1)}, bf16[72,4608]{1,0:T(8,128)(2,1)S(1)}) custom-call(s32[2]{0:T(128)S(1)} %pad_add_fusion.where_ref, f32[2]{0:T(128)S(1)} %pad_maximum_fusion.10.fix_ref, bf16[2,72,4608]{2,1,0:T(8,128)(2,1)} %bitcast.80.g_ref, f32[2,2,72,3456]{3,2,1,0:T(8,128)} %bitcast.195, f32[2,2,72,3456]{3,2,1,0:T(8,128)} %bitcast.197, ...), custom_call_target="tpu_custom_call" | custom-call | flops 1024 | bytes 1024 | tf_op jit(solution)/shard_map/pallas_call | solution.py:644
  646.6 12.1 %shard_map.607 = (f32[2,144,4608]{2,1,0:T(8,128)}, f32[2,144,4608]{2,1,0:T(8,128)}, f32[2,144,4608]{2,1,0:T(8,128)}) custom-call(s32[2]{0:T(128)S(1)} %pad_add_fusion.where_ref, f32[2]{0:T(128)S(1)} %pad_maximum_fusion.10.fix_ref, bf16[144,4608]{1,0:T(8,128)(2,1)S(1)} %copy-done.8, bf16[144,4608]{1,0:T(8,128)(2,1)S(1)} %copy-done.18, ...), custom_call_target="tpu_custom_call" | custom-call | flops 1024 | bytes 1024 | tf_op jit(solution)/shard_map/pallas_call | solution.py:580
  658.8 3.1 collective-permute-done.33
  661.8 12.8 %collective-permute-done.34.refs_1_ = bf16[144,4608]{1,0:T(8,128)(2,1)S(1)} collective-permute-done((bf16[144,4608]{1,0:T(8,128)(2,1)}, bf16[144,4608]{1,0:T(8,128)(2,1)S(1)}, u32[]{:S(2)}, u32[]{:S(2)}) %collective-permute-start.34) | collective-permute-done | bytes 1327136 | tf_op jit(solution)/shard_map/ppermute | solution.py:67
  679.3 15.8 %shard_map.610 = (f32[2,2,72,4608]{3,2,1,0:T(8,128)}, f32[2,2,72,4608]{3,2,1,0:T(8,128)}, f32[2,2,72,4608]{3,2,1,0:T(8,128)}) custom-call(s32[2]{0:T(128)S(1)} %pad_add_fusion.where_ref, bf16[72,4608]{1,0:T(8,128)(2,1)S(1)} %add_convert_fusion.6.refs_0_, bf16[72,4608]{1,0:T(8,128)(2,1)S(1)} %collective-permute-done.30.refs_1_, ...), custom_call_target="tpu_custom_call" | custom-call | flops 1024 | bytes 1024 | tf_op jit(solution)/shard_map/pallas_call | solution.py:692
  695.1 10.2 %shard_map.608 = (f32[2,144,3456]{2,1,0:T(8,128)}, f32[2,144,3456]{2,1,0:T(8,128)}, f32[2,144,3456]{2,1,0:T(8,128)}) custom-call(s32[2]{0:T(128)S(1)} %pad_add_fusion.where_ref, f32[2]{0:T(128)S(1)} %pad_maximum_fusion.10.fix_ref, bf16[144,4608]{1,0:T(8,128)(2,1)} %reduce-scatter.8.cloned.1.call-done.refs_0_, ...), custom_call_target="tpu_custom_call" | custom-call | flops 1024 | bytes 1024 | tf_op jit(solution)/shard_map/pallas_call | solution.py:580
  705.3 3.7 shard_map.609
  711.3 3.1 collective-permute-done.43
  717.5 12.3 %shard_map.611 = (f32[2,2,72,3456]{3,2,1,0:T(8,128)}, f32[2,2,72,3456]{3,2,1,0:T(8,128)}, f32[2,2,72,3456]{3,2,1,0:T(8,128)}) custom-call(s32[2]{0:T(128)S(1)} %pad_add_fusion.where_ref, bf16[72,4608]{1,0:T(8,128)(2,1)S(1)} %add_convert_fusion.4.refs_0_, bf16[72,4608]{1,0:T(8,128)(2,1)S(1)} %collective-permute-done.37.refs_1_, ...), custom_call_target="tpu_custom_call" | custom-call | flops 1024 | bytes 1024 | tf_op jit(solution)/shard_map/pallas_call | solution.py:692
  732.9 12.2 %shard_map.613 = (f32[2,576,1152]{2,1,0:T(8,128)}, f32[2,576,1152]{2,1,0:T(8,128)}, f32[2,576,1152]{2,1,0:T(8,128)}) custom-call(s32[2]{0:T(128)S(1)} %pad_add_fusion.where_ref, bf16[576,1152]{1,0:T(8,128)(2,1)S(1)} %add_convert_fusion.2.refs_0_, bf16[576,1152]{1,0:T(8,128)(2,1)S(1)} %collective-permute-done.42.refs_1_, f32[2,576,1152]{2,1,0:T(8,128)} %bitcast.188, ...), custom_call_target="tpu_custom_call" | custom-call | flops 1024 | bytes 1024 | tf_op jit(solution)/shard_map/pallas_call | solution.py:692
  (273 shorter events, 107.9 us)
Async XLA Ops:
  7.3 177.3 %all-gather.2.cloned.1.call-start = ((), (), s32[]{:S(2)}) async-start(), calls=%async_computation.3 | async-start | bytes 21897216 | tf_op jit(solution)/shard_map/all_gather | solution.py:851
  10.7 395.5 %reduce-scatter.4.cloned.1.call-start = ((), (), s32[]{:S(2)}) async-start(), calls=%async_computation.4 | async-start | bytes 13271040 | tf_op jit(solution)/shard_map/reduce_scatter | solution.py:901
  14.6 14.1 %collective-permute-start.3 = (bf16[144,1152]{1,0:T(8,128)(2,1)S(1)}, bf16[144,1152]{1,0:T(8,128)(2,1)S(1)}, u32[]{:S(2)}, u32[]{:S(2)}) collective-permute-start(bf16[144,1152]{1,0:T(8,128)(2,1)S(1)} %fusion.5), channel_id=1, source_target_pairs={{0,1},{1,2},{2,3},{3,0},{4,5},{5,6},{6,7},{7,4},{8,9},{9,10},{10,1... | collective-permute-start | bytes 995336 | tf_op jit(solution)/shard_map/ppermute | solution.py:62
  16.8 10.0 %collective-permute-start = (bf16[7488]{0:T(1024)(128)(2,1)S(1)}, bf16[7488]{0:T(1024)(128)(2,1)S(1)}, u32[]{:S(2)}, u32[]{:S(2)}) collective-permute-start(bf16[7488]{0:T(1024)(128)(2,1)S(1)} %pad_maximum_fusion.9), channel_id=1, source_target_pairs={{0,1},{1,2},{2,3},{3,0},{4,5},{5,6},{6,7},{7,4},{8,9},{9,10},{10,1... | collective-permute-start | bytes 44936 | tf_op jit(solution)/shard_map/ppermute | solution.py:62
  18.1 9.9 %collective-permute-start.1 = (bf16[7488]{0:T(1024)(128)(2,1)S(1)}, bf16[7488]{0:T(1024)(128)(2,1)S(1)}, u32[]{:S(2)}, u32[]{:S(2)}) collective-permute-start(bf16[7488]{0:T(1024)(128)(2,1)S(1)} %pad_maximum_fusion.9), channel_id=1, source_target_pairs={{0,2},{1,3},{2,0},{3,1},{4,6},{5,7},{6,4},{7,5},{8,10},{9,11},{10,... | collective-permute-start | bytes 44936 | tf_op jit(solution)/shard_map/ppermute | solution.py:62
  19.2 9.2 %collective-permute-start.2 = (bf16[7488]{0:T(1024)(128)(2,1)S(1)}, bf16[7488]{0:T(1024)(128)(2,1)S(1)}, u32[]{:S(2)}, u32[]{:S(2)}) collective-permute-start(bf16[7488]{0:T(1024)(128)(2,1)S(1)} %pad_maximum_fusion.9), channel_id=1, source_target_pairs={{0,3},{1,0},{2,1},{3,2},{4,7},{5,4},{6,5},{7,6},{8,11},{9,8},{10,9... | collective-permute-start | bytes 44936 | tf_op jit(solution)/shard_map/ppermute | solution.py:62
  21.5 26.2 %collective-permute-start.5 = (bf16[144,1152]{1,0:T(8,128)(2,1)S(1)}, bf16[144,1152]{1,0:T(8,128)(2,1)S(1)}, u32[]{:S(2)}, u32[]{:S(2)}) collective-permute-start(bf16[144,1152]{1,0:T(8,128)(2,1)S(1)} %fusion.5), channel_id=1, source_target_pairs={{0,3},{1,0},{2,1},{3,2},{4,7},{5,4},{6,5},{7,6},{8,11},{9,8},{10,9... | collective-permute-start | bytes 995336 | tf_op jit(solution)/shard_map/ppermute | solution.py:62
  26.8 37.3 %collective-permute-start.4 = (bf16[144,1152]{1,0:T(8,128)(2,1)S(1)}, bf16[144,1152]{1,0:T(8,128)(2,1)S(1)}, u32[]{:S(2)}, u32[]{:S(2)}) collective-permute-start(bf16[144,1152]{1,0:T(8,128)(2,1)S(1)} %fusion.5), channel_id=1, source_target_pairs={{0,2},{1,3},{2,0},{3,1},{4,6},{5,7},{6,4},{7,5},{8,10},{9,11},{10,... | collective-permute-start | bytes 995336 | tf_op jit(solution)/shard_map/ppermute | solution.py:62
  28.8 42.3 %collective-permute-start.9 = (bf16[2,144,1152]{2,1,0:T(8,128)(2,1)S(1)}, bf16[2,144,1152]{2,1,0:T(8,128)(2,1)}, u32[]{:S(2)}, u32[]{:S(2)}) collective-permute-start(bf16[2,144,1152]{2,1,0:T(8,128)(2,1)S(1)} %pad_maximum_fusion.3), channel_id=1, source_target_pairs={{0,16},{8,24},{16,0},{24,8},{1,17},{9,25},{17,1},{25,9},{2,18},{10... | collective-permute-start | bytes 1990664 | tf_op jit(solution)/shard_map/ppermute | solution.py:67
  65.0 25.8 %collective-permute-start.10 = (bf16[2,144,1152]{2,1,0:T(8,128)(2,1)}, bf16[2,144,1152]{2,1,0:T(8,128)(2,1)}, u32[]{:S(2)}, u32[]{:S(2)}) collective-permute-start(bf16[2,144,1152]{2,1,0:T(8,128)(2,1)} %pad_maximum_fusion.4), channel_id=1, source_target_pairs={{0,4},{4,0},{1,5},{5,1},{2,6},{6,2},{3,7},{7,3},{8,12},{12,8},{9,1... | collective-permute-start | bytes 1990664 | tf_op jit(solution)/shard_map/ppermute | solution.py:67
  72.3 48.2 %collective-permute-start.11 = (bf16[4,144,1152]{2,1,0:T(8,128)(2,1)S(1)}, bf16[4,144,1152]{2,1,0:T(8,128)(2,1)}, u32[]{:S(2)}, u32[]{:S(2)}) collective-permute-start(bf16[4,144,1152]{2,1,0:T(8,128)(2,1)S(1)} %pad_maximum_fusion.1.refs_0_), channel_id=1, source_target_pairs={{0,4},{4,0},{1,5},{5,1},{2,6},{6,2},{3,7},{7,3},{8,12},{12,8},{9,1... | collective-permute-start | bytes 3981320 | tf_op jit(solution)/shard_map/ppermute | solution.py:67
  93.1 31.7 %collective-permute-start.12 = (bf16[4,144,1152]{2,1,0:T(8,128)(2,1)}, bf16[4,144,1152]{2,1,0:T(8,128)(2,1)}, u32[]{:S(2)}, u32[]{:S(2)}) collective-permute-start(bf16[4,144,1152]{2,1,0:T(8,128)(2,1)} %pad_maximum_fusion.2.refs_1_), channel_id=1, source_target_pairs={{0,16},{8,24},{16,0},{24,8},{1,17},{9,25},{17,1},{25,9},{2,18},{10... | collective-permute-start | bytes 3981320 | tf_op jit(solution)/shard_map/ppermute | solution.py:67
  94.4 39.2 %collective-permute-start.8 = (f32[3,6912]{1,0:T(4,128)S(1)}, f32[3,6912]{1,0:T(4,128)S(1)}, u32[]{:S(2)}, u32[]{:S(2)}) collective-permute-start(f32[3,6912]{1,0:T(4,128)S(1)} %get-tuple-element.323), channel_id=1, source_target_pairs={{0,3},{1,0},{2,1},{3,2},{4,7},{5,4},{6,5},{7,6},{8,11},{9,8},{10,9... | collective-permute-start | bytes 248840 | tf_op jit(solution)/shard_map/ppermute | solution.py:62
  94.4 39.7 %collective-permute-start.7 = (f32[3,6912]{1,0:T(4,128)S(1)}, f32[3,6912]{1,0:T(4,128)S(1)}, u32[]{:S(2)}, u32[]{:S(2)}) collective-permute-start(f32[3,6912]{1,0:T(4,128)S(1)} %get-tuple-element.324), channel_id=1, source_target_pairs={{0,2},{1,3},{2,0},{3,1},{4,6},{5,7},{6,4},{7,5},{8,10},{9,11},{10,... | collective-permute-start | bytes 248840 | tf_op jit(solution)/shard_map/ppermute | solution.py:62
  94.5 39.7 %collective-permute-start.6 = (f32[3,6912]{1,0:T(4,128)S(1)}, f32[3,6912]{1,0:T(4,128)S(1)}, u32[]{:S(2)}, u32[]{:S(2)}) collective-permute-start(f32[3,6912]{1,0:T(4,128)S(1)} %get-tuple-element.322), channel_id=1, source_target_pairs={{0,1},{1,2},{2,3},{3,0},{4,5},{5,6},{6,7},{7,4},{8,9},{9,10},{10,1... | collective-permute-start | bytes 248840 | tf_op jit(solution)/shard_map/ppermute | solution.py:62
  124.8 13.5 %collective-permute-start.13 = (bf16[4,144,1152]{2,1,0:T(8,128)(2,1)S(1)}, bf16[4,144,1152]{2,1,0:T(8,128)(2,1)}, u32[]{:S(2)}, u32[]{:S(2)}) collective-permute-start(bf16[4,144,1152]{2,1,0:T(8,128)(2,1)S(1)} %pad_maximum_fusion.1.refs_0_), channel_id=1, source_target_pairs={{0,8},{8,0},{16,24},{24,16},{1,9},{9,1},{17,25},{25,17},{2,10},{10... | collective-permute-start | bytes 3981320 | tf_op jit(solution)/shard_map/ppermute | solution.py:67
  133.6 5.1 collective-permute-start.14
  133.6 7.1 collective-permute-start.15
  134.1 8.5 %collective-permute-start.16 = (bf16[4,144,1152]{2,1,0:T(8,128)(2,1)}, bf16[4,144,1152]{2,1,0:T(8,128)(2,1)}, u32[]{:S(2)}, u32[]{:S(2)}) collective-permute-start(bf16[4,144,1152]{2,1,0:T(8,128)(2,1)} %collective-permute-done.12.refs_3_), channel_id=1, source_target_pairs={{0,8},{8,0},{16,24},{24,16},{1,9},{9,1},{17,25},{25,17},{2,10},{10... | collective-permute-start | bytes 3981320 | tf_op jit(solution)/shard_map/ppermute | solution.py:67
  222.3 290.0 %reduce-scatter.6.cloned.1.call-start = ((), (), s32[]{:S(2)}) async-start(), calls=%async_computation.5 | async-start | bytes 6635520 | tf_op jit(solution)/shard_map/reduce_scatter | solution.py:901
  260.6 117.2 %collective-permute-start.17 = (bf16[4,144,4608]{2,1,0:T(8,128)(2,1)}, bf16[4,144,4608]{2,1,0:T(8,128)(2,1)}, u32[]{:S(2)}, u32[]{:S(2)}) collective-permute-start(bf16[4,144,4608]{2,1,0:T(8,128)(2,1)} %dynamic-slice_bitcast_fusion), channel_id=1, source_target_pairs={{0,4},{4,0},{1,5},{5,1},{2,6},{6,2},{3,7},{7,3},{8,12},{12,8},{9,1... | collective-permute-start | bytes 15925256 | tf_op jit(solution)/shard_map/ppermute | solution.py:67
  352.0 54.2 %collective-permute-start.18 = (bf16[4,144,1152]{2,1,0:T(8,128)(2,1)}, bf16[4,144,1152]{2,1,0:T(8,128)(2,1)}, u32[]{:S(2)}, u32[]{:S(2)}) collective-permute-start(bf16[4,144,1152]{2,1,0:T(8,128)(2,1)} %dynamic-slice_bitcast_fusion.2), channel_id=1, source_target_pairs={{0,4},{4,0},{1,5},{5,1},{2,6},{6,2},{3,7},{7,3},{8,12},{12,8},{9,1... | collective-permute-start | bytes 3981320 | tf_op jit(solution)/shard_map/ppermute | solution.py:67
  408.5 3.2 collective-permute-start.19
  409.8 220.0 %reduce-scatter.8.cloned.1.call-start = ((), (), s32[]{:S(2)}) async-start(), calls=%async_computation.6 | async-start | bytes 6635520 | tf_op jit(solution)/shard_map/reduce_scatter | solution.py:901
  409.8 87.3 %collective-permute-start.23 = (bf16[4,144,3456]{2,1,0:T(8,128)(2,1)}, bf16[4,144,3456]{2,1,0:T(8,128)(2,1)}, u32[]{:S(2)}, u32[]{:S(2)}) collective-permute-start(bf16[4,144,3456]{2,1,0:T(8,128)(2,1)} %dynamic-slice_bitcast_fusion.1), channel_id=1, source_target_pairs={{0,4},{4,0},{1,5},{5,1},{2,6},{6,2},{3,7},{7,3},{8,12},{12,8},{9,1... | collective-permute-start | bytes 11943944 | tf_op jit(solution)/shard_map/ppermute | solution.py:67
  412.4 7.8 %collective-permute-start.20 = (bf16[2,33408]{1,0:T(2,128)(2,1)S(1)}, bf16[2,33408]{1,0:T(2,128)(2,1)S(1)}, u32[]{:S(2)}, u32[]{:S(2)}) collective-permute-start(bf16[2,33408]{1,0:T(2,128)(2,1)S(1)} %get-tuple-element.321), channel_id=1, source_target_pairs={{0,1},{1,2},{2,3},{3,0},{4,5},{5,6},{6,7},{7,4},{8,9},{9,10},{10,1... | collective-permute-start | bytes 400904 | tf_op jit(solution)/shard_map/ppermute | solution.py:62
  418.4 15.0 %collective-permute-start.21 = (bf16[2,33408]{1,0:T(2,128)(2,1)S(1)}, bf16[2,33408]{1,0:T(2,128)(2,1)S(1)}, u32[]{:S(2)}, u32[]{:S(2)}) collective-permute-start(bf16[2,33408]{1,0:T(2,128)(2,1)S(1)} %get-tuple-element.321), channel_id=1, source_target_pairs={{0,2},{1,3},{2,0},{3,1},{4,6},{5,7},{6,4},{7,5},{8,10},{9,11},{10,... | collective-permute-start | bytes 400904 | tf_op jit(solution)/shard_map/ppermute | solution.py:62
  418.4 15.1 %collective-permute-start.22 = (bf16[2,33408]{1,0:T(2,128)(2,1)S(1)}, bf16[2,33408]{1,0:T(2,128)(2,1)S(1)}, u32[]{:S(2)}, u32[]{:S(2)}) collective-permute-start(bf16[2,33408]{1,0:T(2,128)(2,1)S(1)} %get-tuple-element.321), channel_id=1, source_target_pairs={{0,3},{1,0},{2,1},{3,2},{4,7},{5,4},{6,5},{7,6},{8,11},{9,8},{10,9... | collective-permute-start | bytes 400904 | tf_op jit(solution)/shard_map/ppermute | solution.py:62
  519.5 4.4 collective-permute-start.25
  526.5 44.7 %collective-permute-start.26 = (bf16[144,6912]{1,0:T(8,128)(2,1)S(1)}, bf16[144,6912]{1,0:T(8,128)(2,1)S(1)}, u32[]{:S(2)}, u32[]{:S(2)}) collective-permute-start(bf16[144,6912]{1,0:T(8,128)(2,1)S(1)} %add_convert_fusion.1), channel_id=1, source_target_pairs={{0,16},{8,24},{16,0},{24,8},{1,17},{9,25},{17,1},{25,9},{2,18},{10... | collective-permute-start | bytes 5971976 | tf_op jit(solution)/shard_map/ppermute | solution.py:67
  527.8 58.6 %collective-permute-start.24 = (bf16[1152,1152]{1,0:T(8,128)(2,1)S(1)}, bf16[1152,1152]{1,0:T(8,128)(2,1)S(1)}, u32[]{:S(2)}, u32[]{:S(2)}) collective-permute-start(bf16[1152,1152]{1,0:T(8,128)(2,1)S(1)} %copy-done.11), channel_id=1, source_target_pairs={{0,4},{4,0},{1,5},{5,1},{2,6},{6,2},{3,7},{7,3},{8,12},{12,8},{9,1... | collective-permute-start | bytes 7962632 | tf_op jit(solution)/shard_map/ppermute | solution.py:67
  536.9 35.9 %collective-permute-start.28 = (bf16[72,4608]{1,0:T(8,128)(2,1)S(1)}, bf16[72,4608]{1,0:T(8,128)(2,1)S(1)}, u32[]{:S(2)}, u32[]{:S(2)}) collective-permute-start(bf16[72,4608]{1,0:T(8,128)(2,1)S(1)} %get-tuple-element.260), channel_id=1, source_target_pairs={{0,8},{8,0},{16,24},{24,16},{1,9},{9,1},{17,25},{25,17},{2,10},{10... | collective-permute-start | bytes 1990664 | tf_op jit(solution)/shard_map/ppermute | solution.py:67
  571.7 18.2 %collective-permute-start.27 = (bf16[144,6912]{1,0:T(8,128)(2,1)S(1)}, bf16[144,6912]{1,0:T(8,128)(2,1)S(1)}, u32[]{:S(2)}, u32[]{:S(2)}) collective-permute-start(bf16[144,6912]{1,0:T(8,128)(2,1)S(1)} %add_convert_fusion.refs_0_), channel_id=1, source_target_pairs={{0,8},{8,0},{16,24},{24,16},{1,9},{9,1},{17,25},{25,17},{2,10},{10... | collective-permute-start | bytes 5971976 | tf_op jit(solution)/shard_map/ppermute | solution.py:67
  573.0 16.7 %collective-permute-start.29 = (bf16[72,4608]{1,0:T(8,128)(2,1)S(1)}, bf16[72,4608]{1,0:T(8,128)(2,1)S(1)}, u32[]{:S(2)}, u32[]{:S(2)}) collective-permute-start(bf16[72,4608]{1,0:T(8,128)(2,1)S(1)} %add_convert_fusion.7), channel_id=1, source_target_pairs={{0,16},{8,24},{16,0},{24,8},{1,17},{9,25},{17,1},{25,9},{2,18},{10... | collective-permute-start | bytes 1990664 | tf_op jit(solution)/shard_map/ppermute | solution.py:67
  586.4 40.4 %collective-permute-start.31 = (bf16[144,4608]{1,0:T(8,128)(2,1)S(1)}, bf16[144,4608]{1,0:T(8,128)(2,1)S(1)}, u32[]{:S(2)}, u32[]{:S(2)}) collective-permute-start(bf16[144,4608]{1,0:T(8,128)(2,1)S(1)} %copy-done.7), channel_id=1, source_target_pairs={{0,4},{4,0},{1,5},{5,1},{2,6},{6,2},{3,7},{7,3},{8,12},{12,8},{9,1... | collective-permute-start | bytes 3981320 | tf_op jit(solution)/shard_map/ppermute | solution.py:67
  607.6 22.2 %collective-permute-start.30 = (bf16[72,4608]{1,0:T(8,128)(2,1)S(1)}, bf16[72,4608]{1,0:T(8,128)(2,1)S(1)}, u32[]{:S(2)}, u32[]{:S(2)}) collective-permute-start(bf16[72,4608]{1,0:T(8,128)(2,1)S(1)} %add_convert_fusion.6.refs_0_), channel_id=1, source_target_pairs={{0,4},{4,0},{1,5},{5,1},{2,6},{6,2},{3,7},{7,3},{8,12},{12,8},{9,1... | collective-permute-start | bytes 1990664 | tf_op jit(solution)/shard_map/ppermute | solution.py:67
  641.4 4.1 collective-permute-start.32
  643.8 30.9 %collective-permute-start.34 = (bf16[144,4608]{1,0:T(8,128)(2,1)}, bf16[144,4608]{1,0:T(8,128)(2,1)S(1)}, u32[]{:S(2)}, u32[]{:S(2)}) collective-permute-start(bf16[144,4608]{1,0:T(8,128)(2,1)} %reduce-scatter.8.cloned.1.call-done.refs_0_), channel_id=1, source_target_pairs={{0,4},{4,0},{1,5},{5,1},{2,6},{6,2},{3,7},{7,3},{8,12},{12,8},{9,1... | collective-permute-start | bytes 3981320 | tf_op jit(solution)/shard_map/ppermute | solution.py:67
  645.6 16.2 %collective-permute-start.33 = (bf16[72,4608]{1,0:T(8,128)(2,1)S(1)}, bf16[72,4608]{1,0:T(8,128)(2,1)S(1)}, u32[]{:S(2)}, u32[]{:S(2)}) collective-permute-start(bf16[72,4608]{1,0:T(8,128)(2,1)S(1)} %add_convert_fusion.5), channel_id=1, source_target_pairs={{0,16},{8,24},{16,0},{24,8},{1,17},{9,25},{17,1},{25,9},{2,18},{10... | collective-permute-start | bytes 1990664 | tf_op jit(solution)/shard_map/ppermute | solution.py:67
  646.0 28.9 %collective-permute-start.35 = (bf16[576,1152]{1,0:T(8,128)(2,1)S(1)}, bf16[576,1152]{1,0:T(8,128)(2,1)S(1)}, u32[]{:S(2)}, u32[]{:S(2)}) collective-permute-start(bf16[576,1152]{1,0:T(8,128)(2,1)S(1)} %copy-done.22), channel_id=1, source_target_pairs={{0,8},{8,0},{16,24},{24,16},{1,9},{9,1},{17,25},{25,17},{2,10},{10... | collective-permute-start | bytes 3981320 | tf_op jit(solution)/shard_map/ppermute | solution.py:67
  675.2 33.8 %collective-permute-start.36 = (bf16[576,1152]{1,0:T(8,128)(2,1)S(1)}, bf16[576,1152]{1,0:T(8,128)(2,1)S(1)}, u32[]{:S(2)}, u32[]{:S(2)}) collective-permute-start(bf16[576,1152]{1,0:T(8,128)(2,1)S(1)} %add_convert_fusion.3), channel_id=1, source_target_pairs={{0,16},{8,24},{16,0},{24,8},{1,17},{9,25},{17,1},{25,9},{2,18},{10... | collective-permute-start | bytes 3981320 | tf_op jit(solution)/shard_map/ppermute | solution.py:67
  675.5 2.9 collective-permute-start.38
  676.7 2.7 collective-permute-start.39
  676.7 32.3 %collective-permute-start.37 = (bf16[72,4608]{1,0:T(8,128)(2,1)S(1)}, bf16[72,4608]{1,0:T(8,128)(2,1)S(1)}, u32[]{:S(2)}, u32[]{:S(2)}) collective-permute-start(bf16[72,4608]{1,0:T(8,128)(2,1)S(1)} %add_convert_fusion.4.refs_0_), channel_id=1, source_target_pairs={{0,4},{4,0},{1,5},{5,1},{2,6},{6,2},{3,7},{7,3},{8,12},{12,8},{9,1... | collective-permute-start | bytes 1990664 | tf_op jit(solution)/shard_map/ppermute | solution.py:67
  709.3 23.6 %collective-permute-start.42 = (bf16[576,1152]{1,0:T(8,128)(2,1)S(1)}, bf16[576,1152]{1,0:T(8,128)(2,1)S(1)}, u32[]{:S(2)}, u32[]{:S(2)}) collective-permute-start(bf16[576,1152]{1,0:T(8,128)(2,1)S(1)} %add_convert_fusion.2.refs_0_), channel_id=1, source_target_pairs={{0,8},{8,0},{16,24},{24,16},{1,9},{9,1},{17,25},{25,17},{2,10},{10... | collective-permute-start | bytes 3981320 | tf_op jit(solution)/shard_map/ppermute | solution.py:67
  709.8 7.7 %collective-permute-start.40 = (bf16[72,4608]{1,0:T(8,128)(2,1)S(1)}, bf16[72,4608]{1,0:T(8,128)(2,1)S(1)}, u32[]{:S(2)}, u32[]{:S(2)}) collective-permute-start(bf16[72,4608]{1,0:T(8,128)(2,1)S(1)} %add_convert_fusion.4.refs_0_), channel_id=1, source_target_pairs={{0,8},{8,0},{16,24},{24,16},{1,9},{9,1},{17,25},{25,17},{2,10},{10... | collective-permute-start | bytes 1990664 | tf_op jit(solution)/shard_map/ppermute | solution.py:67
  710.2 7.4 collective-permute-start.41
  711.0 3.4 collective-permute-start.43
  (43 other events, 579.6 us)
Sparse Core Ops, SparseCore 0:
  11.6 172.9 all-gather.1
  222.4 181.0 reduce-scatter.3
  409.9 102.3 reduce-scatter.5
  520.1 96.1 reduce-scatter.7

commit v6 on v5

--- a/solution.py
+++ b/solution.py
@@ -1010,12 +1010,14 @@
     )
     attn_half = line_sum(attn_both)
     ada_total = sum_far(sum_near(ada_keep, ada_give))
-    one_total = sum_far(sum_near(*adam_own(where, fixes, one_half, [state(3)])))
+    one_near = sum_near(*adam_own(where, fixes, one_half, [state(3)]))
+    one_far = swap_with(one_near, "rep", 2)
     two_there = swap_with(two_line, "dp", 1)
-    two_there, one_half = after(two_there, one_half)
+    ada_total, one_half = after(ada_total, one_half)
     one_there = swap_with(one_half, "dp", 1)
     outer_step(0, [ada_total, swap_with(ada_total, "rep", 1)])
-    two_there, weights_out[0], one_total = after(two_there, weights_out[0], one_total)
+    two_there, weights_out[0], one_far = after(two_there, weights_out[0], one_far)
+    one_total = (one_near.astype(F32) + one_far.astype(F32)).astype(BF16)
     one_pair = swap_with(one_total, "dp", 1)
     reduced[4], firsts_out[4], seconds_out[4], two_keep, two_give = adam_whole(
         "sum", where, fixes, [two_line, two_there], *state(4)
@@ -1030,30 +1032,31 @@
     deltas_out[5] = bias_total / groups
     outers_out[5] = OUTER_MOMENTUM * outer_bias + deltas_out[5]
     weights_out[5] = biases - OUTER_RATE * (deltas_out[5] + OUTER_MOMENTUM * outers_out[5])
-    attn_half, two_keep, two_give = after(attn_half, two_keep, two_give, one_pair, one_there)[:3]
+    attn_half, two_keep, two_give, one_there, one_pair = after(
+        attn_half, two_keep, two_give, one_there, one_pair
+    )
     attn_near = sum_near(*adam_own(where, fixes, attn_half, [state(1), state(2)]))
     attn_there = swap_with(attn_half, "dp", 1)
     attn_far = swap_with(attn_near, "rep", 2)
     reduced[3], firsts_out[3], seconds_out[3] = adam_whole(
         "halves", where, fixes, [one_half, one_there], *state(3)
     )
-    attn_far, attn_there, firsts_out[3] = after(attn_far, attn_there, firsts_out[3])
+    outer_step(
+        3, [one_total, one_pair, swap_with(one_total, "rep", 1), swap_with(one_pair, "rep", 1)]
+    )
+    attn_far, attn_there, firsts_out[3], weights_out[3] = after(
+        attn_far, attn_there, firsts_out[3], weights_out[3]
+    )
     attn_total = (attn_near.astype(F32) + attn_far.astype(F32)).astype(BF16)
     attn_pair = swap_with(attn_total, "dp", 1)
     two_near, attn_total = after(sum_near(two_keep, two_give), attn_total)
     two_far = swap_with(two_near, "rep", 2)
-    outer_step(
-        3, [one_total, one_pair, swap_with(one_total, "rep", 1), swap_with(one_pair, "rep", 1)]
-    )
-    attn_pair, weights_out[3] = after(attn_pair, weights_out[3])
     attn_units = 3
     for index, shift in ((1, 0), (2, attn_units)):
         reduced[index], firsts_out[index], seconds_out[index] = adam_whole(
             "halves", where, fixes, [attn_half, attn_there], *state(index), shift=shift
         )
-    two_far, firsts_out[1], firsts_out[2], weights_out[3] = after(
-        two_far, firsts_out[1], firsts_out[2], weights_out[3]
-    )
+    two_far, firsts_out[1], firsts_out[2] = after(two_far, firsts_out[1], firsts_out[2])
     two_total = (two_near.astype(F32) + two_far.astype(F32)).astype(BF16)
     outer_step(4, [two_total, swap_with(two_total, "rep", 1)])
     totals = [attn_total, attn_pair, swap_with(attn_total, "rep", 1), swap_with(attn_pair, "rep", 1)]

time: 762 us -> 759 us (level)
  transfers between devices with their start and end apart: 49 -> 49, of which waited for: 30 -> 26; matrix products, arithmetic and copies ran while one was open for 7% -> 7% of each run, Pallas kernels for 38% -> 38%
where the time goes in v6:
time: 759 us; the launch traced here: 749 us
  Pallas kernels  340 us (45%)
  waiting for transfers between devices  262 us (35%)
  starting transfers between devices  48.5 us (6%)
  local copies, waits for them, and re-layouts  41.7 us (5%)
  other arithmetic  31 us (4%)
  between operations  16.4 us (2%)
  matrix products  9.15 us (1%)
    ppermute x33, waiting for transfers between devices, swap_with(): return lax.ppermute(value, axis, [(i, i ^ bit) for i in range(size)])  192 us
    pallas_call x5, Pallas kernels, adam_whole(): pl.pallas_call(functools.partial(whole_kernel, mode, rate), grid_spec=plt...  63.9 us
    pallas_call x5, Pallas kernels, outer_whole(): pl.pallas_call(functools.partial(outer_kernel, 1.0 / groups), grid_spec=p...  61.1 us
    ppermute x12, waiting for transfers between devices, shift_by(): lax.ppermute(value, axis, [(i, (i + step) % size) for i in range(size)])  52 us
    ppermute x33, starting transfers between devices, swap_with(): return lax.ppermute(value, axis, [(i, i ^ bit) for i in range(size)])  35.1 us
    pallas_call x3, Pallas kernels, grad_columns(): pl.pallas_call(grad_kernel, grid=(width // rows,), in_specs=[whole_spec((...  29.8 us
    pallas_call x1, Pallas kernels, mlp_rest(): pl.pallas_call(mlp_rest_kernel, grid=(units,), in_specs=[column, column,...  29.2 us
    pallas_call x1, Pallas kernels, attention_forward(): pl.pallas_call(attention_forward_kernel, grid=(slots,), in_specs=[row, ro...  26.7 us
  transfers between devices with their start and end apart: 49, of which 26 were waited for; matrix products, arithmetic and copies ran while one was open for 7% of the time, Pallas kernels for 38%

profile of v6, /device:TPU:1, one launch (start us, length us, event | category | flops | bytes accessed | tf_op | source)
XLA Modules:
  0.0 748.6 jit_solution(10056537145759075572)
XLA Ops:
  22.3 4.5 collective-permute-done
  29.9 17.7 %collective-permute-done.5 = bf16[144,1152]{1,0:T(8,128)(2,1)S(1)} collective-permute-done((bf16[144,1152]{1,0:T(8,128)(2,1)S(1)}, bf16[144,1152]{1,0:T(8,128)(2,1)S(1)}, u32[]{:S(2)}, u32[]{:S(2)}) %collective-permute-start.5) | collective-permute-done | bytes 331808 | tf_op jit(solution)/shard_map/ppermute | solution.py:62
  47.7 16.4 %collective-permute-done.4 = bf16[144,1152]{1,0:T(8,128)(2,1)S(1)} collective-permute-done((bf16[144,1152]{1,0:T(8,128)(2,1)S(1)}, bf16[144,1152]{1,0:T(8,128)(2,1)S(1)}, u32[]{:S(2)}, u32[]{:S(2)}) %collective-permute-start.4) | collective-permute-done | bytes 331808 | tf_op jit(solution)/shard_map/ppermute | solution.py:62
  66.3 4.6 fusion.2
  72.4 18.4 %collective-permute-done.10 = bf16[2,144,1152]{2,1,0:T(8,128)(2,1)} collective-permute-done((bf16[2,144,1152]{2,1,0:T(8,128)(2,1)}, bf16[2,144,1152]{2,1,0:T(8,128)(2,1)}, u32[]{:S(2)}, u32[]{:S(2)}) %collective-permute-start.10) | collective-permute-done | bytes 663584 | tf_op jit(solution)/shard_map/ppermute | solution.py:67
  96.7 23.8 %collective-permute-done.11.refs_2_ = bf16[4,144,1152]{2,1,0:T(8,128)(2,1)} collective-permute-done((bf16[4,144,1152]{2,1,0:T(8,128)(2,1)S(1)}, bf16[4,144,1152]{2,1,0:T(8,128)(2,1)}, u32[]{:S(2)}, u32[]{:S(2)}) %collective-permute-start.11) | collective-permute-done | bytes 1327136 | tf_op jit(solution)/shard_map/ppermute | solution.py:67
  120.5 4.3 collective-permute-done.12.refs_3_
  124.8 8.8 %collective-permute-start.13 = (bf16[4,144,1152]{2,1,0:T(8,128)(2,1)S(1)}, bf16[4,144,1152]{2,1,0:T(8,128)(2,1)}, u32[]{:S(2)}, u32[]{:S(2)}) collective-permute-start(bf16[4,144,1152]{2,1,0:T(8,128)(2,1)S(1)} %pad_maximum_fusion.1.refs_0_), channel_id=1, source_target_pairs={{0,8},{8,0},{16,24},{24,16},{1,9},{9,1},{17,25},{25,17},{2,10},{10... | collective-permute-start | bytes 3981320 | tf_op jit(solution)/shard_map/ppermute | solution.py:67
  134.4 3.9 collective-permute-done.13.refs_4_
  142.6 9.0 %shard_map.590 = bf16[32,144,1152]{2,1,0:T(8,128)(2,1)} custom-call(s32[32]{0:T(128)S(1)} %stack.178.order_ref, bf16[4,144,1152]{2,1,0:T(8,128)(2,1)S(1)} %pad_maximum_fusion.1.refs_0_, bf16[4,144,1152]{2,1,0:T(8,128)(2,1)} %pad_maximum_fusion.2.refs_1_, bf16[4,144,1152]{2,1,0:T(8,128)(2,1)} %collective-permute-done.11.refs_2_, ...), custom_call_target="tpu_custom_call" | custom-call | bytes 21233664 | tf_op jit(solution)/shard_map/pallas_call | solution.py:729
  151.6 26.7 %shard_map.591 = (bf16[768,1152]{1,0:T(8,128)(2,1)S(1)}, bf16[768,3456]{1,0:T(8,128)(2,1)}, bf16[768,1152]{1,0:T(8,128)(2,1)S(1)}, f32[768,128]{1,0:T(8,128)S(1)...) custom-call(bf16[768,1152]{1,0:T(8,128)(2,1)} %bitcast.176, ...), custom_call_target="tpu_custom_call" | custom-call | flops 8153726976 | bytes 41943040 | tf_op jit(solution)/shard_map/pallas_call | solution.py:190
  186.1 21.3 %shard_map.592 = (bf16[768,4608]{1,0:T(8,128)(2,1)}, bf16[768,4608]{1,0:T(8,128)(2,1)}) custom-call(bf16[768,1152]{1,0:T(8,128)(2,1)S(1)} %copy-done.28, bf16[4,4,2,2,144,1152]{5,4,3,2,1,0:T(8,128)(2,1)} %bitcast.227, f32[1,4608]{1,0:T(1,128)S(1)} %reshape.445.bias_ref), custom_call_target="tpu_custom_call" | custom-call | flops 8153726976 | bytes 27262976 | tf_op jit(solution)/shard_map/pallas_call | solution.py:256
  207.3 14.9 %shard_map.593 = bf16[4608,1152]{1,0:T(8,128)(2,1)} custom-call(bf16[768,4608]{1,0:T(8,128)(2,1)} %get-tuple-element.206.left_ref.act_ref, bf16[768,1152]{1,0:T(8,128)(2,1)S(1)} %copy-done.23), custom_call_target="tpu_custom_call" | custom-call | flops 8153726976 | bytes 24772608 | tf_op jit(solution)/shard_map/pallas_call | solution.py:501
  223.7 16.7 %shard_map.594 = (bf16[768,4608]{1,0:T(8,128)(2,1)}, f32[8,4608]{1,0:T(8,128)S(1)}) custom-call(bf16[768,1152]{1,0:T(8,128)(2,1)S(1)} %copy-done.24, bf16[4,4,2,2,144,1152]{5,4,3,2,1,0:T(8,128)(2,1)} %bitcast.228, bf16[768,4608]{1,0:T(8,128)(2,1)} %get-tuple-element.209.slope_ref), custom_call_target="tpu_custom_call" | custom-call | flops 8153726976 | bytes 27262976 | tf_op jit(solution)/shard_map/pallas_call | solution.py:287
  240.4 14.9 %shard_map.595 = bf16[1152,4608]{1,0:T(8,128)(2,1)} custom-call(bf16[768,1152]{1,0:T(8,128)(2,1)S(1)} %copy-done.29, bf16[768,4608]{1,0:T(8,128)(2,1)} %get-tuple-element.211.right_ref.d_hidden_ref), custom_call_target="tpu_custom_call" | custom-call | flops 8153726976 | bytes 24772608 | tf_op jit(solution)/shard_map/pallas_call | solution.py:485
  255.4 5.2 dynamic-slice_bitcast_fusion
  264.0 29.2 %shard_map.596 = (f32[768,1152]{1,0:T(8,128)S(1)}, f32[768,1152]{1,0:T(8,128)}) custom-call(bf16[768,4608]{1,0:T(8,128)(2,1)} %get-tuple-element.206.left_ref.act_ref, bf16[768,4608]{1,0:T(8,128)(2,1)} %get-tuple-element.211.right_ref.d_hidden_ref, bf16[4,4,2,2,144,1152]{5,4,3,2,1,0:T(8,128)(2,1)} %bitcast.229, bf16[4,4,2,2,144,1152]{5,4,3,2,1,0:T(8,128)(2,1)} %bitcast.230), custom_call_target="tpu_custom_call" | custom-call | flops 16307453952 | bytes 44040192 | tf_op jit(solution)/shard_map/pallas_call | solution.py:325
  295.0 12.4 %shard_map.597 = (bf16[768,1152]{1,0:T(8,128)(2,1)}, f32[768,1152]{1,0:T(8,128)}, bf16[768,1152]{1,0:T(8,128)(2,1)S(1)}, bf16[768,1152]{1,0:T(8,128)(2,1)S(1)}, f32[3,8,1152]{2,1,0:T(8,128)S(1)}) custom-call(f32[768,1152]{1,0:T(8,128)} %copy-done.9, f32[8,1152]{1,0:T(8,128)S(1)} %scatter.19.bias_ref, f32[768,1152]{1,0:T(8,128)} %get-tuple-element.213.d_in_ref, ...), custom_call_target="tpu_custom_call" | custom-call | flops 2038431744 | bytes 31457280 | tf_op jit(solution)/shard_map/pallas_call | solution.py:366
  311.7 24.0 %shard_map.599 = (bf16[768,3456]{1,0:T(8,128)(2,1)}, f32[3,8,1152]{2,1,0:T(8,128)S(1)}) custom-call(bf16[768,3456]{1,0:T(8,128)(2,1)} %get-tuple-element.219.packed_ref, bf16[768,1152]{1,0:T(8,128)(2,1)S(1)} %get-tuple-element.223.d_att_ref, f32[768,128]{1,0:T(8,128)S(1)} %get-tuple-element.224.log_ref), custom_call_target="tpu_custom_call" | custom-call | flops 8053063680 | bytes 14680064 | tf_op jit(solution)/shard_map/pallas_call | solution.py:421
  335.7 11.9 %shard_map.600 = bf16[1152,3456]{1,0:T(8,128)(2,1)} custom-call(bf16[768,1152]{1,0:T(8,128)(2,1)S(1)} %copy-done.31, bf16[768,3456]{1,0:T(8,128)(2,1)} %get-tuple-element.228.right_ref.d_packed_ref), custom_call_target="tpu_custom_call" | custom-call | flops 6115295232 | bytes 18579456 | tf_op jit(solution)/shard_map/pallas_call | solution.py:485
  347.6 4.5 dynamic-slice_bitcast_fusion.1
  354.3 14.1 %shard_map.601 = (bf16[768,1152]{1,0:T(8,128)(2,1)}, f32[3,8,1152]{2,1,0:T(8,128)S(1)}) custom-call(bf16[768,3456]{1,0:T(8,128)(2,1)} %get-tuple-element.228.right_ref.d_packed_ref, bf16[4,1152,1152]{2,1,0:T(8,128)(2,1)} %bitcast.184, bf16[768,1152]{1,0:T(8,128)(2,1)S(1)} %bitcast.177, f32[768,1152]{1,0:T(8,128)S(1)} %copy-done.19, ...), custom_call_target="tpu_custom_call" | custom-call | flops 6115295232 | bytes 20971520 | tf_op jit(solution)/shard_map/pallas_call | solution.py:453
  368.4 9.4 %collective-permute-done.17 = bf16[4,144,4608]{2,1,0:T(8,128)(2,1)} collective-permute-done((bf16[4,144,4608]{2,1,0:T(8,128)(2,1)}, bf16[4,144,4608]{2,1,0:T(8,128)(2,1)}, u32[]{:S(2)}, u32[]{:S(2)}) %collective-permute-start.17) | collective-permute-done | bytes 5308448 | tf_op jit(solution)/shard_map/ppermute | solution.py:67
  377.8 7.8 %fusion = bf16[4,144,4608]{2,1,0:T(8,128)(2,1)} fusion(bf16[4,144,4608]{2,1,0:T(8,128)(2,1)} %collective-permute-done.17, bf16[4,2,144,4608]{3,2,1,0:T(8,128)(2,1)} %bitcast.202, s32[]{:T(128)S(6)} %select_n.139), kind=kLoop, calls=%fused_computation.2 | loop fusion | flops 10616832 | bytes 15925252 | tf_op jit(solution)/shard_map/convert_element_type | solution.py:906
  385.6 20.6 %collective-permute-done.18 = bf16[4,144,1152]{2,1,0:T(8,128)(2,1)} collective-permute-done((bf16[4,144,1152]{2,1,0:T(8,128)(2,1)}, bf16[4,144,1152]{2,1,0:T(8,128)(2,1)}, u32[]{:S(2)}, u32[]{:S(2)}) %collective-permute-start.18) | collective-permute-done | bytes 1327136 | tf_op jit(solution)/shard_map/ppermute | solution.py:67
  414.9 3.5 fusion.4
  420.3 13.1 %collective-permute-done.21 = bf16[2,33408]{1,0:T(2,128)(2,1)S(1)} collective-permute-done((bf16[2,33408]{1,0:T(2,128)(2,1)S(1)}, bf16[2,33408]{1,0:T(2,128)(2,1)S(1)}, u32[]{:S(2)}, u32[]{:S(2)}) %collective-permute-start.21) | collective-permute-done | bytes 133664 | tf_op jit(solution)/shard_map/ppermute | solution.py:62
  434.1 4.6 fusion.10
  438.7 21.9 %shard_map.602 = (f32[2,144,6912]{2,1,0:T(8,128)}, f32[2,144,6912]{2,1,0:T(8,128)}, bf16[144,6912]{1,0:T(8,128)(2,1)S(1)}, bf16[144,6912]{1,0:T(8,128)(2,1)}) custom-call(s32[2]{0:T(128)S(1)} %pad_add_fusion.where_ref, f32[2]{0:T(128)S(1)} %pad_maximum_fusion.10.fix_ref, f32[2,144,6912]{2,1,0:T(8,128)} %bitcast.180, f32[2,144,6912]{2,1,0:T(8,128)} %bitcast.178, ...), custom_call_target="tpu_custom_call" | custom-call | flops 1024 | bytes 1024 | tf_op jit(solution)/shard_map/pallas_call | solution.py:580
  462.2 34.9 %collective-permute-done.23 = bf16[4,144,3456]{2,1,0:T(8,128)(2,1)} collective-permute-done((bf16[4,144,3456]{2,1,0:T(8,128)(2,1)}, bf16[4,144,3456]{2,1,0:T(8,128)(2,1)}, u32[]{:S(2)}, u32[]{:S(2)}) %collective-permute-start.23) | collective-permute-done | bytes 3981344 | tf_op jit(solution)/shard_map/ppermute | solution.py:67
  497.1 15.2 %reduce-scatter.6.cloned.1.call-done.refs_0_ = bf16[144,4608]{1,0:T(8,128)(2,1)} async-done(((bf16[576,4608]{1,0:T(8,128)(2,1)}), bf16[144,4608]{1,0:T(8,128)(2,1)}) %reduce-scatter.6.cloned.1.call-update) | async-done | bytes 1327120 | tf_op jit(solution)/shard_map/reduce_scatter | solution.py:901
  512.3 4.4 fusion.1
  520.0 3.9 collective-permute-done.25
  529.0 8.0 %shard_map.604 = (bf16[72,4608]{1,0:T(8,128)(2,1)S(1)}, bf16[72,4608]{1,0:T(8,128)(2,1)S(1)}) custom-call(s32[2]{0:T(128)S(1)} %pad_add_fusion.where_ref, f32[2]{0:T(128)S(1)} %pad_maximum_fusion.10.fix_ref, bf16[2,72,4608]{2,1,0:T(8,128)(2,1)S(1)} %bitcast.169, f32[2,2,72,4608]{3,2,1,0:T(8,128)} %bitcast.185, f32[2,2,72,4608]{3,2,1,0:T(8,128)} %bitcast.190, ...), custom_call_target="tpu_custom_call" | custom-call | flops 1024 | bytes 1024 | tf_op jit(solution)/shard_map/pallas_call | solution.py:644
  537.9 33.3 %collective-permute-done.26 = bf16[144,6912]{1,0:T(8,128)(2,1)S(1)} collective-permute-done((bf16[144,6912]{1,0:T(8,128)(2,1)S(1)}, bf16[144,6912]{1,0:T(8,128)(2,1)S(1)}, u32[]{:S(2)}, u32[]{:S(2)}) %collective-permute-start.26) | collective-permute-done | bytes 1990688 | tf_op jit(solution)/shard_map/ppermute | solution.py:67
  576.5 17.8 %shard_map.603 = (f32[2,144,6912]{2,1,0:T(8,128)}, f32[2,144,6912]{2,1,0:T(8,128)}, f32[2,144,6912]{2,1,0:T(8,128)}) custom-call(s32[2]{0:T(128)S(1)} %pad_add_fusion.where_ref, bf16[144,6912]{1,0:T(8,128)(2,1)S(1)} %add_convert_fusion.refs_0_, bf16[144,6912]{1,0:T(8,128)(2,1)S(1)} %collective-permute-done.27.refs_1_, f32[2,144,6912]{2,1,0:T(8,128)} %bitcast.179, ...), custom_call_target="tpu_custom_call" | custom-call | flops 1024 | bytes 1024 | tf_op jit(solution)/shard_map/pallas_call | solution.py:692
  595.8 16.0 %shard_map.605 = (f32[2,576,1152]{2,1,0:T(8,128)}, f32[2,576,1152]{2,1,0:T(8,128)}, f32[2,576,1152]{2,1,0:T(8,128)}, bf16[576,1152]{1,0:T(8,128)(2,1)S(1)}, bf16[576,1152]{1,0:T(8,128)(2,1)S(1)}) custom-call(s32[2]{0:T(128)S(1)} %pad_add_fusion.where_ref, f32[2]{0:T(128)S(1)} %pad_maximum_fusion.10.fix_ref, bf16[2,576,1152]{2,1,0:T(8,128)(2,1)S(1)} %bitcast.172, ...), custom_call_target="tpu_custom_call" | custom-call | flops 1024 | bytes 1024 | tf_op jit(solution)/shard_map/pallas_call | solution.py:580
  615.9 13.1 %collective-permute-done.31.refs_1_ = bf16[72,4608]{1,0:T(8,128)(2,1)S(1)} collective-permute-done((bf16[72,4608]{1,0:T(8,128)(2,1)S(1)}, bf16[72,4608]{1,0:T(8,128)(2,1)S(1)}, u32[]{:S(2)}, u32[]{:S(2)}) %collective-permute-start.31) | collective-permute-done | bytes 663584 | tf_op jit(solution)/shard_map/ppermute | solution.py:67
  631.6 8.9 %shard_map.606 = (bf16[72,4608]{1,0:T(8,128)(2,1)S(1)}, bf16[72,4608]{1,0:T(8,128)(2,1)S(1)}) custom-call(s32[2]{0:T(128)S(1)} %pad_add_fusion.where_ref, f32[2]{0:T(128)S(1)} %pad_maximum_fusion.10.fix_ref, bf16[2,72,4608]{2,1,0:T(8,128)(2,1)} %bitcast.80.g_ref, f32[2,2,72,3456]{3,2,1,0:T(8,128)} %bitcast.195, f32[2,2,72,3456]{3,2,1,0:T(8,128)} %bitcast.197, ...), custom_call_target="tpu_custom_call" | custom-call | flops 1024 | bytes 1024 | tf_op jit(solution)/shard_map/pallas_call | solution.py:644
  645.0 12.1 %shard_map.607 = (f32[2,144,4608]{2,1,0:T(8,128)}, f32[2,144,4608]{2,1,0:T(8,128)}, f32[2,144,4608]{2,1,0:T(8,128)}) custom-call(s32[2]{0:T(128)S(1)} %pad_add_fusion.where_ref, f32[2]{0:T(128)S(1)} %pad_maximum_fusion.10.fix_ref, bf16[144,4608]{1,0:T(8,128)(2,1)S(1)} %copy-done.8, bf16[144,4608]{1,0:T(8,128)(2,1)S(1)} %copy-done.18, ...), custom_call_target="tpu_custom_call" | custom-call | flops 1024 | bytes 1024 | tf_op jit(solution)/shard_map/pallas_call | solution.py:580
  657.1 15.8 %shard_map.608 = (f32[2,2,72,4608]{3,2,1,0:T(8,128)}, f32[2,2,72,4608]{3,2,1,0:T(8,128)}, f32[2,2,72,4608]{3,2,1,0:T(8,128)}) custom-call(s32[2]{0:T(128)S(1)} %pad_add_fusion.where_ref, bf16[72,4608]{1,0:T(8,128)(2,1)S(1)} %add_convert_fusion.6.refs_0_, bf16[72,4608]{1,0:T(8,128)(2,1)S(1)} %collective-permute-done.31.refs_1_, ...), custom_call_target="tpu_custom_call" | custom-call | flops 1024 | bytes 1024 | tf_op jit(solution)/shard_map/pallas_call | solution.py:692
  677.1 10.2 %shard_map.609 = (f32[2,144,3456]{2,1,0:T(8,128)}, f32[2,144,3456]{2,1,0:T(8,128)}, f32[2,144,3456]{2,1,0:T(8,128)}) custom-call(s32[2]{0:T(128)S(1)} %pad_add_fusion.where_ref, f32[2]{0:T(128)S(1)} %pad_maximum_fusion.10.fix_ref, bf16[144,4608]{1,0:T(8,128)(2,1)} %reduce-scatter.8.cloned.1.call-done.refs_0_, ...), custom_call_target="tpu_custom_call" | custom-call | flops 1024 | bytes 1024 | tf_op jit(solution)/shard_map/pallas_call | solution.py:580
  687.3 3.7 shard_map.610
  691.0 14.3 %collective-permute-done.38 = bf16[576,1152]{1,0:T(8,128)(2,1)S(1)} collective-permute-done((bf16[576,1152]{1,0:T(8,128)(2,1)S(1)}, bf16[576,1152]{1,0:T(8,128)(2,1)S(1)}, u32[]{:S(2)}, u32[]{:S(2)}) %collective-permute-start.38) | collective-permute-done | bytes 1327136 | tf_op jit(solution)/shard_map/ppermute | solution.py:67
  707.9 3.3 collective-permute-done.43
  714.3 12.3 %shard_map.611 = (f32[2,2,72,3456]{3,2,1,0:T(8,128)}, f32[2,2,72,3456]{3,2,1,0:T(8,128)}, f32[2,2,72,3456]{3,2,1,0:T(8,128)}) custom-call(s32[2]{0:T(128)S(1)} %pad_add_fusion.where_ref, bf16[72,4608]{1,0:T(8,128)(2,1)S(1)} %add_convert_fusion.4.refs_0_, bf16[72,4608]{1,0:T(8,128)(2,1)S(1)} %collective-permute-done.39.refs_1_, ...), custom_call_target="tpu_custom_call" | custom-call | flops 1024 | bytes 1024 | tf_op jit(solution)/shard_map/pallas_call | solution.py:692
  726.6 3.1 shard_map.612
  729.7 12.2 %shard_map.613 = (f32[2,576,1152]{2,1,0:T(8,128)}, f32[2,576,1152]{2,1,0:T(8,128)}, f32[2,576,1152]{2,1,0:T(8,128)}) custom-call(s32[2]{0:T(128)S(1)} %pad_add_fusion.where_ref, bf16[576,1152]{1,0:T(8,128)(2,1)S(1)} %add_convert_fusion.2.refs_0_, bf16[576,1152]{1,0:T(8,128)(2,1)S(1)} %collective-permute-done.42.refs_1_, f32[2,576,1152]{2,1,0:T(8,128)} %bitcast.188, ...), custom_call_target="tpu_custom_call" | custom-call | flops 1024 | bytes 1024 | tf_op jit(solution)/shard_map/pallas_call | solution.py:692
  (273 shorter events, 101.8 us)
Async XLA Ops:
  7.3 177.3 %all-gather.2.cloned.1.call-start = ((), (), s32[]{:S(2)}) async-start(), calls=%async_computation.3 | async-start | bytes 21897216 | tf_op jit(solution)/shard_map/all_gather | solution.py:851
  10.7 395.5 %reduce-scatter.4.cloned.1.call-start = ((), (), s32[]{:S(2)}) async-start(), calls=%async_computation.4 | async-start | bytes 13271040 | tf_op jit(solution)/shard_map/reduce_scatter | solution.py:901
  14.6 14.1 %collective-permute-start.3 = (bf16[144,1152]{1,0:T(8,128)(2,1)S(1)}, bf16[144,1152]{1,0:T(8,128)(2,1)S(1)}, u32[]{:S(2)}, u32[]{:S(2)}) collective-permute-start(bf16[144,1152]{1,0:T(8,128)(2,1)S(1)} %fusion.5), channel_id=1, source_target_pairs={{0,1},{1,2},{2,3},{3,0},{4,5},{5,6},{6,7},{7,4},{8,9},{9,10},{10,1... | collective-permute-start | bytes 995336 | tf_op jit(solution)/shard_map/ppermute | solution.py:62
  16.8 10.0 %collective-permute-start = (bf16[7488]{0:T(1024)(128)(2,1)S(1)}, bf16[7488]{0:T(1024)(128)(2,1)S(1)}, u32[]{:S(2)}, u32[]{:S(2)}) collective-permute-start(bf16[7488]{0:T(1024)(128)(2,1)S(1)} %pad_maximum_fusion.9), channel_id=1, source_target_pairs={{0,1},{1,2},{2,3},{3,0},{4,5},{5,6},{6,7},{7,4},{8,9},{9,10},{10,1... | collective-permute-start | bytes 44936 | tf_op jit(solution)/shard_map/ppermute | solution.py:62
  18.1 9.9 %collective-permute-start.1 = (bf16[7488]{0:T(1024)(128)(2,1)S(1)}, bf16[7488]{0:T(1024)(128)(2,1)S(1)}, u32[]{:S(2)}, u32[]{:S(2)}) collective-permute-start(bf16[7488]{0:T(1024)(128)(2,1)S(1)} %pad_maximum_fusion.9), channel_id=1, source_target_pairs={{0,2},{1,3},{2,0},{3,1},{4,6},{5,7},{6,4},{7,5},{8,10},{9,11},{10,... | collective-permute-start | bytes 44936 | tf_op jit(solution)/shard_map/ppermute | solution.py:62
  19.2 9.2 %collective-permute-start.2 = (bf16[7488]{0:T(1024)(128)(2,1)S(1)}, bf16[7488]{0:T(1024)(128)(2,1)S(1)}, u32[]{:S(2)}, u32[]{:S(2)}) collective-permute-start(bf16[7488]{0:T(1024)(128)(2,1)S(1)} %pad_maximum_fusion.9), channel_id=1, source_target_pairs={{0,3},{1,0},{2,1},{3,2},{4,7},{5,4},{6,5},{7,6},{8,11},{9,8},{10,9... | collective-permute-start | bytes 44936 | tf_op jit(solution)/shard_map/ppermute | solution.py:62
  21.5 26.2 %collective-permute-start.5 = (bf16[144,1152]{1,0:T(8,128)(2,1)S(1)}, bf16[144,1152]{1,0:T(8,128)(2,1)S(1)}, u32[]{:S(2)}, u32[]{:S(2)}) collective-permute-start(bf16[144,1152]{1,0:T(8,128)(2,1)S(1)} %fusion.5), channel_id=1, source_target_pairs={{0,3},{1,0},{2,1},{3,2},{4,7},{5,4},{6,5},{7,6},{8,11},{9,8},{10,9... | collective-permute-start | bytes 995336 | tf_op jit(solution)/shard_map/ppermute | solution.py:62
  26.8 37.3 %collective-permute-start.4 = (bf16[144,1152]{1,0:T(8,128)(2,1)S(1)}, bf16[144,1152]{1,0:T(8,128)(2,1)S(1)}, u32[]{:S(2)}, u32[]{:S(2)}) collective-permute-start(bf16[144,1152]{1,0:T(8,128)(2,1)S(1)} %fusion.5), channel_id=1, source_target_pairs={{0,2},{1,3},{2,0},{3,1},{4,6},{5,7},{6,4},{7,5},{8,10},{9,11},{10,... | collective-permute-start | bytes 995336 | tf_op jit(solution)/shard_map/ppermute | solution.py:62
  28.8 42.3 %collective-permute-start.9 = (bf16[2,144,1152]{2,1,0:T(8,128)(2,1)S(1)}, bf16[2,144,1152]{2,1,0:T(8,128)(2,1)}, u32[]{:S(2)}, u32[]{:S(2)}) collective-permute-start(bf16[2,144,1152]{2,1,0:T(8,128)(2,1)S(1)} %pad_maximum_fusion.3), channel_id=1, source_target_pairs={{0,16},{8,24},{16,0},{24,8},{1,17},{9,25},{17,1},{25,9},{2,18},{10... | collective-permute-start | bytes 1990664 | tf_op jit(solution)/shard_map/ppermute | solution.py:67
  65.0 25.8 %collective-permute-start.10 = (bf16[2,144,1152]{2,1,0:T(8,128)(2,1)}, bf16[2,144,1152]{2,1,0:T(8,128)(2,1)}, u32[]{:S(2)}, u32[]{:S(2)}) collective-permute-start(bf16[2,144,1152]{2,1,0:T(8,128)(2,1)} %pad_maximum_fusion.4), channel_id=1, source_target_pairs={{0,4},{4,0},{1,5},{5,1},{2,6},{6,2},{3,7},{7,3},{8,12},{12,8},{9,1... | collective-permute-start | bytes 1990664 | tf_op jit(solution)/shard_map/ppermute | solution.py:67
  72.3 48.2 %collective-permute-start.11 = (bf16[4,144,1152]{2,1,0:T(8,128)(2,1)S(1)}, bf16[4,144,1152]{2,1,0:T(8,128)(2,1)}, u32[]{:S(2)}, u32[]{:S(2)}) collective-permute-start(bf16[4,144,1152]{2,1,0:T(8,128)(2,1)S(1)} %pad_maximum_fusion.1.refs_0_), channel_id=1, source_target_pairs={{0,4},{4,0},{1,5},{5,1},{2,6},{6,2},{3,7},{7,3},{8,12},{12,8},{9,1... | collective-permute-start | bytes 3981320 | tf_op jit(solution)/shard_map/ppermute | solution.py:67
  93.1 31.7 %collective-permute-start.12 = (bf16[4,144,1152]{2,1,0:T(8,128)(2,1)}, bf16[4,144,1152]{2,1,0:T(8,128)(2,1)}, u32[]{:S(2)}, u32[]{:S(2)}) collective-permute-start(bf16[4,144,1152]{2,1,0:T(8,128)(2,1)} %pad_maximum_fusion.2.refs_1_), channel_id=1, source_target_pairs={{0,16},{8,24},{16,0},{24,8},{1,17},{9,25},{17,1},{25,9},{2,18},{10... | collective-permute-start | bytes 3981320 | tf_op jit(solution)/shard_map/ppermute | solution.py:67
  94.4 39.2 %collective-permute-start.8 = (f32[3,6912]{1,0:T(4,128)S(1)}, f32[3,6912]{1,0:T(4,128)S(1)}, u32[]{:S(2)}, u32[]{:S(2)}) collective-permute-start(f32[3,6912]{1,0:T(4,128)S(1)} %get-tuple-element.323), channel_id=1, source_target_pairs={{0,3},{1,0},{2,1},{3,2},{4,7},{5,4},{6,5},{7,6},{8,11},{9,8},{10,9... | collective-permute-start | bytes 248840 | tf_op jit(solution)/shard_map/ppermute | solution.py:62
  94.4 39.7 %collective-permute-start.7 = (f32[3,6912]{1,0:T(4,128)S(1)}, f32[3,6912]{1,0:T(4,128)S(1)}, u32[]{:S(2)}, u32[]{:S(2)}) collective-permute-start(f32[3,6912]{1,0:T(4,128)S(1)} %get-tuple-element.324), channel_id=1, source_target_pairs={{0,2},{1,3},{2,0},{3,1},{4,6},{5,7},{6,4},{7,5},{8,10},{9,11},{10,... | collective-permute-start | bytes 248840 | tf_op jit(solution)/shard_map/ppermute | solution.py:62
  94.5 39.7 %collective-permute-start.6 = (f32[3,6912]{1,0:T(4,128)S(1)}, f32[3,6912]{1,0:T(4,128)S(1)}, u32[]{:S(2)}, u32[]{:S(2)}) collective-permute-start(f32[3,6912]{1,0:T(4,128)S(1)} %get-tuple-element.322), channel_id=1, source_target_pairs={{0,1},{1,2},{2,3},{3,0},{4,5},{5,6},{6,7},{7,4},{8,9},{9,10},{10,1... | collective-permute-start | bytes 248840 | tf_op jit(solution)/shard_map/ppermute | solution.py:62
  124.8 13.5 %collective-permute-start.13 = (bf16[4,144,1152]{2,1,0:T(8,128)(2,1)S(1)}, bf16[4,144,1152]{2,1,0:T(8,128)(2,1)}, u32[]{:S(2)}, u32[]{:S(2)}) collective-permute-start(bf16[4,144,1152]{2,1,0:T(8,128)(2,1)S(1)} %pad_maximum_fusion.1.refs_0_), channel_id=1, source_target_pairs={{0,8},{8,0},{16,24},{24,16},{1,9},{9,1},{17,25},{25,17},{2,10},{10... | collective-permute-start | bytes 3981320 | tf_op jit(solution)/shard_map/ppermute | solution.py:67
  133.6 5.1 collective-permute-start.14
  133.6 7.1 collective-permute-start.15
  134.1 8.5 %collective-permute-start.16 = (bf16[4,144,1152]{2,1,0:T(8,128)(2,1)}, bf16[4,144,1152]{2,1,0:T(8,128)(2,1)}, u32[]{:S(2)}, u32[]{:S(2)}) collective-permute-start(bf16[4,144,1152]{2,1,0:T(8,128)(2,1)} %collective-permute-done.12.refs_3_), channel_id=1, source_target_pairs={{0,8},{8,0},{16,24},{24,16},{1,9},{9,1},{17,25},{25,17},{2,10},{10... | collective-permute-start | bytes 3981320 | tf_op jit(solution)/shard_map/ppermute | solution.py:67
  222.3 290.0 %reduce-scatter.6.cloned.1.call-start = ((), (), s32[]{:S(2)}) async-start(), calls=%async_computation.5 | async-start | bytes 6635520 | tf_op jit(solution)/shard_map/reduce_scatter | solution.py:901
  260.6 117.2 %collective-permute-start.17 = (bf16[4,144,4608]{2,1,0:T(8,128)(2,1)}, bf16[4,144,4608]{2,1,0:T(8,128)(2,1)}, u32[]{:S(2)}, u32[]{:S(2)}) collective-permute-start(bf16[4,144,4608]{2,1,0:T(8,128)(2,1)} %dynamic-slice_bitcast_fusion), channel_id=1, source_target_pairs={{0,4},{4,0},{1,5},{5,1},{2,6},{6,2},{3,7},{7,3},{8,12},{12,8},{9,1... | collective-permute-start | bytes 15925256 | tf_op jit(solution)/shard_map/ppermute | solution.py:67
  352.0 54.2 %collective-permute-start.18 = (bf16[4,144,1152]{2,1,0:T(8,128)(2,1)}, bf16[4,144,1152]{2,1,0:T(8,128)(2,1)}, u32[]{:S(2)}, u32[]{:S(2)}) collective-permute-start(bf16[4,144,1152]{2,1,0:T(8,128)(2,1)} %dynamic-slice_bitcast_fusion.2), channel_id=1, source_target_pairs={{0,4},{4,0},{1,5},{5,1},{2,6},{6,2},{3,7},{7,3},{8,12},{12,8},{9,1... | collective-permute-start | bytes 3981320 | tf_op jit(solution)/shard_map/ppermute | solution.py:67
  408.5 3.2 collective-permute-start.19
  409.8 219.2 %reduce-scatter.8.cloned.1.call-start = ((), (), s32[]{:S(2)}) async-start(), calls=%async_computation.6 | async-start | bytes 6635520 | tf_op jit(solution)/shard_map/reduce_scatter | solution.py:901
  409.8 87.3 %collective-permute-start.23 = (bf16[4,144,3456]{2,1,0:T(8,128)(2,1)}, bf16[4,144,3456]{2,1,0:T(8,128)(2,1)}, u32[]{:S(2)}, u32[]{:S(2)}) collective-permute-start(bf16[4,144,3456]{2,1,0:T(8,128)(2,1)} %dynamic-slice_bitcast_fusion.1), channel_id=1, source_target_pairs={{0,4},{4,0},{1,5},{5,1},{2,6},{6,2},{3,7},{7,3},{8,12},{12,8},{9,1... | collective-permute-start | bytes 11943944 | tf_op jit(solution)/shard_map/ppermute | solution.py:67
  412.4 7.8 %collective-permute-start.20 = (bf16[2,33408]{1,0:T(2,128)(2,1)S(1)}, bf16[2,33408]{1,0:T(2,128)(2,1)S(1)}, u32[]{:S(2)}, u32[]{:S(2)}) collective-permute-start(bf16[2,33408]{1,0:T(2,128)(2,1)S(1)} %get-tuple-element.321), channel_id=1, source_target_pairs={{0,1},{1,2},{2,3},{3,0},{4,5},{5,6},{6,7},{7,4},{8,9},{9,10},{10,1... | collective-permute-start | bytes 400904 | tf_op jit(solution)/shard_map/ppermute | solution.py:62
  418.4 15.0 %collective-permute-start.21 = (bf16[2,33408]{1,0:T(2,128)(2,1)S(1)}, bf16[2,33408]{1,0:T(2,128)(2,1)S(1)}, u32[]{:S(2)}, u32[]{:S(2)}) collective-permute-start(bf16[2,33408]{1,0:T(2,128)(2,1)S(1)} %get-tuple-element.321), channel_id=1, source_target_pairs={{0,2},{1,3},{2,0},{3,1},{4,6},{5,7},{6,4},{7,5},{8,10},{9,11},{10,... | collective-permute-start | bytes 400904 | tf_op jit(solution)/shard_map/ppermute | solution.py:62
  418.4 15.1 %collective-permute-start.22 = (bf16[2,33408]{1,0:T(2,128)(2,1)S(1)}, bf16[2,33408]{1,0:T(2,128)(2,1)S(1)}, u32[]{:S(2)}, u32[]{:S(2)}) collective-permute-start(bf16[2,33408]{1,0:T(2,128)(2,1)S(1)} %get-tuple-element.321), channel_id=1, source_target_pairs={{0,3},{1,0},{2,1},{3,2},{4,7},{5,4},{6,5},{7,6},{8,11},{9,8},{10,9... | collective-permute-start | bytes 400904 | tf_op jit(solution)/shard_map/ppermute | solution.py:62
  519.5 4.4 collective-permute-start.25
  526.5 44.7 %collective-permute-start.26 = (bf16[144,6912]{1,0:T(8,128)(2,1)S(1)}, bf16[144,6912]{1,0:T(8,128)(2,1)S(1)}, u32[]{:S(2)}, u32[]{:S(2)}) collective-permute-start(bf16[144,6912]{1,0:T(8,128)(2,1)S(1)} %add_convert_fusion.1), channel_id=1, source_target_pairs={{0,16},{8,24},{16,0},{24,8},{1,17},{9,25},{17,1},{25,9},{2,18},{10... | collective-permute-start | bytes 5971976 | tf_op jit(solution)/shard_map/ppermute | solution.py:67
  527.8 66.5 %collective-permute-start.24 = (bf16[1152,1152]{1,0:T(8,128)(2,1)S(1)}, bf16[1152,1152]{1,0:T(8,128)(2,1)S(1)}, u32[]{:S(2)}, u32[]{:S(2)}) collective-permute-start(bf16[1152,1152]{1,0:T(8,128)(2,1)S(1)} %copy-done.11), channel_id=1, source_target_pairs={{0,4},{4,0},{1,5},{5,1},{2,6},{6,2},{3,7},{7,3},{8,12},{12,8},{9,1... | collective-permute-start | bytes 7962632 | tf_op jit(solution)/shard_map/ppermute | solution.py:67
  536.9 35.9 %collective-permute-start.28 = (bf16[72,4608]{1,0:T(8,128)(2,1)S(1)}, bf16[72,4608]{1,0:T(8,128)(2,1)S(1)}, u32[]{:S(2)}, u32[]{:S(2)}) collective-permute-start(bf16[72,4608]{1,0:T(8,128)(2,1)S(1)} %get-tuple-element.260), channel_id=1, source_target_pairs={{0,8},{8,0},{16,24},{24,16},{1,9},{9,1},{17,25},{25,17},{2,10},{10... | collective-permute-start | bytes 1990664 | tf_op jit(solution)/shard_map/ppermute | solution.py:67
  571.7 4.8 collective-permute-start.27
  573.0 21.2 %collective-permute-start.29 = (bf16[72,4608]{1,0:T(8,128)(2,1)S(1)}, bf16[72,4608]{1,0:T(8,128)(2,1)S(1)}, u32[]{:S(2)}, u32[]{:S(2)}) collective-permute-start(bf16[72,4608]{1,0:T(8,128)(2,1)S(1)} %add_convert_fusion.7), channel_id=1, source_target_pairs={{0,16},{8,24},{16,0},{24,8},{1,17},{9,25},{17,1},{25,9},{2,18},{10... | collective-permute-start | bytes 1990664 | tf_op jit(solution)/shard_map/ppermute | solution.py:67
  574.3 40.5 %collective-permute-start.30 = (bf16[144,4608]{1,0:T(8,128)(2,1)S(1)}, bf16[144,4608]{1,0:T(8,128)(2,1)S(1)}, u32[]{:S(2)}, u32[]{:S(2)}) collective-permute-start(bf16[144,4608]{1,0:T(8,128)(2,1)S(1)} %copy-done.7), channel_id=1, source_target_pairs={{0,4},{4,0},{1,5},{5,1},{2,6},{6,2},{3,7},{7,3},{8,12},{12,8},{9,1... | collective-permute-start | bytes 3981320 | tf_op jit(solution)/shard_map/ppermute | solution.py:67
  594.5 34.5 %collective-permute-start.31 = (bf16[72,4608]{1,0:T(8,128)(2,1)S(1)}, bf16[72,4608]{1,0:T(8,128)(2,1)S(1)}, u32[]{:S(2)}, u32[]{:S(2)}) collective-permute-start(bf16[72,4608]{1,0:T(8,128)(2,1)S(1)} %add_convert_fusion.6.refs_0_), channel_id=1, source_target_pairs={{0,4},{4,0},{1,5},{5,1},{2,6},{6,2},{3,7},{7,3},{8,12},{12,8},{9,1... | collective-permute-start | bytes 1990664 | tf_op jit(solution)/shard_map/ppermute | solution.py:67
  640.5 3.5 collective-permute-start.32
  642.1 15.0 %collective-permute-start.35 = (bf16[72,4608]{1,0:T(8,128)(2,1)S(1)}, bf16[72,4608]{1,0:T(8,128)(2,1)S(1)}, u32[]{:S(2)}, u32[]{:S(2)}) collective-permute-start(bf16[72,4608]{1,0:T(8,128)(2,1)S(1)} %add_convert_fusion.6.refs_0_), channel_id=1, source_target_pairs={{0,8},{8,0},{16,24},{24,16},{1,9},{9,1},{17,25},{25,17},{2,10},{10... | collective-permute-start | bytes 1990664 | tf_op jit(solution)/shard_map/ppermute | solution.py:67
  642.1 30.8 %collective-permute-start.34 = (bf16[144,4608]{1,0:T(8,128)(2,1)}, bf16[144,4608]{1,0:T(8,128)(2,1)S(1)}, u32[]{:S(2)}, u32[]{:S(2)}) collective-permute-start(bf16[144,4608]{1,0:T(8,128)(2,1)} %reduce-scatter.8.cloned.1.call-done.refs_0_), channel_id=1, source_target_pairs={{0,4},{4,0},{1,5},{5,1},{2,6},{6,2},{3,7},{7,3},{8,12},{12,8},{9,1... | collective-permute-start | bytes 3981320 | tf_op jit(solution)/shard_map/ppermute | solution.py:67
  643.3 13.8 %collective-permute-start.36 = (bf16[72,4608]{1,0:T(8,128)(2,1)S(1)}, bf16[72,4608]{1,0:T(8,128)(2,1)S(1)}, u32[]{:S(2)}, u32[]{:S(2)}) collective-permute-start(bf16[72,4608]{1,0:T(8,128)(2,1)S(1)} %collective-permute-done.31.refs_1_), channel_id=1, source_target_pairs={{0,8},{8,0},{16,24},{24,16},{1,9},{9,1},{17,25},{25,17},{2,10},{10... | collective-permute-start | bytes 1990664 | tf_op jit(solution)/shard_map/ppermute | solution.py:67
  644.2 28.7 %collective-permute-start.33 = (bf16[72,4608]{1,0:T(8,128)(2,1)S(1)}, bf16[72,4608]{1,0:T(8,128)(2,1)S(1)}, u32[]{:S(2)}, u32[]{:S(2)}) collective-permute-start(bf16[72,4608]{1,0:T(8,128)(2,1)S(1)} %add_convert_fusion.5), channel_id=1, source_target_pairs={{0,16},{8,24},{16,0},{24,8},{1,17},{9,25},{17,1},{25,9},{2,18},{10... | collective-permute-start | bytes 1990664 | tf_op jit(solution)/shard_map/ppermute | solution.py:67
  644.5 28.6 %collective-permute-start.37 = (bf16[576,1152]{1,0:T(8,128)(2,1)S(1)}, bf16[576,1152]{1,0:T(8,128)(2,1)S(1)}, u32[]{:S(2)}, u32[]{:S(2)}) collective-permute-start(bf16[576,1152]{1,0:T(8,128)(2,1)S(1)} %copy-done.22), channel_id=1, source_target_pairs={{0,8},{8,0},{16,24},{24,16},{1,9},{9,1},{17,25},{25,17},{2,10},{10... | collective-permute-start | bytes 3981320 | tf_op jit(solution)/shard_map/ppermute | solution.py:67
  674.5 30.7 %collective-permute-start.38 = (bf16[576,1152]{1,0:T(8,128)(2,1)S(1)}, bf16[576,1152]{1,0:T(8,128)(2,1)S(1)}, u32[]{:S(2)}, u32[]{:S(2)}) collective-permute-start(bf16[576,1152]{1,0:T(8,128)(2,1)S(1)} %add_convert_fusion.3), channel_id=1, source_target_pairs={{0,16},{8,24},{16,0},{24,8},{1,17},{9,25},{17,1},{25,9},{2,18},{10... | collective-permute-start | bytes 3981320 | tf_op jit(solution)/shard_map/ppermute | solution.py:67
  675.9 30.8 %collective-permute-start.39 = (bf16[72,4608]{1,0:T(8,128)(2,1)S(1)}, bf16[72,4608]{1,0:T(8,128)(2,1)S(1)}, u32[]{:S(2)}, u32[]{:S(2)}) collective-permute-start(bf16[72,4608]{1,0:T(8,128)(2,1)S(1)} %add_convert_fusion.4.refs_0_), channel_id=1, source_target_pairs={{0,4},{4,0},{1,5},{5,1},{2,6},{6,2},{3,7},{7,3},{8,12},{12,8},{9,1... | collective-permute-start | bytes 1990664 | tf_op jit(solution)/shard_map/ppermute | solution.py:67
  705.6 24.1 %collective-permute-start.42 = (bf16[576,1152]{1,0:T(8,128)(2,1)S(1)}, bf16[576,1152]{1,0:T(8,128)(2,1)S(1)}, u32[]{:S(2)}, u32[]{:S(2)}) collective-permute-start(bf16[576,1152]{1,0:T(8,128)(2,1)S(1)} %add_convert_fusion.2.refs_0_), channel_id=1, source_target_pairs={{0,8},{8,0},{16,24},{24,16},{1,9},{9,1},{17,25},{25,17},{2,10},{10... | collective-permute-start | bytes 3981320 | tf_op jit(solution)/shard_map/ppermute | solution.py:67
  706.6 7.7 %collective-permute-start.40 = (bf16[72,4608]{1,0:T(8,128)(2,1)S(1)}, bf16[72,4608]{1,0:T(8,128)(2,1)S(1)}, u32[]{:S(2)}, u32[]{:S(2)}) collective-permute-start(bf16[72,4608]{1,0:T(8,128)(2,1)S(1)} %add_convert_fusion.4.refs_0_), channel_id=1, source_target_pairs={{0,8},{8,0},{16,24},{24,16},{1,9},{9,1},{17,25},{25,17},{2,10},{10... | collective-permute-start | bytes 1990664 | tf_op jit(solution)/shard_map/ppermute | solution.py:67
  706.7 7.6 %collective-permute-start.41 = (bf16[72,4608]{1,0:T(8,128)(2,1)S(1)}, bf16[72,4608]{1,0:T(8,128)(2,1)S(1)}, u32[]{:S(2)}, u32[]{:S(2)}) collective-permute-start(bf16[72,4608]{1,0:T(8,128)(2,1)S(1)} %collective-permute-done.39.refs_1_), channel_id=1, source_target_pairs={{0,8},{8,0},{16,24},{24,16},{1,9},{9,1},{17,25},{25,17},{2,10},{10... | collective-permute-start | bytes 1990664 | tf_op jit(solution)/shard_map/ppermute | solution.py:67
  707.8 3.4 collective-permute-start.43
  (43 other events, 583.8 us)
Sparse Core Ops, SparseCore 0:
  11.6 172.9 all-gather.1
  222.4 181.0 reduce-scatter.3
  409.9 102.3 reduce-scatter.5
  520.1 96.1 reduce-scatter.7

commit v7 on v6

--- a/solution.py
+++ b/solution.py
@@ -1032,9 +1032,7 @@
     deltas_out[5] = bias_total / groups
     outers_out[5] = OUTER_MOMENTUM * outer_bias + deltas_out[5]
     weights_out[5] = biases - OUTER_RATE * (deltas_out[5] + OUTER_MOMENTUM * outers_out[5])
-    attn_half, two_keep, two_give, one_there, one_pair = after(
-        attn_half, two_keep, two_give, one_there, one_pair
-    )
+    attn_half, two_keep, two_give, one_there = after(attn_half, two_keep, two_give, one_there)
     attn_near = sum_near(*adam_own(where, fixes, attn_half, [state(1), state(2)]))
     attn_there = swap_with(attn_half, "dp", 1)
     attn_far = swap_with(attn_near, "rep", 2)
@@ -1049,7 +1047,7 @@
     )
     attn_total = (attn_near.astype(F32) + attn_far.astype(F32)).astype(BF16)
     attn_pair = swap_with(attn_total, "dp", 1)
-    two_near, attn_total = after(sum_near(two_keep, two_give), attn_total)
+    two_near = sum_near(two_keep, two_give)
     two_far = swap_with(two_near, "rep", 2)
     attn_units = 3
     for index, shift in ((1, 0), (2, attn_units)):

time: 759 us -> 733 us (0.966)
  waiting for transfers between devices: 262 us -> 236 us
    ppermute x33, waiting for transfers between devices: 192 us -> 167 us  [swap_with(): return lax.ppermute(value, axis, [(i, i ^ bit) for i in range(size)])]
    unnamed x90 -> x94, local copies, waits for them, and re-layouts: 20.7 us -> 22.4 us
  transfers between devices with their start and end apart: 49 -> 49, of which waited for: 26 -> 27; matrix products, arithmetic and copies ran while one was open for 7% -> 7% of each run, Pallas kernels for 38% -> 40%
where the time goes in v7:
time: 733 us; the launch traced here: 723 us
  Pallas kernels  339 us (46%)
  waiting for transfers between devices  236 us (32%)
  starting transfers between devices  47.5 us (6%)
  local copies, waits for them, and re-layouts  43.4 us (6%)
  other arithmetic  30.4 us (4%)
  between operations  16.3 us (2%)
  matrix products  9.15 us (1%)
    ppermute x33, waiting for transfers between devices, swap_with(): return lax.ppermute(value, axis, [(i, i ^ bit) for i in range(size)])  167 us
    pallas_call x5, Pallas kernels, adam_whole(): pl.pallas_call(functools.partial(whole_kernel, mode, rate), grid_spec=plt...  63.2 us
    pallas_call x5, Pallas kernels, outer_whole(): pl.pallas_call(functools.partial(outer_kernel, 1.0 / groups), grid_spec=p...  61.2 us
    ppermute x12, waiting for transfers between devices, shift_by(): lax.ppermute(value, axis, [(i, (i + step) % size) for i in range(size)])  52 us
    ppermute x33, starting transfers between devices, swap_with(): return lax.ppermute(value, axis, [(i, i ^ bit) for i in range(size)])  34.1 us
    pallas_call x3, Pallas kernels, grad_columns(): pl.pallas_call(grad_kernel, grid=(width // rows,), in_specs=[whole_spec((...  29.8 us
    pallas_call x1, Pallas kernels, mlp_rest(): pl.pallas_call(mlp_rest_kernel, grid=(units,), in_specs=[column, column,...  29.2 us
    pallas_call x1, Pallas kernels, attention_forward(): pl.pallas_call(attention_forward_kernel, grid=(slots,), in_specs=[row, ro...  26.9 us
  transfers between devices with their start and end apart: 49, of which 27 were waited for; matrix products, arithmetic and copies ran while one was open for 7% of the time, Pallas kernels for 40%

profile of v7, /device:TPU:1, one launch (start us, length us, event | category | flops | bytes accessed | tf_op | source)
XLA Modules:
  0.0 722.6 jit_solution(6685145505432693925)
XLA Ops:
  22.3 4.5 collective-permute-done
  29.9 17.7 %collective-permute-done.5 = bf16[144,1152]{1,0:T(8,128)(2,1)S(1)} collective-permute-done((bf16[144,1152]{1,0:T(8,128)(2,1)S(1)}, bf16[144,1152]{1,0:T(8,128)(2,1)S(1)}, u32[]{:S(2)}, u32[]{:S(2)}) %collective-permute-start.5) | collective-permute-done | bytes 331808 | tf_op jit(solution)/shard_map/ppermute | solution.py:62
  47.7 16.4 %collective-permute-done.4 = bf16[144,1152]{1,0:T(8,128)(2,1)S(1)} collective-permute-done((bf16[144,1152]{1,0:T(8,128)(2,1)S(1)}, bf16[144,1152]{1,0:T(8,128)(2,1)S(1)}, u32[]{:S(2)}, u32[]{:S(2)}) %collective-permute-start.4) | collective-permute-done | bytes 331808 | tf_op jit(solution)/shard_map/ppermute | solution.py:62
  66.3 4.6 fusion.2
  72.4 18.4 %collective-permute-done.10 = bf16[2,144,1152]{2,1,0:T(8,128)(2,1)} collective-permute-done((bf16[2,144,1152]{2,1,0:T(8,128)(2,1)}, bf16[2,144,1152]{2,1,0:T(8,128)(2,1)}, u32[]{:S(2)}, u32[]{:S(2)}) %collective-permute-start.10) | collective-permute-done | bytes 663584 | tf_op jit(solution)/shard_map/ppermute | solution.py:67
  96.7 23.8 %collective-permute-done.11.refs_2_ = bf16[4,144,1152]{2,1,0:T(8,128)(2,1)} collective-permute-done((bf16[4,144,1152]{2,1,0:T(8,128)(2,1)S(1)}, bf16[4,144,1152]{2,1,0:T(8,128)(2,1)}, u32[]{:S(2)}, u32[]{:S(2)}) %collective-permute-start.11) | collective-permute-done | bytes 1327136 | tf_op jit(solution)/shard_map/ppermute | solution.py:67
  120.5 4.3 collective-permute-done.12.refs_3_
  124.8 8.8 %collective-permute-start.13 = (bf16[4,144,1152]{2,1,0:T(8,128)(2,1)S(1)}, bf16[4,144,1152]{2,1,0:T(8,128)(2,1)}, u32[]{:S(2)}, u32[]{:S(2)}) collective-permute-start(bf16[4,144,1152]{2,1,0:T(8,128)(2,1)S(1)} %pad_maximum_fusion.1.refs_0_), channel_id=1, source_target_pairs={{0,8},{8,0},{16,24},{24,16},{1,9},{9,1},{17,25},{25,17},{2,10},{10... | collective-permute-start | bytes 3981320 | tf_op jit(solution)/shard_map/ppermute | solution.py:67
  134.4 3.9 collective-permute-done.13.refs_4_
  142.6 9.0 %shard_map.590 = bf16[32,144,1152]{2,1,0:T(8,128)(2,1)} custom-call(s32[32]{0:T(128)S(1)} %stack.178.order_ref, bf16[4,144,1152]{2,1,0:T(8,128)(2,1)S(1)} %pad_maximum_fusion.1.refs_0_, bf16[4,144,1152]{2,1,0:T(8,128)(2,1)} %pad_maximum_fusion.2.refs_1_, bf16[4,144,1152]{2,1,0:T(8,128)(2,1)} %collective-permute-done.11.refs_2_, ...), custom_call_target="tpu_custom_call" | custom-call | bytes 21233664 | tf_op jit(solution)/shard_map/pallas_call | solution.py:729
  151.6 26.9 %shard_map.591 = (bf16[768,1152]{1,0:T(8,128)(2,1)S(1)}, bf16[768,3456]{1,0:T(8,128)(2,1)}, bf16[768,1152]{1,0:T(8,128)(2,1)S(1)}, f32[768,128]{1,0:T(8,128)S(1)...) custom-call(bf16[768,1152]{1,0:T(8,128)(2,1)} %bitcast.176, ...), custom_call_target="tpu_custom_call" | custom-call | flops 8153726976 | bytes 41943040 | tf_op jit(solution)/shard_map/pallas_call | solution.py:190
  186.1 21.3 %shard_map.592 = (bf16[768,4608]{1,0:T(8,128)(2,1)}, bf16[768,4608]{1,0:T(8,128)(2,1)}) custom-call(bf16[768,1152]{1,0:T(8,128)(2,1)S(1)} %copy-done.30, bf16[4,4,2,2,144,1152]{5,4,3,2,1,0:T(8,128)(2,1)} %bitcast.227, f32[1,4608]{1,0:T(1,128)S(1)} %reshape.445.bias_ref), custom_call_target="tpu_custom_call" | custom-call | flops 8153726976 | bytes 27262976 | tf_op jit(solution)/shard_map/pallas_call | solution.py:256
  207.4 14.9 %shard_map.593 = bf16[4608,1152]{1,0:T(8,128)(2,1)} custom-call(bf16[768,4608]{1,0:T(8,128)(2,1)} %get-tuple-element.203.left_ref.act_ref, bf16[768,1152]{1,0:T(8,128)(2,1)S(1)} %copy-done.25), custom_call_target="tpu_custom_call" | custom-call | flops 8153726976 | bytes 24772608 | tf_op jit(solution)/shard_map/pallas_call | solution.py:501
  223.8 16.8 %shard_map.594 = (bf16[768,4608]{1,0:T(8,128)(2,1)}, f32[8,4608]{1,0:T(8,128)S(1)}) custom-call(bf16[768,1152]{1,0:T(8,128)(2,1)S(1)} %copy-done.26, bf16[4,4,2,2,144,1152]{5,4,3,2,1,0:T(8,128)(2,1)} %bitcast.228, bf16[768,4608]{1,0:T(8,128)(2,1)} %get-tuple-element.206.slope_ref), custom_call_target="tpu_custom_call" | custom-call | flops 8153726976 | bytes 27262976 | tf_op jit(solution)/shard_map/pallas_call | solution.py:287
  240.6 14.9 %shard_map.595 = bf16[1152,4608]{1,0:T(8,128)(2,1)} custom-call(bf16[768,1152]{1,0:T(8,128)(2,1)S(1)} %copy-done.31, bf16[768,4608]{1,0:T(8,128)(2,1)} %get-tuple-element.208.right_ref.d_hidden_ref), custom_call_target="tpu_custom_call" | custom-call | flops 8153726976 | bytes 24772608 | tf_op jit(solution)/shard_map/pallas_call | solution.py:485
  255.6 5.2 dynamic-slice_bitcast_fusion
  264.2 29.2 %shard_map.596 = (f32[768,1152]{1,0:T(8,128)S(1)}, f32[768,1152]{1,0:T(8,128)}) custom-call(bf16[768,4608]{1,0:T(8,128)(2,1)} %get-tuple-element.203.left_ref.act_ref, bf16[768,4608]{1,0:T(8,128)(2,1)} %get-tuple-element.208.right_ref.d_hidden_ref, bf16[4,4,2,2,144,1152]{5,4,3,2,1,0:T(8,128)(2,1)} %bitcast.229, bf16[4,4,2,2,144,1152]{5,4,3,2,1,0:T(8,128)(2,1)} %bitcast.230), custom_call_target="tpu_custom_call" | custom-call | flops 16307453952 | bytes 44040192 | tf_op jit(solution)/shard_map/pallas_call | solution.py:325
  295.2 12.5 %shard_map.597 = (bf16[768,1152]{1,0:T(8,128)(2,1)}, f32[768,1152]{1,0:T(8,128)}, bf16[768,1152]{1,0:T(8,128)(2,1)S(1)}, bf16[768,1152]{1,0:T(8,128)(2,1)S(1)}, f32[3,8,1152]{2,1,0:T(8,128)S(1)}) custom-call(f32[768,1152]{1,0:T(8,128)} %copy-done.9, f32[8,1152]{1,0:T(8,128)S(1)} %scatter.19.bias_ref, f32[768,1152]{1,0:T(8,128)} %get-tuple-element.210.d_in_ref, ...), custom_call_target="tpu_custom_call" | custom-call | flops 2038431744 | bytes 31457280 | tf_op jit(solution)/shard_map/pallas_call | solution.py:366
  307.7 3.0 shard_map.598
  312.0 23.9 %shard_map.599 = (bf16[768,3456]{1,0:T(8,128)(2,1)}, f32[3,8,1152]{2,1,0:T(8,128)S(1)}) custom-call(bf16[768,3456]{1,0:T(8,128)(2,1)} %get-tuple-element.216.packed_ref, bf16[768,1152]{1,0:T(8,128)(2,1)S(1)} %get-tuple-element.220.d_att_ref, f32[768,128]{1,0:T(8,128)S(1)} %get-tuple-element.221.log_ref), custom_call_target="tpu_custom_call" | custom-call | flops 8053063680 | bytes 14680064 | tf_op jit(solution)/shard_map/pallas_call | solution.py:421
  335.9 11.9 %shard_map.600 = bf16[1152,3456]{1,0:T(8,128)(2,1)} custom-call(bf16[768,1152]{1,0:T(8,128)(2,1)S(1)} %copy-done.33, bf16[768,3456]{1,0:T(8,128)(2,1)} %get-tuple-element.225.right_ref.d_packed_ref), custom_call_target="tpu_custom_call" | custom-call | flops 6115295232 | bytes 18579456 | tf_op jit(solution)/shard_map/pallas_call | solution.py:485
  347.8 4.5 dynamic-slice_bitcast_fusion.1
  354.5 14.1 %shard_map.601 = (bf16[768,1152]{1,0:T(8,128)(2,1)}, f32[3,8,1152]{2,1,0:T(8,128)S(1)}) custom-call(bf16[768,3456]{1,0:T(8,128)(2,1)} %get-tuple-element.225.right_ref.d_packed_ref, bf16[4,1152,1152]{2,1,0:T(8,128)(2,1)} %bitcast.184, bf16[768,1152]{1,0:T(8,128)(2,1)S(1)} %bitcast.177, f32[768,1152]{1,0:T(8,128)S(1)} %copy-done.19, ...), custom_call_target="tpu_custom_call" | custom-call | flops 6115295232 | bytes 20971520 | tf_op jit(solution)/shard_map/pallas_call | solution.py:453
  368.6 9.3 %collective-permute-done.17 = bf16[4,144,4608]{2,1,0:T(8,128)(2,1)} collective-permute-done((bf16[4,144,4608]{2,1,0:T(8,128)(2,1)}, bf16[4,144,4608]{2,1,0:T(8,128)(2,1)}, u32[]{:S(2)}, u32[]{:S(2)}) %collective-permute-start.17) | collective-permute-done | bytes 5308448 | tf_op jit(solution)/shard_map/ppermute | solution.py:67
  378.0 7.8 %fusion = bf16[4,144,4608]{2,1,0:T(8,128)(2,1)} fusion(bf16[4,144,4608]{2,1,0:T(8,128)(2,1)} %collective-permute-done.17, bf16[4,2,144,4608]{3,2,1,0:T(8,128)(2,1)} %bitcast.202, s32[]{:T(128)S(6)} %select_n.139), kind=kLoop, calls=%fused_computation.2 | loop fusion | flops 10616832 | bytes 15925252 | tf_op jit(solution)/shard_map/convert_element_type | solution.py:906
  385.7 20.6 %collective-permute-done.18 = bf16[4,144,1152]{2,1,0:T(8,128)(2,1)} collective-permute-done((bf16[4,144,1152]{2,1,0:T(8,128)(2,1)}, bf16[4,144,1152]{2,1,0:T(8,128)(2,1)}, u32[]{:S(2)}, u32[]{:S(2)}) %collective-permute-start.18) | collective-permute-done | bytes 1327136 | tf_op jit(solution)/shard_map/ppermute | solution.py:67
  415.1 3.5 fusion.4
  420.5 13.1 %collective-permute-done.21 = bf16[2,33408]{1,0:T(2,128)(2,1)S(1)} collective-permute-done((bf16[2,33408]{1,0:T(2,128)(2,1)S(1)}, bf16[2,33408]{1,0:T(2,128)(2,1)S(1)}, u32[]{:S(2)}, u32[]{:S(2)}) %collective-permute-start.21) | collective-permute-done | bytes 133664 | tf_op jit(solution)/shard_map/ppermute | solution.py:62
  434.3 4.6 fusion.10
  438.9 21.2 %shard_map.602 = (f32[2,144,6912]{2,1,0:T(8,128)}, f32[2,144,6912]{2,1,0:T(8,128)}, bf16[144,6912]{1,0:T(8,128)(2,1)S(1)}, bf16[144,6912]{1,0:T(8,128)(2,1)S(1)}) custom-call(s32[2]{0:T(128)S(1)} %pad_add_fusion.where_ref, f32[2]{0:T(128)S(1)} %pad_maximum_fusion.10.fix_ref, f32[2,144,6912]{2,1,0:T(8,128)} %bitcast.180, f32[2,144,6912]{2,1,0:T(8,128)} %bitcast.178, ...), custom_call_target="tpu_custom_call" | custom-call | flops 1024 | bytes 1024 | tf_op jit(solution)/shard_map/pallas_call | solution.py:580
  463.0 34.3 %collective-permute-done.23 = bf16[4,144,3456]{2,1,0:T(8,128)(2,1)} collective-permute-done((bf16[4,144,3456]{2,1,0:T(8,128)(2,1)}, bf16[4,144,3456]{2,1,0:T(8,128)(2,1)}, u32[]{:S(2)}, u32[]{:S(2)}) %collective-permute-start.23) | collective-permute-done | bytes 3981344 | tf_op jit(solution)/shard_map/ppermute | solution.py:67
  497.3 15.2 %reduce-scatter.6.cloned.1.call-done.refs_0_ = bf16[144,4608]{1,0:T(8,128)(2,1)} async-done(((bf16[576,4608]{1,0:T(8,128)(2,1)}), bf16[144,4608]{1,0:T(8,128)(2,1)}) %reduce-scatter.6.cloned.1.call-update) | async-done | bytes 1327120 | tf_op jit(solution)/shard_map/reduce_scatter | solution.py:901
  512.5 4.4 fusion.1
  516.9 2.8 pad_maximum_fusion
  521.7 3.6 collective-permute-done.25
  529.8 8.0 %shard_map.604 = (bf16[72,4608]{1,0:T(8,128)(2,1)S(1)}, bf16[72,4608]{1,0:T(8,128)(2,1)S(1)}) custom-call(s32[2]{0:T(128)S(1)} %pad_add_fusion.where_ref, f32[2]{0:T(128)S(1)} %pad_maximum_fusion.10.fix_ref, bf16[2,72,4608]{2,1,0:T(8,128)(2,1)S(1)} %bitcast.169, f32[2,2,72,4608]{3,2,1,0:T(8,128)} %bitcast.185, f32[2,2,72,4608]{3,2,1,0:T(8,128)} %bitcast.190, ...), custom_call_target="tpu_custom_call" | custom-call | flops 1024 | bytes 1024 | tf_op jit(solution)/shard_map/pallas_call | solution.py:644
  538.7 33.3 %collective-permute-done.26 = bf16[144,6912]{1,0:T(8,128)(2,1)S(1)} collective-permute-done((bf16[144,6912]{1,0:T(8,128)(2,1)S(1)}, bf16[144,6912]{1,0:T(8,128)(2,1)S(1)}, u32[]{:S(2)}, u32[]{:S(2)}) %collective-permute-start.26) | collective-permute-done | bytes 1990688 | tf_op jit(solution)/shard_map/ppermute | solution.py:67
  577.3 17.8 %shard_map.603 = (f32[2,144,6912]{2,1,0:T(8,128)}, f32[2,144,6912]{2,1,0:T(8,128)}, f32[2,144,6912]{2,1,0:T(8,128)}) custom-call(s32[2]{0:T(128)S(1)} %pad_add_fusion.where_ref, bf16[144,6912]{1,0:T(8,128)(2,1)S(1)} %add_convert_fusion.refs_0_, bf16[144,6912]{1,0:T(8,128)(2,1)S(1)} %collective-permute-done.27.refs_1_, f32[2,144,6912]{2,1,0:T(8,128)} %bitcast.179, ...), custom_call_target="tpu_custom_call" | custom-call | flops 1024 | bytes 1024 | tf_op jit(solution)/shard_map/pallas_call | solution.py:692
  596.6 16.0 %shard_map.605 = (f32[2,576,1152]{2,1,0:T(8,128)}, f32[2,576,1152]{2,1,0:T(8,128)}, f32[2,576,1152]{2,1,0:T(8,128)}, bf16[576,1152]{1,0:T(8,128)(2,1)S(1)}, bf16[576,1152]{1,0:T(8,128)(2,1)S(1)}) custom-call(s32[2]{0:T(128)S(1)} %pad_add_fusion.where_ref, f32[2]{0:T(128)S(1)} %pad_maximum_fusion.10.fix_ref, bf16[2,576,1152]{2,1,0:T(8,128)(2,1)S(1)} %bitcast.172, ...), custom_call_target="tpu_custom_call" | custom-call | flops 1024 | bytes 1024 | tf_op jit(solution)/shard_map/pallas_call | solution.py:580
  619.2 8.7 %shard_map.606 = (bf16[72,4608]{1,0:T(8,128)(2,1)S(1)}, bf16[72,4608]{1,0:T(8,128)(2,1)S(1)}) custom-call(s32[2]{0:T(128)S(1)} %pad_add_fusion.where_ref, f32[2]{0:T(128)S(1)} %pad_maximum_fusion.10.fix_ref, bf16[2,72,4608]{2,1,0:T(8,128)(2,1)} %bitcast.80.g_ref, f32[2,2,72,3456]{3,2,1,0:T(8,128)} %bitcast.195, f32[2,2,72,3456]{3,2,1,0:T(8,128)} %bitcast.197, ...), custom_call_target="tpu_custom_call" | custom-call | flops 1024 | bytes 1024 | tf_op jit(solution)/shard_map/pallas_call | solution.py:644
  636.2 15.9 %shard_map.608 = (f32[2,2,72,4608]{3,2,1,0:T(8,128)}, f32[2,2,72,4608]{3,2,1,0:T(8,128)}, f32[2,2,72,4608]{3,2,1,0:T(8,128)}) custom-call(s32[2]{0:T(128)S(1)} %pad_add_fusion.where_ref, bf16[72,4608]{1,0:T(8,128)(2,1)S(1)} %add_convert_fusion.5.refs_0_, bf16[72,4608]{1,0:T(8,128)(2,1)S(1)} %collective-permute-done.34.refs_1_, ...), custom_call_target="tpu_custom_call" | custom-call | flops 1024 | bytes 1024 | tf_op jit(solution)/shard_map/pallas_call | solution.py:692
  652.1 12.1 %shard_map.607 = (f32[2,144,4608]{2,1,0:T(8,128)}, f32[2,144,4608]{2,1,0:T(8,128)}, f32[2,144,4608]{2,1,0:T(8,128)}) custom-call(s32[2]{0:T(128)S(1)} %pad_add_fusion.where_ref, f32[2]{0:T(128)S(1)} %pad_maximum_fusion.10.fix_ref, bf16[144,4608]{1,0:T(8,128)(2,1)S(1)} %copy-done.8, bf16[144,4608]{1,0:T(8,128)(2,1)S(1)} %copy-done.18, ...), custom_call_target="tpu_custom_call" | custom-call | flops 1024 | bytes 1024 | tf_op jit(solution)/shard_map/pallas_call | solution.py:580
  665.7 10.2 %shard_map.609 = (f32[2,144,3456]{2,1,0:T(8,128)}, f32[2,144,3456]{2,1,0:T(8,128)}, f32[2,144,3456]{2,1,0:T(8,128)}) custom-call(s32[2]{0:T(128)S(1)} %pad_add_fusion.where_ref, f32[2]{0:T(128)S(1)} %pad_maximum_fusion.10.fix_ref, bf16[144,4608]{1,0:T(8,128)(2,1)} %reduce-scatter.8.cloned.1.call-done.refs_0_, ...), custom_call_target="tpu_custom_call" | custom-call | flops 1024 | bytes 1024 | tf_op jit(solution)/shard_map/pallas_call | solution.py:580
  675.8 3.7 shard_map.610
  682.4 2.7 collective-permute-done.43
  688.3 12.3 %shard_map.611 = (f32[2,2,72,3456]{3,2,1,0:T(8,128)}, f32[2,2,72,3456]{3,2,1,0:T(8,128)}, f32[2,2,72,3456]{3,2,1,0:T(8,128)}) custom-call(s32[2]{0:T(128)S(1)} %pad_add_fusion.where_ref, bf16[72,4608]{1,0:T(8,128)(2,1)S(1)} %add_convert_fusion.4.refs_0_, bf16[72,4608]{1,0:T(8,128)(2,1)S(1)} %collective-permute-done.39.refs_1_, ...), custom_call_target="tpu_custom_call" | custom-call | flops 1024 | bytes 1024 | tf_op jit(solution)/shard_map/pallas_call | solution.py:692
  700.6 3.1 shard_map.612
  703.7 12.2 %shard_map.613 = (f32[2,576,1152]{2,1,0:T(8,128)}, f32[2,576,1152]{2,1,0:T(8,128)}, f32[2,576,1152]{2,1,0:T(8,128)}) custom-call(s32[2]{0:T(128)S(1)} %pad_add_fusion.where_ref, bf16[576,1152]{1,0:T(8,128)(2,1)S(1)} %add_convert_fusion.2.refs_0_, bf16[576,1152]{1,0:T(8,128)(2,1)S(1)} %collective-permute-done.42.refs_1_, f32[2,576,1152]{2,1,0:T(8,128)} %bitcast.188, ...), custom_call_target="tpu_custom_call" | custom-call | flops 1024 | bytes 1024 | tf_op jit(solution)/shard_map/pallas_call | solution.py:692
  (277 shorter events, 99.4 us)
Async XLA Ops:
  7.3 177.3 %all-gather.2.cloned.1.call-start = ((), (), s32[]{:S(2)}) async-start(), calls=%async_computation.3 | async-start | bytes 21897216 | tf_op jit(solution)/shard_map/all_gather | solution.py:851
  10.7 395.7 %reduce-scatter.4.cloned.1.call-start = ((), (), s32[]{:S(2)}) async-start(), calls=%async_computation.4 | async-start | bytes 13271040 | tf_op jit(solution)/shard_map/reduce_scatter | solution.py:901
  14.6 14.1 %collective-permute-start.3 = (bf16[144,1152]{1,0:T(8,128)(2,1)S(1)}, bf16[144,1152]{1,0:T(8,128)(2,1)S(1)}, u32[]{:S(2)}, u32[]{:S(2)}) collective-permute-start(bf16[144,1152]{1,0:T(8,128)(2,1)S(1)} %fusion.5), channel_id=1, source_target_pairs={{0,1},{1,2},{2,3},{3,0},{4,5},{5,6},{6,7},{7,4},{8,9},{9,10},{10,1... | collective-permute-start | bytes 995336 | tf_op jit(solution)/shard_map/ppermute | solution.py:62
  16.8 10.0 %collective-permute-start = (bf16[7488]{0:T(1024)(128)(2,1)S(1)}, bf16[7488]{0:T(1024)(128)(2,1)S(1)}, u32[]{:S(2)}, u32[]{:S(2)}) collective-permute-start(bf16[7488]{0:T(1024)(128)(2,1)S(1)} %pad_maximum_fusion.9), channel_id=1, source_target_pairs={{0,1},{1,2},{2,3},{3,0},{4,5},{5,6},{6,7},{7,4},{8,9},{9,10},{10,1... | collective-permute-start | bytes 44936 | tf_op jit(solution)/shard_map/ppermute | solution.py:62
  18.1 9.9 %collective-permute-start.1 = (bf16[7488]{0:T(1024)(128)(2,1)S(1)}, bf16[7488]{0:T(1024)(128)(2,1)S(1)}, u32[]{:S(2)}, u32[]{:S(2)}) collective-permute-start(bf16[7488]{0:T(1024)(128)(2,1)S(1)} %pad_maximum_fusion.9), channel_id=1, source_target_pairs={{0,2},{1,3},{2,0},{3,1},{4,6},{5,7},{6,4},{7,5},{8,10},{9,11},{10,... | collective-permute-start | bytes 44936 | tf_op jit(solution)/shard_map/ppermute | solution.py:62
  19.2 9.2 %collective-permute-start.2 = (bf16[7488]{0:T(1024)(128)(2,1)S(1)}, bf16[7488]{0:T(1024)(128)(2,1)S(1)}, u32[]{:S(2)}, u32[]{:S(2)}) collective-permute-start(bf16[7488]{0:T(1024)(128)(2,1)S(1)} %pad_maximum_fusion.9), channel_id=1, source_target_pairs={{0,3},{1,0},{2,1},{3,2},{4,7},{5,4},{6,5},{7,6},{8,11},{9,8},{10,9... | collective-permute-start | bytes 44936 | tf_op jit(solution)/shard_map/ppermute | solution.py:62
  21.5 26.2 %collective-permute-start.5 = (bf16[144,1152]{1,0:T(8,128)(2,1)S(1)}, bf16[144,1152]{1,0:T(8,128)(2,1)S(1)}, u32[]{:S(2)}, u32[]{:S(2)}) collective-permute-start(bf16[144,1152]{1,0:T(8,128)(2,1)S(1)} %fusion.5), channel_id=1, source_target_pairs={{0,3},{1,0},{2,1},{3,2},{4,7},{5,4},{6,5},{7,6},{8,11},{9,8},{10,9... | collective-permute-start | bytes 995336 | tf_op jit(solution)/shard_map/ppermute | solution.py:62
  26.8 37.3 %collective-permute-start.4 = (bf16[144,1152]{1,0:T(8,128)(2,1)S(1)}, bf16[144,1152]{1,0:T(8,128)(2,1)S(1)}, u32[]{:S(2)}, u32[]{:S(2)}) collective-permute-start(bf16[144,1152]{1,0:T(8,128)(2,1)S(1)} %fusion.5), channel_id=1, source_target_pairs={{0,2},{1,3},{2,0},{3,1},{4,6},{5,7},{6,4},{7,5},{8,10},{9,11},{10,... | collective-permute-start | bytes 995336 | tf_op jit(solution)/shard_map/ppermute | solution.py:62
  28.8 42.3 %collective-permute-start.9 = (bf16[2,144,1152]{2,1,0:T(8,128)(2,1)S(1)}, bf16[2,144,1152]{2,1,0:T(8,128)(2,1)}, u32[]{:S(2)}, u32[]{:S(2)}) collective-permute-start(bf16[2,144,1152]{2,1,0:T(8,128)(2,1)S(1)} %pad_maximum_fusion.3), channel_id=1, source_target_pairs={{0,16},{8,24},{16,0},{24,8},{1,17},{9,25},{17,1},{25,9},{2,18},{10... | collective-permute-start | bytes 1990664 | tf_op jit(solution)/shard_map/ppermute | solution.py:67
  65.0 25.8 %collective-permute-start.10 = (bf16[2,144,1152]{2,1,0:T(8,128)(2,1)}, bf16[2,144,1152]{2,1,0:T(8,128)(2,1)}, u32[]{:S(2)}, u32[]{:S(2)}) collective-permute-start(bf16[2,144,1152]{2,1,0:T(8,128)(2,1)} %pad_maximum_fusion.4), channel_id=1, source_target_pairs={{0,4},{4,0},{1,5},{5,1},{2,6},{6,2},{3,7},{7,3},{8,12},{12,8},{9,1... | collective-permute-start | bytes 1990664 | tf_op jit(solution)/shard_map/ppermute | solution.py:67
  72.3 48.2 %collective-permute-start.11 = (bf16[4,144,1152]{2,1,0:T(8,128)(2,1)S(1)}, bf16[4,144,1152]{2,1,0:T(8,128)(2,1)}, u32[]{:S(2)}, u32[]{:S(2)}) collective-permute-start(bf16[4,144,1152]{2,1,0:T(8,128)(2,1)S(1)} %pad_maximum_fusion.1.refs_0_), channel_id=1, source_target_pairs={{0,4},{4,0},{1,5},{5,1},{2,6},{6,2},{3,7},{7,3},{8,12},{12,8},{9,1... | collective-permute-start | bytes 3981320 | tf_op jit(solution)/shard_map/ppermute | solution.py:67
  93.1 31.7 %collective-permute-start.12 = (bf16[4,144,1152]{2,1,0:T(8,128)(2,1)}, bf16[4,144,1152]{2,1,0:T(8,128)(2,1)}, u32[]{:S(2)}, u32[]{:S(2)}) collective-permute-start(bf16[4,144,1152]{2,1,0:T(8,128)(2,1)} %pad_maximum_fusion.2.refs_1_), channel_id=1, source_target_pairs={{0,16},{8,24},{16,0},{24,8},{1,17},{9,25},{17,1},{25,9},{2,18},{10... | collective-permute-start | bytes 3981320 | tf_op jit(solution)/shard_map/ppermute | solution.py:67
  94.4 39.2 %collective-permute-start.8 = (f32[3,6912]{1,0:T(4,128)S(1)}, f32[3,6912]{1,0:T(4,128)S(1)}, u32[]{:S(2)}, u32[]{:S(2)}) collective-permute-start(f32[3,6912]{1,0:T(4,128)S(1)} %get-tuple-element.317), channel_id=1, source_target_pairs={{0,3},{1,0},{2,1},{3,2},{4,7},{5,4},{6,5},{7,6},{8,11},{9,8},{10,9... | collective-permute-start | bytes 248840 | tf_op jit(solution)/shard_map/ppermute | solution.py:62
  94.4 39.7 %collective-permute-start.7 = (f32[3,6912]{1,0:T(4,128)S(1)}, f32[3,6912]{1,0:T(4,128)S(1)}, u32[]{:S(2)}, u32[]{:S(2)}) collective-permute-start(f32[3,6912]{1,0:T(4,128)S(1)} %get-tuple-element.318), channel_id=1, source_target_pairs={{0,2},{1,3},{2,0},{3,1},{4,6},{5,7},{6,4},{7,5},{8,10},{9,11},{10,... | collective-permute-start | bytes 248840 | tf_op jit(solution)/shard_map/ppermute | solution.py:62
  94.5 39.7 %collective-permute-start.6 = (f32[3,6912]{1,0:T(4,128)S(1)}, f32[3,6912]{1,0:T(4,128)S(1)}, u32[]{:S(2)}, u32[]{:S(2)}) collective-permute-start(f32[3,6912]{1,0:T(4,128)S(1)} %get-tuple-element.316), channel_id=1, source_target_pairs={{0,1},{1,2},{2,3},{3,0},{4,5},{5,6},{6,7},{7,4},{8,9},{9,10},{10,1... | collective-permute-start | bytes 248840 | tf_op jit(solution)/shard_map/ppermute | solution.py:62
  124.8 13.5 %collective-permute-start.13 = (bf16[4,144,1152]{2,1,0:T(8,128)(2,1)S(1)}, bf16[4,144,1152]{2,1,0:T(8,128)(2,1)}, u32[]{:S(2)}, u32[]{:S(2)}) collective-permute-start(bf16[4,144,1152]{2,1,0:T(8,128)(2,1)S(1)} %pad_maximum_fusion.1.refs_0_), channel_id=1, source_target_pairs={{0,8},{8,0},{16,24},{24,16},{1,9},{9,1},{17,25},{25,17},{2,10},{10... | collective-permute-start | bytes 3981320 | tf_op jit(solution)/shard_map/ppermute | solution.py:67
  133.6 5.1 collective-permute-start.14
  133.6 7.1 collective-permute-start.15
  134.1 8.5 %collective-permute-start.16 = (bf16[4,144,1152]{2,1,0:T(8,128)(2,1)}, bf16[4,144,1152]{2,1,0:T(8,128)(2,1)}, u32[]{:S(2)}, u32[]{:S(2)}) collective-permute-start(bf16[4,144,1152]{2,1,0:T(8,128)(2,1)} %collective-permute-done.12.refs_3_), channel_id=1, source_target_pairs={{0,8},{8,0},{16,24},{24,16},{1,9},{9,1},{17,25},{25,17},{2,10},{10... | collective-permute-start | bytes 3981320 | tf_op jit(solution)/shard_map/ppermute | solution.py:67
  222.4 290.1 %reduce-scatter.6.cloned.1.call-start = ((), (), s32[]{:S(2)}) async-start(), calls=%async_computation.5 | async-start | bytes 6635520 | tf_op jit(solution)/shard_map/reduce_scatter | solution.py:901
  260.8 117.2 %collective-permute-start.17 = (bf16[4,144,4608]{2,1,0:T(8,128)(2,1)}, bf16[4,144,4608]{2,1,0:T(8,128)(2,1)}, u32[]{:S(2)}, u32[]{:S(2)}) collective-permute-start(bf16[4,144,4608]{2,1,0:T(8,128)(2,1)} %dynamic-slice_bitcast_fusion), channel_id=1, source_target_pairs={{0,4},{4,0},{1,5},{5,1},{2,6},{6,2},{3,7},{7,3},{8,12},{12,8},{9,1... | collective-permute-start | bytes 15925256 | tf_op jit(solution)/shard_map/ppermute | solution.py:67
  352.3 54.1 %collective-permute-start.18 = (bf16[4,144,1152]{2,1,0:T(8,128)(2,1)}, bf16[4,144,1152]{2,1,0:T(8,128)(2,1)}, u32[]{:S(2)}, u32[]{:S(2)}) collective-permute-start(bf16[4,144,1152]{2,1,0:T(8,128)(2,1)} %dynamic-slice_bitcast_fusion.2), channel_id=1, source_target_pairs={{0,4},{4,0},{1,5},{5,1},{2,6},{6,2},{3,7},{7,3},{8,12},{12,8},{9,1... | collective-permute-start | bytes 3981320 | tf_op jit(solution)/shard_map/ppermute | solution.py:67
  408.7 3.2 collective-permute-start.19
  410.0 206.6 %reduce-scatter.8.cloned.1.call-start = ((), (), s32[]{:S(2)}) async-start(), calls=%async_computation.6 | async-start | bytes 6635520 | tf_op jit(solution)/shard_map/reduce_scatter | solution.py:901
  410.0 87.3 %collective-permute-start.23 = (bf16[4,144,3456]{2,1,0:T(8,128)(2,1)}, bf16[4,144,3456]{2,1,0:T(8,128)(2,1)}, u32[]{:S(2)}, u32[]{:S(2)}) collective-permute-start(bf16[4,144,3456]{2,1,0:T(8,128)(2,1)} %dynamic-slice_bitcast_fusion.1), channel_id=1, source_target_pairs={{0,4},{4,0},{1,5},{5,1},{2,6},{6,2},{3,7},{7,3},{8,12},{12,8},{9,1... | collective-permute-start | bytes 11943944 | tf_op jit(solution)/shard_map/ppermute | solution.py:67
  412.6 7.8 %collective-permute-start.20 = (bf16[2,33408]{1,0:T(2,128)(2,1)S(1)}, bf16[2,33408]{1,0:T(2,128)(2,1)S(1)}, u32[]{:S(2)}, u32[]{:S(2)}) collective-permute-start(bf16[2,33408]{1,0:T(2,128)(2,1)S(1)} %get-tuple-element.315), channel_id=1, source_target_pairs={{0,1},{1,2},{2,3},{3,0},{4,5},{5,6},{6,7},{7,4},{8,9},{9,10},{10,1... | collective-permute-start | bytes 400904 | tf_op jit(solution)/shard_map/ppermute | solution.py:62
  418.6 15.0 %collective-permute-start.21 = (bf16[2,33408]{1,0:T(2,128)(2,1)S(1)}, bf16[2,33408]{1,0:T(2,128)(2,1)S(1)}, u32[]{:S(2)}, u32[]{:S(2)}) collective-permute-start(bf16[2,33408]{1,0:T(2,128)(2,1)S(1)} %get-tuple-element.315), channel_id=1, source_target_pairs={{0,2},{1,3},{2,0},{3,1},{4,6},{5,7},{6,4},{7,5},{8,10},{9,11},{10,... | collective-permute-start | bytes 400904 | tf_op jit(solution)/shard_map/ppermute | solution.py:62
  418.6 15.1 %collective-permute-start.22 = (bf16[2,33408]{1,0:T(2,128)(2,1)S(1)}, bf16[2,33408]{1,0:T(2,128)(2,1)S(1)}, u32[]{:S(2)}, u32[]{:S(2)}) collective-permute-start(bf16[2,33408]{1,0:T(2,128)(2,1)S(1)} %get-tuple-element.315), channel_id=1, source_target_pairs={{0,3},{1,0},{2,1},{3,2},{4,7},{5,4},{6,5},{7,6},{8,11},{9,8},{10,9... | collective-permute-start | bytes 400904 | tf_op jit(solution)/shard_map/ppermute | solution.py:62
  521.2 4.1 collective-permute-start.25
  527.3 44.7 %collective-permute-start.26 = (bf16[144,6912]{1,0:T(8,128)(2,1)S(1)}, bf16[144,6912]{1,0:T(8,128)(2,1)S(1)}, u32[]{:S(2)}, u32[]{:S(2)}) collective-permute-start(bf16[144,6912]{1,0:T(8,128)(2,1)S(1)} %add_convert_fusion.1), channel_id=1, source_target_pairs={{0,16},{8,24},{16,0},{24,8},{1,17},{9,25},{17,1},{25,9},{2,18},{10... | collective-permute-start | bytes 5971976 | tf_op jit(solution)/shard_map/ppermute | solution.py:67
  528.6 66.5 %collective-permute-start.24 = (bf16[1152,1152]{1,0:T(8,128)(2,1)S(1)}, bf16[1152,1152]{1,0:T(8,128)(2,1)S(1)}, u32[]{:S(2)}, u32[]{:S(2)}) collective-permute-start(bf16[1152,1152]{1,0:T(8,128)(2,1)S(1)} %copy-done.11), channel_id=1, source_target_pairs={{0,4},{4,0},{1,5},{5,1},{2,6},{6,2},{3,7},{7,3},{8,12},{12,8},{9,1... | collective-permute-start | bytes 7962632 | tf_op jit(solution)/shard_map/ppermute | solution.py:67
  537.8 35.9 %collective-permute-start.28 = (bf16[72,4608]{1,0:T(8,128)(2,1)S(1)}, bf16[72,4608]{1,0:T(8,128)(2,1)S(1)}, u32[]{:S(2)}, u32[]{:S(2)}) collective-permute-start(bf16[72,4608]{1,0:T(8,128)(2,1)S(1)} %get-tuple-element.257), channel_id=1, source_target_pairs={{0,8},{8,0},{16,24},{24,16},{1,9},{9,1},{17,25},{25,17},{2,10},{10... | collective-permute-start | bytes 1990664 | tf_op jit(solution)/shard_map/ppermute | solution.py:67
  572.5 4.8 collective-permute-start.27
  573.8 21.2 %collective-permute-start.29 = (bf16[72,4608]{1,0:T(8,128)(2,1)S(1)}, bf16[72,4608]{1,0:T(8,128)(2,1)S(1)}, u32[]{:S(2)}, u32[]{:S(2)}) collective-permute-start(bf16[72,4608]{1,0:T(8,128)(2,1)S(1)} %add_convert_fusion.7), channel_id=1, source_target_pairs={{0,16},{8,24},{16,0},{24,8},{1,17},{9,25},{17,1},{25,9},{2,18},{10... | collective-permute-start | bytes 1990664 | tf_op jit(solution)/shard_map/ppermute | solution.py:67
  575.1 40.4 %collective-permute-start.30 = (bf16[144,4608]{1,0:T(8,128)(2,1)S(1)}, bf16[144,4608]{1,0:T(8,128)(2,1)S(1)}, u32[]{:S(2)}, u32[]{:S(2)}) collective-permute-start(bf16[144,4608]{1,0:T(8,128)(2,1)S(1)} %copy-done.7), channel_id=1, source_target_pairs={{0,4},{4,0},{1,5},{5,1},{2,6},{6,2},{3,7},{7,3},{8,12},{12,8},{9,1... | collective-permute-start | bytes 3981320 | tf_op jit(solution)/shard_map/ppermute | solution.py:67
  595.3 35.9 %collective-permute-start.34 = (bf16[72,4608]{1,0:T(8,128)(2,1)S(1)}, bf16[72,4608]{1,0:T(8,128)(2,1)S(1)}, u32[]{:S(2)}, u32[]{:S(2)}) collective-permute-start(bf16[72,4608]{1,0:T(8,128)(2,1)S(1)} %add_convert_fusion.5.refs_0_), channel_id=1, source_target_pairs={{0,4},{4,0},{1,5},{5,1},{2,6},{6,2},{3,7},{7,3},{8,12},{12,8},{9,1... | collective-permute-start | bytes 1990664 | tf_op jit(solution)/shard_map/ppermute | solution.py:67
  627.9 4.5 collective-permute-start.31
  630.6 3.6 collective-permute-start.37
  630.7 4.5 collective-permute-start.35
  631.2 5.0 collective-permute-start.36
  631.3 33.0 %collective-permute-start.33 = (bf16[144,4608]{1,0:T(8,128)(2,1)}, bf16[144,4608]{1,0:T(8,128)(2,1)S(1)}, u32[]{:S(2)}, u32[]{:S(2)}) collective-permute-start(bf16[144,4608]{1,0:T(8,128)(2,1)} %reduce-scatter.8.cloned.1.call-done.refs_0_), channel_id=1, source_target_pairs={{0,4},{4,0},{1,5},{5,1},{2,6},{6,2},{3,7},{7,3},{8,12},{12,8},{9,1... | collective-permute-start | bytes 3981320 | tf_op jit(solution)/shard_map/ppermute | solution.py:67
  632.6 31.6 %collective-permute-start.32 = (bf16[72,4608]{1,0:T(8,128)(2,1)S(1)}, bf16[72,4608]{1,0:T(8,128)(2,1)S(1)}, u32[]{:S(2)}, u32[]{:S(2)}) collective-permute-start(bf16[72,4608]{1,0:T(8,128)(2,1)S(1)} %add_convert_fusion.6), channel_id=1, source_target_pairs={{0,16},{8,24},{16,0},{24,8},{1,17},{9,25},{17,1},{25,9},{2,18},{10... | collective-permute-start | bytes 1990664 | tf_op jit(solution)/shard_map/ppermute | solution.py:67
  634.6 44.9 %collective-permute-start.38 = (bf16[576,1152]{1,0:T(8,128)(2,1)S(1)}, bf16[576,1152]{1,0:T(8,128)(2,1)S(1)}, u32[]{:S(2)}, u32[]{:S(2)}) collective-permute-start(bf16[576,1152]{1,0:T(8,128)(2,1)S(1)} %add_convert_fusion.3), channel_id=1, source_target_pairs={{0,16},{8,24},{16,0},{24,8},{1,17},{9,25},{17,1},{25,9},{2,18},{10... | collective-permute-start | bytes 3981320 | tf_op jit(solution)/shard_map/ppermute | solution.py:67
  664.4 16.6 %collective-permute-start.39 = (bf16[72,4608]{1,0:T(8,128)(2,1)S(1)}, bf16[72,4608]{1,0:T(8,128)(2,1)S(1)}, u32[]{:S(2)}, u32[]{:S(2)}) collective-permute-start(bf16[72,4608]{1,0:T(8,128)(2,1)S(1)} %add_convert_fusion.4.refs_0_), channel_id=1, source_target_pairs={{0,4},{4,0},{1,5},{5,1},{2,6},{6,2},{3,7},{7,3},{8,12},{12,8},{9,1... | collective-permute-start | bytes 1990664 | tf_op jit(solution)/shard_map/ppermute | solution.py:67
  679.9 23.9 %collective-permute-start.42 = (bf16[576,1152]{1,0:T(8,128)(2,1)S(1)}, bf16[576,1152]{1,0:T(8,128)(2,1)S(1)}, u32[]{:S(2)}, u32[]{:S(2)}) collective-permute-start(bf16[576,1152]{1,0:T(8,128)(2,1)S(1)} %add_convert_fusion.2.refs_0_), channel_id=1, source_target_pairs={{0,8},{8,0},{16,24},{24,16},{1,9},{9,1},{17,25},{25,17},{2,10},{10... | collective-permute-start | bytes 3981320 | tf_op jit(solution)/shard_map/ppermute | solution.py:67
  680.6 7.7 %collective-permute-start.40 = (bf16[72,4608]{1,0:T(8,128)(2,1)S(1)}, bf16[72,4608]{1,0:T(8,128)(2,1)S(1)}, u32[]{:S(2)}, u32[]{:S(2)}) collective-permute-start(bf16[72,4608]{1,0:T(8,128)(2,1)S(1)} %add_convert_fusion.4.refs_0_), channel_id=1, source_target_pairs={{0,8},{8,0},{16,24},{24,16},{1,9},{9,1},{17,25},{25,17},{2,10},{10... | collective-permute-start | bytes 1990664 | tf_op jit(solution)/shard_map/ppermute | solution.py:67
  681.0 7.3 %collective-permute-start.41 = (bf16[72,4608]{1,0:T(8,128)(2,1)S(1)}, bf16[72,4608]{1,0:T(8,128)(2,1)S(1)}, u32[]{:S(2)}, u32[]{:S(2)}) collective-permute-start(bf16[72,4608]{1,0:T(8,128)(2,1)S(1)} %collective-permute-done.39.refs_1_), channel_id=1, source_target_pairs={{0,8},{8,0},{16,24},{24,16},{1,9},{9,1},{17,25},{25,17},{2,10},{10... | collective-permute-start | bytes 1990664 | tf_op jit(solution)/shard_map/ppermute | solution.py:67
  682.4 2.7 collective-permute-start.43
  (45 other events, 533.9 us)
Sparse Core Ops, SparseCore 0:
  11.6 172.9 all-gather.1
  222.5 181.0 reduce-scatter.3
  410.1 102.3 reduce-scatter.5
  519.8 96.3 reduce-scatter.7
